TPU v7x, 32 devices: a whole 2x2x4 slice. The times are simulated.
32 devices in a mesh: chan: 4 (over y, x), facet: 8 (over z, core).
Axes of the slice: x: 2, y: 2, z: 4, core: 2. Of those that a mesh axis runs over, the one named last changes fastest.
Arguments:
- dirty_image: float32 [64, 256, 256], P('chan', 'facet'), may hold values from -6 to 6
- image_start: float32 [64, 256, 256], P('chan', 'facet'), may hold values from 0 to 1
- dual_start: float32 [64, 2, 256, 256], P('chan', None, 'facet'), may hold values from -1.8 to 1.8
- psf_rows: float32 [64, 17], P('chan'), may hold values from -1 to 1, as said below
- psf_cols: float32 [64, 17], P('chan'), may hold values from -1 to 1, as said below
- wavelet_taps: float32 [2, 17], replicated, may hold values from -1 to 1, as said below
- channel_flags: int32 [64], P('chan'), may hold values 0 or 1
Outputs:
- image_final: float32 [64, 256, 256], P('chan', 'facet')
- dual_final: float32 [64, 2, 256, 256], P('chan', None, 'facet')
Inputs may be any that keep to these rules, and one draw needn't show every extreme that they name: `psf_rows`: each channel's taps have absolute values summing to 1. `psf_cols`: each channel's taps have absolute values summing to 1. `wavelet_taps`: each filter sums to zero and its absolute values sum to 1.
All inputs are finite; a program needn't handle non-finite values. No bound on the sum of `channel_flags` on one device may be relied on, other than what follows from the above.
Results may differ from a plain program's by a relative error of at most 0.0001.
Values sent between devices are 32-bit elements; how exact they have to be, the bound alone decides.
No kernel may reach another device: no remote copies, remote signals or barrier semaphores. Data moves between devices by JAX's collectives and lax.ppermute only.
A program may use at most 128 MiB of HBM per device.

v0:
```python
import functools

import jax
import jax.numpy as jnp
from jax import lax
from jax.experimental import pallas as pl
from jax.experimental.pallas import tpu as pltpu
from jax.sharding import PartitionSpec as P

PSF_HALF = 8
WAV_HALF = 8
OUTER = 2
INNER = 3

STEP_PRIMAL = 0.9
STEP_DUAL = 0.2
RADIUS_SCALE = 0.06
WEIGHT_OFFSET = 1.0

F32 = jnp.float32
BF16 = jnp.bfloat16
VMEM_LIMIT = 24 * 1024 * 1024
PARAMS = pltpu.CompilerParams(vmem_limit_bytes=VMEM_LIMIT)


def split(values):
    head = values.astype(BF16)
    return head, (values - head.astype(F32)).astype(BF16)


def times_columns(values, head, rest):
    rows = values.shape[0]
    first, second = split(values)
    both = jnp.dot(jnp.concatenate([first, second], axis=0), head, preferred_element_type=F32)
    return both[:rows] + both[rows:] + jnp.dot(first, rest, preferred_element_type=F32)


def stacked(values):
    first, second = split(values)
    return jnp.concatenate([first, second, first], axis=0)


VM = pl.BlockSpec(memory_space=pltpu.VMEM)
SM = pl.BlockSpec(memory_space=pltpu.SMEM)


def call(kernel, ins, outs, name, scalars=0):
    return pl.pallas_call(
        kernel,
        out_shape=[jax.ShapeDtypeStruct(*shape) for shape in outs],
        in_specs=[SM] * scalars + [VM] * (len(ins) - scalars),
        out_specs=[VM] * len(outs),
        compiler_params=PARAMS,
        name=name,
    )(*ins)


def rows_kernel(odd_ref, own_ref, near_ref, far_ref, mats_ref, dual_ref, old_ref, sum1_ref, band_ref, part_ref, moved_ref, sums_ref):
    chans, height, width = own_ref.shape
    reach = band_ref.shape[1]
    odd = odd_ref[0] == 1

    def body(c, total):
        near, far = near_ref[c], far_ref[c]
        before, after = jnp.where(odd, near, far), jnp.where(odd, far, near)
        extended = jnp.concatenate([before, own_ref[c], after], axis=0)
        product = jnp.dot(mats_ref[c], stacked(extended), preferred_element_type=F32)
        band = product[:reach]
        band_ref[c] = band
        part_ref[c] = product[reach:]
        moved = dual_ref[c] + STEP_DUAL * (2.0 * band - old_ref[c])
        moved_ref[c] = moved
        return total + moved * moved

    total = lax.fori_loop(0, chans, body, jnp.zeros((reach, width), F32), unroll=2)
    sums_ref[:reach] = total
    sums_ref[reach:] = sum1_ref[...]


def first_rows_kernel(
    odd_ref, own_ref, near_ref, far_ref, mats_ref, start_ref, dirty_ref, sum1_ref,
    band_ref, part_ref, dual_ref, data_ref, sums_ref,
):
    chans, height, width = own_ref.shape
    reach = band_ref.shape[1]
    send, edge = (mats_ref.shape[2] // 3 - height) // 2, (reach - height) // 2
    odd = odd_ref[0] == 1

    def body(c, total):
        near, far = near_ref[c], far_ref[c]
        before, after = jnp.where(odd, near, far), jnp.where(odd, far, near)
        extended = jnp.concatenate([before[:send], own_ref[c], after[:send]], axis=0)
        product = jnp.dot(mats_ref[c], stacked(extended), preferred_element_type=F32)
        band = product[:reach]
        band_ref[c] = band
        part_ref[c] = product[reach:]
        at = send + edge
        dual_ref[c] = jnp.concatenate([before[send:at], start_ref[c, 0], after[send:at]], axis=0)
        data_ref[c] = jnp.concatenate([before[at:], dirty_ref[c], after[at:]], axis=0)
        return total + band * band

    total = lax.fori_loop(0, chans, body, jnp.zeros((reach, width), F32), unroll=2)
    sums_ref[:reach] = total
    sums_ref[reach:] = sum1_ref[...]


def squares_kernel(first_ref, second_ref, out_ref):
    low = first_ref.shape[1]
    out_ref[:low] = jnp.sum(first_ref[...] * first_ref[...], axis=0)
    out_ref[low:] = jnp.sum(second_ref[...] * second_ref[...], axis=0)


def pack_kernel(est_ref, dual_ref, dirty_ref, near_ref, far_ref, sems):
    chans, height, width = est_ref.shape
    total = near_ref.shape[1]
    send, edge = total // 2, total // 4
    odd = lax.rem(lax.axis_index("facet"), 2)
    copies = []
    for out_ref, low in ((near_ref, 1 - odd), (far_ref, odd)):
        at = 0
        for ref, rows in (
            (est_ref, send), (dual_ref.at[:, 0], edge), (dirty_ref, edge)
        ):
            start = pl.multiple_of(low * (height - rows), 8)
            copies.append(
                pltpu.make_async_copy(
                    ref.at[:, pl.ds(start, rows)], out_ref.at[:, at : at + rows], sems.at[len(copies)]
                )
            )
            at += rows
    for copy in copies:
        copy.start()
    for copy in copies:
        copy.wait()


LANES = 128


def banded(line, rows):
    return pltpu.roll(
        jnp.broadcast_to(line, (rows, LANES)), 0, 1, stride=1, stride_axis=0
    )


def square_band(line, width, half):
    around = banded(line, LANES)
    offset = lax.broadcasted_iota(jnp.int32, (LANES, LANES), 1) - lax.broadcasted_iota(
        jnp.int32, (LANES, LANES), 0
    )
    parts = []
    for piece in split(around):
        piece = piece.astype(F32)
        middle = jnp.where(jnp.abs(offset) <= half, piece, 0.0).astype(BF16)
        right = jnp.where(offset <= half - LANES, piece, 0.0).astype(BF16)
        left = jnp.where(offset >= LANES - half, piece, 0.0).astype(BF16)
        blank = jnp.zeros((LANES, LANES), BF16)
        tiles = width // LANES
        kinds = {0: middle, 1: right, -1: left}
        parts.append(
            jnp.concatenate(
                [
                    jnp.concatenate([kinds.get(j - i, blank) for j in range(tiles)], axis=1)
                    for i in range(tiles)
                ],
                axis=0,
            )
        )
    return parts


def matrices_kernel(
    flags_ref, lines_ref, mats_ref, adj_ref, wav_rows_ref,
    around_head_ref, around_rest_ref, back_head_ref, back_rest_ref,
    wav_head_ref, wav_rest_ref, wav_head_t_ref, wav_rest_t_ref,
):
    chans, width = around_head_ref.shape[:2]
    both, tall = mats_ref.shape[1], mats_ref.shape[2] // 3
    height, reach = wav_rows_ref.shape[0], wav_rows_ref.shape[1] // 3
    edge = (reach - height) // 2
    facet, facets = lax.axis_index("facet"), lax.axis_size("facet")

    def inside(shape, dim):
        at = lax.broadcasted_iota(jnp.int32, shape, dim)
        low = jnp.where(facet > 0, 0, edge)
        high = jnp.where(facet < facets - 1, reach, reach - edge)
        return jnp.where((at >= low) & (at < high), 1.0, 0.0)

    def line(c, k):
        return lines_ref[c, :, k * LANES : (k + 1) * LANES]

    def wide_rows(matrix):
        first, second = split(matrix)
        first, second = first.astype(F32), second.astype(F32)
        return jnp.concatenate([first, first, second], axis=1).astype(BF16)

    wav_head_ref[...], wav_rest_ref[...] = square_band(line(chans, 0), width, WAV_HALF)
    wav_head_t_ref[...], wav_rest_t_ref[...] = square_band(line(chans, 1), width, WAV_HALF)
    wav_rows_ref[...] = wide_rows(banded(line(chans, 3), height)[:, :reach])
    band = wide_rows((banded(line(chans, 2), reach) * inside((reach, LANES), 0))[:, :tall])

    def body(c, carry):
        head, rest = square_band(line(c, 0), width, PSF_HALF)
        back_head, back_rest = square_band(line(c, 1), width, PSF_HALF)
        back_head_ref[c] = back_head
        back_rest_ref[c] = back_rest
        around = (
            jnp.dot(head, back_head, preferred_element_type=F32)
            + jnp.dot(rest, back_head, preferred_element_type=F32)
            + jnp.dot(head, back_rest, preferred_element_type=F32)
        )
        around_head_ref[c], around_rest_ref[c] = split(around)
        flag = flags_ref[c].astype(F32)
        adjoint = banded(line(c, 3), height) * flag
        adj_ref[c] = wide_rows(adjoint[:, :reach])
        adjoint = adjoint * inside((height, LANES), 1)
        forward = banded(line(c, 2), reach)
        first, second = split(adjoint[:, :reach])
        head, rest = split(forward)
        normal = (
            jnp.dot(first, head, preferred_element_type=F32)
            + jnp.dot(second, head, preferred_element_type=F32)
            + jnp.dot(first, rest, preferred_element_type=F32)
        )
        mats_ref[c, :reach] = band
        mats_ref[c, reach:] = wide_rows(normal[:, :tall])
        return carry

    lax.fori_loop(0, chans, body, 0)


def columns_kernel(own_ref, head_ref, rest_ref, dual_ref, old_ref, band_ref, moved_ref, sum_ref):
    chans, height, width = own_ref.shape
    group = 8
    total = jnp.zeros((height, width), F32)
    for c in range(0, chans, group):
        n = min(group, chans - c)
        band = times_columns(
            own_ref[c : c + n].reshape(n * height, width), head_ref[...], rest_ref[...]
        ).reshape(n, height, width)
        band_ref[c : c + n] = band
        moved = dual_ref[c : c + n] + STEP_DUAL * (2.0 * band - old_ref[c : c + n])
        moved_ref[c : c + n] = moved
        total = total + jnp.sum(moved * moved, axis=0)
    sum_ref[...] = total


def first_columns_kernel(own_ref, head_ref, rest_ref, band_ref, sum_ref):
    chans, height, width = own_ref.shape
    group = 8
    total = jnp.zeros((height, width), F32)
    for c in range(0, chans, group):
        n = min(group, chans - c)
        band = times_columns(
            own_ref[c : c + n].reshape(n * height, width), head_ref[...], rest_ref[...]
        ).reshape(n, height, width)
        band_ref[c : c + n] = band
        total = total + jnp.sum(band * band, axis=0)
    sum_ref[...] = total


def first_gradient_kernel(
    part_ref, head_ref, rest_ref, dirty_ref, back_head_ref, back_rest_ref, adj_ref, data_ref, grad_ref
):
    chans = part_ref.shape[0]

    def body(c, carry):
        across = times_columns(dirty_ref[c], back_head_ref[c], back_rest_ref[c])
        data = jnp.dot(adj_ref[c], stacked(across), preferred_element_type=F32)
        data_ref[c] = data
        grad_ref[c] = times_columns(part_ref[c], head_ref[c], rest_ref[c]) - data
        return carry

    lax.fori_loop(0, chans, body, 0, unroll=2)


def gradient_kernel(part_ref, head_ref, rest_ref, data_ref, grad_ref):
    chans = part_ref.shape[0]

    def body(c, carry):
        grad_ref[c] = times_columns(part_ref[c], head_ref[c], rest_ref[c]) - data_ref[c]
        return carry

    lax.fori_loop(0, chans, body, 0, unroll=2)


def scaled(sums_refs, radius):
    total = sums_refs[0][...]
    for ref in sums_refs[1:]:
        total = total + ref[...]
    length = jnp.sqrt(total)
    return radius / jnp.maximum(length, radius)


def radius_kernel(factor, *refs):
    *sums_refs, out_ref = refs
    total = sums_refs[0][...]
    for ref in sums_refs[1:]:
        total = total + ref[...]
    out_ref[...] = factor / (jnp.sqrt(total) + WEIGHT_OFFSET)


def update_kernel(n_sums, odd_ref, *refs):
    sums_refs, refs = refs[:n_sums], refs[n_sums:]
    if n_sums:
        radius_ref, refs = refs[0], refs[1:]
    (
        moved0_ref, moved1_ref, own_ref, grad_ref, rows_ref, head_ref, rest_ref,
        new_ref, near_ref, far_ref, *duals,
    ) = refs
    chans, height, width = own_ref.shape
    reach = moved0_ref.shape[1]
    send = near_ref.shape[1]
    odd = odd_ref[0] == 1
    if n_sums:
        dual0_ref, dual1_ref = duals
        scale = scaled(sums_refs, radius_ref[...])
        scale0, scale1 = scale[:reach], scale[reach:]
    group = 4
    for c0 in range(0, chans, group):
        n = min(group, chans - c0)
        dual1 = moved1_ref[c0 : c0 + n]
        if n_sums:
            dual1 = dual1 * scale1[None]
            dual1_ref[c0 : c0 + n] = dual1
        across = times_columns(dual1.reshape(n * height, width), head_ref[...], rest_ref[...])
        for c in range(c0, c0 + n):
            dual0 = moved0_ref[c]
            if n_sums:
                dual0 = dual0 * scale0
                dual0_ref[c] = dual0
            down = jnp.dot(rows_ref[...], stacked(dual0), preferred_element_type=F32)
            at = (c - c0) * height
            step = grad_ref[c] + (down + across[at : at + height])
            new = jnp.maximum(own_ref[c] - STEP_PRIMAL * step, 0.0)
            new_ref[c] = new
            top, bottom = new[:send], new[height - send :]
            near_ref[c] = jnp.where(odd, top, bottom)
            far_ref[c] = jnp.where(odd, bottom, top)


def final_kernel(n_sums, *refs):
    sums_refs, refs = refs[:n_sums], refs[n_sums:]
    radius_ref, moved0_ref, moved1_ref, dual_ref = refs
    height = moved1_ref.shape[1]
    reach = moved0_ref.shape[1]
    pad = (reach - height) // 2
    scale = scaled(sums_refs, radius_ref[...])
    scale0, scale1 = scale[pad : pad + height], scale[reach:]
    for c in range(moved1_ref.shape[0]):
        dual_ref[c, 0] = moved0_ref[c, pad : pad + height] * scale0
        dual_ref[c, 1] = moved1_ref[c] * scale1


def exchange(near, far):
    n = lax.axis_size("facet")
    pair = [(i, i ^ 1) for i in range(n)]
    cross = [(i, ((i + 1) ^ 1) - 1) for i in range(n) if 0 <= ((i + 1) ^ 1) - 1 < n]
    return lax.ppermute(near, "facet", pair), lax.ppermute(far, "facet", cross)


def gathered(sums):
    n = lax.axis_size("chan")
    if n & (n - 1):
        return [lax.psum(sums, "chan")]
    low = 1
    terms = [sums]
    while low < n:
        radix = min(4, n // low)
        total = terms[0]
        for term in terms[1:]:
            total = total + term
        terms = [total] + [
            lax.ppermute(total, "chan", [(i, i ^ (k * low)) for i in range(n)])
            for k in range(1, radix)
        ]
        low *= radix
    return terms


def on_device(
    dirty_image, image_start, dual_start, psf_rows, psf_cols, wavelet_taps, channel_flags
):
    chans, height, width = image_start.shape
    total_chans = chans * lax.axis_size("chan")
    edge = max(PSF_HALF, WAV_HALF)
    reach, send = height + 2 * edge, 2 * edge
    tall = height + 2 * send
    passes = OUTER * INNER
    odd = (lax.axis_index("facet") % 2).astype(jnp.int32)[None]

    own = ((chans, height, width), F32)
    taller = ((chans, reach, width), F32)
    sides = ((chans, send, width), F32)
    summed = ((reach + height, width), F32)
    square = ((width, width), BF16)
    squares = ((chans, width, width), BF16)

    first_sides = ((chans, 2 * send, width), F32)
    near, far = pl.pallas_call(
        pack_kernel,
        out_shape=[jax.ShapeDtypeStruct(*first_sides)] * 2,
        in_specs=[pl.BlockSpec(memory_space=pltpu.HBM)] * 3,
        out_specs=[VM] * 2,
        scratch_shapes=[pltpu.SemaphoreType.DMA((6,))],
        compiler_params=PARAMS,
        name="pack",
    )(image_start, dual_start, dirty_image)
    near, far = exchange(near, far)

    def lines(cols, rows, half_c, half_r):
        def circle(taps, half):
            gap = jnp.zeros((taps.shape[0], LANES - 2 * half - 1), F32)
            return jnp.concatenate([taps[:, half:], gap, taps[:, :half]], axis=1)

        def ramp(taps, half):
            lead = jnp.zeros((taps.shape[0], edge - half), F32)
            gap = jnp.zeros((taps.shape[0], LANES - half - edge - 1), F32)
            return jnp.concatenate([lead, taps, gap], axis=1)

        return jnp.concatenate(
            [circle(cols[:, ::-1], half_c), circle(cols, half_c), ramp(rows, half_r), ramp(rows[:, ::-1], half_r)],
            axis=1,
        )

    table = jnp.concatenate(
        [
            lines(psf_cols, psf_rows, PSF_HALF, PSF_HALF),
            lines(wavelet_taps[1:2], wavelet_taps[0:1], WAV_HALF, WAV_HALF),
        ],
        axis=0,
    )
    (
        mats, adjoint, wav_rows, around_head, around_rest, back_head, back_rest,
        wav_head, wav_rest, wav_head_t, wav_rest_t,
    ) = call(
        matrices_kernel, (channel_flags, table[:, None]),
        (
            ((chans, reach + height, 3 * tall), BF16), ((chans, height, 3 * reach), BF16),
            ((height, 3 * reach), BF16), squares, squares, squares, squares,
            square, square, square, square,
        ),
        "matrices", 1,
    )
    band1, sum1 = call(
        first_columns_kernel, (image_start, wav_head, wav_rest), (own, ((height, width), F32)), "first_columns"
    )
    band0, part, dual0, dirty, weight_sums = call(
        first_rows_kernel, (odd, image_start, near, far, mats, dual_start, dirty_image, sum1),
        (taller, own, taller, taller, summed), "first_rows", 1,
    )
    data, grad = call(
        first_gradient_kernel,
        (part, around_head, around_rest, dirty, back_head, back_rest, adjoint), (own, own), "first_gradient",
    )
    dual1 = dual_start[:, 1]
    estimate, near, far = call(
        functools.partial(update_kernel, 0),
        (odd, dual0, dual1, image_start, grad, wav_rows, wav_head_t, wav_rest_t),
        (own, sides, sides), "first_update", 1,
    )
    for step in range(passes):
        near, far = exchange(near, far)
        if step % INNER == 0:
            terms = gathered(weight_sums)
        band1, moved1, sum1 = call(
            columns_kernel, (estimate, wav_head, wav_rest, dual1, band1),
            (own, own, ((height, width), F32)), "columns",
        )
        if step % INNER == 0:
            radius = call(
                functools.partial(radius_kernel, RADIUS_SCALE * total_chans), tuple(terms), (summed,), "radius"
            )[0]
        band0, part, moved0, sums = call(
            rows_kernel, (odd, estimate, near, far, mats, dual0, band0, sum1),
            (taller, own, taller, summed), "rows", 1,
        )
        terms = gathered(sums)
        if step % INNER == INNER - 1 and step + 1 < passes:
            weight_sums = call(squares_kernel, (band0, band1), (summed,), "squares")[0]
        if step + 1 < passes:
            grad = call(gradient_kernel, (part, around_head, around_rest, data), (own,), "gradient")[0]
            estimate, near, far, dual0, dual1 = call(
                functools.partial(update_kernel, len(terms)),
                (odd, *terms, radius, moved0, moved1, estimate, grad, wav_rows, wav_head_t, wav_rest_t),
                (own, sides, sides, taller, own), "update", 1,
            )
        else:
            dual_final = call(
                functools.partial(final_kernel, len(terms)), (*terms, radius, moved0, moved1),
                (((chans, 2, height, width), F32),), "final",
            )[0]
    return (estimate, dual_final)


def solution(mesh):
    return jax.shard_map(
        on_device,
        mesh=mesh,
        in_specs=(
            P("chan", "facet", None),
            P("chan", "facet", None),
            P("chan", None, "facet", None),
            P("chan", None),
            P("chan", None),
            P(),
            P("chan"),
        ),
        out_specs=(P("chan", "facet", None), P("chan", None, "facet", None)),
        check_vma=False,
    )
```

profile of v0, /device:TPU:16, one launch (start us, length us, event | category | flops | bytes accessed | tf_op | source)
XLA Modules:
  0.0 130.9 jit_solution(5674239495448755226)
XLA Ops:
  1.7 1.2 copy-done.2
  5.2 2.4 %collective-permute-start.1 = (f32[16,32,256]{2,1,0:T(8,128)}, f32[16,32,256]{2,1,0:T(8,128)S(1)}, u32[]{:S(2)}, u32[]{:S(2)}) collective-permute-start(f32[16,32,256]{2,1,0:T(8,128)} %get-tuple-element.92), channel_id=1, source_target_pairs={{1,2},{2,1},{3,4},{4,3},{5,6},{6,5},{9,10},{10,9},{11,12},{12,11},... | collective-permute-start | bytes 1572872 | tf_op jit(solution)/shard_map/ppermute | solution.py:359
  8.8 7.7 %matrices.1 = (bf16[16,80,192]{2,1,0:T(8,128)(2,1)S(1)}, bf16[16,32,144]{2,1,0:T(8,128)(2,1)S(1)}, bf16[32,144]{1,0:T(8,128)(2,1)S(1)}, bf16[16,256,256]{2,1,0:T...) custom-call(s32[16]{0:T(128)S(1)} %copy-done.8, ...), custom_call_target="tpu_custom_call" | custom-call | tf_op jit(solution)/shard_map/matrices/pallas_call | solution.py:48
  17.0 1.5 %first_rows.1 = (f32[16,48,256]{2,1,0:T(8,128)S(1)}, f32[16,32,256]{2,1,0:T(8,128)S(1)}, f32[16,48,256]{2,1,0:T(8,128)S(1)}, f32[16,48,256]{2,1,0:T(8,128)S(1)}, f32[80,256]{1,0:T(8,128)S(1)}) custom-call(s32[1]{0:T(128)} %bitcast.odd_ref, f32[16,32,256]{2,1,0:T(8,128)S(1)} %copy-done.1, f32[16,32,256]{2,1,0:T(8,128)S(1)} %collective-permute-done.near_ref, ...), custom_call_target="tpu_custom_call" | custom-call | tf_op jit(solution)/shard_map/first_rows/pallas_call | solution.py:48
  18.5 3.8 %first_gradient.1 = (f32[16,32,256]{2,1,0:T(8,128)S(1)}, f32[16,32,256]{2,1,0:T(8,128)S(1)}) custom-call(f32[16,32,256]{2,1,0:T(8,128)S(1)} %get-tuple-element.98.part_ref, bf16[16,256,256]{2,1,0:T(8,128)(2,1)S(1)} %get-tuple-element.99.head_ref, bf16[16,256,256]{2,1,0:T(8,128)(2,1)S(1)} %get-tuple-element.100.rest_ref, ...), custom_call_target="tpu_custom_call" | custom-call | tf_op jit(solution)/shard_map/first_gradient/pallas_call | solution.py:48
  22.9 1.2 collective-permute-start.2
  24.1 2.0 %collective-permute-start.3 = (f32[16,16,256]{2,1,0:T(8,128)S(1)}, f32[16,16,256]{2,1,0:T(8,128)S(1)}, u32[]{:S(2)}, u32[]{:S(2)}) collective-permute-start(f32[16,16,256]{2,1,0:T(8,128)S(1)} %get-tuple-element.111), channel_id=1, source_target_pairs={{1,2},{2,1},{3,4},{4,3},{5,6},{6,5},{9,10},{10,9},{11,12},{12,11},... | collective-permute-start | bytes 786440 | tf_op jit(solution)/shard_map/ppermute | solution.py:359
  26.1 1.6 %collective-permute-start.7 = (f32[80,256]{1,0:T(8,128)S(1)}, f32[80,256]{1,0:T(8,128)S(1)}, u32[]{:S(2)}, u32[]{:S(2)}) collective-permute-start(f32[80,256]{1,0:T(8,128)S(1)} %get-tuple-element.116.refs_0_), channel_id=1, source_target_pairs={{0,8},{8,0},{16,24},{24,16},{1,9},{9,1},{17,25},{25,17},{2,10},{10... | collective-permute-start | bytes 245768 | tf_op jit(solution)/shard_map/ppermute | solution.py:374
  27.7 1.5 %collective-permute-start.8 = (f32[80,256]{1,0:T(8,128)S(1)}, f32[80,256]{1,0:T(8,128)S(1)}, u32[]{:S(2)}, u32[]{:S(2)}) collective-permute-start(f32[80,256]{1,0:T(8,128)S(1)} %get-tuple-element.116.refs_0_), channel_id=1, source_target_pairs={{0,16},{8,24},{16,0},{24,8},{1,17},{9,25},{17,1},{25,9},{2,18},{10... | collective-permute-start | bytes 245768 | tf_op jit(solution)/shard_map/ppermute | solution.py:374
  30.1 1.7 %collective-permute-done.3.far_ref = f32[16,16,256]{2,1,0:T(8,128)S(1)} collective-permute-done((f32[16,16,256]{2,1,0:T(8,128)S(1)}, f32[16,16,256]{2,1,0:T(8,128)S(1)}, u32[]{:S(2)}, u32[]{:S(2)}) %collective-permute-start.3) | collective-permute-done | bytes 262176 | tf_op jit(solution)/shard_map/ppermute | solution.py:359
  31.8 1.5 %rows.6 = (f32[16,48,256]{2,1,0:T(8,128)S(1)}, f32[16,32,256]{2,1,0:T(8,128)S(1)}, f32[16,48,256]{2,1,0:T(8,128)S(1)}, f32[80,256]{1,0:T(8,128)S(1)}) custom-call(s32[1]{0:T(128)} %bitcast.odd_ref, f32[16,32,256]{2,1,0:T(8,128)S(1)} %get-tuple-element.109.own_ref.refs_7_, f32[16,16,256]{2,1,0:T(8,128)S(1)} %collective-permute-done.2.near_ref, ...), custom_call_target="tpu_custom_call" | custom-call | tf_op jit(solution)/shard_map/rows/pallas_call | solution.py:48
  33.3 1.6 %collective-permute-start.4 = (f32[80,256]{1,0:T(8,128)S(1)}, f32[80,256]{1,0:T(8,128)S(1)}, u32[]{:S(2)}, u32[]{:S(2)}) collective-permute-start(f32[80,256]{1,0:T(8,128)S(1)} %get-tuple-element.115.refs_0_), channel_id=1, source_target_pairs={{0,8},{8,0},{16,24},{24,16},{1,9},{9,1},{17,25},{25,17},{2,10},{10... | collective-permute-start | bytes 245768 | tf_op jit(solution)/shard_map/ppermute | solution.py:374
  34.8 1.5 %collective-permute-start.5 = (f32[80,256]{1,0:T(8,128)S(1)}, f32[80,256]{1,0:T(8,128)S(1)}, u32[]{:S(2)}, u32[]{:S(2)}) collective-permute-start(f32[80,256]{1,0:T(8,128)S(1)} %get-tuple-element.115.refs_0_), channel_id=1, source_target_pairs={{0,16},{8,24},{16,0},{24,8},{1,17},{9,25},{17,1},{25,9},{2,18},{10... | collective-permute-start | bytes 245768 | tf_op jit(solution)/shard_map/ppermute | solution.py:374
  36.9 1.6 %gradient.5.refs_8_ = f32[16,32,256]{2,1,0:T(8,128)S(1)} custom-call(f32[16,32,256]{2,1,0:T(8,128)S(1)} %get-tuple-element.119.part_ref, bf16[16,256,256]{2,1,0:T(8,128)(2,1)S(1)} %get-tuple-element.99.head_ref, bf16[16,256,256]{2,1,0:T(8,128)(2,1)S(1)} %get-tuple-element.100.rest_ref, f32[16,32,256]{2,1,0:T(8,128)S(1)} %get-tuple-element.120.data_ref), custom_call_target="tpu_custom_call" | custom-call | tf_op jit(solution)/shard_map/gradient/pallas_call | solution.py:48
  38.5 1.6 %collective-permute-done.5.refs_2_ = f32[80,256]{1,0:T(8,128)S(1)} collective-permute-done((f32[80,256]{1,0:T(8,128)S(1)}, f32[80,256]{1,0:T(8,128)S(1)}, u32[]{:S(2)}, u32[]{:S(2)}) %collective-permute-start.5) | collective-permute-done | bytes 81952 | tf_op jit(solution)/shard_map/ppermute | solution.py:374
  40.1 1.6 %collective-permute-done.6.refs_3_ = f32[80,256]{1,0:T(8,128)S(1)} collective-permute-done((f32[80,256]{1,0:T(8,128)S(1)}, f32[80,256]{1,0:T(8,128)S(1)}, u32[]{:S(2)}, u32[]{:S(2)}) %collective-permute-start.6) | collective-permute-done | bytes 81952 | tf_op jit(solution)/shard_map/ppermute | solution.py:374
  42.4 2.4 %collective-permute-start.11 = (f32[16,16,256]{2,1,0:T(8,128)S(1)}, f32[16,16,256]{2,1,0:T(8,128)S(1)}, u32[]{:S(2)}, u32[]{:S(2)}) collective-permute-start(f32[16,16,256]{2,1,0:T(8,128)S(1)} %get-tuple-element.123), channel_id=1, source_target_pairs={{1,2},{2,1},{3,4},{4,3},{5,6},{6,5},{9,10},{10,9},{11,12},{12,11},... | collective-permute-start | bytes 786440 | tf_op jit(solution)/shard_map/ppermute | solution.py:359
  45.3 4.8 %collective-permute-done.11.far_ref = f32[16,16,256]{2,1,0:T(8,128)S(1)} collective-permute-done((f32[16,16,256]{2,1,0:T(8,128)S(1)}, f32[16,16,256]{2,1,0:T(8,128)S(1)}, u32[]{:S(2)}, u32[]{:S(2)}) %collective-permute-start.11) | collective-permute-done | bytes 262176 | tf_op jit(solution)/shard_map/ppermute | solution.py:359
  50.1 1.5 %rows.7 = (f32[16,48,256]{2,1,0:T(8,128)S(1)}, f32[16,32,256]{2,1,0:T(8,128)S(1)}, f32[16,48,256]{2,1,0:T(8,128)S(1)}, f32[80,256]{1,0:T(8,128)S(1)}) custom-call(s32[1]{0:T(128)} %bitcast.odd_ref, f32[16,32,256]{2,1,0:T(8,128)S(1)} %get-tuple-element.121.own_ref.refs_7_, f32[16,16,256]{2,1,0:T(8,128)S(1)} %collective-permute-done.10.near_ref, ...), custom_call_target="tpu_custom_call" | custom-call | tf_op jit(solution)/shard_map/rows/pallas_call | solution.py:48
  53.0 2.1 %collective-permute-start.14 = (f32[80,256]{1,0:T(8,128)S(1)}, f32[80,256]{1,0:T(8,128)S(1)}, u32[]{:S(2)}, u32[]{:S(2)}) collective-permute-start(f32[80,256]{1,0:T(8,128)S(1)} %get-tuple-element.129.refs_0_), channel_id=1, source_target_pairs={{0,24},{8,16},{16,8},{24,0},{1,25},{9,17},{17,9},{25,1},{2,26},{10... | collective-permute-start | bytes 245768 | tf_op jit(solution)/shard_map/ppermute | solution.py:374
  55.1 1.6 %gradient.6.refs_8_ = f32[16,32,256]{2,1,0:T(8,128)S(1)} custom-call(f32[16,32,256]{2,1,0:T(8,128)S(1)} %get-tuple-element.132.part_ref, bf16[16,256,256]{2,1,0:T(8,128)(2,1)S(1)} %get-tuple-element.99.head_ref, bf16[16,256,256]{2,1,0:T(8,128)(2,1)S(1)} %get-tuple-element.100.rest_ref, f32[16,32,256]{2,1,0:T(8,128)S(1)} %get-tuple-element.120.data_ref), custom_call_target="tpu_custom_call" | custom-call | tf_op jit(solution)/shard_map/gradient/pallas_call | solution.py:48
  57.0 1.5 %collective-permute-done.14.refs_3_ = f32[80,256]{1,0:T(8,128)S(1)} collective-permute-done((f32[80,256]{1,0:T(8,128)S(1)}, f32[80,256]{1,0:T(8,128)S(1)}, u32[]{:S(2)}, u32[]{:S(2)}) %collective-permute-start.14) | collective-permute-done | bytes 81952 | tf_op jit(solution)/shard_map/ppermute | solution.py:374
  59.2 2.4 %collective-permute-start.16 = (f32[16,16,256]{2,1,0:T(8,128)S(1)}, f32[16,16,256]{2,1,0:T(8,128)S(1)}, u32[]{:S(2)}, u32[]{:S(2)}) collective-permute-start(f32[16,16,256]{2,1,0:T(8,128)S(1)} %get-tuple-element.135), channel_id=1, source_target_pairs={{1,2},{2,1},{3,4},{4,3},{5,6},{6,5},{9,10},{10,9},{11,12},{12,11},... | collective-permute-start | bytes 786440 | tf_op jit(solution)/shard_map/ppermute | solution.py:359
  62.1 4.8 %collective-permute-done.16.far_ref = f32[16,16,256]{2,1,0:T(8,128)S(1)} collective-permute-done((f32[16,16,256]{2,1,0:T(8,128)S(1)}, f32[16,16,256]{2,1,0:T(8,128)S(1)}, u32[]{:S(2)}, u32[]{:S(2)}) %collective-permute-start.16) | collective-permute-done | bytes 262176 | tf_op jit(solution)/shard_map/ppermute | solution.py:359
  66.9 1.5 %rows.8 = (f32[16,48,256]{2,1,0:T(8,128)S(1)}, f32[16,32,256]{2,1,0:T(8,128)S(1)}, f32[16,48,256]{2,1,0:T(8,128)S(1)}, f32[80,256]{1,0:T(8,128)S(1)}) custom-call(s32[1]{0:T(128)} %bitcast.odd_ref, f32[16,32,256]{2,1,0:T(8,128)S(1)} %get-tuple-element.133.own_ref.refs_7_, f32[16,16,256]{2,1,0:T(8,128)S(1)} %collective-permute-done.15.near_ref, ...), custom_call_target="tpu_custom_call" | custom-call | tf_op jit(solution)/shard_map/rows/pallas_call | solution.py:48
  68.4 1.5 %collective-permute-start.17 = (f32[80,256]{1,0:T(8,128)S(1)}, f32[80,256]{1,0:T(8,128)S(1)}, u32[]{:S(2)}, u32[]{:S(2)}) collective-permute-start(f32[80,256]{1,0:T(8,128)S(1)} %get-tuple-element.141.refs_0_), channel_id=1, source_target_pairs={{0,8},{8,0},{16,24},{24,16},{1,9},{9,1},{17,25},{25,17},{2,10},{10... | collective-permute-start | bytes 245768 | tf_op jit(solution)/shard_map/ppermute | solution.py:374
  71.9 1.6 %gradient.7.refs_8_ = f32[16,32,256]{2,1,0:T(8,128)S(1)} custom-call(f32[16,32,256]{2,1,0:T(8,128)S(1)} %get-tuple-element.144.part_ref, bf16[16,256,256]{2,1,0:T(8,128)(2,1)S(1)} %get-tuple-element.99.head_ref, bf16[16,256,256]{2,1,0:T(8,128)(2,1)S(1)} %get-tuple-element.100.rest_ref, f32[16,32,256]{2,1,0:T(8,128)S(1)} %get-tuple-element.120.data_ref), custom_call_target="tpu_custom_call" | custom-call | tf_op jit(solution)/shard_map/gradient/pallas_call | solution.py:48
  74.5 1.8 %collective-permute-done.19.refs_3_ = f32[80,256]{1,0:T(8,128)S(1)} collective-permute-done((f32[80,256]{1,0:T(8,128)S(1)}, f32[80,256]{1,0:T(8,128)S(1)}, u32[]{:S(2)}, u32[]{:S(2)}) %collective-permute-start.19) | collective-permute-done | bytes 81952 | tf_op jit(solution)/shard_map/ppermute | solution.py:374
  77.0 2.4 %collective-permute-start.21 = (f32[16,16,256]{2,1,0:T(8,128)S(1)}, f32[16,16,256]{2,1,0:T(8,128)S(1)}, u32[]{:S(2)}, u32[]{:S(2)}) collective-permute-start(f32[16,16,256]{2,1,0:T(8,128)S(1)} %get-tuple-element.147), channel_id=1, source_target_pairs={{1,2},{2,1},{3,4},{4,3},{5,6},{6,5},{9,10},{10,9},{11,12},{12,11},... | collective-permute-start | bytes 786440 | tf_op jit(solution)/shard_map/ppermute | solution.py:359
  81.3 1.8 %collective-permute-start.27 = (f32[80,256]{1,0:T(8,128)S(1)}, f32[80,256]{1,0:T(8,128)S(1)}, u32[]{:S(2)}, u32[]{:S(2)}) collective-permute-start(f32[80,256]{1,0:T(8,128)S(1)} %squares.1.refs_0_), channel_id=1, source_target_pairs={{0,24},{8,16},{16,8},{24,0},{1,25},{9,17},{17,9},{25,1},{2,26},{10... | collective-permute-start | bytes 245768 | tf_op jit(solution)/shard_map/ppermute | solution.py:374
  84.7 1.4 %rows.9 = (f32[16,48,256]{2,1,0:T(8,128)S(1)}, f32[16,32,256]{2,1,0:T(8,128)S(1)}, f32[16,48,256]{2,1,0:T(8,128)S(1)}, f32[80,256]{1,0:T(8,128)S(1)}) custom-call(s32[1]{0:T(128)} %bitcast.odd_ref, f32[16,32,256]{2,1,0:T(8,128)S(1)} %get-tuple-element.145.own_ref.refs_7_, f32[16,16,256]{2,1,0:T(8,128)S(1)} %collective-permute-done.20.near_ref, ...), custom_call_target="tpu_custom_call" | custom-call | tf_op jit(solution)/shard_map/rows/pallas_call | solution.py:48
  87.9 1.8 %collective-permute-start.24 = (f32[80,256]{1,0:T(8,128)S(1)}, f32[80,256]{1,0:T(8,128)S(1)}, u32[]{:S(2)}, u32[]{:S(2)}) collective-permute-start(f32[80,256]{1,0:T(8,128)S(1)} %get-tuple-element.153.refs_0_), channel_id=1, source_target_pairs={{0,24},{8,16},{16,8},{24,0},{1,25},{9,17},{17,9},{25,1},{2,26},{10... | collective-permute-start | bytes 245768 | tf_op jit(solution)/shard_map/ppermute | solution.py:374
  89.8 1.6 %gradient.8.refs_8_ = f32[16,32,256]{2,1,0:T(8,128)S(1)} custom-call(f32[16,32,256]{2,1,0:T(8,128)S(1)} %get-tuple-element.156.part_ref, bf16[16,256,256]{2,1,0:T(8,128)(2,1)S(1)} %get-tuple-element.99.head_ref, bf16[16,256,256]{2,1,0:T(8,128)(2,1)S(1)} %get-tuple-element.100.rest_ref, f32[16,32,256]{2,1,0:T(8,128)S(1)} %get-tuple-element.120.data_ref), custom_call_target="tpu_custom_call" | custom-call | tf_op jit(solution)/shard_map/gradient/pallas_call | solution.py:48
  91.9 1.6 %collective-permute-done.24.refs_3_ = f32[80,256]{1,0:T(8,128)S(1)} collective-permute-done((f32[80,256]{1,0:T(8,128)S(1)}, f32[80,256]{1,0:T(8,128)S(1)}, u32[]{:S(2)}, u32[]{:S(2)}) %collective-permute-start.24) | collective-permute-done | bytes 81952 | tf_op jit(solution)/shard_map/ppermute | solution.py:374
  94.3 2.4 %collective-permute-start.29 = (f32[16,16,256]{2,1,0:T(8,128)S(1)}, f32[16,16,256]{2,1,0:T(8,128)S(1)}, u32[]{:S(2)}, u32[]{:S(2)}) collective-permute-start(f32[16,16,256]{2,1,0:T(8,128)S(1)} %get-tuple-element.159), channel_id=1, source_target_pairs={{1,2},{2,1},{3,4},{4,3},{5,6},{6,5},{9,10},{10,9},{11,12},{12,11},... | collective-permute-start | bytes 786440 | tf_op jit(solution)/shard_map/ppermute | solution.py:359
  97.2 4.8 %collective-permute-done.29.far_ref = f32[16,16,256]{2,1,0:T(8,128)S(1)} collective-permute-done((f32[16,16,256]{2,1,0:T(8,128)S(1)}, f32[16,16,256]{2,1,0:T(8,128)S(1)}, u32[]{:S(2)}, u32[]{:S(2)}) %collective-permute-start.29) | collective-permute-done | bytes 262176 | tf_op jit(solution)/shard_map/ppermute | solution.py:359
  102.0 1.4 %rows.10 = (f32[16,48,256]{2,1,0:T(8,128)S(1)}, f32[16,32,256]{2,1,0:T(8,128)S(1)}, f32[16,48,256]{2,1,0:T(8,128)S(1)}, f32[80,256]{1,0:T(8,128)S(1)}) custom-call(s32[1]{0:T(128)} %bitcast.odd_ref, f32[16,32,256]{2,1,0:T(8,128)S(1)} %get-tuple-element.157.own_ref.refs_7_, f32[16,16,256]{2,1,0:T(8,128)S(1)} %collective-permute-done.28.near_ref, ...), custom_call_target="tpu_custom_call" | custom-call | tf_op jit(solution)/shard_map/rows/pallas_call | solution.py:48
  103.4 1.4 %collective-permute-start.30 = (f32[80,256]{1,0:T(8,128)S(1)}, f32[80,256]{1,0:T(8,128)S(1)}, u32[]{:S(2)}, u32[]{:S(2)}) collective-permute-start(f32[80,256]{1,0:T(8,128)S(1)} %get-tuple-element.165.refs_0_), channel_id=1, source_target_pairs={{0,8},{8,0},{16,24},{24,16},{1,9},{9,1},{17,25},{25,17},{2,10},{10... | collective-permute-start | bytes 245768 | tf_op jit(solution)/shard_map/ppermute | solution.py:374
  105.8 1.2 collective-permute-start.32
  107.0 1.6 %gradient.9.refs_8_ = f32[16,32,256]{2,1,0:T(8,128)S(1)} custom-call(f32[16,32,256]{2,1,0:T(8,128)S(1)} %get-tuple-element.168.part_ref, bf16[16,256,256]{2,1,0:T(8,128)(2,1)S(1)} %get-tuple-element.99.head_ref, bf16[16,256,256]{2,1,0:T(8,128)(2,1)S(1)} %get-tuple-element.100.rest_ref, f32[16,32,256]{2,1,0:T(8,128)S(1)} %get-tuple-element.120.data_ref), custom_call_target="tpu_custom_call" | custom-call | tf_op jit(solution)/shard_map/gradient/pallas_call | solution.py:48
  108.6 1.7 %collective-permute-done.31.refs_2_ = f32[80,256]{1,0:T(8,128)S(1)} collective-permute-done((f32[80,256]{1,0:T(8,128)S(1)}, f32[80,256]{1,0:T(8,128)S(1)}, u32[]{:S(2)}, u32[]{:S(2)}) %collective-permute-start.31) | collective-permute-done | bytes 81952 | tf_op jit(solution)/shard_map/ppermute | solution.py:374
  111.1 1.4 %update.9 = (f32[16,32,256]{2,1,0:T(8,128)}, f32[16,16,256]{2,1,0:T(8,128)S(1)}, f32[16,16,256]{2,1,0:T(8,128)S(1)}, f32[16,48,256]{2,1,0:T(8,128)S(1)}, f32[16,32,256]{2,1,0:T(8,128)S(1)}) custom-call(s32[1]{0:T(128)} %bitcast.odd_ref, f32[80,256]{1,0:T(8,128)S(1)} %get-tuple-element.165.refs_0_, f32[80,256]{1,0:T(8,128)S(1)} %collective-permute-done.30.refs_1_, ...), custom_call_target="tpu_custom_call" | custom-call | tf_op jit(solution)/shard_map/update/pallas_call | solution.py:48
  112.6 2.5 %collective-permute-start.34 = (f32[16,16,256]{2,1,0:T(8,128)S(1)}, f32[16,16,256]{2,1,0:T(8,128)S(1)}, u32[]{:S(2)}, u32[]{:S(2)}) collective-permute-start(f32[16,16,256]{2,1,0:T(8,128)S(1)} %get-tuple-element.171), channel_id=1, source_target_pairs={{1,2},{2,1},{3,4},{4,3},{5,6},{6,5},{9,10},{10,9},{11,12},{12,11},... | collective-permute-start | bytes 786440 | tf_op jit(solution)/shard_map/ppermute | solution.py:359
  117.3 3.0 %collective-permute-done.34.far_ref = f32[16,16,256]{2,1,0:T(8,128)S(1)} collective-permute-done((f32[16,16,256]{2,1,0:T(8,128)S(1)}, f32[16,16,256]{2,1,0:T(8,128)S(1)}, u32[]{:S(2)}, u32[]{:S(2)}) %collective-permute-start.34) | collective-permute-done | bytes 262176 | tf_op jit(solution)/shard_map/ppermute | solution.py:359
  120.2 2.5 %rows.11 = (f32[16,48,256]{2,1,0:T(8,128)}, f32[16,32,256]{2,1,0:T(8,128)}, f32[16,48,256]{2,1,0:T(8,128)S(1)}, f32[80,256]{1,0:T(8,128)S(1)}) custom-call(s32[1]{0:T(128)} %bitcast.odd_ref, f32[16,32,256]{2,1,0:T(8,128)S(1)} %copy-done.5, f32[16,16,256]{2,1,0:T(8,128)S(1)} %collective-permute-done.33.near_ref, ...), custom_call_target="tpu_custom_call" | custom-call | tf_op jit(solution)/shard_map/rows/pallas_call | solution.py:48
  124.5 1.8 %collective-permute-start.37 = (f32[80,256]{1,0:T(8,128)S(1)}, f32[80,256]{1,0:T(8,128)S(1)}, u32[]{:S(2)}, u32[]{:S(2)}) collective-permute-start(f32[80,256]{1,0:T(8,128)S(1)} %get-tuple-element.177.refs_0_), channel_id=1, source_target_pairs={{0,24},{8,16},{16,8},{24,0},{1,25},{9,17},{17,9},{25,1},{2,26},{10... | collective-permute-start | bytes 245768 | tf_op jit(solution)/shard_map/ppermute | solution.py:374
  126.2 1.4 %collective-permute-done.35.refs_1_ = f32[80,256]{1,0:T(8,128)S(1)} collective-permute-done((f32[80,256]{1,0:T(8,128)S(1)}, f32[80,256]{1,0:T(8,128)S(1)}, u32[]{:S(2)}, u32[]{:S(2)}) %collective-permute-start.35) | collective-permute-done | bytes 81952 | tf_op jit(solution)/shard_map/ppermute | solution.py:374
  128.3 1.6 %collective-permute-done.37.refs_3_ = f32[80,256]{1,0:T(8,128)S(1)} collective-permute-done((f32[80,256]{1,0:T(8,128)S(1)}, f32[80,256]{1,0:T(8,128)S(1)}, u32[]{:S(2)}, u32[]{:S(2)}) %collective-permute-start.37) | collective-permute-done | bytes 81952 | tf_op jit(solution)/shard_map/ppermute | solution.py:374
  (102 shorter events, 28.7 us)
Async XLA Ops:
  1.7 1.2 copy-start.2
  3.9 3.8 %copy-start.11 = (f32[2,17]{1,0:T(2,128)S(1)}, f32[2,17]{1,0:T(2,128)}, u32[]{:S(2)}) copy-start(f32[2,17]{1,0:T(2,128)} %param.12) | copy-start | bytes 412
  3.9 4.2 %copy-start.9 = (f32[16,17]{1,0:T(8,128)S(1)}, f32[16,17]{1,0:T(8,128)}, u32[]{:S(2)}) copy-start(f32[16,17]{1,0:T(8,128)} %param.11) | copy-start | bytes 3268
  3.9 4.5 %copy-start.10 = (f32[16,17]{1,0:T(8,128)S(1)}, f32[16,17]{1,0:T(8,128)}, u32[]{:S(2)}) copy-start(f32[16,17]{1,0:T(8,128)} %param.10) | copy-start | bytes 3268
  3.9 4.8 %copy-start.8 = (s32[16]{0:T(128)S(1)}, s32[16]{0:T(128)}, u32[]{:S(2)}) copy-start(s32[16]{0:T(128)} %flags_ref.1) | copy-start | bytes 196
  4.0 12.5 %copy-start.1 = (f32[16,32,256]{2,1,0:T(8,128)S(1)}, f32[16,32,256]{2,1,0:T(8,128)}, u32[]{:S(2)}) copy-start(f32[16,32,256]{2,1,0:T(8,128)} %refs_2_.1) | copy-start | bytes 1572868
  4.0 12.9 %copy-start.3 = (f32[16,2,32,256]{3,2,1,0:T(8,128)S(1)}, f32[16,2,32,256]{3,2,1,0:T(8,128)}, u32[]{:S(2)}) copy-start(f32[16,2,32,256]{3,2,1,0:T(8,128)} %start_ref.1) | copy-start | bytes 3145732
  4.0 13.0 %copy-start.7 = (f32[16,32,256]{2,1,0:T(8,128)S(1)}, f32[16,32,256]{2,1,0:T(8,128)}, u32[]{:S(2)}) copy-start(f32[16,32,256]{2,1,0:T(8,128)} %dirty_ref.3) | copy-start | bytes 1572868
  5.2 11.8 %collective-permute-start = (f32[16,32,256]{2,1,0:T(8,128)}, f32[16,32,256]{2,1,0:T(8,128)S(1)}, u32[]{:S(2)}, u32[]{:S(2)}) collective-permute-start(f32[16,32,256]{2,1,0:T(8,128)} %get-tuple-element.91), channel_id=1, source_target_pairs={{0,1},{1,0},{2,3},{3,2},{4,5},{5,4},{6,7},{7,6},{8,9},{9,8},{10,11... | collective-permute-start | bytes 1572872 | tf_op jit(solution)/shard_map/ppermute | solution.py:359
  5.2 11.7 %collective-permute-start.1 = (f32[16,32,256]{2,1,0:T(8,128)}, f32[16,32,256]{2,1,0:T(8,128)S(1)}, u32[]{:S(2)}, u32[]{:S(2)}) collective-permute-start(f32[16,32,256]{2,1,0:T(8,128)} %get-tuple-element.92), channel_id=1, source_target_pairs={{1,2},{2,1},{3,4},{4,3},{5,6},{6,5},{9,10},{10,9},{11,12},{12,11},... | collective-permute-start | bytes 1572872 | tf_op jit(solution)/shard_map/ppermute | solution.py:359
  22.9 7.2 %collective-permute-start.2 = (f32[16,16,256]{2,1,0:T(8,128)S(1)}, f32[16,16,256]{2,1,0:T(8,128)S(1)}, u32[]{:S(2)}, u32[]{:S(2)}) collective-permute-start(f32[16,16,256]{2,1,0:T(8,128)S(1)} %get-tuple-element.110), channel_id=1, source_target_pairs={{0,1},{1,0},{2,3},{3,2},{4,5},{5,4},{6,7},{7,6},{8,9},{9,8},{10,11... | collective-permute-start | bytes 786440 | tf_op jit(solution)/shard_map/ppermute | solution.py:359
  24.1 7.7 %collective-permute-start.3 = (f32[16,16,256]{2,1,0:T(8,128)S(1)}, f32[16,16,256]{2,1,0:T(8,128)S(1)}, u32[]{:S(2)}, u32[]{:S(2)}) collective-permute-start(f32[16,16,256]{2,1,0:T(8,128)S(1)} %get-tuple-element.111), channel_id=1, source_target_pairs={{1,2},{2,1},{3,4},{4,3},{5,6},{6,5},{9,10},{10,9},{11,12},{12,11},... | collective-permute-start | bytes 786440 | tf_op jit(solution)/shard_map/ppermute | solution.py:359
  26.1 10.2 %collective-permute-start.7 = (f32[80,256]{1,0:T(8,128)S(1)}, f32[80,256]{1,0:T(8,128)S(1)}, u32[]{:S(2)}, u32[]{:S(2)}) collective-permute-start(f32[80,256]{1,0:T(8,128)S(1)} %get-tuple-element.116.refs_0_), channel_id=1, source_target_pairs={{0,8},{8,0},{16,24},{24,16},{1,9},{9,1},{17,25},{25,17},{2,10},{10... | collective-permute-start | bytes 245768 | tf_op jit(solution)/shard_map/ppermute | solution.py:374
  27.7 9.2 %collective-permute-start.8 = (f32[80,256]{1,0:T(8,128)S(1)}, f32[80,256]{1,0:T(8,128)S(1)}, u32[]{:S(2)}, u32[]{:S(2)}) collective-permute-start(f32[80,256]{1,0:T(8,128)S(1)} %get-tuple-element.116.refs_0_), channel_id=1, source_target_pairs={{0,16},{8,24},{16,0},{24,8},{1,17},{9,25},{17,1},{25,9},{2,18},{10... | collective-permute-start | bytes 245768 | tf_op jit(solution)/shard_map/ppermute | solution.py:374
  29.2 7.7 %collective-permute-start.9 = (f32[80,256]{1,0:T(8,128)S(1)}, f32[80,256]{1,0:T(8,128)S(1)}, u32[]{:S(2)}, u32[]{:S(2)}) collective-permute-start(f32[80,256]{1,0:T(8,128)S(1)} %get-tuple-element.116.refs_0_), channel_id=1, source_target_pairs={{0,24},{8,16},{16,8},{24,0},{1,25},{9,17},{17,9},{25,1},{2,26},{10... | collective-permute-start | bytes 245768 | tf_op jit(solution)/shard_map/ppermute | solution.py:374
  33.3 5.2 %collective-permute-start.4 = (f32[80,256]{1,0:T(8,128)S(1)}, f32[80,256]{1,0:T(8,128)S(1)}, u32[]{:S(2)}, u32[]{:S(2)}) collective-permute-start(f32[80,256]{1,0:T(8,128)S(1)} %get-tuple-element.115.refs_0_), channel_id=1, source_target_pairs={{0,8},{8,0},{16,24},{24,16},{1,9},{9,1},{17,25},{25,17},{2,10},{10... | collective-permute-start | bytes 245768 | tf_op jit(solution)/shard_map/ppermute | solution.py:374
  34.8 5.3 %collective-permute-start.5 = (f32[80,256]{1,0:T(8,128)S(1)}, f32[80,256]{1,0:T(8,128)S(1)}, u32[]{:S(2)}, u32[]{:S(2)}) collective-permute-start(f32[80,256]{1,0:T(8,128)S(1)} %get-tuple-element.115.refs_0_), channel_id=1, source_target_pairs={{0,16},{8,24},{16,0},{24,8},{1,17},{9,25},{17,1},{25,9},{2,18},{10... | collective-permute-start | bytes 245768 | tf_op jit(solution)/shard_map/ppermute | solution.py:374
  36.4 5.3 %collective-permute-start.6 = (f32[80,256]{1,0:T(8,128)S(1)}, f32[80,256]{1,0:T(8,128)S(1)}, u32[]{:S(2)}, u32[]{:S(2)}) collective-permute-start(f32[80,256]{1,0:T(8,128)S(1)} %get-tuple-element.115.refs_0_), channel_id=1, source_target_pairs={{0,24},{8,16},{16,8},{24,0},{1,25},{9,17},{17,9},{25,1},{2,26},{10... | collective-permute-start | bytes 245768 | tf_op jit(solution)/shard_map/ppermute | solution.py:374
  42.3 3.0 %collective-permute-start.10 = (f32[16,16,256]{2,1,0:T(8,128)S(1)}, f32[16,16,256]{2,1,0:T(8,128)S(1)}, u32[]{:S(2)}, u32[]{:S(2)}) collective-permute-start(f32[16,16,256]{2,1,0:T(8,128)S(1)} %get-tuple-element.122), channel_id=1, source_target_pairs={{0,1},{1,0},{2,3},{3,2},{4,5},{5,4},{6,7},{7,6},{8,9},{9,8},{10,11... | collective-permute-start | bytes 786440 | tf_op jit(solution)/shard_map/ppermute | solution.py:359
  42.4 7.7 %collective-permute-start.11 = (f32[16,16,256]{2,1,0:T(8,128)S(1)}, f32[16,16,256]{2,1,0:T(8,128)S(1)}, u32[]{:S(2)}, u32[]{:S(2)}) collective-permute-start(f32[16,16,256]{2,1,0:T(8,128)S(1)} %get-tuple-element.123), channel_id=1, source_target_pairs={{1,2},{2,1},{3,4},{4,3},{5,6},{6,5},{9,10},{10,9},{11,12},{12,11},... | collective-permute-start | bytes 786440 | tf_op jit(solution)/shard_map/ppermute | solution.py:359
  51.6 5.2 %collective-permute-start.12 = (f32[80,256]{1,0:T(8,128)S(1)}, f32[80,256]{1,0:T(8,128)S(1)}, u32[]{:S(2)}, u32[]{:S(2)}) collective-permute-start(f32[80,256]{1,0:T(8,128)S(1)} %get-tuple-element.129.refs_0_), channel_id=1, source_target_pairs={{0,8},{8,0},{16,24},{24,16},{1,9},{9,1},{17,25},{25,17},{2,10},{10... | collective-permute-start | bytes 245768 | tf_op jit(solution)/shard_map/ppermute | solution.py:374
  52.2 4.8 %collective-permute-start.13 = (f32[80,256]{1,0:T(8,128)S(1)}, f32[80,256]{1,0:T(8,128)S(1)}, u32[]{:S(2)}, u32[]{:S(2)}) collective-permute-start(f32[80,256]{1,0:T(8,128)S(1)} %get-tuple-element.129.refs_0_), channel_id=1, source_target_pairs={{0,16},{8,24},{16,0},{24,8},{1,17},{9,25},{17,1},{25,9},{2,18},{10... | collective-permute-start | bytes 245768 | tf_op jit(solution)/shard_map/ppermute | solution.py:374
  53.0 5.5 %collective-permute-start.14 = (f32[80,256]{1,0:T(8,128)S(1)}, f32[80,256]{1,0:T(8,128)S(1)}, u32[]{:S(2)}, u32[]{:S(2)}) collective-permute-start(f32[80,256]{1,0:T(8,128)S(1)} %get-tuple-element.129.refs_0_), channel_id=1, source_target_pairs={{0,24},{8,16},{16,8},{24,0},{1,25},{9,17},{17,9},{25,1},{2,26},{10... | collective-permute-start | bytes 245768 | tf_op jit(solution)/shard_map/ppermute | solution.py:374
  59.2 3.0 %collective-permute-start.15 = (f32[16,16,256]{2,1,0:T(8,128)S(1)}, f32[16,16,256]{2,1,0:T(8,128)S(1)}, u32[]{:S(2)}, u32[]{:S(2)}) collective-permute-start(f32[16,16,256]{2,1,0:T(8,128)S(1)} %get-tuple-element.134), channel_id=1, source_target_pairs={{0,1},{1,0},{2,3},{3,2},{4,5},{5,4},{6,7},{7,6},{8,9},{9,8},{10,11... | collective-permute-start | bytes 786440 | tf_op jit(solution)/shard_map/ppermute | solution.py:359
  59.2 7.7 %collective-permute-start.16 = (f32[16,16,256]{2,1,0:T(8,128)S(1)}, f32[16,16,256]{2,1,0:T(8,128)S(1)}, u32[]{:S(2)}, u32[]{:S(2)}) collective-permute-start(f32[16,16,256]{2,1,0:T(8,128)S(1)} %get-tuple-element.135), channel_id=1, source_target_pairs={{1,2},{2,1},{3,4},{4,3},{5,6},{6,5},{9,10},{10,9},{11,12},{12,11},... | collective-permute-start | bytes 786440 | tf_op jit(solution)/shard_map/ppermute | solution.py:359
  68.4 5.2 %collective-permute-start.17 = (f32[80,256]{1,0:T(8,128)S(1)}, f32[80,256]{1,0:T(8,128)S(1)}, u32[]{:S(2)}, u32[]{:S(2)}) collective-permute-start(f32[80,256]{1,0:T(8,128)S(1)} %get-tuple-element.141.refs_0_), channel_id=1, source_target_pairs={{0,8},{8,0},{16,24},{24,16},{1,9},{9,1},{17,25},{25,17},{2,10},{10... | collective-permute-start | bytes 245768 | tf_op jit(solution)/shard_map/ppermute | solution.py:374
  69.9 4.6 %collective-permute-start.18 = (f32[80,256]{1,0:T(8,128)S(1)}, f32[80,256]{1,0:T(8,128)S(1)}, u32[]{:S(2)}, u32[]{:S(2)}) collective-permute-start(f32[80,256]{1,0:T(8,128)S(1)} %get-tuple-element.141.refs_0_), channel_id=1, source_target_pairs={{0,16},{8,24},{16,0},{24,8},{1,17},{9,25},{17,1},{25,9},{2,18},{10... | collective-permute-start | bytes 245768 | tf_op jit(solution)/shard_map/ppermute | solution.py:374
  71.0 5.3 %collective-permute-start.19 = (f32[80,256]{1,0:T(8,128)S(1)}, f32[80,256]{1,0:T(8,128)S(1)}, u32[]{:S(2)}, u32[]{:S(2)}) collective-permute-start(f32[80,256]{1,0:T(8,128)S(1)} %get-tuple-element.141.refs_0_), channel_id=1, source_target_pairs={{0,24},{8,16},{16,8},{24,0},{1,25},{9,17},{17,9},{25,1},{2,26},{10... | collective-permute-start | bytes 245768 | tf_op jit(solution)/shard_map/ppermute | solution.py:374
  77.0 6.6 %collective-permute-start.20 = (f32[16,16,256]{2,1,0:T(8,128)S(1)}, f32[16,16,256]{2,1,0:T(8,128)S(1)}, u32[]{:S(2)}, u32[]{:S(2)}) collective-permute-start(f32[16,16,256]{2,1,0:T(8,128)S(1)} %get-tuple-element.146), channel_id=1, source_target_pairs={{0,1},{1,0},{2,3},{3,2},{4,5},{5,4},{6,7},{7,6},{8,9},{9,8},{10,11... | collective-permute-start | bytes 786440 | tf_op jit(solution)/shard_map/ppermute | solution.py:359
  77.0 7.7 %collective-permute-start.21 = (f32[16,16,256]{2,1,0:T(8,128)S(1)}, f32[16,16,256]{2,1,0:T(8,128)S(1)}, u32[]{:S(2)}, u32[]{:S(2)}) collective-permute-start(f32[16,16,256]{2,1,0:T(8,128)S(1)} %get-tuple-element.147), channel_id=1, source_target_pairs={{1,2},{2,1},{3,4},{4,3},{5,6},{6,5},{9,10},{10,9},{11,12},{12,11},... | collective-permute-start | bytes 786440 | tf_op jit(solution)/shard_map/ppermute | solution.py:359
  79.6 8.3 %collective-permute-start.25 = (f32[80,256]{1,0:T(8,128)S(1)}, f32[80,256]{1,0:T(8,128)S(1)}, u32[]{:S(2)}, u32[]{:S(2)}) collective-permute-start(f32[80,256]{1,0:T(8,128)S(1)} %squares.1.refs_0_), channel_id=1, source_target_pairs={{0,8},{8,0},{16,24},{24,16},{1,9},{9,1},{17,25},{25,17},{2,10},{10... | collective-permute-start | bytes 245768 | tf_op jit(solution)/shard_map/ppermute | solution.py:374
  80.3 9.4 %collective-permute-start.26 = (f32[80,256]{1,0:T(8,128)S(1)}, f32[80,256]{1,0:T(8,128)S(1)}, u32[]{:S(2)}, u32[]{:S(2)}) collective-permute-start(f32[80,256]{1,0:T(8,128)S(1)} %squares.1.refs_0_), channel_id=1, source_target_pairs={{0,16},{8,24},{16,0},{24,8},{1,17},{9,25},{17,1},{25,9},{2,18},{10... | collective-permute-start | bytes 245768 | tf_op jit(solution)/shard_map/ppermute | solution.py:374
  81.3 8.4 %collective-permute-start.27 = (f32[80,256]{1,0:T(8,128)S(1)}, f32[80,256]{1,0:T(8,128)S(1)}, u32[]{:S(2)}, u32[]{:S(2)}) collective-permute-start(f32[80,256]{1,0:T(8,128)S(1)} %squares.1.refs_0_), channel_id=1, source_target_pairs={{0,24},{8,16},{16,8},{24,0},{1,25},{9,17},{17,9},{25,1},{2,26},{10... | collective-permute-start | bytes 245768 | tf_op jit(solution)/shard_map/ppermute | solution.py:374
  86.2 5.4 %collective-permute-start.22 = (f32[80,256]{1,0:T(8,128)S(1)}, f32[80,256]{1,0:T(8,128)S(1)}, u32[]{:S(2)}, u32[]{:S(2)}) collective-permute-start(f32[80,256]{1,0:T(8,128)S(1)} %get-tuple-element.153.refs_0_), channel_id=1, source_target_pairs={{0,8},{8,0},{16,24},{24,16},{1,9},{9,1},{17,25},{25,17},{2,10},{10... | collective-permute-start | bytes 245768 | tf_op jit(solution)/shard_map/ppermute | solution.py:374
  86.9 5.0 %collective-permute-start.23 = (f32[80,256]{1,0:T(8,128)S(1)}, f32[80,256]{1,0:T(8,128)S(1)}, u32[]{:S(2)}, u32[]{:S(2)}) collective-permute-start(f32[80,256]{1,0:T(8,128)S(1)} %get-tuple-element.153.refs_0_), channel_id=1, source_target_pairs={{0,16},{8,24},{16,0},{24,8},{1,17},{9,25},{17,1},{25,9},{2,18},{10... | collective-permute-start | bytes 245768 | tf_op jit(solution)/shard_map/ppermute | solution.py:374
  87.9 5.6 %collective-permute-start.24 = (f32[80,256]{1,0:T(8,128)S(1)}, f32[80,256]{1,0:T(8,128)S(1)}, u32[]{:S(2)}, u32[]{:S(2)}) collective-permute-start(f32[80,256]{1,0:T(8,128)S(1)} %get-tuple-element.153.refs_0_), channel_id=1, source_target_pairs={{0,24},{8,16},{16,8},{24,0},{1,25},{9,17},{17,9},{25,1},{2,26},{10... | collective-permute-start | bytes 245768 | tf_op jit(solution)/shard_map/ppermute | solution.py:374
  94.2 3.0 %collective-permute-start.28 = (f32[16,16,256]{2,1,0:T(8,128)S(1)}, f32[16,16,256]{2,1,0:T(8,128)S(1)}, u32[]{:S(2)}, u32[]{:S(2)}) collective-permute-start(f32[16,16,256]{2,1,0:T(8,128)S(1)} %get-tuple-element.158), channel_id=1, source_target_pairs={{0,1},{1,0},{2,3},{3,2},{4,5},{5,4},{6,7},{7,6},{8,9},{9,8},{10,11... | collective-permute-start | bytes 786440 | tf_op jit(solution)/shard_map/ppermute | solution.py:359
  94.3 7.7 %collective-permute-start.29 = (f32[16,16,256]{2,1,0:T(8,128)S(1)}, f32[16,16,256]{2,1,0:T(8,128)S(1)}, u32[]{:S(2)}, u32[]{:S(2)}) collective-permute-start(f32[16,16,256]{2,1,0:T(8,128)S(1)} %get-tuple-element.159), channel_id=1, source_target_pairs={{1,2},{2,1},{3,4},{4,3},{5,6},{6,5},{9,10},{10,9},{11,12},{12,11},... | collective-permute-start | bytes 786440 | tf_op jit(solution)/shard_map/ppermute | solution.py:359
  103.4 5.2 %collective-permute-start.30 = (f32[80,256]{1,0:T(8,128)S(1)}, f32[80,256]{1,0:T(8,128)S(1)}, u32[]{:S(2)}, u32[]{:S(2)}) collective-permute-start(f32[80,256]{1,0:T(8,128)S(1)} %get-tuple-element.165.refs_0_), channel_id=1, source_target_pairs={{0,8},{8,0},{16,24},{24,16},{1,9},{9,1},{17,25},{25,17},{2,10},{10... | collective-permute-start | bytes 245768 | tf_op jit(solution)/shard_map/ppermute | solution.py:374
  104.8 5.4 %collective-permute-start.31 = (f32[80,256]{1,0:T(8,128)S(1)}, f32[80,256]{1,0:T(8,128)S(1)}, u32[]{:S(2)}, u32[]{:S(2)}) collective-permute-start(f32[80,256]{1,0:T(8,128)S(1)} %get-tuple-element.165.refs_0_), channel_id=1, source_target_pairs={{0,16},{8,24},{16,0},{24,8},{1,17},{9,25},{17,1},{25,9},{2,18},{10... | collective-permute-start | bytes 245768 | tf_op jit(solution)/shard_map/ppermute | solution.py:374
  105.8 5.3 %collective-permute-start.32 = (f32[80,256]{1,0:T(8,128)S(1)}, f32[80,256]{1,0:T(8,128)S(1)}, u32[]{:S(2)}, u32[]{:S(2)}) collective-permute-start(f32[80,256]{1,0:T(8,128)S(1)} %get-tuple-element.165.refs_0_), channel_id=1, source_target_pairs={{0,24},{8,16},{16,8},{24,0},{1,25},{9,17},{17,9},{25,1},{2,26},{10... | collective-permute-start | bytes 245768 | tf_op jit(solution)/shard_map/ppermute | solution.py:374
  112.6 4.7 %collective-permute-start.33 = (f32[16,16,256]{2,1,0:T(8,128)S(1)}, f32[16,16,256]{2,1,0:T(8,128)S(1)}, u32[]{:S(2)}, u32[]{:S(2)}) collective-permute-start(f32[16,16,256]{2,1,0:T(8,128)S(1)} %get-tuple-element.170), channel_id=1, source_target_pairs={{0,1},{1,0},{2,3},{3,2},{4,5},{5,4},{6,7},{7,6},{8,9},{9,8},{10,11... | collective-permute-start | bytes 786440 | tf_op jit(solution)/shard_map/ppermute | solution.py:359
  112.6 7.7 %collective-permute-start.34 = (f32[16,16,256]{2,1,0:T(8,128)S(1)}, f32[16,16,256]{2,1,0:T(8,128)S(1)}, u32[]{:S(2)}, u32[]{:S(2)}) collective-permute-start(f32[16,16,256]{2,1,0:T(8,128)S(1)} %get-tuple-element.171), channel_id=1, source_target_pairs={{1,2},{2,1},{3,4},{4,3},{5,6},{6,5},{9,10},{10,9},{11,12},{12,11},... | collective-permute-start | bytes 786440 | tf_op jit(solution)/shard_map/ppermute | solution.py:359
  115.0 1.0 copy-start.4
  116.1 4.2 %copy-start.5 = (f32[16,32,256]{2,1,0:T(8,128)S(1)}, f32[16,32,256]{2,1,0:T(8,128)}, u32[]{:S(2)}) copy-start(f32[16,32,256]{2,1,0:T(8,128)} %get-tuple-element.89.own_ref) | copy-start | bytes 1572868
  122.8 4.9 %collective-permute-start.35 = (f32[80,256]{1,0:T(8,128)S(1)}, f32[80,256]{1,0:T(8,128)S(1)}, u32[]{:S(2)}, u32[]{:S(2)}) collective-permute-start(f32[80,256]{1,0:T(8,128)S(1)} %get-tuple-element.177.refs_0_), channel_id=1, source_target_pairs={{0,8},{8,0},{16,24},{24,16},{1,9},{9,1},{17,25},{25,17},{2,10},{10... | collective-permute-start | bytes 245768 | tf_op jit(solution)/shard_map/ppermute | solution.py:374
  123.5 4.7 %collective-permute-start.36 = (f32[80,256]{1,0:T(8,128)S(1)}, f32[80,256]{1,0:T(8,128)S(1)}, u32[]{:S(2)}, u32[]{:S(2)}) collective-permute-start(f32[80,256]{1,0:T(8,128)S(1)} %get-tuple-element.177.refs_0_), channel_id=1, source_target_pairs={{0,16},{8,24},{16,0},{24,8},{1,17},{9,25},{17,1},{25,9},{2,18},{10... | collective-permute-start | bytes 245768 | tf_op jit(solution)/shard_map/ppermute | solution.py:374
  124.5 5.4 %collective-permute-start.37 = (f32[80,256]{1,0:T(8,128)S(1)}, f32[80,256]{1,0:T(8,128)S(1)}, u32[]{:S(2)}, u32[]{:S(2)}) collective-permute-start(f32[80,256]{1,0:T(8,128)S(1)} %get-tuple-element.177.refs_0_), channel_id=1, source_target_pairs={{0,24},{8,16},{16,8},{24,0},{1,25},{9,17},{17,9},{25,1},{2,26},{10... | collective-permute-start | bytes 245768 | tf_op jit(solution)/shard_map/ppermute | solution.py:374
  (2 other events, 2.1 us)
where the time goes:
time: 131 us
  starting transfers between devices  46.6 us (36%)
  Pallas kernels  41.5 us (32%)
  waiting for transfers between devices  36.3 us (28%)
  local copies, waits for them, and re-layouts  5.42 us (4%)
    pallas_call x31, Pallas kernels, call(): pl.pallas_call(kernel, out_shape=[jax.ShapeDtypeStruct(*shape) for shape...  40.3 us
    ppermute x24, starting transfers between devices, gathered(): lax.ppermute(total, 'chan', [(i, i ^ k * low) for i in range(n)])  28.4 us
    ppermute x7, waiting for transfers between devices, exchange(): lax.ppermute(far, 'facet', cross)  20.2 us
    ppermute x7, starting transfers between devices, exchange(): lax.ppermute(far, 'facet', cross)  16.7 us
    ppermute x24, waiting for transfers between devices, gathered(): lax.ppermute(total, 'chan', [(i, i ^ k * low) for i in range(n)])  16 us
    unnamed x24, local copies, waits for them, and re-layouts  4.37 us
  transfers between devices with their start and end apart: 38, of which 20 were waited for; matrix products, arithmetic and copies ran while one was open for 1% of the time, Pallas kernels for 17%

commit v1 on v0

--- a/solution.py
+++ b/solution.py
@@ -19,6 +19,9 @@
 
 F32 = jnp.float32
 BF16 = jnp.bfloat16
+LANES = 128
+UNROLL = 4
+GROUP = 8
 VMEM_LIMIT = 24 * 1024 * 1024
 PARAMS = pltpu.CompilerParams(vmem_limit_bytes=VMEM_LIMIT)
 
@@ -44,53 +47,97 @@
 SM = pl.BlockSpec(memory_space=pltpu.SMEM)
 
 
-def call(kernel, ins, outs, name, scalars=0):
+def call(kernel, ins, outs, name, scalars=0, aliases=None):
     return pl.pallas_call(
         kernel,
         out_shape=[jax.ShapeDtypeStruct(*shape) for shape in outs],
         in_specs=[SM] * scalars + [VM] * (len(ins) - scalars),
         out_specs=[VM] * len(outs),
+        input_output_aliases=aliases or {},
         compiler_params=PARAMS,
         name=name,
     )(*ins)
 
 
-def rows_kernel(odd_ref, own_ref, near_ref, far_ref, mats_ref, dual_ref, old_ref, sum1_ref, band_ref, part_ref, moved_ref, sums_ref):
+def sided(odd, near, far, send):
+    rows, width = near.shape
+    if rows < send:
+        blank = jnp.zeros((send - rows, width), F32)
+        above = lambda rim: jnp.concatenate([blank, rim], axis=0)
+        below = lambda rim: jnp.concatenate([rim, blank], axis=0)
+        near = jnp.where(odd, above(near), below(near))
+        far = jnp.where(odd, below(far), above(far))
+    return near, far
+
+
+def near_kernel(
+    send, odd_ref, own_ref, near_ref, mats_ref, dual0_ref, old0_ref, head_ref, rest_ref, dual1_ref, old1_ref,
+    band0_ref, part_ref, moved0_ref, band1_ref, moved1_ref, sums_ref,
+):
     chans, height, width = own_ref.shape
-    reach = band_ref.shape[1]
+    reach = band0_ref.shape[1]
     odd = odd_ref[0] == 1
 
     def body(c, total):
-        near, far = near_ref[c], far_ref[c]
-        before, after = jnp.where(odd, near, far), jnp.where(odd, far, near)
-        extended = jnp.concatenate([before, own_ref[c], after], axis=0)
-        product = jnp.dot(mats_ref[c], stacked(extended), preferred_element_type=F32)
+        near, _ = sided(odd, near_ref[c], near_ref[c], send)
+        rows = jnp.concatenate([own_ref[c], near], axis=0)
+        product = jnp.dot(mats_ref[c], stacked(rows), preferred_element_type=F32)
         band = product[:reach]
-        band_ref[c] = band
+        band0_ref[c] = band
         part_ref[c] = product[reach:]
-        moved = dual_ref[c] + STEP_DUAL * (2.0 * band - old_ref[c])
-        moved_ref[c] = moved
+        moved = dual0_ref[c] + STEP_DUAL * (2.0 * band - old0_ref[c])
+        moved0_ref[c] = moved
         return total + moved * moved
 
-    total = lax.fori_loop(0, chans, body, jnp.zeros((reach, width), F32), unroll=2)
-    sums_ref[:reach] = total
-    sums_ref[reach:] = sum1_ref[...]
+    sums_ref[:reach] = lax.fori_loop(0, chans, body, jnp.zeros((reach, width), F32), unroll=UNROLL)
+    total = jnp.zeros((height, width), F32)
+    for c in range(0, chans, GROUP):
+        n = min(GROUP, chans - c)
+        band = times_columns(
+            own_ref[c : c + n].reshape(n * height, width), head_ref[...], rest_ref[...]
+        ).reshape(n, height, width)
+        band1_ref[c : c + n] = band
+        moved = dual1_ref[c : c + n] + STEP_DUAL * (2.0 * band - old1_ref[c : c + n])
+        moved1_ref[c : c + n] = moved
+        total = total + jnp.sum(moved * moved, axis=0)
+    sums_ref[reach:] = total
+
+
+def far_kernel(send, odd_ref, far_ref, mats_ref, band_in_ref, moved_in_ref, sums_in_ref, band_ref, moved_ref, sums_ref):
+    del band_in_ref, moved_in_ref
+    chans, reach, width = band_ref.shape
+    odd = odd_ref[0] == 1
+    start = pl.multiple_of(odd_ref[0] * (reach - send), 16)
+    touched = pl.ds(start, send)
+
+    def body(c, total):
+        _, far = sided(odd, far_ref[c], far_ref[c], send)
+        product = jnp.dot(mats_ref[c, touched, :], stacked(far), preferred_element_type=F32)
+        band_ref[c, touched, :] = band_ref[c, touched, :] + product
+        moved = moved_ref[c, touched, :] + (2.0 * STEP_DUAL) * product
+        moved_ref[c, touched, :] = moved
+        return total + moved * moved
+
+    sums_ref[...] = sums_in_ref[...]
+    sums_ref[touched, :] = lax.fori_loop(0, chans, body, jnp.zeros((send, width), F32), unroll=UNROLL)
 
 
 def first_rows_kernel(
-    odd_ref, own_ref, near_ref, far_ref, mats_ref, start_ref, dirty_ref, sum1_ref,
+    odd_ref, own_ref, near_ref, far_ref, mats_ref, far_mats_ref, start_ref, dirty_ref, sum1_ref,
     band_ref, part_ref, dual_ref, data_ref, sums_ref,
 ):
     chans, height, width = own_ref.shape
     reach = band_ref.shape[1]
-    send, edge = (mats_ref.shape[2] // 3 - height) // 2, (reach - height) // 2
+    send, edge = far_mats_ref.shape[2] // 3, (reach - height) // 2
     odd = odd_ref[0] == 1
 
     def body(c, total):
         near, far = near_ref[c], far_ref[c]
         before, after = jnp.where(odd, near, far), jnp.where(odd, far, near)
-        extended = jnp.concatenate([before[:send], own_ref[c], after[:send]], axis=0)
-        product = jnp.dot(mats_ref[c], stacked(extended), preferred_element_type=F32)
+        rows = jnp.concatenate([own_ref[c], near[:send]], axis=0)
+        product = jnp.dot(mats_ref[c], stacked(rows), preferred_element_type=F32) + jnp.dot(
+            far_mats_ref[c], stacked(far[:send]), preferred_element_type=F32
+        )
         band = product[:reach]
         band_ref[c] = band
         part_ref[c] = product[reach:]
@@ -99,8 +146,7 @@
         data_ref[c] = jnp.concatenate([before[at:], dirty_ref[c], after[at:]], axis=0)
         return total + band * band
 
-    total = lax.fori_loop(0, chans, body, jnp.zeros((reach, width), F32), unroll=2)
-    sums_ref[:reach] = total
+    sums_ref[:reach] = lax.fori_loop(0, chans, body, jnp.zeros((reach, width), F32), unroll=UNROLL)
     sums_ref[reach:] = sum1_ref[...]
 
 
@@ -134,9 +180,6 @@
         copy.wait()
 
 
-LANES = 128
-
-
 def banded(line, rows):
     return pltpu.roll(
         jnp.broadcast_to(line, (rows, LANES)), 0, 1, stride=1, stride_axis=0
@@ -170,15 +213,16 @@
 
 
 def matrices_kernel(
-    flags_ref, lines_ref, mats_ref, adj_ref, wav_rows_ref,
+    flags_ref, lines_ref, mats_ref, far_mats_ref, adj_ref, wav_rows_ref,
     around_head_ref, around_rest_ref, back_head_ref, back_rest_ref,
     wav_head_ref, wav_rest_ref, wav_head_t_ref, wav_rest_t_ref,
 ):
     chans, width = around_head_ref.shape[:2]
-    both, tall = mats_ref.shape[1], mats_ref.shape[2] // 3
+    send = far_mats_ref.shape[2] // 3
     height, reach = wav_rows_ref.shape[0], wav_rows_ref.shape[1] // 3
     edge = (reach - height) // 2
     facet, facets = lax.axis_index("facet"), lax.axis_size("facet")
+    odd = lax.rem(facet, 2) == 1
 
     def inside(shape, dim):
         at = lax.broadcasted_iota(jnp.int32, shape, dim)
@@ -197,7 +241,14 @@
     wav_head_ref[...], wav_rest_ref[...] = square_band(line(chans, 0), width, WAV_HALF)
     wav_head_t_ref[...], wav_rest_t_ref[...] = square_band(line(chans, 1), width, WAV_HALF)
     wav_rows_ref[...] = wide_rows(banded(line(chans, 3), height)[:, :reach])
-    band = wide_rows((banded(line(chans, 2), reach) * inside((reach, LANES), 0))[:, :tall])
+
+    def by_side(matrix):
+        low, own = matrix[:, :send], matrix[:, send : send + height]
+        high = matrix[:, send + height : 2 * send + height]
+        near, far = jnp.where(odd, low, high), jnp.where(odd, high, low)
+        return wide_rows(jnp.concatenate([own, near], axis=1)), wide_rows(far)
+
+    band, far_band = by_side(banded(line(chans, 2), reach) * inside((reach, LANES), 0))
 
     def body(c, carry):
         head, rest = square_band(line(c, 0), width, PSF_HALF)
@@ -223,34 +274,18 @@
             + jnp.dot(first, rest, preferred_element_type=F32)
         )
         mats_ref[c, :reach] = band
-        mats_ref[c, reach:] = wide_rows(normal[:, :tall])
+        far_mats_ref[c, :reach] = far_band
+        mats_ref[c, reach:], far_mats_ref[c, reach:] = by_side(normal)
         return carry
 
-    lax.fori_loop(0, chans, body, 0)
-
-
-def columns_kernel(own_ref, head_ref, rest_ref, dual_ref, old_ref, band_ref, moved_ref, sum_ref):
-    chans, height, width = own_ref.shape
-    group = 8
-    total = jnp.zeros((height, width), F32)
-    for c in range(0, chans, group):
-        n = min(group, chans - c)
-        band = times_columns(
-            own_ref[c : c + n].reshape(n * height, width), head_ref[...], rest_ref[...]
-        ).reshape(n, height, width)
-        band_ref[c : c + n] = band
-        moved = dual_ref[c : c + n] + STEP_DUAL * (2.0 * band - old_ref[c : c + n])
-        moved_ref[c : c + n] = moved
-        total = total + jnp.sum(moved * moved, axis=0)
-    sum_ref[...] = total
+    lax.fori_loop(0, chans, body, 0, unroll=2)
 
 
 def first_columns_kernel(own_ref, head_ref, rest_ref, band_ref, sum_ref):
     chans, height, width = own_ref.shape
-    group = 8
     total = jnp.zeros((height, width), F32)
-    for c in range(0, chans, group):
-        n = min(group, chans - c)
+    for c in range(0, chans, GROUP):
+        n = min(GROUP, chans - c)
         band = times_columns(
             own_ref[c : c + n].reshape(n * height, width), head_ref[...], rest_ref[...]
         ).reshape(n, height, width)
@@ -271,17 +306,21 @@
         grad_ref[c] = times_columns(part_ref[c], head_ref[c], rest_ref[c]) - data
         return carry
 
-    lax.fori_loop(0, chans, body, 0, unroll=2)
-
-
-def gradient_kernel(part_ref, head_ref, rest_ref, data_ref, grad_ref):
-    chans = part_ref.shape[0]
+    lax.fori_loop(0, chans, body, 0, unroll=UNROLL)
+
+
+def gradient_kernel(part_ref, far_ref, far_mats_ref, head_ref, rest_ref, data_ref, grad_ref):
+    chans, height = part_ref.shape[:2]
+    reach = far_mats_ref.shape[1] - height
 
     def body(c, carry):
-        grad_ref[c] = times_columns(part_ref[c], head_ref[c], rest_ref[c]) - data_ref[c]
+        part = part_ref[c] + jnp.dot(
+            far_mats_ref[c, reach:], stacked(far_ref[c]), preferred_element_type=F32
+        )
+        grad_ref[c] = times_columns(part, head_ref[c], rest_ref[c]) - data_ref[c]
         return carry
 
-    lax.fori_loop(0, chans, body, 0, unroll=2)
+    lax.fori_loop(0, chans, body, 0, unroll=UNROLL)
 
 
 def scaled(sums_refs, radius):
@@ -316,9 +355,8 @@
         dual0_ref, dual1_ref = duals
         scale = scaled(sums_refs, radius_ref[...])
         scale0, scale1 = scale[:reach], scale[reach:]
-    group = 4
-    for c0 in range(0, chans, group):
-        n = min(group, chans - c0)
+    for c0 in range(0, chans, GROUP // 2):
+        n = min(GROUP // 2, chans - c0)
         dual1 = moved1_ref[c0 : c0 + n]
         if n_sums:
             dual1 = dual1 * scale1[None]
@@ -352,11 +390,18 @@
         dual_ref[c, 1] = moved1_ref[c] * scale1
 
 
+def publish_kernel(own_ref, _, out_ref, sem):
+    copy = pltpu.make_async_copy(own_ref, out_ref, sem)
+    copy.start()
+    copy.wait()
+
+
 def exchange(near, far):
     n = lax.axis_size("facet")
     pair = [(i, i ^ 1) for i in range(n)]
     cross = [(i, ((i + 1) ^ 1) - 1) for i in range(n) if 0 <= ((i + 1) ^ 1) - 1 < n]
-    return lax.ppermute(near, "facet", pair), lax.ppermute(far, "facet", cross)
+    far = lax.ppermute(far, "facet", cross)
+    return lax.ppermute(near, "facet", pair), far
 
 
 def gathered(sums):
@@ -372,7 +417,7 @@
             total = total + term
         terms = [total] + [
             lax.ppermute(total, "chan", [(i, i ^ (k * low)) for i in range(n)])
-            for k in range(1, radix)
+            for k in sorted(range(1, radix), key=lambda k: -k.bit_count())
         ]
         low *= radix
     return terms
@@ -385,7 +430,6 @@
     total_chans = chans * lax.axis_size("chan")
     edge = max(PSF_HALF, WAV_HALF)
     reach, send = height + 2 * edge, 2 * edge
-    tall = height + 2 * send
     passes = OUTER * INNER
     odd = (lax.axis_index("facet") % 2).astype(jnp.int32)[None]
 
@@ -405,7 +449,7 @@
         scratch_shapes=[pltpu.SemaphoreType.DMA((6,))],
         compiler_params=PARAMS,
         name="pack",
-    )(image_start, dual_start, dirty_image)
+    )(*(pltpu.with_memory_space_constraint(x, pltpu.HBM) for x in (image_start, dual_start, dirty_image)))
     near, far = exchange(near, far)
 
     def lines(cols, rows, half_c, half_r):
@@ -431,12 +475,13 @@
         axis=0,
     )
     (
-        mats, adjoint, wav_rows, around_head, around_rest, back_head, back_rest,
+        mats, far_mats, adjoint, wav_rows, around_head, around_rest, back_head, back_rest,
         wav_head, wav_rest, wav_head_t, wav_rest_t,
     ) = call(
         matrices_kernel, (channel_flags, table[:, None]),
         (
-            ((chans, reach + height, 3 * tall), BF16), ((chans, height, 3 * reach), BF16),
+            ((chans, reach + height, 3 * (height + send)), BF16), ((chans, reach + height, 3 * send), BF16),
+            ((chans, height, 3 * reach), BF16),
             ((height, 3 * reach), BF16), squares, squares, squares, squares,
             square, square, square, square,
         ),
@@ -446,7 +491,7 @@
         first_columns_kernel, (image_start, wav_head, wav_rest), (own, ((height, width), F32)), "first_columns"
     )
     band0, part, dual0, dirty, weight_sums = call(
-        first_rows_kernel, (odd, image_start, near, far, mats, dual_start, dirty_image, sum1),
+        first_rows_kernel, (odd, image_start, near, far, mats, far_mats, dual_start, dirty_image, sum1),
         (taller, own, taller, taller, summed), "first_rows", 1,
     )
     data, grad = call(
@@ -463,34 +508,47 @@
         near, far = exchange(near, far)
         if step % INNER == 0:
             terms = gathered(weight_sums)
-        band1, moved1, sum1 = call(
-            columns_kernel, (estimate, wav_head, wav_rest, dual1, band1),
-            (own, own, ((height, width), F32)), "columns",
+        band0, part, moved0, band1, moved1, sums = call(
+            functools.partial(near_kernel, send),
+            (odd, estimate, near, mats, dual0, band0, wav_head, wav_rest, dual1, band1),
+            (taller, own, taller, own, own, summed), "near", 1,
         )
         if step % INNER == 0:
             radius = call(
                 functools.partial(radius_kernel, RADIUS_SCALE * total_chans), tuple(terms), (summed,), "radius"
             )[0]
-        band0, part, moved0, sums = call(
-            rows_kernel, (odd, estimate, near, far, mats, dual0, band0, sum1),
-            (taller, own, taller, summed), "rows", 1,
+        band0, moved0, sums = call(
+            functools.partial(far_kernel, send), (odd, far, far_mats, band0, moved0, sums),
+            (taller, taller, summed), "far", 1, {3: 0, 4: 1},
         )
         terms = gathered(sums)
         if step % INNER == INNER - 1 and step + 1 < passes:
             weight_sums = call(squares_kernel, (band0, band1), (summed,), "squares")[0]
         if step + 1 < passes:
-            grad = call(gradient_kernel, (part, around_head, around_rest, data), (own,), "gradient")[0]
+            grad = call(
+                gradient_kernel, (part, far, far_mats, around_head, around_rest, data), (own,), "gradient"
+            )[0]
+            rim = ((chans, send if step + 2 < passes else WAV_HALF, width), F32)
             estimate, near, far, dual0, dual1 = call(
                 functools.partial(update_kernel, len(terms)),
                 (odd, *terms, radius, moved0, moved1, estimate, grad, wav_rows, wav_head_t, wav_rest_t),
-                (own, sides, sides, taller, own), "update", 1,
+                (own, rim, rim, taller, own), "update", 1,
             )
         else:
+            image_final = pl.pallas_call(
+                publish_kernel,
+                out_shape=jax.ShapeDtypeStruct(*own),
+                in_specs=[VM, pl.BlockSpec(memory_space=pl.ANY)],
+                out_specs=pl.BlockSpec(memory_space=pltpu.HBM),
+                scratch_shapes=[pltpu.SemaphoreType.DMA],
+                compiler_params=PARAMS,
+                name="publish",
+            )(estimate, sums)
             dual_final = call(
                 functools.partial(final_kernel, len(terms)), (*terms, radius, moved0, moved1),
                 (((chans, 2, height, width), F32),), "final",
             )[0]
-    return (estimate, dual_final)
+    return (image_final, dual_final)
 
 
 def solution(mesh):

time: 131 us -> 118 us (0.901)
  waiting for transfers between devices: 36.3 us -> 29.9 us
  local copies, waits for them, and re-layouts: 5.42 us -> 1.08 us
  Pallas kernels: 41.5 us -> 39 us
    ppermute x14, waiting for transfers between devices: 20.3 us -> 15.7 us  [the longest x7 15.7 us: exchange(): far = lax.ppermute(far, 'facet', cross)]
    pallas_call x31, Pallas kernels: 40.3 us -> 35.8 us  [call(): pl.pallas_call(kernel, out_shape=[jax.ShapeDtypeStruct(*shape) for shape...]
    unnamed x24 -> x14, local copies, waits for them, and re-layouts: 4.37 us -> 0.03 us
    ppermute x24, waiting for transfers between devices: 16 us -> 14.2 us  [gathered(): lax.ppermute(total, 'chan', [(i, i ^ k * low) for i in range(n)])]
  transfers between devices with their start and end apart: 38 -> 38, of which waited for: 20 -> 25; matrix products, arithmetic and copies ran while one was open for 1% -> 1% of each run, Pallas kernels for 17% -> 22%
where the time goes in v1:
time: 118 us; the launch traced here: 117 us
  starting transfers between devices  46.2 us (39%)
  Pallas kernels  39 us (33%)
  waiting for transfers between devices  29.9 us (25%)
    pallas_call x31, Pallas kernels, call(): pl.pallas_call(kernel, out_shape=[jax.ShapeDtypeStruct(*shape) for shape...  35.8 us
    ppermute x24, starting transfers between devices, gathered(): lax.ppermute(total, 'chan', [(i, i ^ k * low) for i in range(n)])  28.4 us
    ppermute x7, starting transfers between devices, exchange(): far = lax.ppermute(far, 'facet', cross)  16.5 us
    ppermute x7, waiting for transfers between devices, exchange(): far = lax.ppermute(far, 'facet', cross)  15.7 us
    ppermute x24, waiting for transfers between devices, gathered(): lax.ppermute(total, 'chan', [(i, i ^ k * low) for i in range(n)])  14.2 us
    pallas_call x1, Pallas kernels, on_device(): pl.pallas_call(pack_kernel, out_shape=[jax.ShapeDtypeStruct(*first_sides)...  2.39 us
  transfers between devices with their start and end apart: 38, of which 25 were waited for; matrix products, arithmetic and copies ran while one was open for 1% of the time, Pallas kernels for 22%

profile of v1, /device:TPU:16, one launch (start us, length us, event | category | flops | bytes accessed | tf_op | source)
XLA Modules:
  0.0 117.3 jit_solution(9933132396390319780)
XLA Ops:
  0.7 2.4 %pack.1 = (f32[16,32,256]{2,1,0:T(8,128)}, f32[16,32,256]{2,1,0:T(8,128)}) custom-call(f32[16,32,256]{2,1,0:T(8,128)} %refs_2_.1, f32[16,2,32,256]{3,2,1,0:T(8,128)} %start_ref.1, f32[16,32,256]{2,1,0:T(8,128)} %dirty_ref.3), custom_call_target="tpu_custom_call" | custom-call | tf_op jit(solution)/shard_map/pack/pallas_call | solution.py:444
  3.2 2.4 %collective-permute-start.1 = (f32[16,32,256]{2,1,0:T(8,128)}, f32[16,32,256]{2,1,0:T(8,128)S(1)}, u32[]{:S(2)}, u32[]{:S(2)}) collective-permute-start(f32[16,32,256]{2,1,0:T(8,128)} %get-tuple-element.105), channel_id=1, source_target_pairs={{1,2},{2,1},{3,4},{4,3},{5,6},{6,5},{9,10},{10,9},{11,12},{12,11},... | collective-permute-start | bytes 1572872 | tf_op jit(solution)/shard_map/ppermute | solution.py:403
  6.7 6.3 %matrices.1 = (bf16[16,80,144]{2,1,0:T(8,128)(2,1)S(1)}, bf16[16,80,48]{2,1,0:T(8,128)(2,1)S(1)}, bf16[16,32,144]{2,1,0:T(8,128)(2,1)S(1)}, bf16[32,144]{1,0:T(8...) custom-call(s32[16]{0:T(128)S(1)} %copy-done.3, ...), custom_call_target="tpu_custom_call" | custom-call | tf_op jit(solution)/shard_map/matrices/pallas_call | solution.py:51
  13.9 1.0 first_rows.1
  14.9 2.4 %first_gradient.1 = (f32[16,32,256]{2,1,0:T(8,128)S(1)}, f32[16,32,256]{2,1,0:T(8,128)S(1)}) custom-call(f32[16,32,256]{2,1,0:T(8,128)S(1)} %get-tuple-element.112.part_ref, bf16[16,256,256]{2,1,0:T(8,128)(2,1)S(1)} %get-tuple-element.113.head_ref, bf16[16,256,256]{2,1,0:T(8,128)(2,1)S(1)} %get-tuple-element.114.rest_ref, ...), custom_call_target="tpu_custom_call" | custom-call | tf_op jit(solution)/shard_map/first_gradient/pallas_call | solution.py:51
  17.9 0.8 collective-permute-start.3
  18.7 2.0 %collective-permute-start.2 = (f32[16,16,256]{2,1,0:T(8,128)S(1)}, f32[16,16,256]{2,1,0:T(8,128)S(1)}, u32[]{:S(2)}, u32[]{:S(2)}) collective-permute-start(f32[16,16,256]{2,1,0:T(8,128)S(1)} %get-tuple-element.123), channel_id=1, source_target_pairs={{1,2},{2,1},{3,4},{4,3},{5,6},{6,5},{9,10},{10,9},{11,12},{12,11},... | collective-permute-start | bytes 786440 | tf_op jit(solution)/shard_map/ppermute | solution.py:403
  20.7 2.5 %collective-permute-start.7 = (f32[80,256]{1,0:T(8,128)S(1)}, f32[80,256]{1,0:T(8,128)S(1)}, u32[]{:S(2)}, u32[]{:S(2)}) collective-permute-start(f32[80,256]{1,0:T(8,128)S(1)} %get-tuple-element.132.refs_0_), channel_id=1, source_target_pairs={{0,24},{8,16},{16,8},{24,0},{1,25},{9,17},{17,9},{25,1},{2,26},{10... | collective-permute-start | bytes 245768 | tf_op jit(solution)/shard_map/ppermute | solution.py:419
  24.3 1.2 %near.6 = (f32[16,48,256]{2,1,0:T(8,128)S(1)}, f32[16,32,256]{2,1,0:T(8,128)S(1)}, f32[16,48,256]{2,1,0:T(8,128)S(1)}, f32[16,32,256]{2,1,0:T(8,128)S(1)}, f32[1...) custom-call(s32[1]{0:T(128)} %bitcast.odd_ref, f32[16,32,256]{2,1,0:T(8,128)S(1)} %get-tuple-element.124.own_ref.refs_7_, ...), custom_call_target="tpu_custom_call" | custom-call | tf_op jit(solution)/shard_map/near/pallas_call | solution.py:51
  25.5 0.9 collective-permute-done.2.far_ref
  27.0 2.5 %collective-permute-start.4 = (f32[80,256]{1,0:T(8,128)S(1)}, f32[80,256]{1,0:T(8,128)S(1)}, u32[]{:S(2)}, u32[]{:S(2)}) collective-permute-start(f32[80,256]{1,0:T(8,128)S(1)} %get-tuple-element.131.refs_0_), channel_id=1, source_target_pairs={{0,24},{8,16},{16,8},{24,0},{1,25},{9,17},{17,9},{25,1},{2,26},{10... | collective-permute-start | bytes 245768 | tf_op jit(solution)/shard_map/ppermute | solution.py:419
  30.6 1.9 %gradient.5.refs_8_ = f32[16,32,256]{2,1,0:T(8,128)S(1)} custom-call(f32[16,32,256]{2,1,0:T(8,128)S(1)} %get-tuple-element.135.part_ref, f32[16,16,256]{2,1,0:T(8,128)S(1)} %collective-permute-done.2.far_ref, bf16[16,80,48]{2,1,0:T(8,128)(2,1)S(1)} %get-tuple-element.107.far_mats_ref.mats_ref, bf16[16,256,256]{2,1,0:T(8,128)(2,1)S(1)} %get-tuple-element.113.head_ref, ...), custom_call_target="tpu_custom_call" | custom-call | tf_op jit(solution)/shard_map/gradient/pallas_call | solution.py:51
  33.1 1.3 %collective-permute-done.5.refs_2_ = f32[80,256]{1,0:T(8,128)S(1)} collective-permute-done((f32[80,256]{1,0:T(8,128)S(1)}, f32[80,256]{1,0:T(8,128)S(1)}, u32[]{:S(2)}, u32[]{:S(2)}) %collective-permute-start.5) | collective-permute-done | bytes 81952 | tf_op jit(solution)/shard_map/ppermute | solution.py:419
  35.2 2.4 %collective-permute-start.10 = (f32[16,16,256]{2,1,0:T(8,128)S(1)}, f32[16,16,256]{2,1,0:T(8,128)S(1)}, u32[]{:S(2)}, u32[]{:S(2)}) collective-permute-start(f32[16,16,256]{2,1,0:T(8,128)S(1)} %get-tuple-element.137), channel_id=1, source_target_pairs={{1,2},{2,1},{3,4},{4,3},{5,6},{6,5},{9,10},{10,9},{11,12},{12,11},... | collective-permute-start | bytes 786440 | tf_op jit(solution)/shard_map/ppermute | solution.py:403
  37.7 1.2 %near.7 = (f32[16,48,256]{2,1,0:T(8,128)S(1)}, f32[16,32,256]{2,1,0:T(8,128)S(1)}, f32[16,48,256]{2,1,0:T(8,128)S(1)}, f32[16,32,256]{2,1,0:T(8,128)S(1)}, f32[1...) custom-call(s32[1]{0:T(128)} %bitcast.odd_ref, f32[16,32,256]{2,1,0:T(8,128)S(1)} %get-tuple-element.138.own_ref.refs_7_, ...), custom_call_target="tpu_custom_call" | custom-call | tf_op jit(solution)/shard_map/near/pallas_call | solution.py:51
  38.9 4.1 %collective-permute-done.10.far_ref = f32[16,16,256]{2,1,0:T(8,128)S(1)} collective-permute-done((f32[16,16,256]{2,1,0:T(8,128)S(1)}, f32[16,16,256]{2,1,0:T(8,128)S(1)}, u32[]{:S(2)}, u32[]{:S(2)}) %collective-permute-start.10) | collective-permute-done | bytes 262176 | tf_op jit(solution)/shard_map/ppermute | solution.py:403
  43.5 2.4 %collective-permute-start.12 = (f32[80,256]{1,0:T(8,128)S(1)}, f32[80,256]{1,0:T(8,128)S(1)}, u32[]{:S(2)}, u32[]{:S(2)}) collective-permute-start(f32[80,256]{1,0:T(8,128)S(1)} %get-tuple-element.147.refs_0_), channel_id=1, source_target_pairs={{0,24},{8,16},{16,8},{24,0},{1,25},{9,17},{17,9},{25,1},{2,26},{10... | collective-permute-start | bytes 245768 | tf_op jit(solution)/shard_map/ppermute | solution.py:419
  47.1 1.9 %gradient.6.refs_8_ = f32[16,32,256]{2,1,0:T(8,128)S(1)} custom-call(f32[16,32,256]{2,1,0:T(8,128)S(1)} %get-tuple-element.150.part_ref, f32[16,16,256]{2,1,0:T(8,128)S(1)} %collective-permute-done.10.far_ref, bf16[16,80,48]{2,1,0:T(8,128)(2,1)S(1)} %get-tuple-element.107.far_mats_ref.mats_ref, bf16[16,256,256]{2,1,0:T(8,128)(2,1)S(1)} %get-tuple-element.113.head_ref, ...), custom_call_target="tpu_custom_call" | custom-call | tf_op jit(solution)/shard_map/gradient/pallas_call | solution.py:51
  48.9 0.9 collective-permute-done.12.refs_1_
  49.8 1.2 %collective-permute-done.13.refs_2_ = f32[80,256]{1,0:T(8,128)S(1)} collective-permute-done((f32[80,256]{1,0:T(8,128)S(1)}, f32[80,256]{1,0:T(8,128)S(1)}, u32[]{:S(2)}, u32[]{:S(2)}) %collective-permute-start.13) | collective-permute-done | bytes 81952 | tf_op jit(solution)/shard_map/ppermute | solution.py:419
  51.8 2.4 %collective-permute-start.15 = (f32[16,16,256]{2,1,0:T(8,128)S(1)}, f32[16,16,256]{2,1,0:T(8,128)S(1)}, u32[]{:S(2)}, u32[]{:S(2)}) collective-permute-start(f32[16,16,256]{2,1,0:T(8,128)S(1)} %get-tuple-element.151), channel_id=1, source_target_pairs={{1,2},{2,1},{3,4},{4,3},{5,6},{6,5},{9,10},{10,9},{11,12},{12,11},... | collective-permute-start | bytes 786440 | tf_op jit(solution)/shard_map/ppermute | solution.py:403
  54.2 1.2 %near.8 = (f32[16,48,256]{2,1,0:T(8,128)S(1)}, f32[16,32,256]{2,1,0:T(8,128)S(1)}, f32[16,48,256]{2,1,0:T(8,128)S(1)}, f32[16,32,256]{2,1,0:T(8,128)S(1)}, f32[1...) custom-call(s32[1]{0:T(128)} %bitcast.odd_ref, f32[16,32,256]{2,1,0:T(8,128)S(1)} %get-tuple-element.152.own_ref.refs_7_, ...), custom_call_target="tpu_custom_call" | custom-call | tf_op jit(solution)/shard_map/near/pallas_call | solution.py:51
  55.5 4.0 %collective-permute-done.15.far_ref = f32[16,16,256]{2,1,0:T(8,128)S(1)} collective-permute-done((f32[16,16,256]{2,1,0:T(8,128)S(1)}, f32[16,16,256]{2,1,0:T(8,128)S(1)}, u32[]{:S(2)}, u32[]{:S(2)}) %collective-permute-start.15) | collective-permute-done | bytes 262176 | tf_op jit(solution)/shard_map/ppermute | solution.py:403
  60.1 2.3 %collective-permute-start.17 = (f32[80,256]{1,0:T(8,128)S(1)}, f32[80,256]{1,0:T(8,128)S(1)}, u32[]{:S(2)}, u32[]{:S(2)}) collective-permute-start(f32[80,256]{1,0:T(8,128)S(1)} %get-tuple-element.161.refs_0_), channel_id=1, source_target_pairs={{0,24},{8,16},{16,8},{24,0},{1,25},{9,17},{17,9},{25,1},{2,26},{10... | collective-permute-start | bytes 245768 | tf_op jit(solution)/shard_map/ppermute | solution.py:419
  63.6 1.9 %gradient.7.refs_8_ = f32[16,32,256]{2,1,0:T(8,128)S(1)} custom-call(f32[16,32,256]{2,1,0:T(8,128)S(1)} %get-tuple-element.164.part_ref, f32[16,16,256]{2,1,0:T(8,128)S(1)} %collective-permute-done.15.far_ref, bf16[16,80,48]{2,1,0:T(8,128)(2,1)S(1)} %get-tuple-element.107.far_mats_ref.mats_ref, bf16[16,256,256]{2,1,0:T(8,128)(2,1)S(1)} %get-tuple-element.113.head_ref, ...), custom_call_target="tpu_custom_call" | custom-call | tf_op jit(solution)/shard_map/gradient/pallas_call | solution.py:51
  65.5 0.9 collective-permute-done.17.refs_1_
  66.4 1.1 collective-permute-done.18.refs_2_
  68.4 2.4 %collective-permute-start.20 = (f32[16,16,256]{2,1,0:T(8,128)S(1)}, f32[16,16,256]{2,1,0:T(8,128)S(1)}, u32[]{:S(2)}, u32[]{:S(2)}) collective-permute-start(f32[16,16,256]{2,1,0:T(8,128)S(1)} %get-tuple-element.165), channel_id=1, source_target_pairs={{1,2},{2,1},{3,4},{4,3},{5,6},{6,5},{9,10},{10,9},{11,12},{12,11},... | collective-permute-start | bytes 786440 | tf_op jit(solution)/shard_map/ppermute | solution.py:403
  70.9 2.3 %collective-permute-start.25 = (f32[80,256]{1,0:T(8,128)S(1)}, f32[80,256]{1,0:T(8,128)S(1)}, u32[]{:S(2)}, u32[]{:S(2)}) collective-permute-start(f32[80,256]{1,0:T(8,128)S(1)} %squares.1.refs_0_), channel_id=1, source_target_pairs={{0,24},{8,16},{16,8},{24,0},{1,25},{9,17},{17,9},{25,1},{2,26},{10... | collective-permute-start | bytes 245768 | tf_op jit(solution)/shard_map/ppermute | solution.py:419
  74.5 1.2 %near.9 = (f32[16,48,256]{2,1,0:T(8,128)S(1)}, f32[16,32,256]{2,1,0:T(8,128)S(1)}, f32[16,48,256]{2,1,0:T(8,128)S(1)}, f32[16,32,256]{2,1,0:T(8,128)S(1)}, f32[1...) custom-call(s32[1]{0:T(128)} %bitcast.odd_ref, f32[16,32,256]{2,1,0:T(8,128)S(1)} %get-tuple-element.166.own_ref.refs_7_, ...), custom_call_target="tpu_custom_call" | custom-call | tf_op jit(solution)/shard_map/near/pallas_call | solution.py:51
  76.6 2.3 %collective-permute-start.22 = (f32[80,256]{1,0:T(8,128)S(1)}, f32[80,256]{1,0:T(8,128)S(1)}, u32[]{:S(2)}, u32[]{:S(2)}) collective-permute-start(f32[80,256]{1,0:T(8,128)S(1)} %get-tuple-element.175.refs_0_), channel_id=1, source_target_pairs={{0,24},{8,16},{16,8},{24,0},{1,25},{9,17},{17,9},{25,1},{2,26},{10... | collective-permute-start | bytes 245768 | tf_op jit(solution)/shard_map/ppermute | solution.py:419
  80.3 1.9 %gradient.8.refs_8_ = f32[16,32,256]{2,1,0:T(8,128)S(1)} custom-call(f32[16,32,256]{2,1,0:T(8,128)S(1)} %get-tuple-element.178.part_ref, f32[16,16,256]{2,1,0:T(8,128)S(1)} %collective-permute-done.20.far_ref, bf16[16,80,48]{2,1,0:T(8,128)(2,1)S(1)} %get-tuple-element.107.far_mats_ref.mats_ref, bf16[16,256,256]{2,1,0:T(8,128)(2,1)S(1)} %get-tuple-element.113.head_ref, ...), custom_call_target="tpu_custom_call" | custom-call | tf_op jit(solution)/shard_map/gradient/pallas_call | solution.py:51
  82.9 1.4 %collective-permute-done.23.refs_2_ = f32[80,256]{1,0:T(8,128)S(1)} collective-permute-done((f32[80,256]{1,0:T(8,128)S(1)}, f32[80,256]{1,0:T(8,128)S(1)}, u32[]{:S(2)}, u32[]{:S(2)}) %collective-permute-start.23) | collective-permute-done | bytes 81952 | tf_op jit(solution)/shard_map/ppermute | solution.py:419
  85.2 2.4 %collective-permute-start.28 = (f32[16,16,256]{2,1,0:T(8,128)S(1)}, f32[16,16,256]{2,1,0:T(8,128)S(1)}, u32[]{:S(2)}, u32[]{:S(2)}) collective-permute-start(f32[16,16,256]{2,1,0:T(8,128)S(1)} %get-tuple-element.179), channel_id=1, source_target_pairs={{1,2},{2,1},{3,4},{4,3},{5,6},{6,5},{9,10},{10,9},{11,12},{12,11},... | collective-permute-start | bytes 786440 | tf_op jit(solution)/shard_map/ppermute | solution.py:403
  87.7 1.2 %near.10 = (f32[16,48,256]{2,1,0:T(8,128)S(1)}, f32[16,32,256]{2,1,0:T(8,128)S(1)}, f32[16,48,256]{2,1,0:T(8,128)S(1)}, f32[16,32,256]{2,1,0:T(8,128)S(1)}, f32[...) custom-call(s32[1]{0:T(128)} %bitcast.odd_ref, f32[16,32,256]{2,1,0:T(8,128)S(1)} %get-tuple-element.180.own_ref.refs_7_, ...), custom_call_target="tpu_custom_call" | custom-call | tf_op jit(solution)/shard_map/near/pallas_call | solution.py:51
  88.9 4.0 %collective-permute-done.28.far_ref = f32[16,16,256]{2,1,0:T(8,128)S(1)} collective-permute-done((f32[16,16,256]{2,1,0:T(8,128)S(1)}, f32[16,16,256]{2,1,0:T(8,128)S(1)}, u32[]{:S(2)}, u32[]{:S(2)}) %collective-permute-start.28) | collective-permute-done | bytes 262176 | tf_op jit(solution)/shard_map/ppermute | solution.py:403
  93.5 2.3 %collective-permute-start.30 = (f32[80,256]{1,0:T(8,128)S(1)}, f32[80,256]{1,0:T(8,128)S(1)}, u32[]{:S(2)}, u32[]{:S(2)}) collective-permute-start(f32[80,256]{1,0:T(8,128)S(1)} %get-tuple-element.189.refs_0_), channel_id=1, source_target_pairs={{0,24},{8,16},{16,8},{24,0},{1,25},{9,17},{17,9},{25,1},{2,26},{10... | collective-permute-start | bytes 245768 | tf_op jit(solution)/shard_map/ppermute | solution.py:419
  97.0 1.9 %gradient.9.refs_8_ = f32[16,32,256]{2,1,0:T(8,128)S(1)} custom-call(f32[16,32,256]{2,1,0:T(8,128)S(1)} %get-tuple-element.192.part_ref, f32[16,16,256]{2,1,0:T(8,128)S(1)} %collective-permute-done.28.far_ref, bf16[16,80,48]{2,1,0:T(8,128)(2,1)S(1)} %get-tuple-element.107.far_mats_ref.mats_ref, bf16[16,256,256]{2,1,0:T(8,128)(2,1)S(1)} %get-tuple-element.113.head_ref, ...), custom_call_target="tpu_custom_call" | custom-call | tf_op jit(solution)/shard_map/gradient/pallas_call | solution.py:51
  98.9 0.9 collective-permute-done.30.refs_1_
  99.8 1.1 collective-permute-done.31.refs_2_
  101.8 2.4 %collective-permute-start.33 = (f32[16,8,256]{2,1,0:T(8,128)S(1)}, f32[16,8,256]{2,1,0:T(8,128)S(1)}, u32[]{:S(2)}, u32[]{:S(2)}) collective-permute-start(f32[16,8,256]{2,1,0:T(8,128)S(1)} %get-tuple-element.194), channel_id=1, source_target_pairs={{1,2},{2,1},{3,4},{4,3},{5,6},{6,5},{9,10},{10,9},{11,12},{12,11},... | collective-permute-start | bytes 393224 | tf_op jit(solution)/shard_map/ppermute | solution.py:403
  104.2 2.0 %near.11 = (f32[16,48,256]{2,1,0:T(8,128)S(1)}, f32[16,32,256]{2,1,0:T(8,128)}, f32[16,48,256]{2,1,0:T(8,128)S(1)}, f32[16,32,256]{2,1,0:T(8,128)}, f32[16,32,256]{2,1,0:T(8,128)S(1)}, /*index=5*/f32[80,256]{1,0:T(8,128)S(1)}) custom-call(s32[1]{0:T(128)} %bitcast.odd_ref, f32[16,32,256]{2,1,0:T(8,128)S(1)} %get-tuple-element.193.own_ref, ...), custom_call_target="tpu_custom_call" | custom-call | tf_op jit(solution)/shard_map/near/pallas_call | solution.py:51
  106.2 1.8 %collective-permute-done.33.far_ref = f32[16,8,256]{2,1,0:T(8,128)S(1)} collective-permute-done((f32[16,8,256]{2,1,0:T(8,128)S(1)}, f32[16,8,256]{2,1,0:T(8,128)S(1)}, u32[]{:S(2)}, u32[]{:S(2)}) %collective-permute-start.33) | collective-permute-done | bytes 131104 | tf_op jit(solution)/shard_map/ppermute | solution.py:403
  108.6 2.3 %collective-permute-start.35 = (f32[80,256]{1,0:T(8,128)S(1)}, f32[80,256]{1,0:T(8,128)S(1)}, u32[]{:S(2)}, u32[]{:S(2)}) collective-permute-start(f32[80,256]{1,0:T(8,128)S(1)} %get-tuple-element.203._.refs_0_), channel_id=1, source_target_pairs={{0,24},{8,16},{16,8},{24,0},{1,25},{9,17},{17,9},{25,1},{2,26},{10... | collective-permute-start | bytes 245768 | tf_op jit(solution)/shard_map/ppermute | solution.py:419
  112.2 0.8 publish.1
  113.0 1.9 %collective-permute-done.35.refs_1_ = f32[80,256]{1,0:T(8,128)S(1)} collective-permute-done((f32[80,256]{1,0:T(8,128)S(1)}, f32[80,256]{1,0:T(8,128)S(1)}, u32[]{:S(2)}, u32[]{:S(2)}) %collective-permute-start.35) | collective-permute-done | bytes 81952 | tf_op jit(solution)/shard_map/ppermute | solution.py:419
  114.9 1.1 collective-permute-done.36.refs_2_
  116.2 1.1 final.1
  (93 shorter events, 22.0 us)
Async XLA Ops:
  0.6 12.4 %copy-start = (f32[16,32,256]{2,1,0:T(8,128)S(1)}, f32[16,32,256]{2,1,0:T(8,128)}, u32[]{:S(2)}) copy-start(f32[16,32,256]{2,1,0:T(8,128)} %refs_2_.1) | copy-start | bytes 1572868
  0.6 13.3 %copy-start.2 = (f32[16,32,256]{2,1,0:T(8,128)S(1)}, f32[16,32,256]{2,1,0:T(8,128)}, u32[]{:S(2)}) copy-start(f32[16,32,256]{2,1,0:T(8,128)} %dirty_ref.3) | copy-start | bytes 1572868
  0.7 12.8 %copy-start.1 = (f32[16,2,32,256]{3,2,1,0:T(8,128)S(1)}, f32[16,2,32,256]{3,2,1,0:T(8,128)}, u32[]{:S(2)}) copy-start(f32[16,2,32,256]{3,2,1,0:T(8,128)} %start_ref.1) | copy-start | bytes 3145732
  0.7 5.0 %copy-start.6 = (f32[2,17]{1,0:T(2,128)S(1)}, f32[2,17]{1,0:T(2,128)}, u32[]{:S(2)}) copy-start(f32[2,17]{1,0:T(2,128)} %param.12) | copy-start | bytes 412
  0.7 5.4 %copy-start.4 = (f32[16,17]{1,0:T(8,128)S(1)}, f32[16,17]{1,0:T(8,128)}, u32[]{:S(2)}) copy-start(f32[16,17]{1,0:T(8,128)} %param.11) | copy-start | bytes 3268
  0.7 5.7 %copy-start.5 = (f32[16,17]{1,0:T(8,128)S(1)}, f32[16,17]{1,0:T(8,128)}, u32[]{:S(2)}) copy-start(f32[16,17]{1,0:T(8,128)} %param.10) | copy-start | bytes 3268
  0.7 6.0 %copy-start.3 = (s32[16]{0:T(128)S(1)}, s32[16]{0:T(128)}, u32[]{:S(2)}) copy-start(s32[16]{0:T(128)} %flags_ref.1) | copy-start | bytes 196
  3.1 10.4 %collective-permute-start = (f32[16,32,256]{2,1,0:T(8,128)}, f32[16,32,256]{2,1,0:T(8,128)S(1)}, u32[]{:S(2)}, u32[]{:S(2)}) collective-permute-start(f32[16,32,256]{2,1,0:T(8,128)} %get-tuple-element.104), channel_id=1, source_target_pairs={{0,1},{1,0},{2,3},{3,2},{4,5},{5,4},{6,7},{7,6},{8,9},{9,8},{10,11... | collective-permute-start | bytes 1572872 | tf_op jit(solution)/shard_map/ppermute | solution.py:404
  3.2 10.7 %collective-permute-start.1 = (f32[16,32,256]{2,1,0:T(8,128)}, f32[16,32,256]{2,1,0:T(8,128)S(1)}, u32[]{:S(2)}, u32[]{:S(2)}) collective-permute-start(f32[16,32,256]{2,1,0:T(8,128)} %get-tuple-element.105), channel_id=1, source_target_pairs={{1,2},{2,1},{3,4},{4,3},{5,6},{6,5},{9,10},{10,9},{11,12},{12,11},... | collective-permute-start | bytes 1572872 | tf_op jit(solution)/shard_map/ppermute | solution.py:403
  17.9 6.4 %collective-permute-start.3 = (f32[16,16,256]{2,1,0:T(8,128)S(1)}, f32[16,16,256]{2,1,0:T(8,128)S(1)}, u32[]{:S(2)}, u32[]{:S(2)}) collective-permute-start(f32[16,16,256]{2,1,0:T(8,128)S(1)} %get-tuple-element.125), channel_id=1, source_target_pairs={{0,1},{1,0},{2,3},{3,2},{4,5},{5,4},{6,7},{7,6},{8,9},{9,8},{10,11... | collective-permute-start | bytes 786440 | tf_op jit(solution)/shard_map/ppermute | solution.py:404
  18.7 7.7 %collective-permute-start.2 = (f32[16,16,256]{2,1,0:T(8,128)S(1)}, f32[16,16,256]{2,1,0:T(8,128)S(1)}, u32[]{:S(2)}, u32[]{:S(2)}) collective-permute-start(f32[16,16,256]{2,1,0:T(8,128)S(1)} %get-tuple-element.123), channel_id=1, source_target_pairs={{1,2},{2,1},{3,4},{4,3},{5,6},{6,5},{9,10},{10,9},{11,12},{12,11},... | collective-permute-start | bytes 786440 | tf_op jit(solution)/shard_map/ppermute | solution.py:403
  20.7 9.3 %collective-permute-start.7 = (f32[80,256]{1,0:T(8,128)S(1)}, f32[80,256]{1,0:T(8,128)S(1)}, u32[]{:S(2)}, u32[]{:S(2)}) collective-permute-start(f32[80,256]{1,0:T(8,128)S(1)} %get-tuple-element.132.refs_0_), channel_id=1, source_target_pairs={{0,24},{8,16},{16,8},{24,0},{1,25},{9,17},{17,9},{25,1},{2,26},{10... | collective-permute-start | bytes 245768 | tf_op jit(solution)/shard_map/ppermute | solution.py:419
  23.2 7.3 %collective-permute-start.8 = (f32[80,256]{1,0:T(8,128)S(1)}, f32[80,256]{1,0:T(8,128)S(1)}, u32[]{:S(2)}, u32[]{:S(2)}) collective-permute-start(f32[80,256]{1,0:T(8,128)S(1)} %get-tuple-element.132.refs_0_), channel_id=1, source_target_pairs={{0,8},{8,0},{16,24},{24,16},{1,9},{9,1},{17,25},{25,17},{2,10},{10... | collective-permute-start | bytes 245768 | tf_op jit(solution)/shard_map/ppermute | solution.py:419
  23.8 6.8 %collective-permute-start.9 = (f32[80,256]{1,0:T(8,128)S(1)}, f32[80,256]{1,0:T(8,128)S(1)}, u32[]{:S(2)}, u32[]{:S(2)}) collective-permute-start(f32[80,256]{1,0:T(8,128)S(1)} %get-tuple-element.132.refs_0_), channel_id=1, source_target_pairs={{0,16},{8,24},{16,0},{24,8},{1,17},{9,25},{17,1},{25,9},{2,18},{10... | collective-permute-start | bytes 245768 | tf_op jit(solution)/shard_map/ppermute | solution.py:419
  27.0 6.2 %collective-permute-start.4 = (f32[80,256]{1,0:T(8,128)S(1)}, f32[80,256]{1,0:T(8,128)S(1)}, u32[]{:S(2)}, u32[]{:S(2)}) collective-permute-start(f32[80,256]{1,0:T(8,128)S(1)} %get-tuple-element.131.refs_0_), channel_id=1, source_target_pairs={{0,24},{8,16},{16,8},{24,0},{1,25},{9,17},{17,9},{25,1},{2,26},{10... | collective-permute-start | bytes 245768 | tf_op jit(solution)/shard_map/ppermute | solution.py:419
  29.5 4.9 %collective-permute-start.5 = (f32[80,256]{1,0:T(8,128)S(1)}, f32[80,256]{1,0:T(8,128)S(1)}, u32[]{:S(2)}, u32[]{:S(2)}) collective-permute-start(f32[80,256]{1,0:T(8,128)S(1)} %get-tuple-element.131.refs_0_), channel_id=1, source_target_pairs={{0,8},{8,0},{16,24},{24,16},{1,9},{9,1},{17,25},{25,17},{2,10},{10... | collective-permute-start | bytes 245768 | tf_op jit(solution)/shard_map/ppermute | solution.py:419
  30.0 4.5 %collective-permute-start.6 = (f32[80,256]{1,0:T(8,128)S(1)}, f32[80,256]{1,0:T(8,128)S(1)}, u32[]{:S(2)}, u32[]{:S(2)}) collective-permute-start(f32[80,256]{1,0:T(8,128)S(1)} %get-tuple-element.131.refs_0_), channel_id=1, source_target_pairs={{0,16},{8,24},{16,0},{24,8},{1,17},{9,25},{17,1},{25,9},{2,18},{10... | collective-permute-start | bytes 245768 | tf_op jit(solution)/shard_map/ppermute | solution.py:419
  35.2 2.5 %collective-permute-start.11 = (f32[16,16,256]{2,1,0:T(8,128)S(1)}, f32[16,16,256]{2,1,0:T(8,128)S(1)}, u32[]{:S(2)}, u32[]{:S(2)}) collective-permute-start(f32[16,16,256]{2,1,0:T(8,128)S(1)} %get-tuple-element.139), channel_id=1, source_target_pairs={{0,1},{1,0},{2,3},{3,2},{4,5},{5,4},{6,7},{7,6},{8,9},{9,8},{10,11... | collective-permute-start | bytes 786440 | tf_op jit(solution)/shard_map/ppermute | solution.py:404
  35.2 7.7 %collective-permute-start.10 = (f32[16,16,256]{2,1,0:T(8,128)S(1)}, f32[16,16,256]{2,1,0:T(8,128)S(1)}, u32[]{:S(2)}, u32[]{:S(2)}) collective-permute-start(f32[16,16,256]{2,1,0:T(8,128)S(1)} %get-tuple-element.137), channel_id=1, source_target_pairs={{1,2},{2,1},{3,4},{4,3},{5,6},{6,5},{9,10},{10,9},{11,12},{12,11},... | collective-permute-start | bytes 786440 | tf_op jit(solution)/shard_map/ppermute | solution.py:403
  43.5 6.3 %collective-permute-start.12 = (f32[80,256]{1,0:T(8,128)S(1)}, f32[80,256]{1,0:T(8,128)S(1)}, u32[]{:S(2)}, u32[]{:S(2)}) collective-permute-start(f32[80,256]{1,0:T(8,128)S(1)} %get-tuple-element.147.refs_0_), channel_id=1, source_target_pairs={{0,24},{8,16},{16,8},{24,0},{1,25},{9,17},{17,9},{25,1},{2,26},{10... | collective-permute-start | bytes 245768 | tf_op jit(solution)/shard_map/ppermute | solution.py:419
  45.9 5.1 %collective-permute-start.13 = (f32[80,256]{1,0:T(8,128)S(1)}, f32[80,256]{1,0:T(8,128)S(1)}, u32[]{:S(2)}, u32[]{:S(2)}) collective-permute-start(f32[80,256]{1,0:T(8,128)S(1)} %get-tuple-element.147.refs_0_), channel_id=1, source_target_pairs={{0,8},{8,0},{16,24},{24,16},{1,9},{9,1},{17,25},{25,17},{2,10},{10... | collective-permute-start | bytes 245768 | tf_op jit(solution)/shard_map/ppermute | solution.py:419
  46.4 4.7 %collective-permute-start.14 = (f32[80,256]{1,0:T(8,128)S(1)}, f32[80,256]{1,0:T(8,128)S(1)}, u32[]{:S(2)}, u32[]{:S(2)}) collective-permute-start(f32[80,256]{1,0:T(8,128)S(1)} %get-tuple-element.147.refs_0_), channel_id=1, source_target_pairs={{0,16},{8,24},{16,0},{24,8},{1,17},{9,25},{17,1},{25,9},{2,18},{10... | collective-permute-start | bytes 245768 | tf_op jit(solution)/shard_map/ppermute | solution.py:419
  51.7 2.5 %collective-permute-start.16 = (f32[16,16,256]{2,1,0:T(8,128)S(1)}, f32[16,16,256]{2,1,0:T(8,128)S(1)}, u32[]{:S(2)}, u32[]{:S(2)}) collective-permute-start(f32[16,16,256]{2,1,0:T(8,128)S(1)} %get-tuple-element.153), channel_id=1, source_target_pairs={{0,1},{1,0},{2,3},{3,2},{4,5},{5,4},{6,7},{7,6},{8,9},{9,8},{10,11... | collective-permute-start | bytes 786440 | tf_op jit(solution)/shard_map/ppermute | solution.py:404
  51.8 7.7 %collective-permute-start.15 = (f32[16,16,256]{2,1,0:T(8,128)S(1)}, f32[16,16,256]{2,1,0:T(8,128)S(1)}, u32[]{:S(2)}, u32[]{:S(2)}) collective-permute-start(f32[16,16,256]{2,1,0:T(8,128)S(1)} %get-tuple-element.151), channel_id=1, source_target_pairs={{1,2},{2,1},{3,4},{4,3},{5,6},{6,5},{9,10},{10,9},{11,12},{12,11},... | collective-permute-start | bytes 786440 | tf_op jit(solution)/shard_map/ppermute | solution.py:403
  60.1 6.3 %collective-permute-start.17 = (f32[80,256]{1,0:T(8,128)S(1)}, f32[80,256]{1,0:T(8,128)S(1)}, u32[]{:S(2)}, u32[]{:S(2)}) collective-permute-start(f32[80,256]{1,0:T(8,128)S(1)} %get-tuple-element.161.refs_0_), channel_id=1, source_target_pairs={{0,24},{8,16},{16,8},{24,0},{1,25},{9,17},{17,9},{25,1},{2,26},{10... | collective-permute-start | bytes 245768 | tf_op jit(solution)/shard_map/ppermute | solution.py:419
  62.4 5.1 %collective-permute-start.18 = (f32[80,256]{1,0:T(8,128)S(1)}, f32[80,256]{1,0:T(8,128)S(1)}, u32[]{:S(2)}, u32[]{:S(2)}) collective-permute-start(f32[80,256]{1,0:T(8,128)S(1)} %get-tuple-element.161.refs_0_), channel_id=1, source_target_pairs={{0,8},{8,0},{16,24},{24,16},{1,9},{9,1},{17,25},{25,17},{2,10},{10... | collective-permute-start | bytes 245768 | tf_op jit(solution)/shard_map/ppermute | solution.py:419
  62.9 4.7 %collective-permute-start.19 = (f32[80,256]{1,0:T(8,128)S(1)}, f32[80,256]{1,0:T(8,128)S(1)}, u32[]{:S(2)}, u32[]{:S(2)}) collective-permute-start(f32[80,256]{1,0:T(8,128)S(1)} %get-tuple-element.161.refs_0_), channel_id=1, source_target_pairs={{0,16},{8,24},{16,0},{24,8},{1,17},{9,25},{17,1},{25,9},{2,18},{10... | collective-permute-start | bytes 245768 | tf_op jit(solution)/shard_map/ppermute | solution.py:419
  68.3 6.2 %collective-permute-start.21 = (f32[16,16,256]{2,1,0:T(8,128)S(1)}, f32[16,16,256]{2,1,0:T(8,128)S(1)}, u32[]{:S(2)}, u32[]{:S(2)}) collective-permute-start(f32[16,16,256]{2,1,0:T(8,128)S(1)} %get-tuple-element.167), channel_id=1, source_target_pairs={{0,1},{1,0},{2,3},{3,2},{4,5},{5,4},{6,7},{7,6},{8,9},{9,8},{10,11... | collective-permute-start | bytes 786440 | tf_op jit(solution)/shard_map/ppermute | solution.py:404
  68.4 7.7 %collective-permute-start.20 = (f32[16,16,256]{2,1,0:T(8,128)S(1)}, f32[16,16,256]{2,1,0:T(8,128)S(1)}, u32[]{:S(2)}, u32[]{:S(2)}) collective-permute-start(f32[16,16,256]{2,1,0:T(8,128)S(1)} %get-tuple-element.165), channel_id=1, source_target_pairs={{1,2},{2,1},{3,4},{4,3},{5,6},{6,5},{9,10},{10,9},{11,12},{12,11},... | collective-permute-start | bytes 786440 | tf_op jit(solution)/shard_map/ppermute | solution.py:403
  70.9 8.5 %collective-permute-start.25 = (f32[80,256]{1,0:T(8,128)S(1)}, f32[80,256]{1,0:T(8,128)S(1)}, u32[]{:S(2)}, u32[]{:S(2)}) collective-permute-start(f32[80,256]{1,0:T(8,128)S(1)} %squares.1.refs_0_), channel_id=1, source_target_pairs={{0,24},{8,16},{16,8},{24,0},{1,25},{9,17},{17,9},{25,1},{2,26},{10... | collective-permute-start | bytes 245768 | tf_op jit(solution)/shard_map/ppermute | solution.py:419
  73.2 7.0 %collective-permute-start.26 = (f32[80,256]{1,0:T(8,128)S(1)}, f32[80,256]{1,0:T(8,128)S(1)}, u32[]{:S(2)}, u32[]{:S(2)}) collective-permute-start(f32[80,256]{1,0:T(8,128)S(1)} %squares.1.refs_0_), channel_id=1, source_target_pairs={{0,8},{8,0},{16,24},{24,16},{1,9},{9,1},{17,25},{25,17},{2,10},{10... | collective-permute-start | bytes 245768 | tf_op jit(solution)/shard_map/ppermute | solution.py:419
  73.8 6.4 %collective-permute-start.27 = (f32[80,256]{1,0:T(8,128)S(1)}, f32[80,256]{1,0:T(8,128)S(1)}, u32[]{:S(2)}, u32[]{:S(2)}) collective-permute-start(f32[80,256]{1,0:T(8,128)S(1)} %squares.1.refs_0_), channel_id=1, source_target_pairs={{0,16},{8,24},{16,0},{24,8},{1,17},{9,25},{17,1},{25,9},{2,18},{10... | collective-permute-start | bytes 245768 | tf_op jit(solution)/shard_map/ppermute | solution.py:419
  76.6 6.3 %collective-permute-start.22 = (f32[80,256]{1,0:T(8,128)S(1)}, f32[80,256]{1,0:T(8,128)S(1)}, u32[]{:S(2)}, u32[]{:S(2)}) collective-permute-start(f32[80,256]{1,0:T(8,128)S(1)} %get-tuple-element.175.refs_0_), channel_id=1, source_target_pairs={{0,24},{8,16},{16,8},{24,0},{1,25},{9,17},{17,9},{25,1},{2,26},{10... | collective-permute-start | bytes 245768 | tf_op jit(solution)/shard_map/ppermute | solution.py:419
  78.9 5.4 %collective-permute-start.23 = (f32[80,256]{1,0:T(8,128)S(1)}, f32[80,256]{1,0:T(8,128)S(1)}, u32[]{:S(2)}, u32[]{:S(2)}) collective-permute-start(f32[80,256]{1,0:T(8,128)S(1)} %get-tuple-element.175.refs_0_), channel_id=1, source_target_pairs={{0,8},{8,0},{16,24},{24,16},{1,9},{9,1},{17,25},{25,17},{2,10},{10... | collective-permute-start | bytes 245768 | tf_op jit(solution)/shard_map/ppermute | solution.py:419
  79.5 5.0 %collective-permute-start.24 = (f32[80,256]{1,0:T(8,128)S(1)}, f32[80,256]{1,0:T(8,128)S(1)}, u32[]{:S(2)}, u32[]{:S(2)}) collective-permute-start(f32[80,256]{1,0:T(8,128)S(1)} %get-tuple-element.175.refs_0_), channel_id=1, source_target_pairs={{0,16},{8,24},{16,0},{24,8},{1,17},{9,25},{17,1},{25,9},{2,18},{10... | collective-permute-start | bytes 245768 | tf_op jit(solution)/shard_map/ppermute | solution.py:419
  85.1 2.5 %collective-permute-start.29 = (f32[16,16,256]{2,1,0:T(8,128)S(1)}, f32[16,16,256]{2,1,0:T(8,128)S(1)}, u32[]{:S(2)}, u32[]{:S(2)}) collective-permute-start(f32[16,16,256]{2,1,0:T(8,128)S(1)} %get-tuple-element.181), channel_id=1, source_target_pairs={{0,1},{1,0},{2,3},{3,2},{4,5},{5,4},{6,7},{7,6},{8,9},{9,8},{10,11... | collective-permute-start | bytes 786440 | tf_op jit(solution)/shard_map/ppermute | solution.py:404
  85.2 7.7 %collective-permute-start.28 = (f32[16,16,256]{2,1,0:T(8,128)S(1)}, f32[16,16,256]{2,1,0:T(8,128)S(1)}, u32[]{:S(2)}, u32[]{:S(2)}) collective-permute-start(f32[16,16,256]{2,1,0:T(8,128)S(1)} %get-tuple-element.179), channel_id=1, source_target_pairs={{1,2},{2,1},{3,4},{4,3},{5,6},{6,5},{9,10},{10,9},{11,12},{12,11},... | collective-permute-start | bytes 786440 | tf_op jit(solution)/shard_map/ppermute | solution.py:403
  93.5 6.3 %collective-permute-start.30 = (f32[80,256]{1,0:T(8,128)S(1)}, f32[80,256]{1,0:T(8,128)S(1)}, u32[]{:S(2)}, u32[]{:S(2)}) collective-permute-start(f32[80,256]{1,0:T(8,128)S(1)} %get-tuple-element.189.refs_0_), channel_id=1, source_target_pairs={{0,24},{8,16},{16,8},{24,0},{1,25},{9,17},{17,9},{25,1},{2,26},{10... | collective-permute-start | bytes 245768 | tf_op jit(solution)/shard_map/ppermute | solution.py:419
  95.8 5.1 %collective-permute-start.31 = (f32[80,256]{1,0:T(8,128)S(1)}, f32[80,256]{1,0:T(8,128)S(1)}, u32[]{:S(2)}, u32[]{:S(2)}) collective-permute-start(f32[80,256]{1,0:T(8,128)S(1)} %get-tuple-element.189.refs_0_), channel_id=1, source_target_pairs={{0,8},{8,0},{16,24},{24,16},{1,9},{9,1},{17,25},{25,17},{2,10},{10... | collective-permute-start | bytes 245768 | tf_op jit(solution)/shard_map/ppermute | solution.py:419
  96.3 4.7 %collective-permute-start.32 = (f32[80,256]{1,0:T(8,128)S(1)}, f32[80,256]{1,0:T(8,128)S(1)}, u32[]{:S(2)}, u32[]{:S(2)}) collective-permute-start(f32[80,256]{1,0:T(8,128)S(1)} %get-tuple-element.189.refs_0_), channel_id=1, source_target_pairs={{0,16},{8,24},{16,0},{24,8},{1,17},{9,25},{17,1},{25,9},{2,18},{10... | collective-permute-start | bytes 245768 | tf_op jit(solution)/shard_map/ppermute | solution.py:419
  101.7 2.5 %collective-permute-start.34 = (f32[16,8,256]{2,1,0:T(8,128)S(1)}, f32[16,8,256]{2,1,0:T(8,128)S(1)}, u32[]{:S(2)}, u32[]{:S(2)}) collective-permute-start(f32[16,8,256]{2,1,0:T(8,128)S(1)} %get-tuple-element.195), channel_id=1, source_target_pairs={{0,1},{1,0},{2,3},{3,2},{4,5},{5,4},{6,7},{7,6},{8,9},{9,8},{10,11... | collective-permute-start | bytes 393224 | tf_op jit(solution)/shard_map/ppermute | solution.py:404
  101.8 6.3 %collective-permute-start.33 = (f32[16,8,256]{2,1,0:T(8,128)S(1)}, f32[16,8,256]{2,1,0:T(8,128)S(1)}, u32[]{:S(2)}, u32[]{:S(2)}) collective-permute-start(f32[16,8,256]{2,1,0:T(8,128)S(1)} %get-tuple-element.194), channel_id=1, source_target_pairs={{1,2},{2,1},{3,4},{4,3},{5,6},{6,5},{9,10},{10,9},{11,12},{12,11},... | collective-permute-start | bytes 393224 | tf_op jit(solution)/shard_map/ppermute | solution.py:403
  108.6 6.3 %collective-permute-start.35 = (f32[80,256]{1,0:T(8,128)S(1)}, f32[80,256]{1,0:T(8,128)S(1)}, u32[]{:S(2)}, u32[]{:S(2)}) collective-permute-start(f32[80,256]{1,0:T(8,128)S(1)} %get-tuple-element.203._.refs_0_), channel_id=1, source_target_pairs={{0,24},{8,16},{16,8},{24,0},{1,25},{9,17},{17,9},{25,1},{2,26},{10... | collective-permute-start | bytes 245768 | tf_op jit(solution)/shard_map/ppermute | solution.py:419
  110.9 5.1 %collective-permute-start.36 = (f32[80,256]{1,0:T(8,128)S(1)}, f32[80,256]{1,0:T(8,128)S(1)}, u32[]{:S(2)}, u32[]{:S(2)}) collective-permute-start(f32[80,256]{1,0:T(8,128)S(1)} %get-tuple-element.203._.refs_0_), channel_id=1, source_target_pairs={{0,8},{8,0},{16,24},{24,16},{1,9},{9,1},{17,25},{25,17},{2,10},{10... | collective-permute-start | bytes 245768 | tf_op jit(solution)/shard_map/ppermute | solution.py:419
  111.4 4.8 %collective-permute-start.37 = (f32[80,256]{1,0:T(8,128)S(1)}, f32[80,256]{1,0:T(8,128)S(1)}, u32[]{:S(2)}, u32[]{:S(2)}) collective-permute-start(f32[80,256]{1,0:T(8,128)S(1)} %get-tuple-element.203._.refs_0_), channel_id=1, source_target_pairs={{0,16},{8,24},{16,0},{24,8},{1,17},{9,25},{17,1},{25,9},{2,18},{10... | collective-permute-start | bytes 245768 | tf_op jit(solution)/shard_map/ppermute | solution.py:419

commit v2 on v1

v2 whole, which is shorter than its diff:
```python
import functools

import jax
import jax.numpy as jnp
from jax import lax
from jax.experimental import pallas as pl
from jax.experimental.pallas import tpu as pltpu
from jax.sharding import PartitionSpec as P


PSF_HALF = 8
WAV_HALF = 8
OUTER = 2
INNER = 3

STEP_PRIMAL = 0.9
STEP_DUAL = 0.2
RADIUS_SCALE = 0.06
WEIGHT_OFFSET = 1.0


F32 = jnp.float32
BF16 = jnp.bfloat16
LANES = 128
UNROLL = 8
GROUP = 8
VMEM_LIMIT = 24 * 1024 * 1024
PARAMS = pltpu.CompilerParams(vmem_limit_bytes=VMEM_LIMIT)


def split(values):
    head = values.astype(BF16)
    return head, (values - head.astype(F32)).astype(BF16)


def times_columns(values, head, rest):
    rows = values.shape[0]
    first, second = split(values)
    both = jnp.dot(jnp.concatenate([first, second], axis=0), head, preferred_element_type=F32)
    return both[:rows] + both[rows:] + jnp.dot(first, rest, preferred_element_type=F32)


def stacked(values):
    first, second = split(values)
    return jnp.concatenate([first, second, first], axis=0)


VM = pl.BlockSpec(memory_space=pltpu.VMEM)
SM = pl.BlockSpec(memory_space=pltpu.SMEM)


def call(kernel, ins, outs, scalars=0, aliases=None):
    return pl.pallas_call(
        kernel,
        out_shape=[jax.ShapeDtypeStruct(*shape) for shape in outs],
        in_specs=[SM] * scalars + [VM] * (len(ins) - scalars),
        out_specs=[VM] * len(outs),
        input_output_aliases=aliases or {},
        compiler_params=PARAMS,
    )(*ins)


def padded(odd, far, send):
    rows, width = far.shape
    if rows < send:
        blank = jnp.zeros((send - rows, width), F32)
        below, above = jnp.concatenate([far, blank], axis=0), jnp.concatenate([blank, far], axis=0)
        far = jnp.where(odd, below, above)
    return far


def near_kernel(
    near_ref, far_ref, halo_ref, mats_ref, dual_u_ref, dual_t_ref, old_u_ref, old_t_ref,
    head_ref, rest_ref, dual1_ref, old1_ref, *refs,
):
    extra_ref = refs[0] if len(refs) > 8 else None
    band_u_ref, band_t_ref, part_ref, moved_u_ref, moved_t_ref, band1_ref, moved1_ref, sums_ref = refs[-8:]
    chans, half, width = near_ref.shape
    height, touched = 2 * half, band_t_ref.shape[1]
    free = band_u_ref.shape[1]

    def body(c, total):
        rows = jnp.concatenate([near_ref[c], far_ref[c], halo_ref[c]], axis=0)
        product = jnp.dot(mats_ref[c], stacked(rows), preferred_element_type=F32)
        band = product[:free]
        band_u_ref[c] = band
        moved = dual_u_ref[c] + STEP_DUAL * (2.0 * band - old_u_ref[c])
        moved_u_ref[c] = moved
        band_t = product[free : free + touched]
        band_t_ref[c] = band_t
        moved_t_ref[c] = dual_t_ref[c] + STEP_DUAL * (2.0 * band_t - old_t_ref[c])
        part_ref[c] = product[free + touched :]
        return total + moved * moved

    sums_ref[:free] = lax.fori_loop(0, chans, body, jnp.zeros((free, width), F32), unroll=UNROLL)
    total = jnp.zeros((height, width), F32)
    for c in range(0, chans, GROUP):
        n = min(GROUP, chans - c)
        rows = jnp.concatenate([near_ref[c : c + n], far_ref[c : c + n]], axis=1)
        band = times_columns(rows.reshape(n * height, width), head_ref[...], rest_ref[...])
        band = band.reshape(n, height, width)
        band1_ref[c : c + n] = band
        moved = dual1_ref[c : c + n] + STEP_DUAL * (2.0 * band - old1_ref[c : c + n])
        moved1_ref[c : c + n] = moved
        total = total + jnp.sum(moved * moved, axis=0)
    sums_ref[free : free + height] = total
    if extra_ref is not None:
        sums_ref[free + height :] = extra_ref[...]


def far_kernel(send, odd_ref, far_ref, mats_ref, band_in_ref, moved_in_ref, band_ref, moved_ref, sums_ref):
    chans, touched, width = band_ref.shape
    odd = odd_ref[0] == 1

    def body(c, total):
        far = padded(odd, far_ref[c], send)
        product = jnp.dot(mats_ref[...], stacked(far), preferred_element_type=F32)
        band_ref[c] = band_in_ref[c] + product
        moved = moved_in_ref[c] + (2.0 * STEP_DUAL) * product
        moved_ref[c] = moved
        return total + moved * moved

    sums_ref[...] = lax.fori_loop(0, chans, body, jnp.zeros((touched, width), F32), unroll=True)


def first_rows_kernel(
    odd_ref, near_ref, far_ref, halo_ref, far_halo_ref, mats_ref, far_band_ref, far_mats_ref, start_ref, dirty_ref,
    sum1_ref, band_u_ref, band_t_ref, part_ref, dual_u_ref, dual_t_ref, dual1_ref, data_ref, sums_ref,
):
    chans, half, width = near_ref.shape
    height, touched, free = 2 * half, band_t_ref.shape[1], band_u_ref.shape[1]
    reach = touched + free
    send, edge = far_mats_ref.shape[2] // 3, (reach - height) // 2
    odd = odd_ref[0] == 1

    def body(c, totals):
        near, far = halo_ref[c], far_halo_ref[c]
        before, after = jnp.where(odd, near, far), jnp.where(odd, far, near)
        rows = jnp.concatenate([near_ref[c], far_ref[c], near[:send]], axis=0)
        product = jnp.dot(mats_ref[c], stacked(rows), preferred_element_type=F32)
        far_rows = stacked(far[:send])
        band_t = product[free : free + touched] + jnp.dot(
            far_band_ref[...], far_rows, preferred_element_type=F32
        )
        band = product[:free]
        band_u_ref[c] = band
        band_t_ref[c] = band_t
        at = free + touched + half
        part_ref[c, :half] = product[free + touched : at]
        part_ref[c, half:] = product[at:] + jnp.dot(far_mats_ref[c], far_rows, preferred_element_type=F32)
        at = send + edge
        dual = jnp.concatenate([before[send:at], start_ref[c, 0], after[send:at]], axis=0)
        dual_u_ref[c] = jnp.where(odd, dual[:free], dual[touched:])
        dual_t_ref[c] = jnp.where(odd, dual[free:], dual[:touched])
        dual = start_ref[c, 1]
        dual1_ref[c, :half] = jnp.where(odd, dual[:half], dual[half:])
        dual1_ref[c, half:] = jnp.where(odd, dual[half:], dual[:half])
        data_ref[c] = jnp.concatenate([before[at:], dirty_ref[c], after[at:]], axis=0)
        return totals[0] + band * band, totals[1] + band_t * band_t

    zeros = jnp.zeros((free, width), F32), jnp.zeros((touched, width), F32)
    totals = lax.fori_loop(0, chans, body, zeros, unroll=UNROLL)
    sums_ref[:free] = totals[0]
    sums_ref[free : free + height] = sum1_ref[...]
    sums_ref[free + height :] = totals[1]


def squares_kernel(*refs):
    *band_refs, out_ref = refs
    at = 0
    for ref in band_refs:
        rows = ref.shape[1]
        out_ref[at : at + rows] = jnp.sum(ref[...] * ref[...], axis=0)
        at += rows


def pack_kernel(est_ref, dual_ref, dirty_ref, near_ref, far_ref, sems):
    _, height, _ = est_ref.shape
    total = near_ref.shape[1]
    send, edge = total // 2, total // 4
    odd = lax.rem(lax.axis_index("facet"), 2)
    copies = []
    for out_ref, low in ((near_ref, 1 - odd), (far_ref, odd)):
        at = 0
        for ref, rows in (
            (est_ref, send), (dual_ref.at[:, 0], edge), (dirty_ref, edge)
        ):
            start = pl.multiple_of(low * (height - rows), 8)
            copies.append(
                pltpu.make_async_copy(
                    ref.at[:, pl.ds(start, rows)], out_ref.at[:, at : at + rows], sems.at[len(copies)]
                )
            )
            at += rows
    for copy in copies:
        copy.start()
    for copy in copies:
        copy.wait()


def banded(line, rows):
    return pltpu.roll(
        jnp.broadcast_to(line, (rows, LANES)), 0, 1, stride=1, stride_axis=0
    )


def square_band(line, width, half):
    around = banded(line, LANES)
    offset = lax.broadcasted_iota(jnp.int32, (LANES, LANES), 1) - lax.broadcasted_iota(
        jnp.int32, (LANES, LANES), 0
    )
    parts = []
    for piece in split(around):
        piece = piece.astype(F32)
        middle = jnp.where(jnp.abs(offset) <= half, piece, 0.0).astype(BF16)
        right = jnp.where(offset <= half - LANES, piece, 0.0).astype(BF16)
        left = jnp.where(offset >= LANES - half, piece, 0.0).astype(BF16)
        blank = jnp.zeros((LANES, LANES), BF16)
        tiles = width // LANES
        kinds = {0: middle, 1: right, -1: left}
        parts.append(
            jnp.concatenate(
                [
                    jnp.concatenate([kinds.get(j - i, blank) for j in range(tiles)], axis=1)
                    for i in range(tiles)
                ],
                axis=0,
            )
        )
    return parts


def matrices_kernel(
    flags_ref, lines_ref, mats_ref, far_band_ref, far_mats_ref, adj_ref, wav_free_ref, wav_touched_ref,
    around_head_ref, around_rest_ref, back_head_ref, back_rest_ref,
    wav_head_ref, wav_rest_ref, wav_head_t_ref, wav_rest_t_ref,
):
    chans, width = around_head_ref.shape[:2]
    send = far_mats_ref.shape[2] // 3
    height, reach = adj_ref.shape[1], adj_ref.shape[2] // 3
    half, touched = height // 2, far_band_ref.shape[0]
    free = reach - touched
    edge = (reach - height) // 2
    facet, facets = lax.axis_index("facet"), lax.axis_size("facet")
    odd = lax.rem(facet, 2) == 1

    def inside(shape, dim):
        at = lax.broadcasted_iota(jnp.int32, shape, dim)
        low = jnp.where(facet > 0, 0, edge)
        high = jnp.where(facet < facets - 1, reach, reach - edge)
        return jnp.where((at >= low) & (at < high), 1.0, 0.0)

    def line(c, k):
        return lines_ref[c, :, k * LANES : (k + 1) * LANES]

    def wide_rows(matrix):
        first, second = split(matrix)
        first, second = first.astype(F32), second.astype(F32)
        return jnp.concatenate([first, first, second], axis=1).astype(BF16)

    wav_head_ref[...], wav_rest_ref[...] = square_band(line(chans, 0), width, WAV_HALF)
    wav_head_t_ref[...], wav_rest_t_ref[...] = square_band(line(chans, 1), width, WAV_HALF)

    def halves(matrix):
        low, high = matrix[:half], matrix[half:]
        return jnp.where(odd, low, high), jnp.where(odd, high, low)

    def reached(matrix):
        return jnp.where(odd, matrix[:free], matrix[touched:]), jnp.where(odd, matrix[free:], matrix[:touched])

    near, far = halves(banded(line(chans, 3), height)[:, :reach])
    wav_free_ref[...] = wide_rows(
        jnp.concatenate([jnp.where(odd, x[:, :free], x[:, touched:]) for x in (near, far)], axis=0)
    )
    wav_touched_ref[...] = wide_rows(jnp.where(odd, far[:, free:], far[:, :touched]))

    def by_side(matrix):
        low, high = matrix[:, :send], matrix[:, send + height : 2 * send + height]
        first, second = matrix[:, send : send + half], matrix[:, send + half : send + height]
        own = jnp.where(odd, first, second), jnp.where(odd, second, first)
        near, far = jnp.where(odd, low, high), jnp.where(odd, high, low)
        return wide_rows(jnp.concatenate([*own, near], axis=1)), wide_rows(far)

    band = banded(line(chans, 2), reach) * inside((reach, LANES), 0)
    band, far_band = by_side(jnp.concatenate(reached(band), axis=0))
    far_band_ref[...] = far_band[free:]

    def body(c, carry):
        head, rest = square_band(line(c, 0), width, PSF_HALF)
        back_head, back_rest = square_band(line(c, 1), width, PSF_HALF)
        back_head_ref[c] = back_head
        back_rest_ref[c] = back_rest
        around = (
            jnp.dot(head, back_head, preferred_element_type=F32)
            + jnp.dot(rest, back_head, preferred_element_type=F32)
            + jnp.dot(head, back_rest, preferred_element_type=F32)
        )
        around_head_ref[c], around_rest_ref[c] = split(around)
        flag = flags_ref[c].astype(F32)
        adjoint = banded(line(c, 3), height) * flag
        adjoint = jnp.concatenate(halves(adjoint), axis=0)
        adj_ref[c] = wide_rows(adjoint[:, :reach])
        adjoint = adjoint * inside((height, LANES), 1)
        forward = banded(line(c, 2), reach)
        first, second = split(adjoint[:, :reach])
        head, rest = split(forward)
        normal = (
            jnp.dot(first, head, preferred_element_type=F32)
            + jnp.dot(second, head, preferred_element_type=F32)
            + jnp.dot(first, rest, preferred_element_type=F32)
        )
        mats_ref[c, :reach] = band
        mats_ref[c, reach:], far = by_side(normal)
        far_mats_ref[c] = far[half:]
        return carry

    lax.fori_loop(0, chans, body, 0, unroll=2)


def first_columns_kernel(odd_ref, own_ref, head_ref, rest_ref, near_ref, far_ref, band_ref, sum_ref):
    chans, height, width = own_ref.shape
    half = height // 2
    odd = odd_ref[0] == 1
    total = jnp.zeros((height, width), F32)
    for c in range(0, chans, GROUP):
        n = min(GROUP, chans - c)
        low, high = own_ref[c : c + n, :half], own_ref[c : c + n, half:]
        near, far = jnp.where(odd, low, high), jnp.where(odd, high, low)
        near_ref[c : c + n] = near
        far_ref[c : c + n] = far
        rows = jnp.concatenate([near, far], axis=1)
        band = times_columns(rows.reshape(n * height, width), head_ref[...], rest_ref[...])
        band = band.reshape(n, height, width)
        band_ref[c : c + n] = band
        total = total + jnp.sum(band * band, axis=0)
    sum_ref[...] = total


def first_gradient_kernel(
    part_ref, head_ref, rest_ref, dirty_ref, back_head_ref, back_rest_ref, adj_ref, data_ref, grad_ref
):
    chans = part_ref.shape[0]

    def body(c, carry):
        across = times_columns(dirty_ref[c], back_head_ref[c], back_rest_ref[c])
        data = jnp.dot(adj_ref[c], stacked(across), preferred_element_type=F32)
        data_ref[c] = data
        grad_ref[c] = times_columns(part_ref[c], head_ref[c], rest_ref[c]) - data
        return carry

    lax.fori_loop(0, chans, body, 0, unroll=UNROLL)


def gradient_kernel(part_ref, halo_ref, far_mats_ref, head_ref, rest_ref, data_ref, _, grad_ref):
    chans, height = part_ref.shape[:2]
    half = height // 2

    def body(c, carry):
        far = jnp.dot(far_mats_ref[c], stacked(halo_ref[c]), preferred_element_type=F32)
        part = jnp.concatenate([part_ref[c, :half], part_ref[c, half:] + far], axis=0)
        grad_ref[c] = times_columns(part, head_ref[c], rest_ref[c]) - data_ref[c]
        return carry

    lax.fori_loop(0, chans, body, 0, unroll=UNROLL)


def scaled(sums_refs, rows, radius):
    total = sums_refs[0][:rows]
    for ref in sums_refs[1:]:
        total = total + ref[:rows]
    length = jnp.sqrt(total)
    return radius / jnp.maximum(length, radius)


def radius_kernel(factor, *refs):
    *sums_refs, out_ref = refs
    skip = sums_refs[0].shape[0] - out_ref.shape[0]
    total = sums_refs[0][skip:]
    for ref in sums_refs[1:]:
        total = total + ref[skip:]
    out_ref[...] = factor / (jnp.sqrt(total) + WEIGHT_OFFSET)


def early_kernel(n_sums, *refs):
    sums_refs, refs = refs[:n_sums], refs[n_sums:]
    (
        radius_ref, moved_u_ref, moved1_ref, near_ref, far_ref, grad_ref, rows_ref, head_ref, rest_ref,
        dual_u_ref, dual1_ref, new_near_ref, half_far_ref,
    ) = refs
    chans, half, width = near_ref.shape
    height, free = 2 * half, moved_u_ref.shape[1]
    scale = scaled(sums_refs, free + height, radius_ref[: free + height])
    scale_u, scale1 = scale[:free], scale[free:]
    for c0 in range(0, chans, GROUP // 2):
        n = min(GROUP // 2, chans - c0)
        dual1 = moved1_ref[c0 : c0 + n] * scale1[None]
        dual1_ref[c0 : c0 + n] = dual1
        across = times_columns(dual1.reshape(n * height, width), head_ref[...], rest_ref[...])
        for c in range(c0, c0 + n):
            dual = moved_u_ref[c] * scale_u
            dual_u_ref[c] = dual
            down = jnp.dot(rows_ref[...], stacked(dual), preferred_element_type=F32)
            at = (c - c0) * height
            step = STEP_PRIMAL * (grad_ref[c] + (down + across[at : at + height]))
            new_near_ref[c] = jnp.maximum(near_ref[c] - step[:half], 0.0)
            half_far_ref[c] = far_ref[c] - step[half:]


def late_kernel(n_sums, odd_ref, *refs):
    sums_refs, refs = refs[:n_sums], refs[n_sums:]
    radius_ref, moved_ref, half_far_ref, rows_ref, dual_ref, new_ref, *rim_refs = refs
    chans, touched = moved_ref.shape[:2]
    odd = odd_ref[0] == 1
    scale = scaled(sums_refs, touched, radius_ref[radius_ref.shape[0] - touched :])

    def body(c, carry):
        dual = moved_ref[c] * scale
        dual_ref[c] = dual
        down = jnp.dot(rows_ref[...], stacked(dual), preferred_element_type=F32)
        new = jnp.maximum(half_far_ref[c] - STEP_PRIMAL * down, 0.0)
        new_ref[c] = new
        for ref in rim_refs:
            rim = ref.shape[1]
            ref[c] = jnp.where(odd, new[new.shape[0] - rim :], new[:rim])
        return carry

    lax.fori_loop(0, chans, body, 0, unroll=True)


def first_update_kernel(
    dual_u_ref, dual_t_ref, dual1_ref, near_ref, far_ref, grad_ref, rows_ref, rows_t_ref, head_ref, rest_ref,
    new_near_ref, new_far_ref,
):
    chans, half, width = near_ref.shape
    height = 2 * half
    for c0 in range(0, chans, GROUP // 2):
        n = min(GROUP // 2, chans - c0)
        across = times_columns(
            dual1_ref[c0 : c0 + n].reshape(n * height, width), head_ref[...], rest_ref[...]
        )
        for c in range(c0, c0 + n):
            down = jnp.dot(rows_ref[...], stacked(dual_u_ref[c]), preferred_element_type=F32)
            late = jnp.dot(rows_t_ref[...], stacked(dual_t_ref[c]), preferred_element_type=F32)
            at = (c - c0) * height
            step = grad_ref[c] + (down + across[at : at + height])
            new_near_ref[c] = jnp.maximum(near_ref[c] - STEP_PRIMAL * step[:half], 0.0)
            new_far_ref[c] = jnp.maximum(far_ref[c] - STEP_PRIMAL * (step[half:] + late), 0.0)


def final_early_kernel(n_sums, odd_ref, *refs):
    sums_refs, refs = refs[:n_sums], refs[n_sums:]
    radius_ref, moved_u_ref, moved1_ref, dual_u_ref, out_ref, plane, sem = refs
    chans, height, _ = moved1_ref.shape
    half, free = height // 2, moved_u_ref.shape[1]
    odd = odd_ref[0] == 1
    scale = scaled(sums_refs, free + height, radius_ref[: free + height])
    for c in range(chans):
        dual_u_ref[c] = moved_u_ref[c] * scale[:free]
        dual = moved1_ref[c] * scale[free:]
        near, far = dual[:half], dual[half:]
        plane[c, :half] = jnp.where(odd, near, far)
        plane[c, half:] = jnp.where(odd, far, near)
    copy = pltpu.make_async_copy(plane, out_ref.at[:, 1], sem)
    copy.start()
    copy.wait()


def final_late_kernel(n_sums, odd_ref, *refs):
    sums_refs, refs = refs[:n_sums], refs[n_sums:]
    radius_ref, moved_ref, dual_u_ref, _, out_ref, plane, sems = refs
    chans, height, _ = plane.shape
    touched, free = moved_ref.shape[1], dual_u_ref.shape[1]
    edge = (touched + free - height) // 2
    odd = odd_ref[0] == 1
    scale = scaled(sums_refs, touched, radius_ref[radius_ref.shape[0] - touched :])
    group = chans // sems.shape[0]
    copies = []
    for c in range(chans):
        dual = moved_ref[c] * scale
        above = jnp.concatenate([dual_u_ref[c, edge:], dual[: touched - edge]], axis=0)
        below = jnp.concatenate([dual[edge:], dual_u_ref[c, : free - edge]], axis=0)
        plane[c] = jnp.where(odd, above, below)
        if (c + 1) % group == 0:
            part = slice(c + 1 - group, c + 1)
            copies.append(
                pltpu.make_async_copy(plane.at[part], out_ref.at[part, 0], sems.at[len(copies)])
            )
            copies[-1].start()
    for copy in copies:
        copy.wait()


def publish_kernel(near_ref, far_ref, _, out_ref, sems):
    half = near_ref.shape[1]
    odd = lax.rem(lax.axis_index("facet"), 2)
    copies = [
        pltpu.make_async_copy(
            ref, out_ref.at[:, pl.ds(pl.multiple_of(low * half, 8), half)], sems.at[k]
        )
        for k, (ref, low) in enumerate(((near_ref, 1 - odd), (far_ref, odd)))
    ]
    for copy in copies:
        copy.start()
    for copy in copies:
        copy.wait()


def trade(values, across):
    n = lax.axis_size("facet")
    if across:
        pairs = [(i, ((i + 1) ^ 1) - 1) for i in range(n) if 0 <= ((i + 1) ^ 1) - 1 < n]
    else:
        pairs = [(i, i ^ 1) for i in range(n)]
    return lax.ppermute(values, "facet", pairs)


def peers(n, low):
    return sorted(range(1, min(4, n // low)), key=lambda k: -k.bit_count())


def gathered(sums):
    n = lax.axis_size("chan")
    if n & (n - 1):
        return [lax.psum(sums, "chan")]
    low = 1
    terms = [sums]
    while low < n:
        total = terms[0]
        for term in terms[1:]:
            total = total + term
        terms = [total]
        for k in peers(n, low):
            terms.append(lax.ppermute(total, "chan", [(i, i ^ (k * low)) for i in range(n)]))
        low *= min(4, n // low)
    return terms


def on_device(
    dirty_image, image_start, dual_start, psf_rows, psf_cols, wavelet_taps, channel_flags
):
    chans, height, width = image_start.shape
    total_chans = chans * lax.axis_size("chan")
    edge = max(PSF_HALF, WAV_HALF)
    reach, send = height + 2 * edge, 2 * edge
    passes = OUTER * INNER
    odd = (lax.axis_index("facet") % 2).astype(jnp.int32)[None]

    half, touched = height // 2, send
    free = reach - touched
    if half != send:
        raise ValueError("facet height")

    def rows(count):
        return (chans, count, width), F32

    own, side, wavy, late_rows = rows(height), rows(half), rows(free), rows(touched)
    late_sum = ((touched, width), F32)
    summed = ((reach + height, width), F32)
    square = ((width, width), BF16)
    squares = ((chans, width, width), BF16)

    first_sides = rows(2 * send)
    near, far = pl.pallas_call(
        pack_kernel,
        out_shape=[pltpu.VMEM(*first_sides)] * 2,
        in_specs=[pl.BlockSpec(memory_space=pltpu.HBM)] * 3,
        out_specs=[VM] * 2,
        scratch_shapes=[pltpu.SemaphoreType.DMA((6,))],
        compiler_params=PARAMS,
        name="pack",
    )(*(pltpu.with_memory_space_constraint(x, pltpu.HBM) for x in (image_start, dual_start, dirty_image)))
    far, near = trade(far, True), trade(near, False)

    def lines(cols, rows, half_c, half_r):
        def circle(taps, half):
            gap = jnp.zeros((taps.shape[0], LANES - 2 * half - 1), F32)
            return jnp.concatenate([taps[:, half:], gap, taps[:, :half]], axis=1)

        def ramp(taps, half):
            lead = jnp.zeros((taps.shape[0], edge - half), F32)
            gap = jnp.zeros((taps.shape[0], LANES - half - edge - 1), F32)
            return jnp.concatenate([lead, taps, gap], axis=1)

        return jnp.concatenate(
            [circle(cols[:, ::-1], half_c), circle(cols, half_c), ramp(rows, half_r), ramp(rows[:, ::-1], half_r)],
            axis=1,
        )

    table = jnp.concatenate(
        [
            lines(psf_cols, psf_rows, PSF_HALF, PSF_HALF),
            lines(wavelet_taps[1:2], wavelet_taps[0:1], WAV_HALF, WAV_HALF),
        ],
        axis=0,
    )
    (
        mats, far_band, far_mats, adjoint, wav_free, wav_touched, around_head, around_rest, back_head, back_rest,
        wav_head, wav_rest, wav_head_t, wav_rest_t,
    ) = call(
        matrices_kernel, (channel_flags, table[:, None]),
        (
            ((chans, reach + height, 3 * (height + send)), BF16), ((touched, 3 * send), BF16),
            ((chans, half, 3 * send), BF16), ((chans, height, 3 * reach), BF16),
            ((height, 3 * free), BF16), ((half, 3 * touched), BF16),
            squares, squares, squares, squares, square, square, square, square,
        ),
        1,
    )
    est_near, est_far, band1, sum1 = call(
        first_columns_kernel, (odd, image_start, wav_head, wav_rest),
        (side, side, own, ((height, width), F32)), 1,
    )
    band_u, band_t, part, dual_u, dual_t, dual1, dirty, weight_sums = call(
        first_rows_kernel,
        (odd, est_near, est_far, near, far, mats, far_band, far_mats, dual_start, dirty_image, sum1),
        (wavy, late_rows, own, wavy, late_rows, own, rows(reach), summed), 1,
    )
    data, grad = call(
        first_gradient_kernel,
        (part, around_head, around_rest, dirty, back_head, back_rest, adjoint), (own, own),
    )
    est_near, est_far = call(
        first_update_kernel,
        (dual_u, dual_t, dual1, est_near, est_far, grad, wav_free, wav_touched, wav_head_t, wav_rest_t),
        (side, side),
    )
    rim = est_far
    near = trade(est_near, False)
    for step in range(passes):
        last = step + 1 == passes
        far = trade(rim, True)
        weigh = step % INNER == 0
        band_u, band_t, part, moved_u, moved_t, band1, moved1, sums = call(
            near_kernel,
            (est_near, est_far, near, mats, dual_u, dual_t, band_u, band_t, wav_head, wav_rest, dual1, band1)
            + ((weight_sums,) if weigh else ()),
            (
                wavy, late_rows, own, wavy, late_rows, own, own,
                ((free + height + (summed[0][0] if weigh else 0), width), F32),
            ),
        )
        early = gathered(sums)
        if weigh:
            radius = call(functools.partial(radius_kernel, RADIUS_SCALE * total_chans), tuple(early), (summed,))[0]
        band_t, moved_t, sums = call(
            functools.partial(far_kernel, send), (odd, far, far_band, band_t, moved_t),
            (late_rows, late_rows, late_sum), 1,
        )
        late = gathered(sums)
        if last:
            image_final = pl.pallas_call(
                publish_kernel,
                out_shape=jax.ShapeDtypeStruct(*own),
                in_specs=[VM, VM, pl.BlockSpec(memory_space=pl.ANY)],
                out_specs=pl.BlockSpec(memory_space=pltpu.HBM),
                scratch_shapes=[pltpu.SemaphoreType.DMA((2,))],
                compiler_params=PARAMS,
                name="publish",
            )(est_near, est_far, sums)
            in_hbm = pl.BlockSpec(memory_space=pltpu.HBM)
            result = jax.ShapeDtypeStruct((chans, 2, height, width), F32)
            dual_u, dual_final = pl.pallas_call(
                functools.partial(final_early_kernel, len(early)),
                out_shape=[jax.ShapeDtypeStruct(*wavy), result],
                in_specs=[SM] + [VM] * (len(early) + 3),
                out_specs=[VM, in_hbm],
                scratch_shapes=[pltpu.VMEM(*own), pltpu.SemaphoreType.DMA],
                compiler_params=PARAMS,
                name="final_early",
            )(odd, *early, radius, moved_u, moved1)
            dual_final = pl.pallas_call(
                functools.partial(final_late_kernel, len(late)),
                out_shape=result,
                in_specs=[SM] + [VM] * (len(late) + 3) + [in_hbm],
                out_specs=in_hbm,
                scratch_shapes=[pltpu.VMEM(*own), pltpu.SemaphoreType.DMA((4,))],
                input_output_aliases={len(late) + 4: 0},
                compiler_params=PARAMS,
                name="final_late",
            )(odd, *late, radius, moved_t, dual_u, dual_final)
            break
        grad = call(gradient_kernel, (part, far, far_mats, around_head, around_rest, data, sums), (own,))[0]
        dual_u, dual1, est_near, half_far = call(
            functools.partial(early_kernel, len(early)),
            (*early, radius, moved_u, moved1, est_near, est_far, grad, wav_free, wav_head_t, wav_rest_t),
            (wavy, own, side, side),
        )
        near = trade(est_near, False)
        if step % INNER == INNER - 1:
            weight_sums = call(squares_kernel, (band_u, band1, band_t), (summed,))[0]
        small = step + 2 == passes
        dual_t, est_far, *rims = call(
            functools.partial(late_kernel, len(late)),
            (odd, *late, radius, moved_t, half_far, wav_touched),
            (late_rows, side) + ((rows(WAV_HALF),) if small else ()), 1,
        )
        rim = rims[0] if small else est_far
    return (image_final, dual_final)


def solution(mesh):
    return jax.shard_map(
        on_device,
        mesh=mesh,
        in_specs=(
            P("chan", "facet", None),
            P("chan", "facet", None),
            P("chan", None, "facet", None),
            P("chan", None),
            P("chan", None),
            P(),
            P("chan"),
        ),
        out_specs=(P("chan", "facet", None), P("chan", None, "facet", None)),
        check_vma=False,
    )
```

time: 118 us -> 133 us (1.13)
  starting transfers between devices: 46.2 us -> 58.4 us
  waiting for transfers between devices: 29.9 us -> 34.5 us
  Pallas kernels: 39 us -> 36.4 us
    ppermute x24 -> x36, waiting for transfers between devices: 14.2 us -> 28.6 us  [gathered(): lax.ppermute(total, 'chan', [(i, i ^ k * low) for i in range(n)])]
    ppermute x24 -> x36, starting transfers between devices: 28.4 us -> 42.5 us  [gathered(): lax.ppermute(total, 'chan', [(i, i ^ k * low) for i in range(n)])]
    ppermute x14, waiting for transfers between devices: 15.7 us -> 5.98 us  [trade(): return lax.ppermute(values, 'facet', pairs)]
    pallas_call x31 -> x35, Pallas kernels: 35.8 us -> 31.5 us  [call(): pl.pallas_call(kernel, out_shape=[jax.ShapeDtypeStruct(*shape) for shape...]
    ppermute x14, starting transfers between devices: 17.8 us -> 15.9 us  [trade(): return lax.ppermute(values, 'facet', pairs)]
    pallas_call x1 -> x3, Pallas kernels: 2.39 us -> 4.12 us  [the longest x1 2.39 us: on_device(): pl.pallas_call(pack_kernel, out_shape=[pltpu.VMEM(*first_sides)] * 2, in_...]
  transfers between devices with their start and end apart: 38 -> 50, of which waited for: 25 -> 28; matrix products, arithmetic and copies ran while one was open for 1% -> 1% of each run, Pallas kernels for 22% -> 20%
where the time goes in v2:
time: 133 us; the launch traced here: 132 us
  starting transfers between devices  58.4 us (44%)
  Pallas kernels  36.4 us (27%)
  waiting for transfers between devices  34.5 us (26%)
  between operations  1.37 us (1%)
    ppermute x36, starting transfers between devices, gathered(): lax.ppermute(total, 'chan', [(i, i ^ k * low) for i in range(n)])  42.5 us
    pallas_call x35, Pallas kernels, call(): pl.pallas_call(kernel, out_shape=[jax.ShapeDtypeStruct(*shape) for shape...  31.5 us
    ppermute x36, waiting for transfers between devices, gathered(): lax.ppermute(total, 'chan', [(i, i ^ k * low) for i in range(n)])  28.6 us
    ppermute x14, starting transfers between devices, trade(): return lax.ppermute(values, 'facet', pairs)  15.9 us
    ppermute x14, waiting for transfers between devices, trade(): return lax.ppermute(values, 'facet', pairs)  5.98 us
  transfers between devices with their start and end apart: 50, of which 28 were waited for; matrix products, arithmetic and copies ran while one was open for 1% of the time, Pallas kernels for 20%

profile of v2, /device:TPU:16, one launch (start us, length us, event | category | flops | bytes accessed | tf_op | source)
XLA Modules:
  0.0 131.8 jit_solution(15127734733896085201)
XLA Ops:
  0.7 2.4 %pack.1 = (f32[16,32,256]{2,1,0:T(8,128)}, f32[16,32,256]{2,1,0:T(8,128)}) custom-call(f32[16,32,256]{2,1,0:T(8,128)} %est_ref.1, f32[16,2,32,256]{3,2,1,0:T(8,128)} %start_ref.1, f32[16,32,256]{2,1,0:T(8,128)} %dirty_ref.3), custom_call_target="tpu_custom_call" | custom-call | tf_op jit(solution)/shard_map/pack/pallas_call | solution.py:563
  3.2 2.4 %collective-permute-start.1 = (f32[16,32,256]{2,1,0:T(8,128)}, f32[16,32,256]{2,1,0:T(8,128)S(1)}, u32[]{:S(2)}, u32[]{:S(2)}) collective-permute-start(f32[16,32,256]{2,1,0:T(8,128)} %get-tuple-element.134), channel_id=1, source_target_pairs={{1,2},{2,1},{3,4},{4,3},{5,6},{6,5},{9,10},{10,9},{11,12},{12,11},... | collective-permute-start | bytes 1572872 | tf_op jit(solution)/shard_map/ppermute | solution.py:514
  6.7 6.4 %shard_map.86 = (bf16[16,80,144]{2,1,0:T(8,128)(2,1)S(1)}, bf16[16,48]{1,0:T(8,128)(2,1)S(1)}, bf16[16,16,48]{2,1,0:T(8,128)(2,1)S(1)}, bf16[16,32,144]{2,1,0:T(...) custom-call(s32[16]{0:T(128)S(1)} %copy-done.3, ...), custom_call_target="tpu_custom_call" | custom-call | tf_op jit(solution)/shard_map/pallas_call | solution.py:53
  14.7 2.8 %shard_map.89 = (f32[16,32,256]{2,1,0:T(8,128)S(1)}, f32[16,32,256]{2,1,0:T(8,128)S(1)}) custom-call(f32[16,32,256]{2,1,0:T(8,128)S(1)} %get-tuple-element.142.part_ref, bf16[16,256,256]{2,1,0:T(8,128)(2,1)S(1)} %get-tuple-element.143.head_ref, bf16[16,256,256]{2,1,0:T(8,128)(2,1)S(1)} %get-tuple-element.144.rest_ref, ...), custom_call_target="tpu_custom_call" | custom-call | tf_op jit(solution)/shard_map/pallas_call | solution.py:53
  19.1 2.0 %collective-permute-start.6 = (f32[16,16,256]{2,1,0:T(8,128)S(1)}, f32[16,16,256]{2,1,0:T(8,128)S(1)}, u32[]{:S(2)}, u32[]{:S(2)}) collective-permute-start(f32[16,16,256]{2,1,0:T(8,128)S(1)} %get-tuple-element.155.far_ref.refs_8_), channel_id=1, source_target_pairs={{1,2},{2,1},{3,4},{4,3},{5,6},{6,5},{9,10},{10,9},{11,12},{12,11},... | collective-permute-start | bytes 786440 | tf_op jit(solution)/shard_map/ppermute | solution.py:514
  22.1 1.6 %collective-permute-start.5 = (f32[144,256]{1,0:T(8,128)S(1)}, f32[144,256]{1,0:T(8,128)S(1)}, u32[]{:S(2)}, u32[]{:S(2)}) collective-permute-start(f32[144,256]{1,0:T(8,128)S(1)} %get-tuple-element.160.refs_0_), channel_id=1, source_target_pairs={{0,16},{8,24},{16,0},{24,8},{1,17},{9,25},{17,1},{25,9},{2,18},{10... | collective-permute-start | bytes 442376 | tf_op jit(solution)/shard_map/ppermute | solution.py:533
  23.6 1.5 %collective-permute-start.4 = (f32[144,256]{1,0:T(8,128)S(1)}, f32[144,256]{1,0:T(8,128)S(1)}, u32[]{:S(2)}, u32[]{:S(2)}) collective-permute-start(f32[144,256]{1,0:T(8,128)S(1)} %get-tuple-element.160.refs_0_), channel_id=1, source_target_pairs={{0,8},{8,0},{16,24},{24,16},{1,9},{9,1},{17,25},{25,17},{2,10},{10... | collective-permute-start | bytes 442376 | tf_op jit(solution)/shard_map/ppermute | solution.py:533
  27.0 1.7 %shard_map.94.refs_9_ = f32[16,32,256]{2,1,0:T(8,128)S(1)} custom-call(f32[16,32,256]{2,1,0:T(8,128)S(1)} %get-tuple-element.163.part_ref, f32[16,16,256]{2,1,0:T(8,128)S(1)} %collective-permute-done.6.far_ref.halo_ref, bf16[16,16,48]{2,1,0:T(8,128)(2,1)S(1)} %get-tuple-element.137.far_mats_ref, bf16[16,256,256]{2,1,0:T(8,128)(2,1)S(1)} %get-tuple-element.143.head_ref, ...), custom_call_target="tpu_custom_call" | custom-call | tf_op jit(solution)/shard_map/pallas_call | solution.py:53
  28.7 1.7 %collective-permute-done.4.refs_2_ = f32[144,256]{1,0:T(8,128)S(1)} collective-permute-done((f32[144,256]{1,0:T(8,128)S(1)}, f32[144,256]{1,0:T(8,128)S(1)}, u32[]{:S(2)}, u32[]{:S(2)}) %collective-permute-start.4) | collective-permute-done | bytes 147488 | tf_op jit(solution)/shard_map/ppermute | solution.py:533
  30.4 2.6 %collective-permute-done.3.refs_1_ = f32[144,256]{1,0:T(8,128)S(1)} collective-permute-done((f32[144,256]{1,0:T(8,128)S(1)}, f32[144,256]{1,0:T(8,128)S(1)}, u32[]{:S(2)}, u32[]{:S(2)}) %collective-permute-start.3) | collective-permute-done | bytes 147488 | tf_op jit(solution)/shard_map/ppermute | solution.py:533
  33.7 1.6 %collective-permute-start.9 = (f32[16,256]{1,0:T(8,128)S(1)}, f32[16,256]{1,0:T(8,128)S(1)}, u32[]{:S(2)}, u32[]{:S(2)}) collective-permute-start(f32[16,256]{1,0:T(8,128)S(1)} %get-tuple-element.167._.refs_0_), channel_id=1, source_target_pairs={{0,16},{8,24},{16,0},{24,8},{1,17},{9,25},{17,1},{25,9},{2,18},{10... | collective-permute-start | bytes 49160 | tf_op jit(solution)/shard_map/ppermute | solution.py:533
  35.3 1.5 %collective-permute-start.8 = (f32[16,256]{1,0:T(8,128)S(1)}, f32[16,256]{1,0:T(8,128)S(1)}, u32[]{:S(2)}, u32[]{:S(2)}) collective-permute-start(f32[16,256]{1,0:T(8,128)S(1)} %get-tuple-element.167._.refs_0_), channel_id=1, source_target_pairs={{0,8},{8,0},{16,24},{24,16},{1,9},{9,1},{17,25},{25,17},{2,10},{10... | collective-permute-start | bytes 49160 | tf_op jit(solution)/shard_map/ppermute | solution.py:533
  37.5 1.5 %collective-permute-done.8.refs_2_ = f32[16,256]{1,0:T(8,128)S(1)} collective-permute-done((f32[16,256]{1,0:T(8,128)S(1)}, f32[16,256]{1,0:T(8,128)S(1)}, u32[]{:S(2)}, u32[]{:S(2)}) %collective-permute-start.8) | collective-permute-done | bytes 16416 | tf_op jit(solution)/shard_map/ppermute | solution.py:533
  39.0 2.4 %collective-permute-done.7.refs_1_ = f32[16,256]{1,0:T(8,128)S(1)} collective-permute-done((f32[16,256]{1,0:T(8,128)S(1)}, f32[16,256]{1,0:T(8,128)S(1)}, u32[]{:S(2)}, u32[]{:S(2)}) %collective-permute-start.7) | collective-permute-done | bytes 16416 | tf_op jit(solution)/shard_map/ppermute | solution.py:533
  41.6 1.9 %collective-permute-start.14 = (f32[16,16,256]{2,1,0:T(8,128)S(1)}, f32[16,16,256]{2,1,0:T(8,128)S(1)}, u32[]{:S(2)}, u32[]{:S(2)}) collective-permute-start(f32[16,16,256]{2,1,0:T(8,128)S(1)} %get-tuple-element.171.far_ref.refs_8_), channel_id=1, source_target_pairs={{1,2},{2,1},{3,4},{4,3},{5,6},{6,5},{9,10},{10,9},{11,12},{12,11},... | collective-permute-start | bytes 786440 | tf_op jit(solution)/shard_map/ppermute | solution.py:514
  45.6 2.4 %collective-permute-start.11 = (f32[64,256]{1,0:T(8,128)S(1)}, f32[64,256]{1,0:T(8,128)S(1)}, u32[]{:S(2)}, u32[]{:S(2)}) collective-permute-start(f32[64,256]{1,0:T(8,128)S(1)} %get-tuple-element.178.refs_0_), channel_id=1, source_target_pairs={{0,24},{8,16},{16,8},{24,0},{1,25},{9,17},{17,9},{25,1},{2,26},{10... | collective-permute-start | bytes 196616 | tf_op jit(solution)/shard_map/ppermute | solution.py:533
  48.0 1.3 collective-permute-done.14.far_ref.halo_ref
  49.5 1.7 %shard_map.99.refs_9_ = f32[16,32,256]{2,1,0:T(8,128)S(1)} custom-call(f32[16,32,256]{2,1,0:T(8,128)S(1)} %get-tuple-element.181.part_ref, f32[16,16,256]{2,1,0:T(8,128)S(1)} %collective-permute-done.14.far_ref.halo_ref, bf16[16,16,48]{2,1,0:T(8,128)(2,1)S(1)} %get-tuple-element.137.far_mats_ref, bf16[16,256,256]{2,1,0:T(8,128)(2,1)S(1)} %get-tuple-element.143.head_ref, ...), custom_call_target="tpu_custom_call" | custom-call | tf_op jit(solution)/shard_map/pallas_call | solution.py:53
  53.0 1.5 %collective-permute-start.16 = (f32[16,256]{1,0:T(8,128)S(1)}, f32[16,256]{1,0:T(8,128)S(1)}, u32[]{:S(2)}, u32[]{:S(2)}) collective-permute-start(f32[16,256]{1,0:T(8,128)S(1)} %get-tuple-element.184._.refs_0_), channel_id=1, source_target_pairs={{0,8},{8,0},{16,24},{24,16},{1,9},{9,1},{17,25},{25,17},{2,10},{10... | collective-permute-start | bytes 49160 | tf_op jit(solution)/shard_map/ppermute | solution.py:533
  56.7 2.4 %collective-permute-done.15.refs_1_ = f32[16,256]{1,0:T(8,128)S(1)} collective-permute-done((f32[16,256]{1,0:T(8,128)S(1)}, f32[16,256]{1,0:T(8,128)S(1)}, u32[]{:S(2)}, u32[]{:S(2)}) %collective-permute-start.15) | collective-permute-done | bytes 16416 | tf_op jit(solution)/shard_map/ppermute | solution.py:533
  59.3 1.9 %collective-permute-start.22 = (f32[16,16,256]{2,1,0:T(8,128)S(1)}, f32[16,16,256]{2,1,0:T(8,128)S(1)}, u32[]{:S(2)}, u32[]{:S(2)}) collective-permute-start(f32[16,16,256]{2,1,0:T(8,128)S(1)} %get-tuple-element.188.far_ref.refs_8_), channel_id=1, source_target_pairs={{1,2},{2,1},{3,4},{4,3},{5,6},{6,5},{9,10},{10,9},{11,12},{12,11},... | collective-permute-start | bytes 786440 | tf_op jit(solution)/shard_map/ppermute | solution.py:514
  63.7 2.0 %collective-permute-start.19 = (f32[64,256]{1,0:T(8,128)S(1)}, f32[64,256]{1,0:T(8,128)S(1)}, u32[]{:S(2)}, u32[]{:S(2)}) collective-permute-start(f32[64,256]{1,0:T(8,128)S(1)} %get-tuple-element.195.refs_0_), channel_id=1, source_target_pairs={{0,24},{8,16},{16,8},{24,0},{1,25},{9,17},{17,9},{25,1},{2,26},{10... | collective-permute-start | bytes 196616 | tf_op jit(solution)/shard_map/ppermute | solution.py:533
  65.7 1.3 collective-permute-done.22.far_ref.halo_ref
  67.2 1.7 %shard_map.104.refs_9_ = f32[16,32,256]{2,1,0:T(8,128)S(1)} custom-call(f32[16,32,256]{2,1,0:T(8,128)S(1)} %get-tuple-element.198.part_ref, f32[16,16,256]{2,1,0:T(8,128)S(1)} %collective-permute-done.22.far_ref.halo_ref, bf16[16,16,48]{2,1,0:T(8,128)(2,1)S(1)} %get-tuple-element.137.far_mats_ref, bf16[16,256,256]{2,1,0:T(8,128)(2,1)S(1)} %get-tuple-element.143.head_ref, ...), custom_call_target="tpu_custom_call" | custom-call | tf_op jit(solution)/shard_map/pallas_call | solution.py:53
  70.7 1.5 %collective-permute-start.24 = (f32[16,256]{1,0:T(8,128)S(1)}, f32[16,256]{1,0:T(8,128)S(1)}, u32[]{:S(2)}, u32[]{:S(2)}) collective-permute-start(f32[16,256]{1,0:T(8,128)S(1)} %get-tuple-element.201._.refs_0_), channel_id=1, source_target_pairs={{0,8},{8,0},{16,24},{24,16},{1,9},{9,1},{17,25},{25,17},{2,10},{10... | collective-permute-start | bytes 49160 | tf_op jit(solution)/shard_map/ppermute | solution.py:533
  72.2 1.3 collective-permute-start.23
  74.4 2.4 %collective-permute-done.23.refs_1_ = f32[16,256]{1,0:T(8,128)S(1)} collective-permute-done((f32[16,256]{1,0:T(8,128)S(1)}, f32[16,256]{1,0:T(8,128)S(1)}, u32[]{:S(2)}, u32[]{:S(2)}) %collective-permute-start.23) | collective-permute-done | bytes 16416 | tf_op jit(solution)/shard_map/ppermute | solution.py:533
  77.0 2.1 %collective-permute-start.30 = (f32[16,16,256]{2,1,0:T(8,128)S(1)}, f32[16,16,256]{2,1,0:T(8,128)S(1)}, u32[]{:S(2)}, u32[]{:S(2)}) collective-permute-start(f32[16,16,256]{2,1,0:T(8,128)S(1)} %get-tuple-element.205.far_ref.refs_8_), channel_id=1, source_target_pairs={{1,2},{2,1},{3,4},{4,3},{5,6},{6,5},{9,10},{10,9},{11,12},{12,11},... | collective-permute-start | bytes 786440 | tf_op jit(solution)/shard_map/ppermute | solution.py:514
  80.7 1.4 %collective-permute-start.28 = (f32[144,256]{1,0:T(8,128)S(1)}, f32[144,256]{1,0:T(8,128)S(1)}, u32[]{:S(2)}, u32[]{:S(2)}) collective-permute-start(f32[144,256]{1,0:T(8,128)S(1)} %get-tuple-element.212.refs_0_), channel_id=1, source_target_pairs={{0,8},{8,0},{16,24},{24,16},{1,9},{9,1},{17,25},{25,17},{2,10},{10... | collective-permute-start | bytes 442376 | tf_op jit(solution)/shard_map/ppermute | solution.py:533
  82.1 1.6 %collective-permute-start.27 = (f32[144,256]{1,0:T(8,128)S(1)}, f32[144,256]{1,0:T(8,128)S(1)}, u32[]{:S(2)}, u32[]{:S(2)}) collective-permute-start(f32[144,256]{1,0:T(8,128)S(1)} %get-tuple-element.212.refs_0_), channel_id=1, source_target_pairs={{0,24},{8,16},{16,8},{24,0},{1,25},{9,17},{17,9},{25,1},{2,26},{10... | collective-permute-start | bytes 442376 | tf_op jit(solution)/shard_map/ppermute | solution.py:533
  84.9 1.7 %shard_map.111.refs_9_ = f32[16,32,256]{2,1,0:T(8,128)S(1)} custom-call(f32[16,32,256]{2,1,0:T(8,128)S(1)} %get-tuple-element.215.part_ref, f32[16,16,256]{2,1,0:T(8,128)S(1)} %collective-permute-done.30.far_ref.halo_ref, bf16[16,16,48]{2,1,0:T(8,128)(2,1)S(1)} %get-tuple-element.137.far_mats_ref, bf16[16,256,256]{2,1,0:T(8,128)(2,1)S(1)} %get-tuple-element.143.head_ref, ...), custom_call_target="tpu_custom_call" | custom-call | tf_op jit(solution)/shard_map/pallas_call | solution.py:53
  87.5 3.3 %collective-permute-done.27.refs_1_ = f32[144,256]{1,0:T(8,128)S(1)} collective-permute-done((f32[144,256]{1,0:T(8,128)S(1)}, f32[144,256]{1,0:T(8,128)S(1)}, u32[]{:S(2)}, u32[]{:S(2)}) %collective-permute-start.27) | collective-permute-done | bytes 147488 | tf_op jit(solution)/shard_map/ppermute | solution.py:533
  93.0 2.0 %collective-permute-start.31 = (f32[16,256]{1,0:T(8,128)S(1)}, f32[16,256]{1,0:T(8,128)S(1)}, u32[]{:S(2)}, u32[]{:S(2)}) collective-permute-start(f32[16,256]{1,0:T(8,128)S(1)} %get-tuple-element.218._.refs_0_), channel_id=1, source_target_pairs={{0,24},{8,16},{16,8},{24,0},{1,25},{9,17},{17,9},{25,1},{2,26},{10... | collective-permute-start | bytes 49160 | tf_op jit(solution)/shard_map/ppermute | solution.py:533
  95.8 1.9 %collective-permute-done.31.refs_1_ = f32[16,256]{1,0:T(8,128)S(1)} collective-permute-done((f32[16,256]{1,0:T(8,128)S(1)}, f32[16,256]{1,0:T(8,128)S(1)}, u32[]{:S(2)}, u32[]{:S(2)}) %collective-permute-start.31) | collective-permute-done | bytes 16416 | tf_op jit(solution)/shard_map/ppermute | solution.py:533
  97.9 2.3 %collective-permute-start.38 = (f32[16,16,256]{2,1,0:T(8,128)S(1)}, f32[16,16,256]{2,1,0:T(8,128)S(1)}, u32[]{:S(2)}, u32[]{:S(2)}) collective-permute-start(f32[16,16,256]{2,1,0:T(8,128)S(1)} %get-tuple-element.222.far_ref.refs_8_), channel_id=1, source_target_pairs={{1,2},{2,1},{3,4},{4,3},{5,6},{6,5},{9,10},{10,9},{11,12},{12,11},... | collective-permute-start | bytes 786440 | tf_op jit(solution)/shard_map/ppermute | solution.py:514
  101.9 1.5 %collective-permute-start.36 = (f32[64,256]{1,0:T(8,128)S(1)}, f32[64,256]{1,0:T(8,128)S(1)}, u32[]{:S(2)}, u32[]{:S(2)}) collective-permute-start(f32[64,256]{1,0:T(8,128)S(1)} %get-tuple-element.229.refs_0_), channel_id=1, source_target_pairs={{0,8},{8,0},{16,24},{24,16},{1,9},{9,1},{17,25},{25,17},{2,10},{10... | collective-permute-start | bytes 196616 | tf_op jit(solution)/shard_map/ppermute | solution.py:533
  103.4 1.3 collective-permute-start.35
  105.8 1.7 %shard_map.116.refs_9_ = f32[16,32,256]{2,1,0:T(8,128)S(1)} custom-call(f32[16,32,256]{2,1,0:T(8,128)S(1)} %get-tuple-element.232.part_ref, f32[16,16,256]{2,1,0:T(8,128)S(1)} %collective-permute-done.38.far_ref.halo_ref, bf16[16,16,48]{2,1,0:T(8,128)(2,1)S(1)} %get-tuple-element.137.far_mats_ref, bf16[16,256,256]{2,1,0:T(8,128)(2,1)S(1)} %get-tuple-element.143.head_ref, ...), custom_call_target="tpu_custom_call" | custom-call | tf_op jit(solution)/shard_map/pallas_call | solution.py:53
  109.7 1.4 %collective-permute-start.40 = (f32[16,256]{1,0:T(8,128)S(1)}, f32[16,256]{1,0:T(8,128)S(1)}, u32[]{:S(2)}, u32[]{:S(2)}) collective-permute-start(f32[16,256]{1,0:T(8,128)S(1)} %get-tuple-element.235._.refs_0_), channel_id=1, source_target_pairs={{0,8},{8,0},{16,24},{24,16},{1,9},{9,1},{17,25},{25,17},{2,10},{10... | collective-permute-start | bytes 49160 | tf_op jit(solution)/shard_map/ppermute | solution.py:533
  111.1 1.6 %collective-permute-start.39 = (f32[16,256]{1,0:T(8,128)S(1)}, f32[16,256]{1,0:T(8,128)S(1)}, u32[]{:S(2)}, u32[]{:S(2)}) collective-permute-start(f32[16,256]{1,0:T(8,128)S(1)} %get-tuple-element.235._.refs_0_), channel_id=1, source_target_pairs={{0,24},{8,16},{16,8},{24,0},{1,25},{9,17},{17,9},{25,1},{2,26},{10... | collective-permute-start | bytes 49160 | tf_op jit(solution)/shard_map/ppermute | solution.py:533
  113.5 2.2 %collective-permute-done.39.refs_1_ = f32[16,256]{1,0:T(8,128)S(1)} collective-permute-done((f32[16,256]{1,0:T(8,128)S(1)}, f32[16,256]{1,0:T(8,128)S(1)}, u32[]{:S(2)}, u32[]{:S(2)}) %collective-permute-start.39) | collective-permute-done | bytes 16416 | tf_op jit(solution)/shard_map/ppermute | solution.py:533
  115.9 1.9 %collective-permute-start.42 = (f32[16,8,256]{2,1,0:T(8,128)S(1)}, f32[16,8,256]{2,1,0:T(8,128)S(1)}, u32[]{:S(2)}, u32[]{:S(2)}) collective-permute-start(f32[16,8,256]{2,1,0:T(8,128)S(1)} %get-tuple-element.240), channel_id=1, source_target_pairs={{1,2},{2,1},{3,4},{4,3},{5,6},{6,5},{9,10},{10,9},{11,12},{12,11},... | collective-permute-start | bytes 393224 | tf_op jit(solution)/shard_map/ppermute | solution.py:514
  117.9 1.7 %shard_map.119 = (f32[16,32,256]{2,1,0:T(8,128)}, f32[16,16,256]{2,1,0:T(8,128)S(1)}, f32[16,32,256]{2,1,0:T(8,128)}, f32[16,32,256]{2,1,0:T(8,128)S(1)}, f32[16...) custom-call(f32[16,16,256]{2,1,0:T(8,128)S(1)} %get-tuple-element.236.near_re, ...), custom_call_target="tpu_custom_call" | custom-call | tf_op jit(solution)/shard_map/pallas_call | solution.py:53
  120.3 1.5 %collective-permute-start.48 = (f32[64,256]{1,0:T(8,128)S(1)}, f32[64,256]{1,0:T(8,128)S(1)}, u32[]{:S(2)}, u32[]{:S(2)}) collective-permute-start(f32[64,256]{1,0:T(8,128)S(1)} %get-tuple-element.251.refs_0_), channel_id=1, source_target_pairs={{0,8},{8,0},{16,24},{24,16},{1,9},{9,1},{17,25},{25,17},{2,10},{10... | collective-permute-start | bytes 196616 | tf_op jit(solution)/shard_map/ppermute | solution.py:533
  121.8 1.3 collective-permute-start.47
  124.7 1.5 %collective-permute-start.45 = (f32[16,256]{1,0:T(8,128)S(1)}, f32[16,256]{1,0:T(8,128)S(1)}, u32[]{:S(2)}, u32[]{:S(2)}) collective-permute-start(f32[16,256]{1,0:T(8,128)S(1)} %get-tuple-element.249._.refs_0_), channel_id=1, source_target_pairs={{0,8},{8,0},{16,24},{24,16},{1,9},{9,1},{17,25},{25,17},{2,10},{10... | collective-permute-start | bytes 49160 | tf_op jit(solution)/shard_map/ppermute | solution.py:533
  126.2 1.3 collective-permute-start.44
  129.2 1.6 %collective-permute-done.44.refs_1_ = f32[16,256]{1,0:T(8,128)S(1)} collective-permute-done((f32[16,256]{1,0:T(8,128)S(1)}, f32[16,256]{1,0:T(8,128)S(1)}, u32[]{:S(2)}, u32[]{:S(2)}) %collective-permute-start.44) | collective-permute-done | bytes 16416 | tf_op jit(solution)/shard_map/ppermute | solution.py:533
  (122 shorter events, 38.5 us)
Async XLA Ops:
  3.1 10.4 %collective-permute-start = (f32[16,32,256]{2,1,0:T(8,128)}, f32[16,32,256]{2,1,0:T(8,128)S(1)}, u32[]{:S(2)}, u32[]{:S(2)}) collective-permute-start(f32[16,32,256]{2,1,0:T(8,128)} %get-tuple-element.133), channel_id=1, source_target_pairs={{0,1},{1,0},{2,3},{3,2},{4,5},{5,4},{6,7},{7,6},{8,9},{9,8},{10,11... | collective-permute-start | bytes 1572872 | tf_op jit(solution)/shard_map/ppermute | solution.py:514
  3.2 10.7 %collective-permute-start.1 = (f32[16,32,256]{2,1,0:T(8,128)}, f32[16,32,256]{2,1,0:T(8,128)S(1)}, u32[]{:S(2)}, u32[]{:S(2)}) collective-permute-start(f32[16,32,256]{2,1,0:T(8,128)} %get-tuple-element.134), channel_id=1, source_target_pairs={{1,2},{2,1},{3,4},{4,3},{5,6},{6,5},{9,10},{10,9},{11,12},{12,11},... | collective-permute-start | bytes 1572872 | tf_op jit(solution)/shard_map/ppermute | solution.py:514
  19.1 7.7 %collective-permute-start.6 = (f32[16,16,256]{2,1,0:T(8,128)S(1)}, f32[16,16,256]{2,1,0:T(8,128)S(1)}, u32[]{:S(2)}, u32[]{:S(2)}) collective-permute-start(f32[16,16,256]{2,1,0:T(8,128)S(1)} %get-tuple-element.155.far_ref.refs_8_), channel_id=1, source_target_pairs={{1,2},{2,1},{3,4},{4,3},{5,6},{6,5},{9,10},{10,9},{11,12},{12,11},... | collective-permute-start | bytes 786440 | tf_op jit(solution)/shard_map/ppermute | solution.py:514
  22.1 6.6 %collective-permute-start.5 = (f32[144,256]{1,0:T(8,128)S(1)}, f32[144,256]{1,0:T(8,128)S(1)}, u32[]{:S(2)}, u32[]{:S(2)}) collective-permute-start(f32[144,256]{1,0:T(8,128)S(1)} %get-tuple-element.160.refs_0_), channel_id=1, source_target_pairs={{0,16},{8,24},{16,0},{24,8},{1,17},{9,25},{17,1},{25,9},{2,18},{10... | collective-permute-start | bytes 442376 | tf_op jit(solution)/shard_map/ppermute | solution.py:533
  23.6 6.7 %collective-permute-start.4 = (f32[144,256]{1,0:T(8,128)S(1)}, f32[144,256]{1,0:T(8,128)S(1)}, u32[]{:S(2)}, u32[]{:S(2)}) collective-permute-start(f32[144,256]{1,0:T(8,128)S(1)} %get-tuple-element.160.refs_0_), channel_id=1, source_target_pairs={{0,8},{8,0},{16,24},{24,16},{1,9},{9,1},{17,25},{25,17},{2,10},{10... | collective-permute-start | bytes 442376 | tf_op jit(solution)/shard_map/ppermute | solution.py:533
  25.1 7.9 %collective-permute-start.3 = (f32[144,256]{1,0:T(8,128)S(1)}, f32[144,256]{1,0:T(8,128)S(1)}, u32[]{:S(2)}, u32[]{:S(2)}) collective-permute-start(f32[144,256]{1,0:T(8,128)S(1)} %get-tuple-element.160.refs_0_), channel_id=1, source_target_pairs={{0,24},{8,16},{16,8},{24,0},{1,25},{9,17},{17,9},{25,1},{2,26},{10... | collective-permute-start | bytes 442376 | tf_op jit(solution)/shard_map/ppermute | solution.py:533
  33.6 9.9 %collective-permute-start.10 = (f32[16,16,256]{2,1,0:T(8,128)S(1)}, f32[16,16,256]{2,1,0:T(8,128)S(1)}, u32[]{:S(2)}, u32[]{:S(2)}) collective-permute-start(f32[16,16,256]{2,1,0:T(8,128)S(1)} %get-tuple-element.168.near_ref.refs_7_), channel_id=1, source_target_pairs={{0,1},{1,0},{2,3},{3,2},{4,5},{5,4},{6,7},{7,6},{8,9},{9,8},{10,11... | collective-permute-start | bytes 786440 | tf_op jit(solution)/shard_map/ppermute | solution.py:514
  33.7 3.8 %collective-permute-start.9 = (f32[16,256]{1,0:T(8,128)S(1)}, f32[16,256]{1,0:T(8,128)S(1)}, u32[]{:S(2)}, u32[]{:S(2)}) collective-permute-start(f32[16,256]{1,0:T(8,128)S(1)} %get-tuple-element.167._.refs_0_), channel_id=1, source_target_pairs={{0,16},{8,24},{16,0},{24,8},{1,17},{9,25},{17,1},{25,9},{2,18},{10... | collective-permute-start | bytes 49160 | tf_op jit(solution)/shard_map/ppermute | solution.py:533
  35.3 3.7 %collective-permute-start.8 = (f32[16,256]{1,0:T(8,128)S(1)}, f32[16,256]{1,0:T(8,128)S(1)}, u32[]{:S(2)}, u32[]{:S(2)}) collective-permute-start(f32[16,256]{1,0:T(8,128)S(1)} %get-tuple-element.167._.refs_0_), channel_id=1, source_target_pairs={{0,8},{8,0},{16,24},{24,16},{1,9},{9,1},{17,25},{25,17},{2,10},{10... | collective-permute-start | bytes 49160 | tf_op jit(solution)/shard_map/ppermute | solution.py:533
  36.8 4.6 %collective-permute-start.7 = (f32[16,256]{1,0:T(8,128)S(1)}, f32[16,256]{1,0:T(8,128)S(1)}, u32[]{:S(2)}, u32[]{:S(2)}) collective-permute-start(f32[16,256]{1,0:T(8,128)S(1)} %get-tuple-element.167._.refs_0_), channel_id=1, source_target_pairs={{0,24},{8,16},{16,8},{24,0},{1,25},{9,17},{17,9},{25,1},{2,26},{10... | collective-permute-start | bytes 49160 | tf_op jit(solution)/shard_map/ppermute | solution.py:533
  41.6 7.7 %collective-permute-start.14 = (f32[16,16,256]{2,1,0:T(8,128)S(1)}, f32[16,16,256]{2,1,0:T(8,128)S(1)}, u32[]{:S(2)}, u32[]{:S(2)}) collective-permute-start(f32[16,16,256]{2,1,0:T(8,128)S(1)} %get-tuple-element.171.far_ref.refs_8_), channel_id=1, source_target_pairs={{1,2},{2,1},{3,4},{4,3},{5,6},{6,5},{9,10},{10,9},{11,12},{12,11},... | collective-permute-start | bytes 786440 | tf_op jit(solution)/shard_map/ppermute | solution.py:514
  44.5 6.7 %collective-permute-start.13 = (f32[64,256]{1,0:T(8,128)S(1)}, f32[64,256]{1,0:T(8,128)S(1)}, u32[]{:S(2)}, u32[]{:S(2)}) collective-permute-start(f32[64,256]{1,0:T(8,128)S(1)} %get-tuple-element.178.refs_0_), channel_id=1, source_target_pairs={{0,16},{8,24},{16,0},{24,8},{1,17},{9,25},{17,1},{25,9},{2,18},{10... | collective-permute-start | bytes 196616 | tf_op jit(solution)/shard_map/ppermute | solution.py:533
  45.1 6.1 %collective-permute-start.12 = (f32[64,256]{1,0:T(8,128)S(1)}, f32[64,256]{1,0:T(8,128)S(1)}, u32[]{:S(2)}, u32[]{:S(2)}) collective-permute-start(f32[64,256]{1,0:T(8,128)S(1)} %get-tuple-element.178.refs_0_), channel_id=1, source_target_pairs={{0,8},{8,0},{16,24},{24,16},{1,9},{9,1},{17,25},{25,17},{2,10},{10... | collective-permute-start | bytes 196616 | tf_op jit(solution)/shard_map/ppermute | solution.py:533
  45.6 5.6 %collective-permute-start.11 = (f32[64,256]{1,0:T(8,128)S(1)}, f32[64,256]{1,0:T(8,128)S(1)}, u32[]{:S(2)}, u32[]{:S(2)}) collective-permute-start(f32[64,256]{1,0:T(8,128)S(1)} %get-tuple-element.178.refs_0_), channel_id=1, source_target_pairs={{0,24},{8,16},{16,8},{24,0},{1,25},{9,17},{17,9},{25,1},{2,26},{10... | collective-permute-start | bytes 196616 | tf_op jit(solution)/shard_map/ppermute | solution.py:533
  51.8 9.5 %collective-permute-start.18 = (f32[16,16,256]{2,1,0:T(8,128)S(1)}, f32[16,16,256]{2,1,0:T(8,128)S(1)}, u32[]{:S(2)}, u32[]{:S(2)}) collective-permute-start(f32[16,16,256]{2,1,0:T(8,128)S(1)} %get-tuple-element.185.near_ref.refs_7_), channel_id=1, source_target_pairs={{0,1},{1,0},{2,3},{3,2},{4,5},{5,4},{6,7},{7,6},{8,9},{9,8},{10,11... | collective-permute-start | bytes 786440 | tf_op jit(solution)/shard_map/ppermute | solution.py:514
  51.8 3.8 %collective-permute-start.17 = (f32[16,256]{1,0:T(8,128)S(1)}, f32[16,256]{1,0:T(8,128)S(1)}, u32[]{:S(2)}, u32[]{:S(2)}) collective-permute-start(f32[16,256]{1,0:T(8,128)S(1)} %get-tuple-element.184._.refs_0_), channel_id=1, source_target_pairs={{0,16},{8,24},{16,0},{24,8},{1,17},{9,25},{17,1},{25,9},{2,18},{10... | collective-permute-start | bytes 49160 | tf_op jit(solution)/shard_map/ppermute | solution.py:533
  53.0 3.7 %collective-permute-start.16 = (f32[16,256]{1,0:T(8,128)S(1)}, f32[16,256]{1,0:T(8,128)S(1)}, u32[]{:S(2)}, u32[]{:S(2)}) collective-permute-start(f32[16,256]{1,0:T(8,128)S(1)} %get-tuple-element.184._.refs_0_), channel_id=1, source_target_pairs={{0,8},{8,0},{16,24},{24,16},{1,9},{9,1},{17,25},{25,17},{2,10},{10... | collective-permute-start | bytes 49160 | tf_op jit(solution)/shard_map/ppermute | solution.py:533
  54.5 4.6 %collective-permute-start.15 = (f32[16,256]{1,0:T(8,128)S(1)}, f32[16,256]{1,0:T(8,128)S(1)}, u32[]{:S(2)}, u32[]{:S(2)}) collective-permute-start(f32[16,256]{1,0:T(8,128)S(1)} %get-tuple-element.184._.refs_0_), channel_id=1, source_target_pairs={{0,24},{8,16},{16,8},{24,0},{1,25},{9,17},{17,9},{25,1},{2,26},{10... | collective-permute-start | bytes 49160 | tf_op jit(solution)/shard_map/ppermute | solution.py:533
  59.3 7.7 %collective-permute-start.22 = (f32[16,16,256]{2,1,0:T(8,128)S(1)}, f32[16,16,256]{2,1,0:T(8,128)S(1)}, u32[]{:S(2)}, u32[]{:S(2)}) collective-permute-start(f32[16,16,256]{2,1,0:T(8,128)S(1)} %get-tuple-element.188.far_ref.refs_8_), channel_id=1, source_target_pairs={{1,2},{2,1},{3,4},{4,3},{5,6},{6,5},{9,10},{10,9},{11,12},{12,11},... | collective-permute-start | bytes 786440 | tf_op jit(solution)/shard_map/ppermute | solution.py:514
  62.2 6.7 %collective-permute-start.21 = (f32[64,256]{1,0:T(8,128)S(1)}, f32[64,256]{1,0:T(8,128)S(1)}, u32[]{:S(2)}, u32[]{:S(2)}) collective-permute-start(f32[64,256]{1,0:T(8,128)S(1)} %get-tuple-element.195.refs_0_), channel_id=1, source_target_pairs={{0,16},{8,24},{16,0},{24,8},{1,17},{9,25},{17,1},{25,9},{2,18},{10... | collective-permute-start | bytes 196616 | tf_op jit(solution)/shard_map/ppermute | solution.py:533
  62.8 6.1 %collective-permute-start.20 = (f32[64,256]{1,0:T(8,128)S(1)}, f32[64,256]{1,0:T(8,128)S(1)}, u32[]{:S(2)}, u32[]{:S(2)}) collective-permute-start(f32[64,256]{1,0:T(8,128)S(1)} %get-tuple-element.195.refs_0_), channel_id=1, source_target_pairs={{0,8},{8,0},{16,24},{24,16},{1,9},{9,1},{17,25},{25,17},{2,10},{10... | collective-permute-start | bytes 196616 | tf_op jit(solution)/shard_map/ppermute | solution.py:533
  63.7 5.5 %collective-permute-start.19 = (f32[64,256]{1,0:T(8,128)S(1)}, f32[64,256]{1,0:T(8,128)S(1)}, u32[]{:S(2)}, u32[]{:S(2)}) collective-permute-start(f32[64,256]{1,0:T(8,128)S(1)} %get-tuple-element.195.refs_0_), channel_id=1, source_target_pairs={{0,24},{8,16},{16,8},{24,0},{1,25},{9,17},{17,9},{25,1},{2,26},{10... | collective-permute-start | bytes 196616 | tf_op jit(solution)/shard_map/ppermute | solution.py:533
  69.8 9.4 %collective-permute-start.26 = (f32[16,16,256]{2,1,0:T(8,128)S(1)}, f32[16,16,256]{2,1,0:T(8,128)S(1)}, u32[]{:S(2)}, u32[]{:S(2)}) collective-permute-start(f32[16,16,256]{2,1,0:T(8,128)S(1)} %get-tuple-element.202.near_ref.refs_7_), channel_id=1, source_target_pairs={{0,1},{1,0},{2,3},{3,2},{4,5},{5,4},{6,7},{7,6},{8,9},{9,8},{10,11... | collective-permute-start | bytes 786440 | tf_op jit(solution)/shard_map/ppermute | solution.py:514
  69.9 3.8 %collective-permute-start.25 = (f32[16,256]{1,0:T(8,128)S(1)}, f32[16,256]{1,0:T(8,128)S(1)}, u32[]{:S(2)}, u32[]{:S(2)}) collective-permute-start(f32[16,256]{1,0:T(8,128)S(1)} %get-tuple-element.201._.refs_0_), channel_id=1, source_target_pairs={{0,16},{8,24},{16,0},{24,8},{1,17},{9,25},{17,1},{25,9},{2,18},{10... | collective-permute-start | bytes 49160 | tf_op jit(solution)/shard_map/ppermute | solution.py:533
  70.7 3.7 %collective-permute-start.24 = (f32[16,256]{1,0:T(8,128)S(1)}, f32[16,256]{1,0:T(8,128)S(1)}, u32[]{:S(2)}, u32[]{:S(2)}) collective-permute-start(f32[16,256]{1,0:T(8,128)S(1)} %get-tuple-element.201._.refs_0_), channel_id=1, source_target_pairs={{0,8},{8,0},{16,24},{24,16},{1,9},{9,1},{17,25},{25,17},{2,10},{10... | collective-permute-start | bytes 49160 | tf_op jit(solution)/shard_map/ppermute | solution.py:533
  72.2 4.6 %collective-permute-start.23 = (f32[16,256]{1,0:T(8,128)S(1)}, f32[16,256]{1,0:T(8,128)S(1)}, u32[]{:S(2)}, u32[]{:S(2)}) collective-permute-start(f32[16,256]{1,0:T(8,128)S(1)} %get-tuple-element.201._.refs_0_), channel_id=1, source_target_pairs={{0,24},{8,16},{16,8},{24,0},{1,25},{9,17},{17,9},{25,1},{2,26},{10... | collective-permute-start | bytes 49160 | tf_op jit(solution)/shard_map/ppermute | solution.py:533
  77.0 7.7 %collective-permute-start.30 = (f32[16,16,256]{2,1,0:T(8,128)S(1)}, f32[16,16,256]{2,1,0:T(8,128)S(1)}, u32[]{:S(2)}, u32[]{:S(2)}) collective-permute-start(f32[16,16,256]{2,1,0:T(8,128)S(1)} %get-tuple-element.205.far_ref.refs_8_), channel_id=1, source_target_pairs={{1,2},{2,1},{3,4},{4,3},{5,6},{6,5},{9,10},{10,9},{11,12},{12,11},... | collective-permute-start | bytes 786440 | tf_op jit(solution)/shard_map/ppermute | solution.py:514
  80.2 6.4 %collective-permute-start.29 = (f32[144,256]{1,0:T(8,128)S(1)}, f32[144,256]{1,0:T(8,128)S(1)}, u32[]{:S(2)}, u32[]{:S(2)}) collective-permute-start(f32[144,256]{1,0:T(8,128)S(1)} %get-tuple-element.212.refs_0_), channel_id=1, source_target_pairs={{0,16},{8,24},{16,0},{24,8},{1,17},{9,25},{17,1},{25,9},{2,18},{10... | collective-permute-start | bytes 442376 | tf_op jit(solution)/shard_map/ppermute | solution.py:533
  80.7 6.7 %collective-permute-start.28 = (f32[144,256]{1,0:T(8,128)S(1)}, f32[144,256]{1,0:T(8,128)S(1)}, u32[]{:S(2)}, u32[]{:S(2)}) collective-permute-start(f32[144,256]{1,0:T(8,128)S(1)} %get-tuple-element.212.refs_0_), channel_id=1, source_target_pairs={{0,8},{8,0},{16,24},{24,16},{1,9},{9,1},{17,25},{25,17},{2,10},{10... | collective-permute-start | bytes 442376 | tf_op jit(solution)/shard_map/ppermute | solution.py:533
  82.1 8.7 %collective-permute-start.27 = (f32[144,256]{1,0:T(8,128)S(1)}, f32[144,256]{1,0:T(8,128)S(1)}, u32[]{:S(2)}, u32[]{:S(2)}) collective-permute-start(f32[144,256]{1,0:T(8,128)S(1)} %get-tuple-element.212.refs_0_), channel_id=1, source_target_pairs={{0,24},{8,16},{16,8},{24,0},{1,25},{9,17},{17,9},{25,1},{2,26},{10... | collective-permute-start | bytes 442376 | tf_op jit(solution)/shard_map/ppermute | solution.py:533
  91.4 8.8 %collective-permute-start.34 = (f32[16,16,256]{2,1,0:T(8,128)S(1)}, f32[16,16,256]{2,1,0:T(8,128)S(1)}, u32[]{:S(2)}, u32[]{:S(2)}) collective-permute-start(f32[16,16,256]{2,1,0:T(8,128)S(1)} %get-tuple-element.219.near_ref.refs_7_), channel_id=1, source_target_pairs={{0,1},{1,0},{2,3},{3,2},{4,5},{5,4},{6,7},{7,6},{8,9},{9,8},{10,11... | collective-permute-start | bytes 786440 | tf_op jit(solution)/shard_map/ppermute | solution.py:514
  91.5 3.8 %collective-permute-start.33 = (f32[16,256]{1,0:T(8,128)S(1)}, f32[16,256]{1,0:T(8,128)S(1)}, u32[]{:S(2)}, u32[]{:S(2)}) collective-permute-start(f32[16,256]{1,0:T(8,128)S(1)} %get-tuple-element.218._.refs_0_), channel_id=1, source_target_pairs={{0,16},{8,24},{16,0},{24,8},{1,17},{9,25},{17,1},{25,9},{2,18},{10... | collective-permute-start | bytes 49160 | tf_op jit(solution)/shard_map/ppermute | solution.py:533
  93.0 4.6 %collective-permute-start.31 = (f32[16,256]{1,0:T(8,128)S(1)}, f32[16,256]{1,0:T(8,128)S(1)}, u32[]{:S(2)}, u32[]{:S(2)}) collective-permute-start(f32[16,256]{1,0:T(8,128)S(1)} %get-tuple-element.218._.refs_0_), channel_id=1, source_target_pairs={{0,24},{8,16},{16,8},{24,0},{1,25},{9,17},{17,9},{25,1},{2,26},{10... | collective-permute-start | bytes 49160 | tf_op jit(solution)/shard_map/ppermute | solution.py:533
  97.9 7.7 %collective-permute-start.38 = (f32[16,16,256]{2,1,0:T(8,128)S(1)}, f32[16,16,256]{2,1,0:T(8,128)S(1)}, u32[]{:S(2)}, u32[]{:S(2)}) collective-permute-start(f32[16,16,256]{2,1,0:T(8,128)S(1)} %get-tuple-element.222.far_ref.refs_8_), channel_id=1, source_target_pairs={{1,2},{2,1},{3,4},{4,3},{5,6},{6,5},{9,10},{10,9},{11,12},{12,11},... | collective-permute-start | bytes 786440 | tf_op jit(solution)/shard_map/ppermute | solution.py:514
  101.1 6.3 %collective-permute-start.37 = (f32[64,256]{1,0:T(8,128)S(1)}, f32[64,256]{1,0:T(8,128)S(1)}, u32[]{:S(2)}, u32[]{:S(2)}) collective-permute-start(f32[64,256]{1,0:T(8,128)S(1)} %get-tuple-element.229.refs_0_), channel_id=1, source_target_pairs={{0,16},{8,24},{16,0},{24,8},{1,17},{9,25},{17,1},{25,9},{2,18},{10... | collective-permute-start | bytes 196616 | tf_op jit(solution)/shard_map/ppermute | solution.py:533
  101.9 5.6 %collective-permute-start.36 = (f32[64,256]{1,0:T(8,128)S(1)}, f32[64,256]{1,0:T(8,128)S(1)}, u32[]{:S(2)}, u32[]{:S(2)}) collective-permute-start(f32[64,256]{1,0:T(8,128)S(1)} %get-tuple-element.229.refs_0_), channel_id=1, source_target_pairs={{0,8},{8,0},{16,24},{24,16},{1,9},{9,1},{17,25},{25,17},{2,10},{10... | collective-permute-start | bytes 196616 | tf_op jit(solution)/shard_map/ppermute | solution.py:533
  103.4 5.2 %collective-permute-start.35 = (f32[64,256]{1,0:T(8,128)S(1)}, f32[64,256]{1,0:T(8,128)S(1)}, u32[]{:S(2)}, u32[]{:S(2)}) collective-permute-start(f32[64,256]{1,0:T(8,128)S(1)} %get-tuple-element.229.refs_0_), channel_id=1, source_target_pairs={{0,24},{8,16},{16,8},{24,0},{1,25},{9,17},{17,9},{25,1},{2,26},{10... | collective-permute-start | bytes 196616 | tf_op jit(solution)/shard_map/ppermute | solution.py:533
  109.1 8.8 %collective-permute-start.43 = (f32[16,16,256]{2,1,0:T(8,128)S(1)}, f32[16,16,256]{2,1,0:T(8,128)S(1)}, u32[]{:S(2)}, u32[]{:S(2)}) collective-permute-start(f32[16,16,256]{2,1,0:T(8,128)S(1)} %get-tuple-element.236.near_ref), channel_id=1, source_target_pairs={{0,1},{1,0},{2,3},{3,2},{4,5},{5,4},{6,7},{7,6},{8,9},{9,8},{10,11... | collective-permute-start | bytes 786440 | tf_op jit(solution)/shard_map/ppermute | solution.py:514
  109.2 3.8 %collective-permute-start.41 = (f32[16,256]{1,0:T(8,128)S(1)}, f32[16,256]{1,0:T(8,128)S(1)}, u32[]{:S(2)}, u32[]{:S(2)}) collective-permute-start(f32[16,256]{1,0:T(8,128)S(1)} %get-tuple-element.235._.refs_0_), channel_id=1, source_target_pairs={{0,16},{8,24},{16,0},{24,8},{1,17},{9,25},{17,1},{25,9},{2,18},{10... | collective-permute-start | bytes 49160 | tf_op jit(solution)/shard_map/ppermute | solution.py:533
  109.7 3.7 %collective-permute-start.40 = (f32[16,256]{1,0:T(8,128)S(1)}, f32[16,256]{1,0:T(8,128)S(1)}, u32[]{:S(2)}, u32[]{:S(2)}) collective-permute-start(f32[16,256]{1,0:T(8,128)S(1)} %get-tuple-element.235._.refs_0_), channel_id=1, source_target_pairs={{0,8},{8,0},{16,24},{24,16},{1,9},{9,1},{17,25},{25,17},{2,10},{10... | collective-permute-start | bytes 49160 | tf_op jit(solution)/shard_map/ppermute | solution.py:533
  111.1 4.6 %collective-permute-start.39 = (f32[16,256]{1,0:T(8,128)S(1)}, f32[16,256]{1,0:T(8,128)S(1)}, u32[]{:S(2)}, u32[]{:S(2)}) collective-permute-start(f32[16,256]{1,0:T(8,128)S(1)} %get-tuple-element.235._.refs_0_), channel_id=1, source_target_pairs={{0,24},{8,16},{16,8},{24,0},{1,25},{9,17},{17,9},{25,1},{2,26},{10... | collective-permute-start | bytes 49160 | tf_op jit(solution)/shard_map/ppermute | solution.py:533
  115.9 7.1 %collective-permute-start.42 = (f32[16,8,256]{2,1,0:T(8,128)S(1)}, f32[16,8,256]{2,1,0:T(8,128)S(1)}, u32[]{:S(2)}, u32[]{:S(2)}) collective-permute-start(f32[16,8,256]{2,1,0:T(8,128)S(1)} %get-tuple-element.240), channel_id=1, source_target_pairs={{1,2},{2,1},{3,4},{4,3},{5,6},{6,5},{9,10},{10,9},{11,12},{12,11},... | collective-permute-start | bytes 393224 | tf_op jit(solution)/shard_map/ppermute | solution.py:514
  119.6 6.6 %collective-permute-start.49 = (f32[64,256]{1,0:T(8,128)S(1)}, f32[64,256]{1,0:T(8,128)S(1)}, u32[]{:S(2)}, u32[]{:S(2)}) collective-permute-start(f32[64,256]{1,0:T(8,128)S(1)} %get-tuple-element.251.refs_0_), channel_id=1, source_target_pairs={{0,16},{8,24},{16,0},{24,8},{1,17},{9,25},{17,1},{25,9},{2,18},{10... | collective-permute-start | bytes 196616 | tf_op jit(solution)/shard_map/ppermute | solution.py:533
  120.3 8.0 %collective-permute-start.48 = (f32[64,256]{1,0:T(8,128)S(1)}, f32[64,256]{1,0:T(8,128)S(1)}, u32[]{:S(2)}, u32[]{:S(2)}) collective-permute-start(f32[64,256]{1,0:T(8,128)S(1)} %get-tuple-element.251.refs_0_), channel_id=1, source_target_pairs={{0,8},{8,0},{16,24},{24,16},{1,9},{9,1},{17,25},{25,17},{2,10},{10... | collective-permute-start | bytes 196616 | tf_op jit(solution)/shard_map/ppermute | solution.py:533
  121.8 6.5 %collective-permute-start.47 = (f32[64,256]{1,0:T(8,128)S(1)}, f32[64,256]{1,0:T(8,128)S(1)}, u32[]{:S(2)}, u32[]{:S(2)}) collective-permute-start(f32[64,256]{1,0:T(8,128)S(1)} %get-tuple-element.251.refs_0_), channel_id=1, source_target_pairs={{0,24},{8,16},{16,8},{24,0},{1,25},{9,17},{17,9},{25,1},{2,26},{10... | collective-permute-start | bytes 196616 | tf_op jit(solution)/shard_map/ppermute | solution.py:533
  124.0 5.2 %collective-permute-start.46 = (f32[16,256]{1,0:T(8,128)S(1)}, f32[16,256]{1,0:T(8,128)S(1)}, u32[]{:S(2)}, u32[]{:S(2)}) collective-permute-start(f32[16,256]{1,0:T(8,128)S(1)} %get-tuple-element.249._.refs_0_), channel_id=1, source_target_pairs={{0,16},{8,24},{16,0},{24,8},{1,17},{9,25},{17,1},{25,9},{2,18},{10... | collective-permute-start | bytes 49160 | tf_op jit(solution)/shard_map/ppermute | solution.py:533
  124.7 4.5 %collective-permute-start.45 = (f32[16,256]{1,0:T(8,128)S(1)}, f32[16,256]{1,0:T(8,128)S(1)}, u32[]{:S(2)}, u32[]{:S(2)}) collective-permute-start(f32[16,256]{1,0:T(8,128)S(1)} %get-tuple-element.249._.refs_0_), channel_id=1, source_target_pairs={{0,8},{8,0},{16,24},{24,16},{1,9},{9,1},{17,25},{25,17},{2,10},{10... | collective-permute-start | bytes 49160 | tf_op jit(solution)/shard_map/ppermute | solution.py:533
  126.2 4.6 %collective-permute-start.44 = (f32[16,256]{1,0:T(8,128)S(1)}, f32[16,256]{1,0:T(8,128)S(1)}, u32[]{:S(2)}, u32[]{:S(2)}) collective-permute-start(f32[16,256]{1,0:T(8,128)S(1)} %get-tuple-element.249._.refs_0_), channel_id=1, source_target_pairs={{0,24},{8,16},{16,8},{24,0},{1,25},{9,17},{17,9},{25,1},{2,26},{10... | collective-permute-start | bytes 49160 | tf_op jit(solution)/shard_map/ppermute | solution.py:533
  (9 other events, 67.6 us)

commit v3 on v2

--- a/solution.py
+++ b/solution.py
@@ -22,7 +22,6 @@
 F32 = jnp.float32
 BF16 = jnp.bfloat16
 LANES = 128
-UNROLL = 8
 GROUP = 8
 VMEM_LIMIT = 24 * 1024 * 1024
 PARAMS = pltpu.CompilerParams(vmem_limit_bytes=VMEM_LIMIT)
@@ -70,36 +69,40 @@
 
 
 def near_kernel(
-    near_ref, far_ref, halo_ref, mats_ref, dual_u_ref, dual_t_ref, old_u_ref, old_t_ref,
+    weigh, last, near_ref, far_ref, halo_ref, mats_ref, dual_u_ref, dual_t_ref, old_u_ref, old_t_ref,
     head_ref, rest_ref, dual1_ref, old1_ref, *refs,
 ):
-    extra_ref = refs[0] if len(refs) > 8 else None
-    band_u_ref, band_t_ref, part_ref, moved_u_ref, moved_t_ref, band1_ref, moved1_ref, sums_ref = refs[-8:]
+    refs = list(refs)
+    extra_ref = refs.pop(0) if weigh else None
+    moved_u_ref, moved_t_ref, moved1_ref, sums_ref = refs[:4]
     chans, half, width = near_ref.shape
-    height, touched = 2 * half, band_t_ref.shape[1]
-    free = band_u_ref.shape[1]
+    height, touched = 2 * half, moved_t_ref.shape[1]
+    free = moved_u_ref.shape[1]
 
     def body(c, total):
         rows = jnp.concatenate([near_ref[c], far_ref[c], halo_ref[c]], axis=0)
         product = jnp.dot(mats_ref[c], stacked(rows), preferred_element_type=F32)
         band = product[:free]
-        band_u_ref[c] = band
         moved = dual_u_ref[c] + STEP_DUAL * (2.0 * band - old_u_ref[c])
         moved_u_ref[c] = moved
         band_t = product[free : free + touched]
-        band_t_ref[c] = band_t
         moved_t_ref[c] = dual_t_ref[c] + STEP_DUAL * (2.0 * band_t - old_t_ref[c])
-        part_ref[c] = product[free + touched :]
+        if not last:
+            band_u_ref, band_t_ref, part_ref, _ = refs[4:]
+            band_u_ref[c] = band
+            band_t_ref[c] = band_t
+            part_ref[c] = product[free + touched :]
         return total + moved * moved
 
-    sums_ref[:free] = lax.fori_loop(0, chans, body, jnp.zeros((free, width), F32), unroll=UNROLL)
+    sums_ref[:free] = lax.fori_loop(0, chans, body, jnp.zeros((free, width), F32), unroll=True)
     total = jnp.zeros((height, width), F32)
     for c in range(0, chans, GROUP):
         n = min(GROUP, chans - c)
         rows = jnp.concatenate([near_ref[c : c + n], far_ref[c : c + n]], axis=1)
         band = times_columns(rows.reshape(n * height, width), head_ref[...], rest_ref[...])
         band = band.reshape(n, height, width)
-        band1_ref[c : c + n] = band
+        if not last:
+            refs[7][c : c + n] = band
         moved = dual1_ref[c : c + n] + STEP_DUAL * (2.0 * band - old1_ref[c : c + n])
         moved1_ref[c : c + n] = moved
         total = total + jnp.sum(moved * moved, axis=0)
@@ -108,14 +111,15 @@
         sums_ref[free + height :] = extra_ref[...]
 
 
-def far_kernel(send, odd_ref, far_ref, mats_ref, band_in_ref, moved_in_ref, band_ref, moved_ref, sums_ref):
-    chans, touched, width = band_ref.shape
+def far_kernel(send, odd_ref, far_ref, mats_ref, band_in_ref, moved_in_ref, moved_ref, sums_ref, *band_refs):
+    chans, touched, width = moved_ref.shape
     odd = odd_ref[0] == 1
 
     def body(c, total):
         far = padded(odd, far_ref[c], send)
         product = jnp.dot(mats_ref[...], stacked(far), preferred_element_type=F32)
-        band_ref[c] = band_in_ref[c] + product
+        for band_ref in band_refs:
+            band_ref[c] = band_in_ref[c] + product
         moved = moved_in_ref[c] + (2.0 * STEP_DUAL) * product
         moved_ref[c] = moved
         return total + moved * moved
@@ -159,7 +163,7 @@
         return totals[0] + band * band, totals[1] + band_t * band_t
 
     zeros = jnp.zeros((free, width), F32), jnp.zeros((touched, width), F32)
-    totals = lax.fori_loop(0, chans, body, zeros, unroll=UNROLL)
+    totals = lax.fori_loop(0, chans, body, zeros, unroll=True)
     sums_ref[:free] = totals[0]
     sums_ref[free : free + height] = sum1_ref[...]
     sums_ref[free + height :] = totals[1]
@@ -174,28 +178,28 @@
         at += rows
 
 
-def pack_kernel(est_ref, dual_ref, dirty_ref, near_ref, far_ref, sems):
-    _, height, _ = est_ref.shape
+def pack_kernel(est_ref, dual_ref, dirty_ref, far_ref, near_ref, far_rows, near_rows, in_sems, out_sems):
+    height = est_ref.shape[1]
     total = near_ref.shape[1]
     send, edge = total // 2, total // 4
     odd = lax.rem(lax.axis_index("facet"), 2)
-    copies = []
-    for out_ref, low in ((near_ref, 1 - odd), (far_ref, odd)):
+    loads, stores = [], []
+    for out_ref, held, low in ((far_ref, far_rows, odd), (near_ref, near_rows, 1 - odd)):
         at = 0
-        for ref, rows in (
-            (est_ref, send), (dual_ref.at[:, 0], edge), (dirty_ref, edge)
-        ):
+        for ref, rows in ((est_ref, send), (dual_ref.at[:, 0], edge), (dirty_ref, edge)):
             start = pl.multiple_of(low * (height - rows), 8)
-            copies.append(
-                pltpu.make_async_copy(
-                    ref.at[:, pl.ds(start, rows)], out_ref.at[:, at : at + rows], sems.at[len(copies)]
-                )
-            )
+            k = len(loads)
+            piece = (slice(None), slice(at, at + rows))
+            loads.append(pltpu.make_async_copy(ref.at[:, pl.ds(start, rows)], held.at[piece], in_sems.at[k]))
+            stores.append(pltpu.make_async_copy(held.at[piece], out_ref.at[piece], out_sems.at[k]))
             at += rows
-    for copy in copies:
-        copy.start()
-    for copy in copies:
-        copy.wait()
+    for load in loads:
+        load.start()
+    for load, store in zip(loads, stores):
+        load.wait()
+        store.start()
+    for store in stores:
+        store.wait()
 
 
 def banded(line, rows):
@@ -314,7 +318,7 @@
         far_mats_ref[c] = far[half:]
         return carry
 
-    lax.fori_loop(0, chans, body, 0, unroll=2)
+    lax.fori_loop(0, chans, body, 0, unroll=8)
 
 
 def first_columns_kernel(odd_ref, own_ref, head_ref, rest_ref, near_ref, far_ref, band_ref, sum_ref):
@@ -348,7 +352,7 @@
         grad_ref[c] = times_columns(part_ref[c], head_ref[c], rest_ref[c]) - data
         return carry
 
-    lax.fori_loop(0, chans, body, 0, unroll=UNROLL)
+    lax.fori_loop(0, chans, body, 0, unroll=4)
 
 
 def gradient_kernel(part_ref, halo_ref, far_mats_ref, head_ref, rest_ref, data_ref, _, grad_ref):
@@ -361,7 +365,7 @@
         grad_ref[c] = times_columns(part, head_ref[c], rest_ref[c]) - data_ref[c]
         return carry
 
-    lax.fori_loop(0, chans, body, 0, unroll=UNROLL)
+    lax.fori_loop(0, chans, body, 0, unroll=True)
 
 
 def scaled(sums_refs, rows, radius):
@@ -560,18 +564,22 @@
     squares = ((chans, width, width), BF16)
 
     first_sides = rows(2 * send)
-    near, far = pl.pallas_call(
+    inputs = [pltpu.with_memory_space_constraint(x, pltpu.HBM) for x in (image_start, dual_start, dirty_image)]
+
+    in_hbm = pl.BlockSpec(memory_space=pltpu.HBM)
+    far, near = pl.pallas_call(
         pack_kernel,
-        out_shape=[pltpu.VMEM(*first_sides)] * 2,
-        in_specs=[pl.BlockSpec(memory_space=pltpu.HBM)] * 3,
-        out_specs=[VM] * 2,
-        scratch_shapes=[pltpu.SemaphoreType.DMA((6,))],
+        out_shape=[jax.ShapeDtypeStruct(*first_sides)] * 2,
+        in_specs=[in_hbm] * 3,
+        out_specs=[in_hbm] * 2,
+        scratch_shapes=[pltpu.VMEM(*first_sides)] * 2 + [pltpu.SemaphoreType.DMA((6,))] * 2,
         compiler_params=PARAMS,
         name="pack",
-    )(*(pltpu.with_memory_space_constraint(x, pltpu.HBM) for x in (image_start, dual_start, dirty_image)))
-    far, near = trade(far, True), trade(near, False)
-
-    def lines(cols, rows, half_c, half_r):
+    )(*inputs)
+    far = trade(far, True)
+    near = trade(near, False)
+
+    def lines(cols, taps, half_c, half_r):
         def circle(taps, half):
             gap = jnp.zeros((taps.shape[0], LANES - 2 * half - 1), F32)
             return jnp.concatenate([taps[:, half:], gap, taps[:, :half]], axis=1)
@@ -582,7 +590,7 @@
             return jnp.concatenate([lead, taps, gap], axis=1)
 
         return jnp.concatenate(
-            [circle(cols[:, ::-1], half_c), circle(cols, half_c), ramp(rows, half_r), ramp(rows[:, ::-1], half_r)],
+            [circle(cols[:, ::-1], half_c), circle(cols, half_c), ramp(taps, half_r), ramp(taps[:, ::-1], half_r)],
             axis=1,
         )
 
@@ -630,22 +638,24 @@
         last = step + 1 == passes
         far = trade(rim, True)
         weigh = step % INNER == 0
-        band_u, band_t, part, moved_u, moved_t, band1, moved1, sums = call(
-            near_kernel,
+        moved_u, moved_t, moved1, sums, *bands = call(
+            functools.partial(near_kernel, weigh, last),
             (est_near, est_far, near, mats, dual_u, dual_t, band_u, band_t, wav_head, wav_rest, dual1, band1)
             + ((weight_sums,) if weigh else ()),
-            (
-                wavy, late_rows, own, wavy, late_rows, own, own,
-                ((free + height + (summed[0][0] if weigh else 0), width), F32),
-            ),
-        )
+            (wavy, late_rows, own, ((free + height + (summed[0][0] if weigh else 0), width), F32))
+            + (() if last else (wavy, late_rows, own, own)),
+        )
+        if not last:
+            band_u, band_t, part, band1 = bands
         early = gathered(sums)
         if weigh:
             radius = call(functools.partial(radius_kernel, RADIUS_SCALE * total_chans), tuple(early), (summed,))[0]
-        band_t, moved_t, sums = call(
+        moved_t, sums, *bands = call(
             functools.partial(far_kernel, send), (odd, far, far_band, band_t, moved_t),
-            (late_rows, late_rows, late_sum), 1,
-        )
+            (late_rows, late_sum) + (() if last else (late_rows,)), 1,
+        )
+        if not last:
+            band_t = bands[0]
         late = gathered(sums)
         if last:
             image_final = pl.pallas_call(
@@ -657,7 +667,6 @@
                 compiler_params=PARAMS,
                 name="publish",
             )(est_near, est_far, sums)
-            in_hbm = pl.BlockSpec(memory_space=pltpu.HBM)
             result = jax.ShapeDtypeStruct((chans, 2, height, width), F32)
             dual_u, dual_final = pl.pallas_call(
                 functools.partial(final_early_kernel, len(early)),

time: 133 us -> 130 us (0.977)
  Pallas kernels: 36.4 us -> 28.6 us
  waiting for transfers between devices: 34.5 us -> 38.9 us
    pallas_call x35, Pallas kernels: 31.5 us -> 23.9 us  [call(): pl.pallas_call(kernel, out_shape=[jax.ShapeDtypeStruct(*shape) for shape...]
    ppermute x14, waiting for transfers between devices: 5.98 us -> 9.9 us  [trade(): return lax.ppermute(values, 'facet', pairs)]
  transfers between devices with their start and end apart: 50 -> 50, of which waited for: 28 -> 29; matrix products, arithmetic and copies ran while one was open for 1% -> 1% of each run, Pallas kernels for 20% -> 15%
where the time goes in v3:
time: 130 us; the launch traced here: 128 us
  starting transfers between devices  58.2 us (45%)
  waiting for transfers between devices  38.9 us (30%)
  Pallas kernels  28.6 us (22%)
  between operations  1.38 us (1%)
    ppermute x36, starting transfers between devices, gathered(): lax.ppermute(total, 'chan', [(i, i ^ k * low) for i in range(n)])  42.6 us
    ppermute x36, waiting for transfers between devices, gathered(): lax.ppermute(total, 'chan', [(i, i ^ k * low) for i in range(n)])  29 us
    pallas_call x35, Pallas kernels, call(): pl.pallas_call(kernel, out_shape=[jax.ShapeDtypeStruct(*shape) for shape...  23.9 us
    ppermute x14, starting transfers between devices, trade(): return lax.ppermute(values, 'facet', pairs)  15.6 us
    ppermute x14, waiting for transfers between devices, trade(): return lax.ppermute(values, 'facet', pairs)  9.9 us
  transfers between devices with their start and end apart: 50, of which 29 were waited for; matrix products, arithmetic and copies ran while one was open for 1% of the time, Pallas kernels for 15%

profile of v3, /device:TPU:16, one launch (start us, length us, event | category | flops | bytes accessed | tf_op | source)
XLA Modules:
  0.0 128.2 jit_solution(5237573163947357695)
XLA Ops:
  0.7 2.2 %pack.1 = (f32[16,32,256]{2,1,0:T(8,128)}, f32[16,32,256]{2,1,0:T(8,128)}) custom-call(f32[16,32,256]{2,1,0:T(8,128)} %est_ref.1, f32[16,2,32,256]{3,2,1,0:T(8,128)} %start_ref.1, f32[16,32,256]{2,1,0:T(8,128)} %dirty_ref.3), custom_call_target="tpu_custom_call" | custom-call | tf_op jit(solution)/shard_map/pack/pallas_call | solution.py:570
  3.0 2.4 %collective-permute-start.1 = (f32[16,32,256]{2,1,0:T(8,128)}, f32[16,32,256]{2,1,0:T(8,128)S(1)}, u32[]{:S(2)}, u32[]{:S(2)}) collective-permute-start(f32[16,32,256]{2,1,0:T(8,128)} %get-tuple-element.133), channel_id=1, source_target_pairs={{1,2},{2,1},{3,4},{4,3},{5,6},{6,5},{9,10},{10,9},{11,12},{12,11},... | collective-permute-start | bytes 1572872 | tf_op jit(solution)/shard_map/ppermute | solution.py:518
  6.5 3.8 %shard_map.86 = (bf16[16,80,144]{2,1,0:T(8,128)(2,1)S(1)}, bf16[16,48]{1,0:T(8,128)(2,1)S(1)}, bf16[16,16,48]{2,1,0:T(8,128)(2,1)S(1)}, bf16[16,32,144]{2,1,0:T(...) custom-call(s32[16]{0:T(128)S(1)} %copy-done.3, ...), custom_call_target="tpu_custom_call" | custom-call | tf_op jit(solution)/shard_map/pallas_call | solution.py:52
  10.8 2.9 %collective-permute-done.1.far_halo_ref = f32[16,32,256]{2,1,0:T(8,128)S(1)} collective-permute-done((f32[16,32,256]{2,1,0:T(8,128)}, f32[16,32,256]{2,1,0:T(8,128)S(1)}, u32[]{:S(2)}, u32[]{:S(2)}) %collective-permute-start.1) | collective-permute-done | bytes 524320 | tf_op jit(solution)/shard_map/ppermute | solution.py:518
  14.3 2.4 %shard_map.89 = (f32[16,32,256]{2,1,0:T(8,128)S(1)}, f32[16,32,256]{2,1,0:T(8,128)S(1)}) custom-call(f32[16,32,256]{2,1,0:T(8,128)S(1)} %get-tuple-element.141.part_ref, bf16[16,256,256]{2,1,0:T(8,128)(2,1)S(1)} %get-tuple-element.142.head_ref, bf16[16,256,256]{2,1,0:T(8,128)(2,1)S(1)} %get-tuple-element.143.rest_ref, ...), custom_call_target="tpu_custom_call" | custom-call | tf_op jit(solution)/shard_map/pallas_call | solution.py:52
  17.9 2.0 %collective-permute-start.6 = (f32[16,16,256]{2,1,0:T(8,128)S(1)}, f32[16,16,256]{2,1,0:T(8,128)S(1)}, u32[]{:S(2)}, u32[]{:S(2)}) collective-permute-start(f32[16,16,256]{2,1,0:T(8,128)S(1)} %get-tuple-element.154.far_ref.refs_8_), channel_id=1, source_target_pairs={{1,2},{2,1},{3,4},{4,3},{5,6},{6,5},{9,10},{10,9},{11,12},{12,11},... | collective-permute-start | bytes 786440 | tf_op jit(solution)/shard_map/ppermute | solution.py:518
  20.6 1.6 %collective-permute-start.5 = (f32[144,256]{1,0:T(8,128)S(1)}, f32[144,256]{1,0:T(8,128)S(1)}, u32[]{:S(2)}, u32[]{:S(2)}) collective-permute-start(f32[144,256]{1,0:T(8,128)S(1)} %get-tuple-element.159.refs_0_), channel_id=1, source_target_pairs={{0,16},{8,24},{16,0},{24,8},{1,17},{9,25},{17,1},{25,9},{2,18},{10... | collective-permute-start | bytes 442376 | tf_op jit(solution)/shard_map/ppermute | solution.py:537
  22.2 1.5 %collective-permute-start.4 = (f32[144,256]{1,0:T(8,128)S(1)}, f32[144,256]{1,0:T(8,128)S(1)}, u32[]{:S(2)}, u32[]{:S(2)}) collective-permute-start(f32[144,256]{1,0:T(8,128)S(1)} %get-tuple-element.159.refs_0_), channel_id=1, source_target_pairs={{0,8},{8,0},{16,24},{24,16},{1,9},{9,1},{17,25},{25,17},{2,10},{10... | collective-permute-start | bytes 442376 | tf_op jit(solution)/shard_map/ppermute | solution.py:537
  24.1 1.4 %collective-permute-done.6.far_ref.halo_ref = f32[16,16,256]{2,1,0:T(8,128)S(1)} collective-permute-done((f32[16,16,256]{2,1,0:T(8,128)S(1)}, f32[16,16,256]{2,1,0:T(8,128)S(1)}, u32[]{:S(2)}, u32[]{:S(2)}) %collective-permute-start.6) | collective-permute-done | bytes 262176 | tf_op jit(solution)/shard_map/ppermute | solution.py:518
  25.8 1.4 %shard_map.94.refs_9_ = f32[16,32,256]{2,1,0:T(8,128)S(1)} custom-call(f32[16,32,256]{2,1,0:T(8,128)S(1)} %get-tuple-element.162.part_ref, f32[16,16,256]{2,1,0:T(8,128)S(1)} %collective-permute-done.6.far_ref.halo_ref, bf16[16,16,48]{2,1,0:T(8,128)(2,1)S(1)} %get-tuple-element.136.far_mats_ref, bf16[16,256,256]{2,1,0:T(8,128)(2,1)S(1)} %get-tuple-element.142.head_ref, ...), custom_call_target="tpu_custom_call" | custom-call | tf_op jit(solution)/shard_map/pallas_call | solution.py:52
  27.2 1.7 %collective-permute-done.4.refs_2_ = f32[144,256]{1,0:T(8,128)S(1)} collective-permute-done((f32[144,256]{1,0:T(8,128)S(1)}, f32[144,256]{1,0:T(8,128)S(1)}, u32[]{:S(2)}, u32[]{:S(2)}) %collective-permute-start.4) | collective-permute-done | bytes 147488 | tf_op jit(solution)/shard_map/ppermute | solution.py:537
  28.9 3.0 %collective-permute-done.3.refs_1_ = f32[144,256]{1,0:T(8,128)S(1)} collective-permute-done((f32[144,256]{1,0:T(8,128)S(1)}, f32[144,256]{1,0:T(8,128)S(1)}, u32[]{:S(2)}, u32[]{:S(2)}) %collective-permute-start.3) | collective-permute-done | bytes 147488 | tf_op jit(solution)/shard_map/ppermute | solution.py:537
  32.6 1.6 %collective-permute-start.9 = (f32[16,256]{1,0:T(8,128)S(1)}, f32[16,256]{1,0:T(8,128)S(1)}, u32[]{:S(2)}, u32[]{:S(2)}) collective-permute-start(f32[16,256]{1,0:T(8,128)S(1)} %get-tuple-element.166._.refs_0_), channel_id=1, source_target_pairs={{0,16},{8,24},{16,0},{24,8},{1,17},{9,25},{17,1},{25,9},{2,18},{10... | collective-permute-start | bytes 49160 | tf_op jit(solution)/shard_map/ppermute | solution.py:537
  34.2 1.5 %collective-permute-start.8 = (f32[16,256]{1,0:T(8,128)S(1)}, f32[16,256]{1,0:T(8,128)S(1)}, u32[]{:S(2)}, u32[]{:S(2)}) collective-permute-start(f32[16,256]{1,0:T(8,128)S(1)} %get-tuple-element.166._.refs_0_), channel_id=1, source_target_pairs={{0,8},{8,0},{16,24},{24,16},{1,9},{9,1},{17,25},{25,17},{2,10},{10... | collective-permute-start | bytes 49160 | tf_op jit(solution)/shard_map/ppermute | solution.py:537
  36.4 1.5 %collective-permute-done.8.refs_2_ = f32[16,256]{1,0:T(8,128)S(1)} collective-permute-done((f32[16,256]{1,0:T(8,128)S(1)}, f32[16,256]{1,0:T(8,128)S(1)}, u32[]{:S(2)}, u32[]{:S(2)}) %collective-permute-start.8) | collective-permute-done | bytes 16416 | tf_op jit(solution)/shard_map/ppermute | solution.py:537
  37.9 2.4 %collective-permute-done.7.refs_1_ = f32[16,256]{1,0:T(8,128)S(1)} collective-permute-done((f32[16,256]{1,0:T(8,128)S(1)}, f32[16,256]{1,0:T(8,128)S(1)}, u32[]{:S(2)}, u32[]{:S(2)}) %collective-permute-start.7) | collective-permute-done | bytes 16416 | tf_op jit(solution)/shard_map/ppermute | solution.py:537
  40.5 1.9 %collective-permute-start.14 = (f32[16,16,256]{2,1,0:T(8,128)S(1)}, f32[16,16,256]{2,1,0:T(8,128)S(1)}, u32[]{:S(2)}, u32[]{:S(2)}) collective-permute-start(f32[16,16,256]{2,1,0:T(8,128)S(1)} %get-tuple-element.170.far_ref.refs_8_), channel_id=1, source_target_pairs={{1,2},{2,1},{3,4},{4,3},{5,6},{6,5},{9,10},{10,9},{11,12},{12,11},... | collective-permute-start | bytes 786440 | tf_op jit(solution)/shard_map/ppermute | solution.py:518
  44.2 2.5 %collective-permute-start.11 = (f32[64,256]{1,0:T(8,128)S(1)}, f32[64,256]{1,0:T(8,128)S(1)}, u32[]{:S(2)}, u32[]{:S(2)}) collective-permute-start(f32[64,256]{1,0:T(8,128)S(1)} %get-tuple-element.177.refs_0_), channel_id=1, source_target_pairs={{0,24},{8,16},{16,8},{24,0},{1,25},{9,17},{17,9},{25,1},{2,26},{10... | collective-permute-start | bytes 196616 | tf_op jit(solution)/shard_map/ppermute | solution.py:537
  46.7 1.5 %collective-permute-done.14.far_ref.halo_ref = f32[16,16,256]{2,1,0:T(8,128)S(1)} collective-permute-done((f32[16,16,256]{2,1,0:T(8,128)S(1)}, f32[16,16,256]{2,1,0:T(8,128)S(1)}, u32[]{:S(2)}, u32[]{:S(2)}) %collective-permute-start.14) | collective-permute-done | bytes 262176 | tf_op jit(solution)/shard_map/ppermute | solution.py:518
  48.4 1.4 %shard_map.99.refs_9_ = f32[16,32,256]{2,1,0:T(8,128)S(1)} custom-call(f32[16,32,256]{2,1,0:T(8,128)S(1)} %get-tuple-element.180.part_ref, f32[16,16,256]{2,1,0:T(8,128)S(1)} %collective-permute-done.14.far_ref.halo_ref, bf16[16,16,48]{2,1,0:T(8,128)(2,1)S(1)} %get-tuple-element.136.far_mats_ref, bf16[16,256,256]{2,1,0:T(8,128)(2,1)S(1)} %get-tuple-element.142.head_ref, ...), custom_call_target="tpu_custom_call" | custom-call | tf_op jit(solution)/shard_map/pallas_call | solution.py:52
  51.6 1.5 %collective-permute-start.16 = (f32[16,256]{1,0:T(8,128)S(1)}, f32[16,256]{1,0:T(8,128)S(1)}, u32[]{:S(2)}, u32[]{:S(2)}) collective-permute-start(f32[16,256]{1,0:T(8,128)S(1)} %get-tuple-element.183._.refs_0_), channel_id=1, source_target_pairs={{0,8},{8,0},{16,24},{24,16},{1,9},{9,1},{17,25},{25,17},{2,10},{10... | collective-permute-start | bytes 49160 | tf_op jit(solution)/shard_map/ppermute | solution.py:537
  55.3 2.4 %collective-permute-done.15.refs_1_ = f32[16,256]{1,0:T(8,128)S(1)} collective-permute-done((f32[16,256]{1,0:T(8,128)S(1)}, f32[16,256]{1,0:T(8,128)S(1)}, u32[]{:S(2)}, u32[]{:S(2)}) %collective-permute-start.15) | collective-permute-done | bytes 16416 | tf_op jit(solution)/shard_map/ppermute | solution.py:537
  58.0 2.1 %collective-permute-start.22 = (f32[16,16,256]{2,1,0:T(8,128)S(1)}, f32[16,16,256]{2,1,0:T(8,128)S(1)}, u32[]{:S(2)}, u32[]{:S(2)}) collective-permute-start(f32[16,16,256]{2,1,0:T(8,128)S(1)} %get-tuple-element.187.far_ref.refs_8_), channel_id=1, source_target_pairs={{1,2},{2,1},{3,4},{4,3},{5,6},{6,5},{9,10},{10,9},{11,12},{12,11},... | collective-permute-start | bytes 786440 | tf_op jit(solution)/shard_map/ppermute | solution.py:518
  62.3 2.0 %collective-permute-start.19 = (f32[64,256]{1,0:T(8,128)S(1)}, f32[64,256]{1,0:T(8,128)S(1)}, u32[]{:S(2)}, u32[]{:S(2)}) collective-permute-start(f32[64,256]{1,0:T(8,128)S(1)} %get-tuple-element.194.refs_0_), channel_id=1, source_target_pairs={{0,24},{8,16},{16,8},{24,0},{1,25},{9,17},{17,9},{25,1},{2,26},{10... | collective-permute-start | bytes 196616 | tf_op jit(solution)/shard_map/ppermute | solution.py:537
  64.3 1.3 %collective-permute-done.22.far_ref.halo_ref = f32[16,16,256]{2,1,0:T(8,128)S(1)} collective-permute-done((f32[16,16,256]{2,1,0:T(8,128)S(1)}, f32[16,16,256]{2,1,0:T(8,128)S(1)}, u32[]{:S(2)}, u32[]{:S(2)}) %collective-permute-start.22) | collective-permute-done | bytes 262176 | tf_op jit(solution)/shard_map/ppermute | solution.py:518
  65.8 1.4 %shard_map.104.refs_9_ = f32[16,32,256]{2,1,0:T(8,128)S(1)} custom-call(f32[16,32,256]{2,1,0:T(8,128)S(1)} %get-tuple-element.197.part_ref, f32[16,16,256]{2,1,0:T(8,128)S(1)} %collective-permute-done.22.far_ref.halo_ref, bf16[16,16,48]{2,1,0:T(8,128)(2,1)S(1)} %get-tuple-element.136.far_mats_ref, bf16[16,256,256]{2,1,0:T(8,128)(2,1)S(1)} %get-tuple-element.142.head_ref, ...), custom_call_target="tpu_custom_call" | custom-call | tf_op jit(solution)/shard_map/pallas_call | solution.py:52
  69.2 1.5 %collective-permute-start.24 = (f32[16,256]{1,0:T(8,128)S(1)}, f32[16,256]{1,0:T(8,128)S(1)}, u32[]{:S(2)}, u32[]{:S(2)}) collective-permute-start(f32[16,256]{1,0:T(8,128)S(1)} %get-tuple-element.200._.refs_0_), channel_id=1, source_target_pairs={{0,8},{8,0},{16,24},{24,16},{1,9},{9,1},{17,25},{25,17},{2,10},{10... | collective-permute-start | bytes 49160 | tf_op jit(solution)/shard_map/ppermute | solution.py:537
  73.0 2.4 %collective-permute-done.23.refs_1_ = f32[16,256]{1,0:T(8,128)S(1)} collective-permute-done((f32[16,256]{1,0:T(8,128)S(1)}, f32[16,256]{1,0:T(8,128)S(1)}, u32[]{:S(2)}, u32[]{:S(2)}) %collective-permute-start.23) | collective-permute-done | bytes 16416 | tf_op jit(solution)/shard_map/ppermute | solution.py:537
  75.6 1.9 %collective-permute-start.30 = (f32[16,16,256]{2,1,0:T(8,128)S(1)}, f32[16,16,256]{2,1,0:T(8,128)S(1)}, u32[]{:S(2)}, u32[]{:S(2)}) collective-permute-start(f32[16,16,256]{2,1,0:T(8,128)S(1)} %get-tuple-element.204.far_ref.refs_8_), channel_id=1, source_target_pairs={{1,2},{2,1},{3,4},{4,3},{5,6},{6,5},{9,10},{10,9},{11,12},{12,11},... | collective-permute-start | bytes 786440 | tf_op jit(solution)/shard_map/ppermute | solution.py:518
  78.9 1.4 %collective-permute-start.28 = (f32[144,256]{1,0:T(8,128)S(1)}, f32[144,256]{1,0:T(8,128)S(1)}, u32[]{:S(2)}, u32[]{:S(2)}) collective-permute-start(f32[144,256]{1,0:T(8,128)S(1)} %get-tuple-element.211.refs_0_), channel_id=1, source_target_pairs={{0,8},{8,0},{16,24},{24,16},{1,9},{9,1},{17,25},{25,17},{2,10},{10... | collective-permute-start | bytes 442376 | tf_op jit(solution)/shard_map/ppermute | solution.py:537
  80.3 1.6 %collective-permute-start.27 = (f32[144,256]{1,0:T(8,128)S(1)}, f32[144,256]{1,0:T(8,128)S(1)}, u32[]{:S(2)}, u32[]{:S(2)}) collective-permute-start(f32[144,256]{1,0:T(8,128)S(1)} %get-tuple-element.211.refs_0_), channel_id=1, source_target_pairs={{0,24},{8,16},{16,8},{24,0},{1,25},{9,17},{17,9},{25,1},{2,26},{10... | collective-permute-start | bytes 442376 | tf_op jit(solution)/shard_map/ppermute | solution.py:537
  81.9 1.4 %collective-permute-done.30.far_ref.halo_ref = f32[16,16,256]{2,1,0:T(8,128)S(1)} collective-permute-done((f32[16,16,256]{2,1,0:T(8,128)S(1)}, f32[16,16,256]{2,1,0:T(8,128)S(1)}, u32[]{:S(2)}, u32[]{:S(2)}) %collective-permute-start.30) | collective-permute-done | bytes 262176 | tf_op jit(solution)/shard_map/ppermute | solution.py:518
  83.5 1.4 %shard_map.111.refs_9_ = f32[16,32,256]{2,1,0:T(8,128)S(1)} custom-call(f32[16,32,256]{2,1,0:T(8,128)S(1)} %get-tuple-element.214.part_ref, f32[16,16,256]{2,1,0:T(8,128)S(1)} %collective-permute-done.30.far_ref.halo_ref, bf16[16,16,48]{2,1,0:T(8,128)(2,1)S(1)} %get-tuple-element.136.far_mats_ref, bf16[16,256,256]{2,1,0:T(8,128)(2,1)S(1)} %get-tuple-element.142.head_ref, ...), custom_call_target="tpu_custom_call" | custom-call | tf_op jit(solution)/shard_map/pallas_call | solution.py:52
  85.6 3.3 %collective-permute-done.27.refs_1_ = f32[144,256]{1,0:T(8,128)S(1)} collective-permute-done((f32[144,256]{1,0:T(8,128)S(1)}, f32[144,256]{1,0:T(8,128)S(1)}, u32[]{:S(2)}, u32[]{:S(2)}) %collective-permute-start.27) | collective-permute-done | bytes 147488 | tf_op jit(solution)/shard_map/ppermute | solution.py:537
  91.2 2.0 %collective-permute-start.31 = (f32[16,256]{1,0:T(8,128)S(1)}, f32[16,256]{1,0:T(8,128)S(1)}, u32[]{:S(2)}, u32[]{:S(2)}) collective-permute-start(f32[16,256]{1,0:T(8,128)S(1)} %get-tuple-element.217._.refs_0_), channel_id=1, source_target_pairs={{0,24},{8,16},{16,8},{24,0},{1,25},{9,17},{17,9},{25,1},{2,26},{10... | collective-permute-start | bytes 49160 | tf_op jit(solution)/shard_map/ppermute | solution.py:537
  93.9 1.9 %collective-permute-done.31.refs_1_ = f32[16,256]{1,0:T(8,128)S(1)} collective-permute-done((f32[16,256]{1,0:T(8,128)S(1)}, f32[16,256]{1,0:T(8,128)S(1)}, u32[]{:S(2)}, u32[]{:S(2)}) %collective-permute-start.31) | collective-permute-done | bytes 16416 | tf_op jit(solution)/shard_map/ppermute | solution.py:537
  96.0 2.3 %collective-permute-start.38 = (f32[16,16,256]{2,1,0:T(8,128)S(1)}, f32[16,16,256]{2,1,0:T(8,128)S(1)}, u32[]{:S(2)}, u32[]{:S(2)}) collective-permute-start(f32[16,16,256]{2,1,0:T(8,128)S(1)} %get-tuple-element.221.far_ref.refs_8_), channel_id=1, source_target_pairs={{1,2},{2,1},{3,4},{4,3},{5,6},{6,5},{9,10},{10,9},{11,12},{12,11},... | collective-permute-start | bytes 786440 | tf_op jit(solution)/shard_map/ppermute | solution.py:518
  99.8 1.5 %collective-permute-start.36 = (f32[64,256]{1,0:T(8,128)S(1)}, f32[64,256]{1,0:T(8,128)S(1)}, u32[]{:S(2)}, u32[]{:S(2)}) collective-permute-start(f32[64,256]{1,0:T(8,128)S(1)} %get-tuple-element.228.refs_0_), channel_id=1, source_target_pairs={{0,8},{8,0},{16,24},{24,16},{1,9},{9,1},{17,25},{25,17},{2,10},{10... | collective-permute-start | bytes 196616 | tf_op jit(solution)/shard_map/ppermute | solution.py:537
  101.3 1.3 %collective-permute-start.35 = (f32[64,256]{1,0:T(8,128)S(1)}, f32[64,256]{1,0:T(8,128)S(1)}, u32[]{:S(2)}, u32[]{:S(2)}) collective-permute-start(f32[64,256]{1,0:T(8,128)S(1)} %get-tuple-element.228.refs_0_), channel_id=1, source_target_pairs={{0,24},{8,16},{16,8},{24,0},{1,25},{9,17},{17,9},{25,1},{2,26},{10... | collective-permute-start | bytes 196616 | tf_op jit(solution)/shard_map/ppermute | solution.py:537
  103.9 1.4 %shard_map.116.refs_9_ = f32[16,32,256]{2,1,0:T(8,128)S(1)} custom-call(f32[16,32,256]{2,1,0:T(8,128)S(1)} %get-tuple-element.231.part_ref, f32[16,16,256]{2,1,0:T(8,128)S(1)} %collective-permute-done.38.far_ref.halo_ref, bf16[16,16,48]{2,1,0:T(8,128)(2,1)S(1)} %get-tuple-element.136.far_mats_ref, bf16[16,256,256]{2,1,0:T(8,128)(2,1)S(1)} %get-tuple-element.142.head_ref, ...), custom_call_target="tpu_custom_call" | custom-call | tf_op jit(solution)/shard_map/pallas_call | solution.py:52
  107.6 1.4 %collective-permute-start.40 = (f32[16,256]{1,0:T(8,128)S(1)}, f32[16,256]{1,0:T(8,128)S(1)}, u32[]{:S(2)}, u32[]{:S(2)}) collective-permute-start(f32[16,256]{1,0:T(8,128)S(1)} %get-tuple-element.234._.refs_0_), channel_id=1, source_target_pairs={{0,8},{8,0},{16,24},{24,16},{1,9},{9,1},{17,25},{25,17},{2,10},{10... | collective-permute-start | bytes 49160 | tf_op jit(solution)/shard_map/ppermute | solution.py:537
  109.0 1.6 %collective-permute-start.39 = (f32[16,256]{1,0:T(8,128)S(1)}, f32[16,256]{1,0:T(8,128)S(1)}, u32[]{:S(2)}, u32[]{:S(2)}) collective-permute-start(f32[16,256]{1,0:T(8,128)S(1)} %get-tuple-element.234._.refs_0_), channel_id=1, source_target_pairs={{0,24},{8,16},{16,8},{24,0},{1,25},{9,17},{17,9},{25,1},{2,26},{10... | collective-permute-start | bytes 49160 | tf_op jit(solution)/shard_map/ppermute | solution.py:537
  111.4 2.3 %collective-permute-done.39.refs_1_ = f32[16,256]{1,0:T(8,128)S(1)} collective-permute-done((f32[16,256]{1,0:T(8,128)S(1)}, f32[16,256]{1,0:T(8,128)S(1)}, u32[]{:S(2)}, u32[]{:S(2)}) %collective-permute-start.39) | collective-permute-done | bytes 16416 | tf_op jit(solution)/shard_map/ppermute | solution.py:537
  113.9 1.9 %collective-permute-start.42 = (f32[16,8,256]{2,1,0:T(8,128)S(1)}, f32[16,8,256]{2,1,0:T(8,128)S(1)}, u32[]{:S(2)}, u32[]{:S(2)}) collective-permute-start(f32[16,8,256]{2,1,0:T(8,128)S(1)} %get-tuple-element.239), channel_id=1, source_target_pairs={{1,2},{2,1},{3,4},{4,3},{5,6},{6,5},{9,10},{10,9},{11,12},{12,11},... | collective-permute-start | bytes 393224 | tf_op jit(solution)/shard_map/ppermute | solution.py:518
  117.2 1.5 %collective-permute-start.48 = (f32[64,256]{1,0:T(8,128)S(1)}, f32[64,256]{1,0:T(8,128)S(1)}, u32[]{:S(2)}, u32[]{:S(2)}) collective-permute-start(f32[64,256]{1,0:T(8,128)S(1)} %get-tuple-element.249.refs_0_), channel_id=1, source_target_pairs={{0,8},{8,0},{16,24},{24,16},{1,9},{9,1},{17,25},{25,17},{2,10},{10... | collective-permute-start | bytes 196616 | tf_op jit(solution)/shard_map/ppermute | solution.py:537
  121.1 1.5 %collective-permute-start.45 = (f32[16,256]{1,0:T(8,128)S(1)}, f32[16,256]{1,0:T(8,128)S(1)}, u32[]{:S(2)}, u32[]{:S(2)}) collective-permute-start(f32[16,256]{1,0:T(8,128)S(1)} %get-tuple-element.247._.refs_0_), channel_id=1, source_target_pairs={{0,8},{8,0},{16,24},{24,16},{1,9},{9,1},{17,25},{25,17},{2,10},{10... | collective-permute-start | bytes 49160 | tf_op jit(solution)/shard_map/ppermute | solution.py:537
  122.6 1.3 %collective-permute-start.44 = (f32[16,256]{1,0:T(8,128)S(1)}, f32[16,256]{1,0:T(8,128)S(1)}, u32[]{:S(2)}, u32[]{:S(2)}) collective-permute-start(f32[16,256]{1,0:T(8,128)S(1)} %get-tuple-element.247._.refs_0_), channel_id=1, source_target_pairs={{0,24},{8,16},{16,8},{24,0},{1,25},{9,17},{17,9},{25,1},{2,26},{10... | collective-permute-start | bytes 49160 | tf_op jit(solution)/shard_map/ppermute | solution.py:537
  125.6 1.6 %collective-permute-done.44.refs_1_ = f32[16,256]{1,0:T(8,128)S(1)} collective-permute-done((f32[16,256]{1,0:T(8,128)S(1)}, f32[16,256]{1,0:T(8,128)S(1)}, u32[]{:S(2)}, u32[]{:S(2)}) %collective-permute-start.44) | collective-permute-done | bytes 16416 | tf_op jit(solution)/shard_map/ppermute | solution.py:537
  (122 shorter events, 37.1 us)
Async XLA Ops:
  2.9 7.9 %collective-permute-start = (f32[16,32,256]{2,1,0:T(8,128)}, f32[16,32,256]{2,1,0:T(8,128)S(1)}, u32[]{:S(2)}, u32[]{:S(2)}) collective-permute-start(f32[16,32,256]{2,1,0:T(8,128)} %get-tuple-element.132), channel_id=1, source_target_pairs={{0,1},{1,0},{2,3},{3,2},{4,5},{5,4},{6,7},{7,6},{8,9},{9,8},{10,11... | collective-permute-start | bytes 1572872 | tf_op jit(solution)/shard_map/ppermute | solution.py:518
  3.0 10.7 %collective-permute-start.1 = (f32[16,32,256]{2,1,0:T(8,128)}, f32[16,32,256]{2,1,0:T(8,128)S(1)}, u32[]{:S(2)}, u32[]{:S(2)}) collective-permute-start(f32[16,32,256]{2,1,0:T(8,128)} %get-tuple-element.133), channel_id=1, source_target_pairs={{1,2},{2,1},{3,4},{4,3},{5,6},{6,5},{9,10},{10,9},{11,12},{12,11},... | collective-permute-start | bytes 1572872 | tf_op jit(solution)/shard_map/ppermute | solution.py:518
  17.9 7.7 %collective-permute-start.6 = (f32[16,16,256]{2,1,0:T(8,128)S(1)}, f32[16,16,256]{2,1,0:T(8,128)S(1)}, u32[]{:S(2)}, u32[]{:S(2)}) collective-permute-start(f32[16,16,256]{2,1,0:T(8,128)S(1)} %get-tuple-element.154.far_ref.refs_8_), channel_id=1, source_target_pairs={{1,2},{2,1},{3,4},{4,3},{5,6},{6,5},{9,10},{10,9},{11,12},{12,11},... | collective-permute-start | bytes 786440 | tf_op jit(solution)/shard_map/ppermute | solution.py:518
  20.6 6.6 %collective-permute-start.5 = (f32[144,256]{1,0:T(8,128)S(1)}, f32[144,256]{1,0:T(8,128)S(1)}, u32[]{:S(2)}, u32[]{:S(2)}) collective-permute-start(f32[144,256]{1,0:T(8,128)S(1)} %get-tuple-element.159.refs_0_), channel_id=1, source_target_pairs={{0,16},{8,24},{16,0},{24,8},{1,17},{9,25},{17,1},{25,9},{2,18},{10... | collective-permute-start | bytes 442376 | tf_op jit(solution)/shard_map/ppermute | solution.py:537
  22.2 6.7 %collective-permute-start.4 = (f32[144,256]{1,0:T(8,128)S(1)}, f32[144,256]{1,0:T(8,128)S(1)}, u32[]{:S(2)}, u32[]{:S(2)}) collective-permute-start(f32[144,256]{1,0:T(8,128)S(1)} %get-tuple-element.159.refs_0_), channel_id=1, source_target_pairs={{0,8},{8,0},{16,24},{24,16},{1,9},{9,1},{17,25},{25,17},{2,10},{10... | collective-permute-start | bytes 442376 | tf_op jit(solution)/shard_map/ppermute | solution.py:537
  23.6 8.2 %collective-permute-start.3 = (f32[144,256]{1,0:T(8,128)S(1)}, f32[144,256]{1,0:T(8,128)S(1)}, u32[]{:S(2)}, u32[]{:S(2)}) collective-permute-start(f32[144,256]{1,0:T(8,128)S(1)} %get-tuple-element.159.refs_0_), channel_id=1, source_target_pairs={{0,24},{8,16},{16,8},{24,0},{1,25},{9,17},{17,9},{25,1},{2,26},{10... | collective-permute-start | bytes 442376 | tf_op jit(solution)/shard_map/ppermute | solution.py:537
  32.5 9.9 %collective-permute-start.10 = (f32[16,16,256]{2,1,0:T(8,128)S(1)}, f32[16,16,256]{2,1,0:T(8,128)S(1)}, u32[]{:S(2)}, u32[]{:S(2)}) collective-permute-start(f32[16,16,256]{2,1,0:T(8,128)S(1)} %get-tuple-element.167.near_ref.refs_7_), channel_id=1, source_target_pairs={{0,1},{1,0},{2,3},{3,2},{4,5},{5,4},{6,7},{7,6},{8,9},{9,8},{10,11... | collective-permute-start | bytes 786440 | tf_op jit(solution)/shard_map/ppermute | solution.py:518
  32.6 3.8 %collective-permute-start.9 = (f32[16,256]{1,0:T(8,128)S(1)}, f32[16,256]{1,0:T(8,128)S(1)}, u32[]{:S(2)}, u32[]{:S(2)}) collective-permute-start(f32[16,256]{1,0:T(8,128)S(1)} %get-tuple-element.166._.refs_0_), channel_id=1, source_target_pairs={{0,16},{8,24},{16,0},{24,8},{1,17},{9,25},{17,1},{25,9},{2,18},{10... | collective-permute-start | bytes 49160 | tf_op jit(solution)/shard_map/ppermute | solution.py:537
  34.2 3.7 %collective-permute-start.8 = (f32[16,256]{1,0:T(8,128)S(1)}, f32[16,256]{1,0:T(8,128)S(1)}, u32[]{:S(2)}, u32[]{:S(2)}) collective-permute-start(f32[16,256]{1,0:T(8,128)S(1)} %get-tuple-element.166._.refs_0_), channel_id=1, source_target_pairs={{0,8},{8,0},{16,24},{24,16},{1,9},{9,1},{17,25},{25,17},{2,10},{10... | collective-permute-start | bytes 49160 | tf_op jit(solution)/shard_map/ppermute | solution.py:537
  35.7 4.6 %collective-permute-start.7 = (f32[16,256]{1,0:T(8,128)S(1)}, f32[16,256]{1,0:T(8,128)S(1)}, u32[]{:S(2)}, u32[]{:S(2)}) collective-permute-start(f32[16,256]{1,0:T(8,128)S(1)} %get-tuple-element.166._.refs_0_), channel_id=1, source_target_pairs={{0,24},{8,16},{16,8},{24,0},{1,25},{9,17},{17,9},{25,1},{2,26},{10... | collective-permute-start | bytes 49160 | tf_op jit(solution)/shard_map/ppermute | solution.py:537
  40.5 7.7 %collective-permute-start.14 = (f32[16,16,256]{2,1,0:T(8,128)S(1)}, f32[16,16,256]{2,1,0:T(8,128)S(1)}, u32[]{:S(2)}, u32[]{:S(2)}) collective-permute-start(f32[16,16,256]{2,1,0:T(8,128)S(1)} %get-tuple-element.170.far_ref.refs_8_), channel_id=1, source_target_pairs={{1,2},{2,1},{3,4},{4,3},{5,6},{6,5},{9,10},{10,9},{11,12},{12,11},... | collective-permute-start | bytes 786440 | tf_op jit(solution)/shard_map/ppermute | solution.py:518
  43.1 6.7 %collective-permute-start.13 = (f32[64,256]{1,0:T(8,128)S(1)}, f32[64,256]{1,0:T(8,128)S(1)}, u32[]{:S(2)}, u32[]{:S(2)}) collective-permute-start(f32[64,256]{1,0:T(8,128)S(1)} %get-tuple-element.177.refs_0_), channel_id=1, source_target_pairs={{0,16},{8,24},{16,0},{24,8},{1,17},{9,25},{17,1},{25,9},{2,18},{10... | collective-permute-start | bytes 196616 | tf_op jit(solution)/shard_map/ppermute | solution.py:537
  43.7 6.1 %collective-permute-start.12 = (f32[64,256]{1,0:T(8,128)S(1)}, f32[64,256]{1,0:T(8,128)S(1)}, u32[]{:S(2)}, u32[]{:S(2)}) collective-permute-start(f32[64,256]{1,0:T(8,128)S(1)} %get-tuple-element.177.refs_0_), channel_id=1, source_target_pairs={{0,8},{8,0},{16,24},{24,16},{1,9},{9,1},{17,25},{25,17},{2,10},{10... | collective-permute-start | bytes 196616 | tf_op jit(solution)/shard_map/ppermute | solution.py:537
  44.2 5.6 %collective-permute-start.11 = (f32[64,256]{1,0:T(8,128)S(1)}, f32[64,256]{1,0:T(8,128)S(1)}, u32[]{:S(2)}, u32[]{:S(2)}) collective-permute-start(f32[64,256]{1,0:T(8,128)S(1)} %get-tuple-element.177.refs_0_), channel_id=1, source_target_pairs={{0,24},{8,16},{16,8},{24,0},{1,25},{9,17},{17,9},{25,1},{2,26},{10... | collective-permute-start | bytes 196616 | tf_op jit(solution)/shard_map/ppermute | solution.py:537
  50.4 9.7 %collective-permute-start.18 = (f32[16,16,256]{2,1,0:T(8,128)S(1)}, f32[16,16,256]{2,1,0:T(8,128)S(1)}, u32[]{:S(2)}, u32[]{:S(2)}) collective-permute-start(f32[16,16,256]{2,1,0:T(8,128)S(1)} %get-tuple-element.184.near_ref.refs_7_), channel_id=1, source_target_pairs={{0,1},{1,0},{2,3},{3,2},{4,5},{5,4},{6,7},{7,6},{8,9},{9,8},{10,11... | collective-permute-start | bytes 786440 | tf_op jit(solution)/shard_map/ppermute | solution.py:518
  50.5 3.8 %collective-permute-start.17 = (f32[16,256]{1,0:T(8,128)S(1)}, f32[16,256]{1,0:T(8,128)S(1)}, u32[]{:S(2)}, u32[]{:S(2)}) collective-permute-start(f32[16,256]{1,0:T(8,128)S(1)} %get-tuple-element.183._.refs_0_), channel_id=1, source_target_pairs={{0,16},{8,24},{16,0},{24,8},{1,17},{9,25},{17,1},{25,9},{2,18},{10... | collective-permute-start | bytes 49160 | tf_op jit(solution)/shard_map/ppermute | solution.py:537
  51.6 3.7 %collective-permute-start.16 = (f32[16,256]{1,0:T(8,128)S(1)}, f32[16,256]{1,0:T(8,128)S(1)}, u32[]{:S(2)}, u32[]{:S(2)}) collective-permute-start(f32[16,256]{1,0:T(8,128)S(1)} %get-tuple-element.183._.refs_0_), channel_id=1, source_target_pairs={{0,8},{8,0},{16,24},{24,16},{1,9},{9,1},{17,25},{25,17},{2,10},{10... | collective-permute-start | bytes 49160 | tf_op jit(solution)/shard_map/ppermute | solution.py:537
  53.1 4.6 %collective-permute-start.15 = (f32[16,256]{1,0:T(8,128)S(1)}, f32[16,256]{1,0:T(8,128)S(1)}, u32[]{:S(2)}, u32[]{:S(2)}) collective-permute-start(f32[16,256]{1,0:T(8,128)S(1)} %get-tuple-element.183._.refs_0_), channel_id=1, source_target_pairs={{0,24},{8,16},{16,8},{24,0},{1,25},{9,17},{17,9},{25,1},{2,26},{10... | collective-permute-start | bytes 49160 | tf_op jit(solution)/shard_map/ppermute | solution.py:537
  58.0 7.7 %collective-permute-start.22 = (f32[16,16,256]{2,1,0:T(8,128)S(1)}, f32[16,16,256]{2,1,0:T(8,128)S(1)}, u32[]{:S(2)}, u32[]{:S(2)}) collective-permute-start(f32[16,16,256]{2,1,0:T(8,128)S(1)} %get-tuple-element.187.far_ref.refs_8_), channel_id=1, source_target_pairs={{1,2},{2,1},{3,4},{4,3},{5,6},{6,5},{9,10},{10,9},{11,12},{12,11},... | collective-permute-start | bytes 786440 | tf_op jit(solution)/shard_map/ppermute | solution.py:518
  60.8 6.5 %collective-permute-start.21 = (f32[64,256]{1,0:T(8,128)S(1)}, f32[64,256]{1,0:T(8,128)S(1)}, u32[]{:S(2)}, u32[]{:S(2)}) collective-permute-start(f32[64,256]{1,0:T(8,128)S(1)} %get-tuple-element.194.refs_0_), channel_id=1, source_target_pairs={{0,16},{8,24},{16,0},{24,8},{1,17},{9,25},{17,1},{25,9},{2,18},{10... | collective-permute-start | bytes 196616 | tf_op jit(solution)/shard_map/ppermute | solution.py:537
  61.3 5.9 %collective-permute-start.20 = (f32[64,256]{1,0:T(8,128)S(1)}, f32[64,256]{1,0:T(8,128)S(1)}, u32[]{:S(2)}, u32[]{:S(2)}) collective-permute-start(f32[64,256]{1,0:T(8,128)S(1)} %get-tuple-element.194.refs_0_), channel_id=1, source_target_pairs={{0,8},{8,0},{16,24},{24,16},{1,9},{9,1},{17,25},{25,17},{2,10},{10... | collective-permute-start | bytes 196616 | tf_op jit(solution)/shard_map/ppermute | solution.py:537
  62.3 5.6 %collective-permute-start.19 = (f32[64,256]{1,0:T(8,128)S(1)}, f32[64,256]{1,0:T(8,128)S(1)}, u32[]{:S(2)}, u32[]{:S(2)}) collective-permute-start(f32[64,256]{1,0:T(8,128)S(1)} %get-tuple-element.194.refs_0_), channel_id=1, source_target_pairs={{0,24},{8,16},{16,8},{24,0},{1,25},{9,17},{17,9},{25,1},{2,26},{10... | collective-permute-start | bytes 196616 | tf_op jit(solution)/shard_map/ppermute | solution.py:537
  68.4 9.2 %collective-permute-start.26 = (f32[16,16,256]{2,1,0:T(8,128)S(1)}, f32[16,16,256]{2,1,0:T(8,128)S(1)}, u32[]{:S(2)}, u32[]{:S(2)}) collective-permute-start(f32[16,16,256]{2,1,0:T(8,128)S(1)} %get-tuple-element.201.near_ref.refs_7_), channel_id=1, source_target_pairs={{0,1},{1,0},{2,3},{3,2},{4,5},{5,4},{6,7},{7,6},{8,9},{9,8},{10,11... | collective-permute-start | bytes 786440 | tf_op jit(solution)/shard_map/ppermute | solution.py:518
  68.5 3.8 %collective-permute-start.25 = (f32[16,256]{1,0:T(8,128)S(1)}, f32[16,256]{1,0:T(8,128)S(1)}, u32[]{:S(2)}, u32[]{:S(2)}) collective-permute-start(f32[16,256]{1,0:T(8,128)S(1)} %get-tuple-element.200._.refs_0_), channel_id=1, source_target_pairs={{0,16},{8,24},{16,0},{24,8},{1,17},{9,25},{17,1},{25,9},{2,18},{10... | collective-permute-start | bytes 49160 | tf_op jit(solution)/shard_map/ppermute | solution.py:537
  69.2 3.7 %collective-permute-start.24 = (f32[16,256]{1,0:T(8,128)S(1)}, f32[16,256]{1,0:T(8,128)S(1)}, u32[]{:S(2)}, u32[]{:S(2)}) collective-permute-start(f32[16,256]{1,0:T(8,128)S(1)} %get-tuple-element.200._.refs_0_), channel_id=1, source_target_pairs={{0,8},{8,0},{16,24},{24,16},{1,9},{9,1},{17,25},{25,17},{2,10},{10... | collective-permute-start | bytes 49160 | tf_op jit(solution)/shard_map/ppermute | solution.py:537
  70.8 4.6 %collective-permute-start.23 = (f32[16,256]{1,0:T(8,128)S(1)}, f32[16,256]{1,0:T(8,128)S(1)}, u32[]{:S(2)}, u32[]{:S(2)}) collective-permute-start(f32[16,256]{1,0:T(8,128)S(1)} %get-tuple-element.200._.refs_0_), channel_id=1, source_target_pairs={{0,24},{8,16},{16,8},{24,0},{1,25},{9,17},{17,9},{25,1},{2,26},{10... | collective-permute-start | bytes 49160 | tf_op jit(solution)/shard_map/ppermute | solution.py:537
  75.6 7.7 %collective-permute-start.30 = (f32[16,16,256]{2,1,0:T(8,128)S(1)}, f32[16,16,256]{2,1,0:T(8,128)S(1)}, u32[]{:S(2)}, u32[]{:S(2)}) collective-permute-start(f32[16,16,256]{2,1,0:T(8,128)S(1)} %get-tuple-element.204.far_ref.refs_8_), channel_id=1, source_target_pairs={{1,2},{2,1},{3,4},{4,3},{5,6},{6,5},{9,10},{10,9},{11,12},{12,11},... | collective-permute-start | bytes 786440 | tf_op jit(solution)/shard_map/ppermute | solution.py:518
  78.3 6.6 %collective-permute-start.29 = (f32[144,256]{1,0:T(8,128)S(1)}, f32[144,256]{1,0:T(8,128)S(1)}, u32[]{:S(2)}, u32[]{:S(2)}) collective-permute-start(f32[144,256]{1,0:T(8,128)S(1)} %get-tuple-element.211.refs_0_), channel_id=1, source_target_pairs={{0,16},{8,24},{16,0},{24,8},{1,17},{9,25},{17,1},{25,9},{2,18},{10... | collective-permute-start | bytes 442376 | tf_op jit(solution)/shard_map/ppermute | solution.py:537
  78.9 6.7 %collective-permute-start.28 = (f32[144,256]{1,0:T(8,128)S(1)}, f32[144,256]{1,0:T(8,128)S(1)}, u32[]{:S(2)}, u32[]{:S(2)}) collective-permute-start(f32[144,256]{1,0:T(8,128)S(1)} %get-tuple-element.211.refs_0_), channel_id=1, source_target_pairs={{0,8},{8,0},{16,24},{24,16},{1,9},{9,1},{17,25},{25,17},{2,10},{10... | collective-permute-start | bytes 442376 | tf_op jit(solution)/shard_map/ppermute | solution.py:537
  80.3 8.7 %collective-permute-start.27 = (f32[144,256]{1,0:T(8,128)S(1)}, f32[144,256]{1,0:T(8,128)S(1)}, u32[]{:S(2)}, u32[]{:S(2)}) collective-permute-start(f32[144,256]{1,0:T(8,128)S(1)} %get-tuple-element.211.refs_0_), channel_id=1, source_target_pairs={{0,24},{8,16},{16,8},{24,0},{1,25},{9,17},{17,9},{25,1},{2,26},{10... | collective-permute-start | bytes 442376 | tf_op jit(solution)/shard_map/ppermute | solution.py:537
  89.5 8.8 %collective-permute-start.34 = (f32[16,16,256]{2,1,0:T(8,128)S(1)}, f32[16,16,256]{2,1,0:T(8,128)S(1)}, u32[]{:S(2)}, u32[]{:S(2)}) collective-permute-start(f32[16,16,256]{2,1,0:T(8,128)S(1)} %get-tuple-element.218.near_ref.refs_7_), channel_id=1, source_target_pairs={{0,1},{1,0},{2,3},{3,2},{4,5},{5,4},{6,7},{7,6},{8,9},{9,8},{10,11... | collective-permute-start | bytes 786440 | tf_op jit(solution)/shard_map/ppermute | solution.py:518
  89.6 3.8 %collective-permute-start.33 = (f32[16,256]{1,0:T(8,128)S(1)}, f32[16,256]{1,0:T(8,128)S(1)}, u32[]{:S(2)}, u32[]{:S(2)}) collective-permute-start(f32[16,256]{1,0:T(8,128)S(1)} %get-tuple-element.217._.refs_0_), channel_id=1, source_target_pairs={{0,16},{8,24},{16,0},{24,8},{1,17},{9,25},{17,1},{25,9},{2,18},{10... | collective-permute-start | bytes 49160 | tf_op jit(solution)/shard_map/ppermute | solution.py:537
  90.2 3.7 %collective-permute-start.32 = (f32[16,256]{1,0:T(8,128)S(1)}, f32[16,256]{1,0:T(8,128)S(1)}, u32[]{:S(2)}, u32[]{:S(2)}) collective-permute-start(f32[16,256]{1,0:T(8,128)S(1)} %get-tuple-element.217._.refs_0_), channel_id=1, source_target_pairs={{0,8},{8,0},{16,24},{24,16},{1,9},{9,1},{17,25},{25,17},{2,10},{10... | collective-permute-start | bytes 49160 | tf_op jit(solution)/shard_map/ppermute | solution.py:537
  91.2 4.6 %collective-permute-start.31 = (f32[16,256]{1,0:T(8,128)S(1)}, f32[16,256]{1,0:T(8,128)S(1)}, u32[]{:S(2)}, u32[]{:S(2)}) collective-permute-start(f32[16,256]{1,0:T(8,128)S(1)} %get-tuple-element.217._.refs_0_), channel_id=1, source_target_pairs={{0,24},{8,16},{16,8},{24,0},{1,25},{9,17},{17,9},{25,1},{2,26},{10... | collective-permute-start | bytes 49160 | tf_op jit(solution)/shard_map/ppermute | solution.py:537
  96.0 7.7 %collective-permute-start.38 = (f32[16,16,256]{2,1,0:T(8,128)S(1)}, f32[16,16,256]{2,1,0:T(8,128)S(1)}, u32[]{:S(2)}, u32[]{:S(2)}) collective-permute-start(f32[16,16,256]{2,1,0:T(8,128)S(1)} %get-tuple-element.221.far_ref.refs_8_), channel_id=1, source_target_pairs={{1,2},{2,1},{3,4},{4,3},{5,6},{6,5},{9,10},{10,9},{11,12},{12,11},... | collective-permute-start | bytes 786440 | tf_op jit(solution)/shard_map/ppermute | solution.py:518
  99.0 6.3 %collective-permute-start.37 = (f32[64,256]{1,0:T(8,128)S(1)}, f32[64,256]{1,0:T(8,128)S(1)}, u32[]{:S(2)}, u32[]{:S(2)}) collective-permute-start(f32[64,256]{1,0:T(8,128)S(1)} %get-tuple-element.228.refs_0_), channel_id=1, source_target_pairs={{0,16},{8,24},{16,0},{24,8},{1,17},{9,25},{17,1},{25,9},{2,18},{10... | collective-permute-start | bytes 196616 | tf_op jit(solution)/shard_map/ppermute | solution.py:537
  99.8 5.5 %collective-permute-start.36 = (f32[64,256]{1,0:T(8,128)S(1)}, f32[64,256]{1,0:T(8,128)S(1)}, u32[]{:S(2)}, u32[]{:S(2)}) collective-permute-start(f32[64,256]{1,0:T(8,128)S(1)} %get-tuple-element.228.refs_0_), channel_id=1, source_target_pairs={{0,8},{8,0},{16,24},{24,16},{1,9},{9,1},{17,25},{25,17},{2,10},{10... | collective-permute-start | bytes 196616 | tf_op jit(solution)/shard_map/ppermute | solution.py:537
  101.3 5.2 %collective-permute-start.35 = (f32[64,256]{1,0:T(8,128)S(1)}, f32[64,256]{1,0:T(8,128)S(1)}, u32[]{:S(2)}, u32[]{:S(2)}) collective-permute-start(f32[64,256]{1,0:T(8,128)S(1)} %get-tuple-element.228.refs_0_), channel_id=1, source_target_pairs={{0,24},{8,16},{16,8},{24,0},{1,25},{9,17},{17,9},{25,1},{2,26},{10... | collective-permute-start | bytes 196616 | tf_op jit(solution)/shard_map/ppermute | solution.py:537
  107.0 8.8 %collective-permute-start.43 = (f32[16,16,256]{2,1,0:T(8,128)S(1)}, f32[16,16,256]{2,1,0:T(8,128)S(1)}, u32[]{:S(2)}, u32[]{:S(2)}) collective-permute-start(f32[16,16,256]{2,1,0:T(8,128)S(1)} %get-tuple-element.235.near_ref), channel_id=1, source_target_pairs={{0,1},{1,0},{2,3},{3,2},{4,5},{5,4},{6,7},{7,6},{8,9},{9,8},{10,11... | collective-permute-start | bytes 786440 | tf_op jit(solution)/shard_map/ppermute | solution.py:518
  107.1 3.8 %collective-permute-start.41 = (f32[16,256]{1,0:T(8,128)S(1)}, f32[16,256]{1,0:T(8,128)S(1)}, u32[]{:S(2)}, u32[]{:S(2)}) collective-permute-start(f32[16,256]{1,0:T(8,128)S(1)} %get-tuple-element.234._.refs_0_), channel_id=1, source_target_pairs={{0,16},{8,24},{16,0},{24,8},{1,17},{9,25},{17,1},{25,9},{2,18},{10... | collective-permute-start | bytes 49160 | tf_op jit(solution)/shard_map/ppermute | solution.py:537
  109.0 4.6 %collective-permute-start.39 = (f32[16,256]{1,0:T(8,128)S(1)}, f32[16,256]{1,0:T(8,128)S(1)}, u32[]{:S(2)}, u32[]{:S(2)}) collective-permute-start(f32[16,256]{1,0:T(8,128)S(1)} %get-tuple-element.234._.refs_0_), channel_id=1, source_target_pairs={{0,24},{8,16},{16,8},{24,0},{1,25},{9,17},{17,9},{25,1},{2,26},{10... | collective-permute-start | bytes 49160 | tf_op jit(solution)/shard_map/ppermute | solution.py:537
  113.9 6.3 %collective-permute-start.42 = (f32[16,8,256]{2,1,0:T(8,128)S(1)}, f32[16,8,256]{2,1,0:T(8,128)S(1)}, u32[]{:S(2)}, u32[]{:S(2)}) collective-permute-start(f32[16,8,256]{2,1,0:T(8,128)S(1)} %get-tuple-element.239), channel_id=1, source_target_pairs={{1,2},{2,1},{3,4},{4,3},{5,6},{6,5},{9,10},{10,9},{11,12},{12,11},... | collective-permute-start | bytes 393224 | tf_op jit(solution)/shard_map/ppermute | solution.py:518
  116.5 6.1 %collective-permute-start.49 = (f32[64,256]{1,0:T(8,128)S(1)}, f32[64,256]{1,0:T(8,128)S(1)}, u32[]{:S(2)}, u32[]{:S(2)}) collective-permute-start(f32[64,256]{1,0:T(8,128)S(1)} %get-tuple-element.249.refs_0_), channel_id=1, source_target_pairs={{0,16},{8,24},{16,0},{24,8},{1,17},{9,25},{17,1},{25,9},{2,18},{10... | collective-permute-start | bytes 196616 | tf_op jit(solution)/shard_map/ppermute | solution.py:537
  117.2 7.5 %collective-permute-start.48 = (f32[64,256]{1,0:T(8,128)S(1)}, f32[64,256]{1,0:T(8,128)S(1)}, u32[]{:S(2)}, u32[]{:S(2)}) collective-permute-start(f32[64,256]{1,0:T(8,128)S(1)} %get-tuple-element.249.refs_0_), channel_id=1, source_target_pairs={{0,8},{8,0},{16,24},{24,16},{1,9},{9,1},{17,25},{25,17},{2,10},{10... | collective-permute-start | bytes 196616 | tf_op jit(solution)/shard_map/ppermute | solution.py:537
  118.7 6.0 %collective-permute-start.47 = (f32[64,256]{1,0:T(8,128)S(1)}, f32[64,256]{1,0:T(8,128)S(1)}, u32[]{:S(2)}, u32[]{:S(2)}) collective-permute-start(f32[64,256]{1,0:T(8,128)S(1)} %get-tuple-element.249.refs_0_), channel_id=1, source_target_pairs={{0,24},{8,16},{16,8},{24,0},{1,25},{9,17},{17,9},{25,1},{2,26},{10... | collective-permute-start | bytes 196616 | tf_op jit(solution)/shard_map/ppermute | solution.py:537
  120.3 5.3 %collective-permute-start.46 = (f32[16,256]{1,0:T(8,128)S(1)}, f32[16,256]{1,0:T(8,128)S(1)}, u32[]{:S(2)}, u32[]{:S(2)}) collective-permute-start(f32[16,256]{1,0:T(8,128)S(1)} %get-tuple-element.247._.refs_0_), channel_id=1, source_target_pairs={{0,16},{8,24},{16,0},{24,8},{1,17},{9,25},{17,1},{25,9},{2,18},{10... | collective-permute-start | bytes 49160 | tf_op jit(solution)/shard_map/ppermute | solution.py:537
  121.1 4.5 %collective-permute-start.45 = (f32[16,256]{1,0:T(8,128)S(1)}, f32[16,256]{1,0:T(8,128)S(1)}, u32[]{:S(2)}, u32[]{:S(2)}) collective-permute-start(f32[16,256]{1,0:T(8,128)S(1)} %get-tuple-element.247._.refs_0_), channel_id=1, source_target_pairs={{0,8},{8,0},{16,24},{24,16},{1,9},{9,1},{17,25},{25,17},{2,10},{10... | collective-permute-start | bytes 49160 | tf_op jit(solution)/shard_map/ppermute | solution.py:537
  122.6 4.6 %collective-permute-start.44 = (f32[16,256]{1,0:T(8,128)S(1)}, f32[16,256]{1,0:T(8,128)S(1)}, u32[]{:S(2)}, u32[]{:S(2)}) collective-permute-start(f32[16,256]{1,0:T(8,128)S(1)} %get-tuple-element.247._.refs_0_), channel_id=1, source_target_pairs={{0,24},{8,16},{16,8},{24,0},{1,25},{9,17},{17,9},{25,1},{2,26},{10... | collective-permute-start | bytes 49160 | tf_op jit(solution)/shard_map/ppermute | solution.py:537
  (9 other events, 63.2 us)

commit v4 on v3

--- a/solution.py
+++ b/solution.py
@@ -48,13 +48,13 @@
 SM = pl.BlockSpec(memory_space=pltpu.SMEM)
 
 
-def call(kernel, ins, outs, scalars=0, aliases=None):
+def call(kernel, ins, outs, scalars=0, scratch=()):
     return pl.pallas_call(
         kernel,
         out_shape=[jax.ShapeDtypeStruct(*shape) for shape in outs],
         in_specs=[SM] * scalars + [VM] * (len(ins) - scalars),
         out_specs=[VM] * len(outs),
-        input_output_aliases=aliases or {},
+        scratch_shapes=scratch,
         compiler_params=PARAMS,
     )(*ins)
 
@@ -128,21 +128,17 @@
 
 
 def first_rows_kernel(
-    odd_ref, near_ref, far_ref, halo_ref, far_halo_ref, mats_ref, far_band_ref, far_mats_ref, start_ref, dirty_ref,
-    sum1_ref, band_u_ref, band_t_ref, part_ref, dual_u_ref, dual_t_ref, dual1_ref, data_ref, sums_ref,
+    near_ref, far_ref, halo_ref, far_halo_ref, mats_ref, far_band_ref, far_mats_ref, sum1_ref,
+    band_u_ref, band_t_ref, part_ref, sums_ref,
 ):
     chans, half, width = near_ref.shape
     height, touched, free = 2 * half, band_t_ref.shape[1], band_u_ref.shape[1]
-    reach = touched + free
-    send, edge = far_mats_ref.shape[2] // 3, (reach - height) // 2
-    odd = odd_ref[0] == 1
+    send = far_mats_ref.shape[2] // 3
 
     def body(c, totals):
-        near, far = halo_ref[c], far_halo_ref[c]
-        before, after = jnp.where(odd, near, far), jnp.where(odd, far, near)
-        rows = jnp.concatenate([near_ref[c], far_ref[c], near[:send]], axis=0)
+        rows = jnp.concatenate([near_ref[c], far_ref[c], halo_ref[c, :send]], axis=0)
         product = jnp.dot(mats_ref[c], stacked(rows), preferred_element_type=F32)
-        far_rows = stacked(far[:send])
+        far_rows = stacked(far_halo_ref[c])
         band_t = product[free : free + touched] + jnp.dot(
             far_band_ref[...], far_rows, preferred_element_type=F32
         )
@@ -152,21 +148,40 @@
         at = free + touched + half
         part_ref[c, :half] = product[free + touched : at]
         part_ref[c, half:] = product[at:] + jnp.dot(far_mats_ref[c], far_rows, preferred_element_type=F32)
-        at = send + edge
-        dual = jnp.concatenate([before[send:at], start_ref[c, 0], after[send:at]], axis=0)
+        return totals[0] + band * band, totals[1] + band_t * band_t
+
+    zeros = jnp.zeros((free, width), F32), jnp.zeros((touched, width), F32)
+    totals = lax.fori_loop(0, chans, body, zeros, unroll=True)
+    sums_ref[:free] = totals[0]
+    sums_ref[free : free + height] = sum1_ref[...]
+    sums_ref[free + height :] = totals[1]
+
+
+def first_data_kernel(
+    odd_ref, halo_ref, far_halo_ref, start_ref, dirty_ref, adj_ref, back_head_ref, back_rest_ref,
+    dual_u_ref, dual_t_ref, dual1_ref, data_ref,
+):
+    chans, height, _ = data_ref.shape
+    half, touched, free = height // 2, dual_t_ref.shape[1], dual_u_ref.shape[1]
+    edge = (touched + free - height) // 2
+    send = halo_ref.shape[1] - 2 * edge
+    odd = odd_ref[0] == 1
+
+    def body(c, carry):
+        near, far = halo_ref[c, send:], far_halo_ref[c]
+        before, after = jnp.where(odd, near, far), jnp.where(odd, far, near)
+        dual = jnp.concatenate([before[:edge], start_ref[c, 0], after[:edge]], axis=0)
         dual_u_ref[c] = jnp.where(odd, dual[:free], dual[touched:])
         dual_t_ref[c] = jnp.where(odd, dual[free:], dual[:touched])
         dual = start_ref[c, 1]
         dual1_ref[c, :half] = jnp.where(odd, dual[:half], dual[half:])
         dual1_ref[c, half:] = jnp.where(odd, dual[half:], dual[:half])
-        data_ref[c] = jnp.concatenate([before[at:], dirty_ref[c], after[at:]], axis=0)
-        return totals[0] + band * band, totals[1] + band_t * band_t
-
-    zeros = jnp.zeros((free, width), F32), jnp.zeros((touched, width), F32)
-    totals = lax.fori_loop(0, chans, body, zeros, unroll=True)
-    sums_ref[:free] = totals[0]
-    sums_ref[free : free + height] = sum1_ref[...]
-    sums_ref[free + height :] = totals[1]
+        dirty = jnp.concatenate([before[edge:], dirty_ref[c], after[edge:]], axis=0)
+        part = jnp.dot(adj_ref[c], stacked(dirty), preferred_element_type=F32)
+        data_ref[c] = times_columns(part, back_head_ref[c], back_rest_ref[c])
+        return carry
+
+    lax.fori_loop(0, chans, body, 0, unroll=True)
 
 
 def squares_kernel(*refs):
@@ -178,21 +193,28 @@
         at += rows
 
 
-def pack_kernel(est_ref, dual_ref, dirty_ref, far_ref, near_ref, far_rows, near_rows, in_sems, out_sems):
+def pack_kernel(
+    est_ref, dual_ref, dirty_ref, far_ref, later_ref, near_ref, far_rows, later_rows, near_rows, in_sems, out_sems
+):
     height = est_ref.shape[1]
-    total = near_ref.shape[1]
-    send, edge = total // 2, total // 4
+    send = far_ref.shape[1]
+    edge = send // 2
     odd = lax.rem(lax.axis_index("facet"), 2)
+    band_ref = dual_ref.at[:, 0]
     loads, stores = [], []
-    for out_ref, held, low in ((far_ref, far_rows, odd), (near_ref, near_rows, 1 - odd)):
-        at = 0
-        for ref, rows in ((est_ref, send), (dual_ref.at[:, 0], edge), (dirty_ref, edge)):
-            start = pl.multiple_of(low * (height - rows), 8)
-            k = len(loads)
-            piece = (slice(None), slice(at, at + rows))
-            loads.append(pltpu.make_async_copy(ref.at[:, pl.ds(start, rows)], held.at[piece], in_sems.at[k]))
-            stores.append(pltpu.make_async_copy(held.at[piece], out_ref.at[piece], out_sems.at[k]))
-            at += rows
+    for out_ref, held, low, at, ref, rows in (
+        (far_ref, far_rows, odd, 0, est_ref, send),
+        (later_ref, later_rows, odd, 0, band_ref, edge),
+        (later_ref, later_rows, odd, edge, dirty_ref, edge),
+        (near_ref, near_rows, 1 - odd, 0, est_ref, send),
+        (near_ref, near_rows, 1 - odd, send, band_ref, edge),
+        (near_ref, near_rows, 1 - odd, send + edge, dirty_ref, edge),
+    ):
+        start = pl.multiple_of(low * (height - rows), 8)
+        k = len(loads)
+        piece = (slice(None), slice(at, at + rows))
+        loads.append(pltpu.make_async_copy(ref.at[:, pl.ds(start, rows)], held.at[piece], in_sems.at[k]))
+        stores.append(pltpu.make_async_copy(held.at[piece], out_ref.at[piece], out_sems.at[k]))
     for load in loads:
         load.start()
     for load, store in zip(loads, stores):
@@ -235,9 +257,9 @@
 
 
 def matrices_kernel(
-    flags_ref, lines_ref, mats_ref, far_band_ref, far_mats_ref, adj_ref, wav_free_ref, wav_touched_ref,
+    flags_ref, cols_ref, rows_ref, wav_ref, mats_ref, far_band_ref, far_mats_ref, adj_ref, wav_free_ref, wav_touched_ref,
     around_head_ref, around_rest_ref, back_head_ref, back_rest_ref,
-    wav_head_ref, wav_rest_ref, wav_head_t_ref, wav_rest_t_ref,
+    wav_head_ref, wav_rest_ref, wav_head_t_ref, wav_rest_t_ref, lines_ref,
 ):
     chans, width = around_head_ref.shape[:2]
     send = far_mats_ref.shape[2] // 3
@@ -253,6 +275,30 @@
         low = jnp.where(facet > 0, 0, edge)
         high = jnp.where(facet < facets - 1, reach, reach - edge)
         return jnp.where((at >= low) & (at < high), 1.0, 0.0)
+
+    def placed(taps, first, back):
+        count = taps.shape[1]
+        lane = lax.broadcasted_iota(jnp.int32, (count, LANES), 1)
+        tap = lax.broadcasted_iota(jnp.int32, (count, LANES), 0)
+        at = jnp.where(lane >= first, lane - first, lane - first + LANES) if first >= 0 else jnp.where(
+            lane - first < LANES, lane - first, lane - first - LANES
+        )
+        pick = jnp.where((count - 1 - at if back else at) == tap, 1.0, 0.0)
+        return jnp.dot(taps, pick, precision=lax.Precision.HIGHEST, preferred_element_type=F32)
+
+    def put(at, cols, rows, half_c, half_r):
+        lines = jnp.concatenate(
+            [
+                placed(cols, -half_c, True), placed(cols, -half_c, False),
+                placed(rows, edge - half_r, False), placed(rows, edge - half_r, True),
+            ],
+            axis=1,
+        )
+        for c in range(lines.shape[0]):
+            lines_ref[at + c] = lines[c : c + 1]
+
+    put(0, cols_ref[...], rows_ref[...], PSF_HALF, PSF_HALF)
+    put(chans, wav_ref[1:2], wav_ref[0:1], WAV_HALF, WAV_HALF)
 
     def line(c, k):
         return lines_ref[c, :, k * LANES : (k + 1) * LANES]
@@ -340,19 +386,12 @@
     sum_ref[...] = total
 
 
-def first_gradient_kernel(
-    part_ref, head_ref, rest_ref, dirty_ref, back_head_ref, back_rest_ref, adj_ref, data_ref, grad_ref
-):
-    chans = part_ref.shape[0]
-
+def first_gradient_kernel(part_ref, head_ref, rest_ref, grad_ref):
     def body(c, carry):
-        across = times_columns(dirty_ref[c], back_head_ref[c], back_rest_ref[c])
-        data = jnp.dot(adj_ref[c], stacked(across), preferred_element_type=F32)
-        data_ref[c] = data
-        grad_ref[c] = times_columns(part_ref[c], head_ref[c], rest_ref[c]) - data
+        grad_ref[c] = times_columns(part_ref[c], head_ref[c], rest_ref[c])
         return carry
 
-    lax.fori_loop(0, chans, body, 0, unroll=4)
+    lax.fori_loop(0, part_ref.shape[0], body, 0, unroll=True)
 
 
 def gradient_kernel(part_ref, halo_ref, far_mats_ref, head_ref, rest_ref, data_ref, _, grad_ref):
@@ -432,8 +471,8 @@
 
 
 def first_update_kernel(
-    dual_u_ref, dual_t_ref, dual1_ref, near_ref, far_ref, grad_ref, rows_ref, rows_t_ref, head_ref, rest_ref,
-    new_near_ref, new_far_ref,
+    dual_u_ref, dual_t_ref, dual1_ref, near_ref, far_ref, grad_ref, data_ref, rows_ref, rows_t_ref, head_ref,
+    rest_ref, new_near_ref, new_far_ref,
 ):
     chans, half, width = near_ref.shape
     height = 2 * half
@@ -446,52 +485,49 @@
             down = jnp.dot(rows_ref[...], stacked(dual_u_ref[c]), preferred_element_type=F32)
             late = jnp.dot(rows_t_ref[...], stacked(dual_t_ref[c]), preferred_element_type=F32)
             at = (c - c0) * height
-            step = grad_ref[c] + (down + across[at : at + height])
+            step = (grad_ref[c] - data_ref[c]) + (down + across[at : at + height])
             new_near_ref[c] = jnp.maximum(near_ref[c] - STEP_PRIMAL * step[:half], 0.0)
             new_far_ref[c] = jnp.maximum(far_ref[c] - STEP_PRIMAL * (step[half:] + late), 0.0)
 
 
 def final_early_kernel(n_sums, odd_ref, *refs):
     sums_refs, refs = refs[:n_sums], refs[n_sums:]
-    radius_ref, moved_u_ref, moved1_ref, dual_u_ref, out_ref, plane, sem = refs
+    radius_ref, moved_u_ref, moved1_ref, out_ref, across, down, sems = refs
     chans, height, _ = moved1_ref.shape
-    half, free = height // 2, moved_u_ref.shape[1]
+    half, free, kept = height // 2, moved_u_ref.shape[1], down.shape[1]
     odd = odd_ref[0] == 1
     scale = scaled(sums_refs, free + height, radius_ref[: free + height])
+    start = pl.multiple_of((1 - lax.rem(lax.axis_index("facet"), 2)) * (height - kept), 8)
+    low, high = out_ref.at[:, 1], out_ref.at[:, 0, pl.ds(start, kept)]
     for c in range(chans):
-        dual_u_ref[c] = moved_u_ref[c] * scale[:free]
         dual = moved1_ref[c] * scale[free:]
         near, far = dual[:half], dual[half:]
-        plane[c, :half] = jnp.where(odd, near, far)
-        plane[c, half:] = jnp.where(odd, far, near)
-    copy = pltpu.make_async_copy(plane, out_ref.at[:, 1], sem)
+        across[c, :half] = jnp.where(odd, near, far)
+        across[c, half:] = jnp.where(odd, far, near)
+    copies = [pltpu.make_async_copy(across, low, sems.at[0]), pltpu.make_async_copy(down, high, sems.at[1])]
+    copies[0].start()
+    for c in range(chans):
+        dual = moved_u_ref[c] * scale[:free]
+        down[c] = jnp.where(odd, dual[free - kept :], dual[:kept])
+    copies[1].start()
+    for copy in copies:
+        copy.wait()
+
+
+def final_late_kernel(n_sums, odd_ref, *refs):
+    sums_refs, refs = refs[:n_sums], refs[n_sums:]
+    radius_ref, moved_ref, _, out_ref, down, sem = refs
+    chans, height, width = out_ref.shape[0], *out_ref.shape[2:]
+    touched, rest = moved_ref.shape[1], down.shape[1]
+    odd = odd_ref[0] == 1
+    scale = scaled(sums_refs, touched, radius_ref[radius_ref.shape[0] - touched :])
+    for c in range(chans):
+        dual = moved_ref[c] * scale
+        down[c] = jnp.where(odd, dual[:rest], dual[touched - rest :])
+    start = pl.multiple_of(lax.rem(lax.axis_index("facet"), 2) * (height - rest), 8)
+    copy = pltpu.make_async_copy(down, out_ref.at[:, 0, pl.ds(start, rest)], sem)
     copy.start()
     copy.wait()
-
-
-def final_late_kernel(n_sums, odd_ref, *refs):
-    sums_refs, refs = refs[:n_sums], refs[n_sums:]
-    radius_ref, moved_ref, dual_u_ref, _, out_ref, plane, sems = refs
-    chans, height, _ = plane.shape
-    touched, free = moved_ref.shape[1], dual_u_ref.shape[1]
-    edge = (touched + free - height) // 2
-    odd = odd_ref[0] == 1
-    scale = scaled(sums_refs, touched, radius_ref[radius_ref.shape[0] - touched :])
-    group = chans // sems.shape[0]
-    copies = []
-    for c in range(chans):
-        dual = moved_ref[c] * scale
-        above = jnp.concatenate([dual_u_ref[c, edge:], dual[: touched - edge]], axis=0)
-        below = jnp.concatenate([dual[edge:], dual_u_ref[c, : free - edge]], axis=0)
-        plane[c] = jnp.where(odd, above, below)
-        if (c + 1) % group == 0:
-            part = slice(c + 1 - group, c + 1)
-            copies.append(
-                pltpu.make_async_copy(plane.at[part], out_ref.at[part, 0], sems.at[len(copies)])
-            )
-            copies[-1].start()
-    for copy in copies:
-        copy.wait()
 
 
 def publish_kernel(near_ref, far_ref, _, out_ref, sems):
@@ -563,73 +599,52 @@
     square = ((width, width), BF16)
     squares = ((chans, width, width), BF16)
 
-    first_sides = rows(2 * send)
     inputs = [pltpu.with_memory_space_constraint(x, pltpu.HBM) for x in (image_start, dual_start, dirty_image)]
 
     in_hbm = pl.BlockSpec(memory_space=pltpu.HBM)
-    far, near = pl.pallas_call(
+    packs = (rows(send), rows(2 * edge), rows(send + 2 * edge))
+    far, later, near = pl.pallas_call(
         pack_kernel,
-        out_shape=[jax.ShapeDtypeStruct(*first_sides)] * 2,
+        out_shape=[jax.ShapeDtypeStruct(*pack) for pack in packs],
         in_specs=[in_hbm] * 3,
-        out_specs=[in_hbm] * 2,
-        scratch_shapes=[pltpu.VMEM(*first_sides)] * 2 + [pltpu.SemaphoreType.DMA((6,))] * 2,
+        out_specs=[in_hbm] * 3,
+        scratch_shapes=[pltpu.VMEM(*pack) for pack in packs] + [pltpu.SemaphoreType.DMA((6,))] * 2,
         compiler_params=PARAMS,
         name="pack",
     )(*inputs)
     far = trade(far, True)
-    near = trade(near, False)
-
-    def lines(cols, taps, half_c, half_r):
-        def circle(taps, half):
-            gap = jnp.zeros((taps.shape[0], LANES - 2 * half - 1), F32)
-            return jnp.concatenate([taps[:, half:], gap, taps[:, :half]], axis=1)
-
-        def ramp(taps, half):
-            lead = jnp.zeros((taps.shape[0], edge - half), F32)
-            gap = jnp.zeros((taps.shape[0], LANES - half - edge - 1), F32)
-            return jnp.concatenate([lead, taps, gap], axis=1)
-
-        return jnp.concatenate(
-            [circle(cols[:, ::-1], half_c), circle(cols, half_c), ramp(taps, half_r), ramp(taps[:, ::-1], half_r)],
-            axis=1,
-        )
-
-    table = jnp.concatenate(
-        [
-            lines(psf_cols, psf_rows, PSF_HALF, PSF_HALF),
-            lines(wavelet_taps[1:2], wavelet_taps[0:1], WAV_HALF, WAV_HALF),
-        ],
-        axis=0,
-    )
+    later = trade(later, True)
+
     (
         mats, far_band, far_mats, adjoint, wav_free, wav_touched, around_head, around_rest, back_head, back_rest,
         wav_head, wav_rest, wav_head_t, wav_rest_t,
     ) = call(
-        matrices_kernel, (channel_flags, table[:, None]),
+        matrices_kernel, (channel_flags, psf_cols, psf_rows, wavelet_taps),
         (
             ((chans, reach + height, 3 * (height + send)), BF16), ((touched, 3 * send), BF16),
             ((chans, half, 3 * send), BF16), ((chans, height, 3 * reach), BF16),
             ((height, 3 * free), BF16), ((half, 3 * touched), BF16),
             squares, squares, squares, squares, square, square, square, square,
         ),
-        1,
-    )
+        1, scratch=(pltpu.VMEM((chans + 1, 1, 4 * LANES), F32),),
+    )
+    near = trade(near, False)
     est_near, est_far, band1, sum1 = call(
         first_columns_kernel, (odd, image_start, wav_head, wav_rest),
         (side, side, own, ((height, width), F32)), 1,
     )
-    band_u, band_t, part, dual_u, dual_t, dual1, dirty, weight_sums = call(
-        first_rows_kernel,
-        (odd, est_near, est_far, near, far, mats, far_band, far_mats, dual_start, dirty_image, sum1),
-        (wavy, late_rows, own, wavy, late_rows, own, rows(reach), summed), 1,
-    )
-    data, grad = call(
-        first_gradient_kernel,
-        (part, around_head, around_rest, dirty, back_head, back_rest, adjoint), (own, own),
+    band_u, band_t, part, weight_sums = call(
+        first_rows_kernel, (est_near, est_far, near, far, mats, far_band, far_mats, sum1),
+        (wavy, late_rows, own, summed),
+    )
+    grad = call(first_gradient_kernel, (part, around_head, around_rest), (own,))[0]
+    dual_u, dual_t, dual1, data = call(
+        first_data_kernel, (odd, near, later, dual_start, dirty_image, adjoint, back_head, back_rest),
+        (wavy, late_rows, own, own), 1,
     )
     est_near, est_far = call(
         first_update_kernel,
-        (dual_u, dual_t, dual1, est_near, est_far, grad, wav_free, wav_touched, wav_head_t, wav_rest_t),
+        (dual_u, dual_t, dual1, est_near, est_far, grad, data, wav_free, wav_touched, wav_head_t, wav_rest_t),
         (side, side),
     )
     rim = est_far
@@ -668,25 +683,28 @@
                 name="publish",
             )(est_near, est_far, sums)
             result = jax.ShapeDtypeStruct((chans, 2, height, width), F32)
-            dual_u, dual_final = pl.pallas_call(
+            rest = touched - edge
+            dual_final = pl.pallas_call(
                 functools.partial(final_early_kernel, len(early)),
-                out_shape=[jax.ShapeDtypeStruct(*wavy), result],
+                out_shape=result,
                 in_specs=[SM] + [VM] * (len(early) + 3),
-                out_specs=[VM, in_hbm],
-                scratch_shapes=[pltpu.VMEM(*own), pltpu.SemaphoreType.DMA],
+                out_specs=in_hbm,
+                scratch_shapes=[
+                    pltpu.VMEM(*own), pltpu.VMEM(*rows(height - rest)), pltpu.SemaphoreType.DMA((2,))
+                ],
                 compiler_params=PARAMS,
                 name="final_early",
             )(odd, *early, radius, moved_u, moved1)
             dual_final = pl.pallas_call(
                 functools.partial(final_late_kernel, len(late)),
                 out_shape=result,
-                in_specs=[SM] + [VM] * (len(late) + 3) + [in_hbm],
+                in_specs=[SM] + [VM] * (len(late) + 2) + [in_hbm],
                 out_specs=in_hbm,
-                scratch_shapes=[pltpu.VMEM(*own), pltpu.SemaphoreType.DMA((4,))],
-                input_output_aliases={len(late) + 4: 0},
+                scratch_shapes=[pltpu.VMEM(*rows(rest)), pltpu.SemaphoreType.DMA],
+                input_output_aliases={len(late) + 3: 0},
                 compiler_params=PARAMS,
                 name="final_late",
-            )(odd, *late, radius, moved_t, dual_u, dual_final)
+            )(odd, *late, radius, moved_t, dual_final)
             break
         grad = call(gradient_kernel, (part, far, far_mats, around_head, around_rest, data, sums), (own,))[0]
         dual_u, dual1, est_near, half_far = call(

time: 130 us -> 124 us (0.954)
  waiting for transfers between devices: 38.9 us -> 30.8 us
  starting transfers between devices: 58.2 us -> 61.2 us
    ppermute x36, waiting for transfers between devices: 29 us -> 23.8 us  [gathered(): lax.ppermute(total, 'chan', [(i, i ^ k * low) for i in range(n)])]
    ppermute x14 -> x15, starting transfers between devices: 15.6 us -> 18.6 us  [trade(): return lax.ppermute(values, 'facet', pairs)]
    ppermute x14 -> x15, waiting for transfers between devices: 9.9 us -> 6.98 us  [trade(): return lax.ppermute(values, 'facet', pairs)]
    pallas_call x35 -> x36, Pallas kernels: 23.9 us -> 24.5 us  [call(): pl.pallas_call(kernel, out_shape=[jax.ShapeDtypeStruct(*shape) for shape...]
  transfers between devices with their start and end apart: 50 -> 51, of which waited for: 29 -> 31; matrix products, arithmetic and copies ran while one was open for 1% -> 0% of each run, Pallas kernels for 15% -> 17%
where the time goes in v4:
time: 124 us; the launch traced here: 122 us
  starting transfers between devices  61.2 us (49%)
  waiting for transfers between devices  30.8 us (25%)
  Pallas kernels  28.4 us (23%)
  between operations  1.33 us (1%)
    ppermute x36, starting transfers between devices, gathered(): lax.ppermute(total, 'chan', [(i, i ^ k * low) for i in range(n)])  42.6 us
    pallas_call x36, Pallas kernels, call(): pl.pallas_call(kernel, out_shape=[jax.ShapeDtypeStruct(*shape) for shape...  24.5 us
    ppermute x36, waiting for transfers between devices, gathered(): lax.ppermute(total, 'chan', [(i, i ^ k * low) for i in range(n)])  23.8 us
    ppermute x15, starting transfers between devices, trade(): return lax.ppermute(values, 'facet', pairs)  18.6 us
    ppermute x15, waiting for transfers between devices, trade(): return lax.ppermute(values, 'facet', pairs)  6.98 us
  transfers between devices with their start and end apart: 51, of which 31 were waited for; matrix products, arithmetic and copies ran while one was open for 0% of the time, Pallas kernels for 17%

profile of v4, /device:TPU:16, one launch (start us, length us, event | category | flops | bytes accessed | tf_op | source)
XLA Modules:
  0.0 122.3 jit_solution(12473347259224515603)
XLA Ops:
  0.7 1.4 %pack.1 = (f32[16,16,256]{2,1,0:T(8,128)S(1)}, f32[16,16,256]{2,1,0:T(8,128)S(1)}, f32[16,32,256]{2,1,0:T(8,128)S(1)}) custom-call(f32[16,32,256]{2,1,0:T(8,128)} %own_ref.1, f32[16,2,32,256]{3,2,1,0:T(8,128)} %start_ref.1, f32[16,32,256]{2,1,0:T(8,128)} %dirty_ref.3), custom_call_target="tpu_custom_call" | custom-call | tf_op jit(solution)/shard_map/pack/pallas_call | solution.py:606
  2.2 2.4 %collective-permute-start.2 = (f32[16,16,256]{2,1,0:T(8,128)S(1)}, f32[16,16,256]{2,1,0:T(8,128)S(1)}, u32[]{:S(2)}, u32[]{:S(2)}) collective-permute-start(f32[16,16,256]{2,1,0:T(8,128)S(1)} %get-tuple-element.137), channel_id=1, source_target_pairs={{1,2},{2,1},{3,4},{4,3},{5,6},{6,5},{9,10},{10,9},{11,12},{12,11},... | collective-permute-start | bytes 786440 | tf_op jit(solution)/shard_map/ppermute | solution.py:554
  4.7 3.1 %collective-permute-start.1 = (f32[16,16,256]{2,1,0:T(8,128)S(1)}, f32[16,16,256]{2,1,0:T(8,128)S(1)}, u32[]{:S(2)}, u32[]{:S(2)}) collective-permute-start(f32[16,16,256]{2,1,0:T(8,128)S(1)} %get-tuple-element.126), channel_id=1, source_target_pairs={{1,2},{2,1},{3,4},{4,3},{5,6},{6,5},{9,10},{10,9},{11,12},{12,11},... | collective-permute-start | bytes 786440 | tf_op jit(solution)/shard_map/ppermute | solution.py:554
  7.8 4.1 %shard_map.86 = (bf16[16,80,144]{2,1,0:T(8,128)(2,1)S(1)}, bf16[16,48]{1,0:T(8,128)(2,1)S(1)}, bf16[16,16,48]{2,1,0:T(8,128)(2,1)S(1)}, bf16[16,32,144]{2,1,0:T(...) custom-call(s32[16]{0:T(128)S(1)} %copy-done.6, ...), custom_call_target="tpu_custom_call" | custom-call | tf_op jit(solution)/shard_map/pallas_call | solution.py:52
  14.3 1.6 %shard_map.87 = (f32[16,32,256]{2,1,0:T(8,128)S(1)}, f32[16,16,256]{2,1,0:T(8,128)S(1)}, f32[16,32,256]{2,1,0:T(8,128)S(1)}, f32[16,32,256]{2,1,0:T(8,128)S(1)}) custom-call(s32[1]{0:T(128)} %bitcast.odd_ref, f32[16,32,256]{2,1,0:T(8,128)S(1)} %collective-permute-done.halo_ref, f32[16,16,256]{2,1,0:T(8,128)S(1)} %collective-permute-done.1.far_halo_ref, ...), custom_call_target="tpu_custom_call" | custom-call | tf_op jit(solution)/shard_map/pallas_call | solution.py:52
  17.1 2.0 %collective-permute-start.7 = (f32[16,16,256]{2,1,0:T(8,128)S(1)}, f32[16,16,256]{2,1,0:T(8,128)S(1)}, u32[]{:S(2)}, u32[]{:S(2)}) collective-permute-start(f32[16,16,256]{2,1,0:T(8,128)S(1)} %get-tuple-element.151.far_ref.refs_8_), channel_id=1, source_target_pairs={{1,2},{2,1},{3,4},{4,3},{5,6},{6,5},{9,10},{10,9},{11,12},{12,11},... | collective-permute-start | bytes 786440 | tf_op jit(solution)/shard_map/ppermute | solution.py:554
  19.9 2.5 %collective-permute-start.4 = (f32[144,256]{1,0:T(8,128)S(1)}, f32[144,256]{1,0:T(8,128)S(1)}, u32[]{:S(2)}, u32[]{:S(2)}) collective-permute-start(f32[144,256]{1,0:T(8,128)S(1)} %get-tuple-element.156.refs_0_), channel_id=1, source_target_pairs={{0,24},{8,16},{16,8},{24,0},{1,25},{9,17},{17,9},{25,1},{2,26},{10... | collective-permute-start | bytes 442376 | tf_op jit(solution)/shard_map/ppermute | solution.py:573
  23.4 1.4 %collective-permute-done.7.far_ref.halo_ref = f32[16,16,256]{2,1,0:T(8,128)S(1)} collective-permute-done((f32[16,16,256]{2,1,0:T(8,128)S(1)}, f32[16,16,256]{2,1,0:T(8,128)S(1)}, u32[]{:S(2)}, u32[]{:S(2)}) %collective-permute-start.7) | collective-permute-done | bytes 262176 | tf_op jit(solution)/shard_map/ppermute | solution.py:554
  25.0 1.4 %shard_map.95.refs_9_ = f32[16,32,256]{2,1,0:T(8,128)S(1)} custom-call(f32[16,32,256]{2,1,0:T(8,128)S(1)} %get-tuple-element.159.part_ref, f32[16,16,256]{2,1,0:T(8,128)S(1)} %collective-permute-done.7.far_ref.halo_ref, bf16[16,16,48]{2,1,0:T(8,128)(2,1)S(1)} %get-tuple-element.140.far_mats_ref, bf16[16,256,256]{2,1,0:T(8,128)(2,1)S(1)} %get-tuple-element.143.head_ref, ...), custom_call_target="tpu_custom_call" | custom-call | tf_op jit(solution)/shard_map/pallas_call | solution.py:52
  26.4 1.1 collective-permute-done.4.refs_1_
  27.5 3.2 %collective-permute-done.5.refs_2_ = f32[144,256]{1,0:T(8,128)S(1)} collective-permute-done((f32[144,256]{1,0:T(8,128)S(1)}, f32[144,256]{1,0:T(8,128)S(1)}, u32[]{:S(2)}, u32[]{:S(2)}) %collective-permute-start.5) | collective-permute-done | bytes 147488 | tf_op jit(solution)/shard_map/ppermute | solution.py:573
  31.5 2.4 %collective-permute-start.8 = (f32[16,256]{1,0:T(8,128)S(1)}, f32[16,256]{1,0:T(8,128)S(1)}, u32[]{:S(2)}, u32[]{:S(2)}) collective-permute-start(f32[16,256]{1,0:T(8,128)S(1)} %get-tuple-element.162._.refs_0_), channel_id=1, source_target_pairs={{0,24},{8,16},{16,8},{24,0},{1,25},{9,17},{17,9},{25,1},{2,26},{10... | collective-permute-start | bytes 49160 | tf_op jit(solution)/shard_map/ppermute | solution.py:573
  35.0 1.1 collective-permute-done.8.refs_1_
  36.2 1.5 %collective-permute-done.9.refs_2_ = f32[16,256]{1,0:T(8,128)S(1)} collective-permute-done((f32[16,256]{1,0:T(8,128)S(1)}, f32[16,256]{1,0:T(8,128)S(1)}, u32[]{:S(2)}, u32[]{:S(2)}) %collective-permute-start.9) | collective-permute-done | bytes 16416 | tf_op jit(solution)/shard_map/ppermute | solution.py:573
  38.4 1.9 %collective-permute-start.15 = (f32[16,16,256]{2,1,0:T(8,128)S(1)}, f32[16,16,256]{2,1,0:T(8,128)S(1)}, u32[]{:S(2)}, u32[]{:S(2)}) collective-permute-start(f32[16,16,256]{2,1,0:T(8,128)S(1)} %get-tuple-element.166.far_ref.refs_8_), channel_id=1, source_target_pairs={{1,2},{2,1},{3,4},{4,3},{5,6},{6,5},{9,10},{10,9},{11,12},{12,11},... | collective-permute-start | bytes 786440 | tf_op jit(solution)/shard_map/ppermute | solution.py:554
  41.1 1.5 %collective-permute-start.12 = (f32[64,256]{1,0:T(8,128)S(1)}, f32[64,256]{1,0:T(8,128)S(1)}, u32[]{:S(2)}, u32[]{:S(2)}) collective-permute-start(f32[64,256]{1,0:T(8,128)S(1)} %get-tuple-element.173.refs_0_), channel_id=1, source_target_pairs={{0,24},{8,16},{16,8},{24,0},{1,25},{9,17},{17,9},{25,1},{2,26},{10... | collective-permute-start | bytes 196616 | tf_op jit(solution)/shard_map/ppermute | solution.py:573
  43.2 1.5 %collective-permute-start.14 = (f32[64,256]{1,0:T(8,128)S(1)}, f32[64,256]{1,0:T(8,128)S(1)}, u32[]{:S(2)}, u32[]{:S(2)}) collective-permute-start(f32[64,256]{1,0:T(8,128)S(1)} %get-tuple-element.173.refs_0_), channel_id=1, source_target_pairs={{0,16},{8,24},{16,0},{24,8},{1,17},{9,25},{17,1},{25,9},{2,18},{10... | collective-permute-start | bytes 196616 | tf_op jit(solution)/shard_map/ppermute | solution.py:573
  44.6 1.5 %collective-permute-done.15.far_ref.halo_ref = f32[16,16,256]{2,1,0:T(8,128)S(1)} collective-permute-done((f32[16,16,256]{2,1,0:T(8,128)S(1)}, f32[16,16,256]{2,1,0:T(8,128)S(1)}, u32[]{:S(2)}, u32[]{:S(2)}) %collective-permute-start.15) | collective-permute-done | bytes 262176 | tf_op jit(solution)/shard_map/ppermute | solution.py:554
  46.3 1.4 %shard_map.100.refs_9_ = f32[16,32,256]{2,1,0:T(8,128)S(1)} custom-call(f32[16,32,256]{2,1,0:T(8,128)S(1)} %get-tuple-element.176.part_ref, f32[16,16,256]{2,1,0:T(8,128)S(1)} %collective-permute-done.15.far_ref.halo_ref, bf16[16,16,48]{2,1,0:T(8,128)(2,1)S(1)} %get-tuple-element.140.far_mats_ref, bf16[16,256,256]{2,1,0:T(8,128)(2,1)S(1)} %get-tuple-element.143.head_ref, ...), custom_call_target="tpu_custom_call" | custom-call | tf_op jit(solution)/shard_map/pallas_call | solution.py:52
  48.4 2.2 %collective-permute-start.16 = (f32[16,256]{1,0:T(8,128)S(1)}, f32[16,256]{1,0:T(8,128)S(1)}, u32[]{:S(2)}, u32[]{:S(2)}) collective-permute-start(f32[16,256]{1,0:T(8,128)S(1)} %get-tuple-element.179._.refs_0_), channel_id=1, source_target_pairs={{0,24},{8,16},{16,8},{24,0},{1,25},{9,17},{17,9},{25,1},{2,26},{10... | collective-permute-start | bytes 49160 | tf_op jit(solution)/shard_map/ppermute | solution.py:573
  51.9 1.1 collective-permute-done.16.refs_1_
  53.1 1.2 collective-permute-done.17.refs_2_
  55.0 2.1 %collective-permute-start.23 = (f32[16,16,256]{2,1,0:T(8,128)S(1)}, f32[16,16,256]{2,1,0:T(8,128)S(1)}, u32[]{:S(2)}, u32[]{:S(2)}) collective-permute-start(f32[16,16,256]{2,1,0:T(8,128)S(1)} %get-tuple-element.183.far_ref.refs_8_), channel_id=1, source_target_pairs={{1,2},{2,1},{3,4},{4,3},{5,6},{6,5},{9,10},{10,9},{11,12},{12,11},... | collective-permute-start | bytes 786440 | tf_op jit(solution)/shard_map/ppermute | solution.py:554
  57.9 1.8 %collective-permute-start.20 = (f32[64,256]{1,0:T(8,128)S(1)}, f32[64,256]{1,0:T(8,128)S(1)}, u32[]{:S(2)}, u32[]{:S(2)}) collective-permute-start(f32[64,256]{1,0:T(8,128)S(1)} %get-tuple-element.190.refs_0_), channel_id=1, source_target_pairs={{0,24},{8,16},{16,8},{24,0},{1,25},{9,17},{17,9},{25,1},{2,26},{10... | collective-permute-start | bytes 196616 | tf_op jit(solution)/shard_map/ppermute | solution.py:573
  60.3 1.2 collective-permute-start.22
  61.4 1.3 %collective-permute-done.23.far_ref.halo_ref = f32[16,16,256]{2,1,0:T(8,128)S(1)} collective-permute-done((f32[16,16,256]{2,1,0:T(8,128)S(1)}, f32[16,16,256]{2,1,0:T(8,128)S(1)}, u32[]{:S(2)}, u32[]{:S(2)}) %collective-permute-start.23) | collective-permute-done | bytes 262176 | tf_op jit(solution)/shard_map/ppermute | solution.py:554
  62.9 1.4 %shard_map.105.refs_9_ = f32[16,32,256]{2,1,0:T(8,128)S(1)} custom-call(f32[16,32,256]{2,1,0:T(8,128)S(1)} %get-tuple-element.193.part_ref, f32[16,16,256]{2,1,0:T(8,128)S(1)} %collective-permute-done.23.far_ref.halo_ref, bf16[16,16,48]{2,1,0:T(8,128)(2,1)S(1)} %get-tuple-element.140.far_mats_ref, bf16[16,256,256]{2,1,0:T(8,128)(2,1)S(1)} %get-tuple-element.143.head_ref, ...), custom_call_target="tpu_custom_call" | custom-call | tf_op jit(solution)/shard_map/pallas_call | solution.py:52
  65.3 2.0 %collective-permute-start.24 = (f32[16,256]{1,0:T(8,128)S(1)}, f32[16,256]{1,0:T(8,128)S(1)}, u32[]{:S(2)}, u32[]{:S(2)}) collective-permute-start(f32[16,256]{1,0:T(8,128)S(1)} %get-tuple-element.196._.refs_0_), channel_id=1, source_target_pairs={{0,24},{8,16},{16,8},{24,0},{1,25},{9,17},{17,9},{25,1},{2,26},{10... | collective-permute-start | bytes 49160 | tf_op jit(solution)/shard_map/ppermute | solution.py:573
  68.9 1.1 collective-permute-done.24.refs_1_
  70.0 1.0 collective-permute-done.25.refs_2_
  71.8 1.9 %collective-permute-start.31 = (f32[16,16,256]{2,1,0:T(8,128)S(1)}, f32[16,16,256]{2,1,0:T(8,128)S(1)}, u32[]{:S(2)}, u32[]{:S(2)}) collective-permute-start(f32[16,16,256]{2,1,0:T(8,128)S(1)} %get-tuple-element.200.far_ref.refs_8_), channel_id=1, source_target_pairs={{1,2},{2,1},{3,4},{4,3},{5,6},{6,5},{9,10},{10,9},{11,12},{12,11},... | collective-permute-start | bytes 786440 | tf_op jit(solution)/shard_map/ppermute | solution.py:554
  74.6 2.0 %collective-permute-start.28 = (f32[144,256]{1,0:T(8,128)S(1)}, f32[144,256]{1,0:T(8,128)S(1)}, u32[]{:S(2)}, u32[]{:S(2)}) collective-permute-start(f32[144,256]{1,0:T(8,128)S(1)} %get-tuple-element.207.refs_0_), channel_id=1, source_target_pairs={{0,24},{8,16},{16,8},{24,0},{1,25},{9,17},{17,9},{25,1},{2,26},{10... | collective-permute-start | bytes 442376 | tf_op jit(solution)/shard_map/ppermute | solution.py:573
  78.1 1.4 %collective-permute-done.31.far_ref.halo_ref = f32[16,16,256]{2,1,0:T(8,128)S(1)} collective-permute-done((f32[16,16,256]{2,1,0:T(8,128)S(1)}, f32[16,16,256]{2,1,0:T(8,128)S(1)}, u32[]{:S(2)}, u32[]{:S(2)}) %collective-permute-start.31) | collective-permute-done | bytes 262176 | tf_op jit(solution)/shard_map/ppermute | solution.py:554
  79.7 1.4 %shard_map.112.refs_9_ = f32[16,32,256]{2,1,0:T(8,128)S(1)} custom-call(f32[16,32,256]{2,1,0:T(8,128)S(1)} %get-tuple-element.210.part_ref, f32[16,16,256]{2,1,0:T(8,128)S(1)} %collective-permute-done.31.far_ref.halo_ref, bf16[16,16,48]{2,1,0:T(8,128)(2,1)S(1)} %get-tuple-element.140.far_mats_ref, bf16[16,256,256]{2,1,0:T(8,128)(2,1)S(1)} %get-tuple-element.143.head_ref, ...), custom_call_target="tpu_custom_call" | custom-call | tf_op jit(solution)/shard_map/pallas_call | solution.py:52
  81.1 1.2 collective-permute-done.28.refs_1_
  82.3 2.0 %collective-permute-done.29.refs_2_ = f32[144,256]{1,0:T(8,128)S(1)} collective-permute-done((f32[144,256]{1,0:T(8,128)S(1)}, f32[144,256]{1,0:T(8,128)S(1)}, u32[]{:S(2)}, u32[]{:S(2)}) %collective-permute-start.29) | collective-permute-done | bytes 147488 | tf_op jit(solution)/shard_map/ppermute | solution.py:573
  85.6 1.8 %collective-permute-start.32 = (f32[16,256]{1,0:T(8,128)S(1)}, f32[16,256]{1,0:T(8,128)S(1)}, u32[]{:S(2)}, u32[]{:S(2)}) collective-permute-start(f32[16,256]{1,0:T(8,128)S(1)} %get-tuple-element.213._.refs_0_), channel_id=1, source_target_pairs={{0,24},{8,16},{16,8},{24,0},{1,25},{9,17},{17,9},{25,1},{2,26},{10... | collective-permute-start | bytes 49160 | tf_op jit(solution)/shard_map/ppermute | solution.py:573
  88.0 1.2 collective-permute-start.34
  89.2 1.1 collective-permute-done.32.refs_1_
  91.9 2.1 %collective-permute-start.39 = (f32[16,16,256]{2,1,0:T(8,128)S(1)}, f32[16,16,256]{2,1,0:T(8,128)S(1)}, u32[]{:S(2)}, u32[]{:S(2)}) collective-permute-start(f32[16,16,256]{2,1,0:T(8,128)S(1)} %get-tuple-element.217.far_ref.refs_8_), channel_id=1, source_target_pairs={{1,2},{2,1},{3,4},{4,3},{5,6},{6,5},{9,10},{10,9},{11,12},{12,11},... | collective-permute-start | bytes 786440 | tf_op jit(solution)/shard_map/ppermute | solution.py:554
  94.8 2.0 %collective-permute-start.36 = (f32[64,256]{1,0:T(8,128)S(1)}, f32[64,256]{1,0:T(8,128)S(1)}, u32[]{:S(2)}, u32[]{:S(2)}) collective-permute-start(f32[64,256]{1,0:T(8,128)S(1)} %get-tuple-element.224.refs_0_), channel_id=1, source_target_pairs={{0,24},{8,16},{16,8},{24,0},{1,25},{9,17},{17,9},{25,1},{2,26},{10... | collective-permute-start | bytes 196616 | tf_op jit(solution)/shard_map/ppermute | solution.py:573
  98.3 1.3 %collective-permute-done.39.far_ref.halo_ref = f32[16,16,256]{2,1,0:T(8,128)S(1)} collective-permute-done((f32[16,16,256]{2,1,0:T(8,128)S(1)}, f32[16,16,256]{2,1,0:T(8,128)S(1)}, u32[]{:S(2)}, u32[]{:S(2)}) %collective-permute-start.39) | collective-permute-done | bytes 262176 | tf_op jit(solution)/shard_map/ppermute | solution.py:554
  99.8 1.4 %shard_map.117.refs_9_ = f32[16,32,256]{2,1,0:T(8,128)S(1)} custom-call(f32[16,32,256]{2,1,0:T(8,128)S(1)} %get-tuple-element.227.part_ref, f32[16,16,256]{2,1,0:T(8,128)S(1)} %collective-permute-done.39.far_ref.halo_ref, bf16[16,16,48]{2,1,0:T(8,128)(2,1)S(1)} %get-tuple-element.140.far_mats_ref, bf16[16,256,256]{2,1,0:T(8,128)(2,1)S(1)} %get-tuple-element.143.head_ref, ...), custom_call_target="tpu_custom_call" | custom-call | tf_op jit(solution)/shard_map/pallas_call | solution.py:52
  102.2 2.0 %collective-permute-start.40 = (f32[16,256]{1,0:T(8,128)S(1)}, f32[16,256]{1,0:T(8,128)S(1)}, u32[]{:S(2)}, u32[]{:S(2)}) collective-permute-start(f32[16,256]{1,0:T(8,128)S(1)} %get-tuple-element.230._.refs_0_), channel_id=1, source_target_pairs={{0,24},{8,16},{16,8},{24,0},{1,25},{9,17},{17,9},{25,1},{2,26},{10... | collective-permute-start | bytes 49160 | tf_op jit(solution)/shard_map/ppermute | solution.py:573
  105.8 1.1 collective-permute-done.40.refs_1_
  108.7 1.9 %collective-permute-start.43 = (f32[16,8,256]{2,1,0:T(8,128)S(1)}, f32[16,8,256]{2,1,0:T(8,128)S(1)}, u32[]{:S(2)}, u32[]{:S(2)}) collective-permute-start(f32[16,8,256]{2,1,0:T(8,128)S(1)} %get-tuple-element.235), channel_id=1, source_target_pairs={{1,2},{2,1},{3,4},{4,3},{5,6},{6,5},{9,10},{10,9},{11,12},{12,11},... | collective-permute-start | bytes 393224 | tf_op jit(solution)/shard_map/ppermute | solution.py:554
  111.3 2.1 %collective-permute-start.48 = (f32[64,256]{1,0:T(8,128)S(1)}, f32[64,256]{1,0:T(8,128)S(1)}, u32[]{:S(2)}, u32[]{:S(2)}) collective-permute-start(f32[64,256]{1,0:T(8,128)S(1)} %get-tuple-element.245.refs_0_), channel_id=1, source_target_pairs={{0,24},{8,16},{16,8},{24,0},{1,25},{9,17},{17,9},{25,1},{2,26},{10... | collective-permute-start | bytes 196616 | tf_op jit(solution)/shard_map/ppermute | solution.py:573
  115.2 2.0 %collective-permute-start.45 = (f32[16,256]{1,0:T(8,128)S(1)}, f32[16,256]{1,0:T(8,128)S(1)}, u32[]{:S(2)}, u32[]{:S(2)}) collective-permute-start(f32[16,256]{1,0:T(8,128)S(1)} %get-tuple-element.243._.refs_0_), channel_id=1, source_target_pairs={{0,24},{8,16},{16,8},{24,0},{1,25},{9,17},{17,9},{25,1},{2,26},{10... | collective-permute-start | bytes 49160 | tf_op jit(solution)/shard_map/ppermute | solution.py:573
  (108 shorter events, 37.5 us)
Async XLA Ops:
  2.1 10.2 %collective-permute-start = (f32[16,32,256]{2,1,0:T(8,128)S(1)}, f32[16,32,256]{2,1,0:T(8,128)S(1)}, u32[]{:S(2)}, u32[]{:S(2)}) collective-permute-start(f32[16,32,256]{2,1,0:T(8,128)S(1)} %get-tuple-element.125), channel_id=1, source_target_pairs={{0,1},{1,0},{2,3},{3,2},{4,5},{5,4},{6,7},{7,6},{8,9},{9,8},{10,11... | collective-permute-start | bytes 1572872 | tf_op jit(solution)/shard_map/ppermute | solution.py:554
  2.2 10.1 %collective-permute-start.2 = (f32[16,16,256]{2,1,0:T(8,128)S(1)}, f32[16,16,256]{2,1,0:T(8,128)S(1)}, u32[]{:S(2)}, u32[]{:S(2)}) collective-permute-start(f32[16,16,256]{2,1,0:T(8,128)S(1)} %get-tuple-element.137), channel_id=1, source_target_pairs={{1,2},{2,1},{3,4},{4,3},{5,6},{6,5},{9,10},{10,9},{11,12},{12,11},... | collective-permute-start | bytes 786440 | tf_op jit(solution)/shard_map/ppermute | solution.py:554
  4.7 9.1 %collective-permute-start.1 = (f32[16,16,256]{2,1,0:T(8,128)S(1)}, f32[16,16,256]{2,1,0:T(8,128)S(1)}, u32[]{:S(2)}, u32[]{:S(2)}) collective-permute-start(f32[16,16,256]{2,1,0:T(8,128)S(1)} %get-tuple-element.126), channel_id=1, source_target_pairs={{1,2},{2,1},{3,4},{4,3},{5,6},{6,5},{9,10},{10,9},{11,12},{12,11},... | collective-permute-start | bytes 786440 | tf_op jit(solution)/shard_map/ppermute | solution.py:554
  17.1 7.7 %collective-permute-start.7 = (f32[16,16,256]{2,1,0:T(8,128)S(1)}, f32[16,16,256]{2,1,0:T(8,128)S(1)}, u32[]{:S(2)}, u32[]{:S(2)}) collective-permute-start(f32[16,16,256]{2,1,0:T(8,128)S(1)} %get-tuple-element.151.far_ref.refs_8_), channel_id=1, source_target_pairs={{1,2},{2,1},{3,4},{4,3},{5,6},{6,5},{9,10},{10,9},{11,12},{12,11},... | collective-permute-start | bytes 786440 | tf_op jit(solution)/shard_map/ppermute | solution.py:554
  19.9 7.6 %collective-permute-start.4 = (f32[144,256]{1,0:T(8,128)S(1)}, f32[144,256]{1,0:T(8,128)S(1)}, u32[]{:S(2)}, u32[]{:S(2)}) collective-permute-start(f32[144,256]{1,0:T(8,128)S(1)} %get-tuple-element.156.refs_0_), channel_id=1, source_target_pairs={{0,24},{8,16},{16,8},{24,0},{1,25},{9,17},{17,9},{25,1},{2,26},{10... | collective-permute-start | bytes 442376 | tf_op jit(solution)/shard_map/ppermute | solution.py:573
  22.4 8.3 %collective-permute-start.5 = (f32[144,256]{1,0:T(8,128)S(1)}, f32[144,256]{1,0:T(8,128)S(1)}, u32[]{:S(2)}, u32[]{:S(2)}) collective-permute-start(f32[144,256]{1,0:T(8,128)S(1)} %get-tuple-element.156.refs_0_), channel_id=1, source_target_pairs={{0,8},{8,0},{16,24},{24,16},{1,9},{9,1},{17,25},{25,17},{2,10},{10... | collective-permute-start | bytes 442376 | tf_op jit(solution)/shard_map/ppermute | solution.py:573
  22.9 7.8 %collective-permute-start.6 = (f32[144,256]{1,0:T(8,128)S(1)}, f32[144,256]{1,0:T(8,128)S(1)}, u32[]{:S(2)}, u32[]{:S(2)}) collective-permute-start(f32[144,256]{1,0:T(8,128)S(1)} %get-tuple-element.156.refs_0_), channel_id=1, source_target_pairs={{0,16},{8,24},{16,0},{24,8},{1,17},{9,25},{17,1},{25,9},{2,18},{10... | collective-permute-start | bytes 442376 | tf_op jit(solution)/shard_map/ppermute | solution.py:573
  31.3 9.0 %collective-permute-start.11 = (f32[16,16,256]{2,1,0:T(8,128)S(1)}, f32[16,16,256]{2,1,0:T(8,128)S(1)}, u32[]{:S(2)}, u32[]{:S(2)}) collective-permute-start(f32[16,16,256]{2,1,0:T(8,128)S(1)} %get-tuple-element.163.near_ref.refs_7_), channel_id=1, source_target_pairs={{0,1},{1,0},{2,3},{3,2},{4,5},{5,4},{6,7},{7,6},{8,9},{9,8},{10,11... | collective-permute-start | bytes 786440 | tf_op jit(solution)/shard_map/ppermute | solution.py:554
  31.5 4.6 %collective-permute-start.8 = (f32[16,256]{1,0:T(8,128)S(1)}, f32[16,256]{1,0:T(8,128)S(1)}, u32[]{:S(2)}, u32[]{:S(2)}) collective-permute-start(f32[16,256]{1,0:T(8,128)S(1)} %get-tuple-element.162._.refs_0_), channel_id=1, source_target_pairs={{0,24},{8,16},{16,8},{24,0},{1,25},{9,17},{17,9},{25,1},{2,26},{10... | collective-permute-start | bytes 49160 | tf_op jit(solution)/shard_map/ppermute | solution.py:573
  33.9 3.7 %collective-permute-start.9 = (f32[16,256]{1,0:T(8,128)S(1)}, f32[16,256]{1,0:T(8,128)S(1)}, u32[]{:S(2)}, u32[]{:S(2)}) collective-permute-start(f32[16,256]{1,0:T(8,128)S(1)} %get-tuple-element.162._.refs_0_), channel_id=1, source_target_pairs={{0,8},{8,0},{16,24},{24,16},{1,9},{9,1},{17,25},{25,17},{2,10},{10... | collective-permute-start | bytes 49160 | tf_op jit(solution)/shard_map/ppermute | solution.py:573
  34.5 3.7 %collective-permute-start.10 = (f32[16,256]{1,0:T(8,128)S(1)}, f32[16,256]{1,0:T(8,128)S(1)}, u32[]{:S(2)}, u32[]{:S(2)}) collective-permute-start(f32[16,256]{1,0:T(8,128)S(1)} %get-tuple-element.162._.refs_0_), channel_id=1, source_target_pairs={{0,16},{8,24},{16,0},{24,8},{1,17},{9,25},{17,1},{25,9},{2,18},{10... | collective-permute-start | bytes 49160 | tf_op jit(solution)/shard_map/ppermute | solution.py:573
  38.4 7.7 %collective-permute-start.15 = (f32[16,16,256]{2,1,0:T(8,128)S(1)}, f32[16,16,256]{2,1,0:T(8,128)S(1)}, u32[]{:S(2)}, u32[]{:S(2)}) collective-permute-start(f32[16,16,256]{2,1,0:T(8,128)S(1)} %get-tuple-element.166.far_ref.refs_8_), channel_id=1, source_target_pairs={{1,2},{2,1},{3,4},{4,3},{5,6},{6,5},{9,10},{10,9},{11,12},{12,11},... | collective-permute-start | bytes 786440 | tf_op jit(solution)/shard_map/ppermute | solution.py:554
  41.1 6.6 %collective-permute-start.12 = (f32[64,256]{1,0:T(8,128)S(1)}, f32[64,256]{1,0:T(8,128)S(1)}, u32[]{:S(2)}, u32[]{:S(2)}) collective-permute-start(f32[64,256]{1,0:T(8,128)S(1)} %get-tuple-element.173.refs_0_), channel_id=1, source_target_pairs={{0,24},{8,16},{16,8},{24,0},{1,25},{9,17},{17,9},{25,1},{2,26},{10... | collective-permute-start | bytes 196616 | tf_op jit(solution)/shard_map/ppermute | solution.py:573
  42.6 5.1 %collective-permute-start.13 = (f32[64,256]{1,0:T(8,128)S(1)}, f32[64,256]{1,0:T(8,128)S(1)}, u32[]{:S(2)}, u32[]{:S(2)}) collective-permute-start(f32[64,256]{1,0:T(8,128)S(1)} %get-tuple-element.173.refs_0_), channel_id=1, source_target_pairs={{0,8},{8,0},{16,24},{24,16},{1,9},{9,1},{17,25},{25,17},{2,10},{10... | collective-permute-start | bytes 196616 | tf_op jit(solution)/shard_map/ppermute | solution.py:573
  43.2 4.6 %collective-permute-start.14 = (f32[64,256]{1,0:T(8,128)S(1)}, f32[64,256]{1,0:T(8,128)S(1)}, u32[]{:S(2)}, u32[]{:S(2)}) collective-permute-start(f32[64,256]{1,0:T(8,128)S(1)} %get-tuple-element.173.refs_0_), channel_id=1, source_target_pairs={{0,16},{8,24},{16,0},{24,8},{1,17},{9,25},{17,1},{25,9},{2,18},{10... | collective-permute-start | bytes 196616 | tf_op jit(solution)/shard_map/ppermute | solution.py:573
  48.3 8.8 %collective-permute-start.19 = (f32[16,16,256]{2,1,0:T(8,128)S(1)}, f32[16,16,256]{2,1,0:T(8,128)S(1)}, u32[]{:S(2)}, u32[]{:S(2)}) collective-permute-start(f32[16,16,256]{2,1,0:T(8,128)S(1)} %get-tuple-element.180.near_ref.refs_7_), channel_id=1, source_target_pairs={{0,1},{1,0},{2,3},{3,2},{4,5},{5,4},{6,7},{7,6},{8,9},{9,8},{10,11... | collective-permute-start | bytes 786440 | tf_op jit(solution)/shard_map/ppermute | solution.py:554
  48.4 4.7 %collective-permute-start.16 = (f32[16,256]{1,0:T(8,128)S(1)}, f32[16,256]{1,0:T(8,128)S(1)}, u32[]{:S(2)}, u32[]{:S(2)}) collective-permute-start(f32[16,256]{1,0:T(8,128)S(1)} %get-tuple-element.179._.refs_0_), channel_id=1, source_target_pairs={{0,24},{8,16},{16,8},{24,0},{1,25},{9,17},{17,9},{25,1},{2,26},{10... | collective-permute-start | bytes 49160 | tf_op jit(solution)/shard_map/ppermute | solution.py:573
  50.5 3.7 %collective-permute-start.17 = (f32[16,256]{1,0:T(8,128)S(1)}, f32[16,256]{1,0:T(8,128)S(1)}, u32[]{:S(2)}, u32[]{:S(2)}) collective-permute-start(f32[16,256]{1,0:T(8,128)S(1)} %get-tuple-element.179._.refs_0_), channel_id=1, source_target_pairs={{0,8},{8,0},{16,24},{24,16},{1,9},{9,1},{17,25},{25,17},{2,10},{10... | collective-permute-start | bytes 49160 | tf_op jit(solution)/shard_map/ppermute | solution.py:573
  51.1 3.7 %collective-permute-start.18 = (f32[16,256]{1,0:T(8,128)S(1)}, f32[16,256]{1,0:T(8,128)S(1)}, u32[]{:S(2)}, u32[]{:S(2)}) collective-permute-start(f32[16,256]{1,0:T(8,128)S(1)} %get-tuple-element.179._.refs_0_), channel_id=1, source_target_pairs={{0,16},{8,24},{16,0},{24,8},{1,17},{9,25},{17,1},{25,9},{2,18},{10... | collective-permute-start | bytes 49160 | tf_op jit(solution)/shard_map/ppermute | solution.py:573
  55.0 7.7 %collective-permute-start.23 = (f32[16,16,256]{2,1,0:T(8,128)S(1)}, f32[16,16,256]{2,1,0:T(8,128)S(1)}, u32[]{:S(2)}, u32[]{:S(2)}) collective-permute-start(f32[16,16,256]{2,1,0:T(8,128)S(1)} %get-tuple-element.183.far_ref.refs_8_), channel_id=1, source_target_pairs={{1,2},{2,1},{3,4},{4,3},{5,6},{6,5},{9,10},{10,9},{11,12},{12,11},... | collective-permute-start | bytes 786440 | tf_op jit(solution)/shard_map/ppermute | solution.py:554
  57.9 6.4 %collective-permute-start.20 = (f32[64,256]{1,0:T(8,128)S(1)}, f32[64,256]{1,0:T(8,128)S(1)}, u32[]{:S(2)}, u32[]{:S(2)}) collective-permute-start(f32[64,256]{1,0:T(8,128)S(1)} %get-tuple-element.190.refs_0_), channel_id=1, source_target_pairs={{0,24},{8,16},{16,8},{24,0},{1,25},{9,17},{17,9},{25,1},{2,26},{10... | collective-permute-start | bytes 196616 | tf_op jit(solution)/shard_map/ppermute | solution.py:573
  59.7 4.6 %collective-permute-start.21 = (f32[64,256]{1,0:T(8,128)S(1)}, f32[64,256]{1,0:T(8,128)S(1)}, u32[]{:S(2)}, u32[]{:S(2)}) collective-permute-start(f32[64,256]{1,0:T(8,128)S(1)} %get-tuple-element.190.refs_0_), channel_id=1, source_target_pairs={{0,8},{8,0},{16,24},{24,16},{1,9},{9,1},{17,25},{25,17},{2,10},{10... | collective-permute-start | bytes 196616 | tf_op jit(solution)/shard_map/ppermute | solution.py:573
  60.3 4.4 %collective-permute-start.22 = (f32[64,256]{1,0:T(8,128)S(1)}, f32[64,256]{1,0:T(8,128)S(1)}, u32[]{:S(2)}, u32[]{:S(2)}) collective-permute-start(f32[64,256]{1,0:T(8,128)S(1)} %get-tuple-element.190.refs_0_), channel_id=1, source_target_pairs={{0,16},{8,24},{16,0},{24,8},{1,17},{9,25},{17,1},{25,9},{2,18},{10... | collective-permute-start | bytes 196616 | tf_op jit(solution)/shard_map/ppermute | solution.py:573
  65.2 8.6 %collective-permute-start.27 = (f32[16,16,256]{2,1,0:T(8,128)S(1)}, f32[16,16,256]{2,1,0:T(8,128)S(1)}, u32[]{:S(2)}, u32[]{:S(2)}) collective-permute-start(f32[16,16,256]{2,1,0:T(8,128)S(1)} %get-tuple-element.197.near_ref.refs_7_), channel_id=1, source_target_pairs={{0,1},{1,0},{2,3},{3,2},{4,5},{5,4},{6,7},{7,6},{8,9},{9,8},{10,11... | collective-permute-start | bytes 786440 | tf_op jit(solution)/shard_map/ppermute | solution.py:554
  65.3 4.7 %collective-permute-start.24 = (f32[16,256]{1,0:T(8,128)S(1)}, f32[16,256]{1,0:T(8,128)S(1)}, u32[]{:S(2)}, u32[]{:S(2)}) collective-permute-start(f32[16,256]{1,0:T(8,128)S(1)} %get-tuple-element.196._.refs_0_), channel_id=1, source_target_pairs={{0,24},{8,16},{16,8},{24,0},{1,25},{9,17},{17,9},{25,1},{2,26},{10... | collective-permute-start | bytes 49160 | tf_op jit(solution)/shard_map/ppermute | solution.py:573
  67.3 3.7 %collective-permute-start.25 = (f32[16,256]{1,0:T(8,128)S(1)}, f32[16,256]{1,0:T(8,128)S(1)}, u32[]{:S(2)}, u32[]{:S(2)}) collective-permute-start(f32[16,256]{1,0:T(8,128)S(1)} %get-tuple-element.196._.refs_0_), channel_id=1, source_target_pairs={{0,8},{8,0},{16,24},{24,16},{1,9},{9,1},{17,25},{25,17},{2,10},{10... | collective-permute-start | bytes 49160 | tf_op jit(solution)/shard_map/ppermute | solution.py:573
  67.9 3.7 %collective-permute-start.26 = (f32[16,256]{1,0:T(8,128)S(1)}, f32[16,256]{1,0:T(8,128)S(1)}, u32[]{:S(2)}, u32[]{:S(2)}) collective-permute-start(f32[16,256]{1,0:T(8,128)S(1)} %get-tuple-element.196._.refs_0_), channel_id=1, source_target_pairs={{0,16},{8,24},{16,0},{24,8},{1,17},{9,25},{17,1},{25,9},{2,18},{10... | collective-permute-start | bytes 49160 | tf_op jit(solution)/shard_map/ppermute | solution.py:573
  71.8 7.7 %collective-permute-start.31 = (f32[16,16,256]{2,1,0:T(8,128)S(1)}, f32[16,16,256]{2,1,0:T(8,128)S(1)}, u32[]{:S(2)}, u32[]{:S(2)}) collective-permute-start(f32[16,16,256]{2,1,0:T(8,128)S(1)} %get-tuple-element.200.far_ref.refs_8_), channel_id=1, source_target_pairs={{1,2},{2,1},{3,4},{4,3},{5,6},{6,5},{9,10},{10,9},{11,12},{12,11},... | collective-permute-start | bytes 786440 | tf_op jit(solution)/shard_map/ppermute | solution.py:554
  74.6 7.7 %collective-permute-start.28 = (f32[144,256]{1,0:T(8,128)S(1)}, f32[144,256]{1,0:T(8,128)S(1)}, u32[]{:S(2)}, u32[]{:S(2)}) collective-permute-start(f32[144,256]{1,0:T(8,128)S(1)} %get-tuple-element.207.refs_0_), channel_id=1, source_target_pairs={{0,24},{8,16},{16,8},{24,0},{1,25},{9,17},{17,9},{25,1},{2,26},{10... | collective-permute-start | bytes 442376 | tf_op jit(solution)/shard_map/ppermute | solution.py:573
  76.6 7.7 %collective-permute-start.29 = (f32[144,256]{1,0:T(8,128)S(1)}, f32[144,256]{1,0:T(8,128)S(1)}, u32[]{:S(2)}, u32[]{:S(2)}) collective-permute-start(f32[144,256]{1,0:T(8,128)S(1)} %get-tuple-element.207.refs_0_), channel_id=1, source_target_pairs={{0,8},{8,0},{16,24},{24,16},{1,9},{9,1},{17,25},{25,17},{2,10},{10... | collective-permute-start | bytes 442376 | tf_op jit(solution)/shard_map/ppermute | solution.py:573
  77.1 7.8 %collective-permute-start.30 = (f32[144,256]{1,0:T(8,128)S(1)}, f32[144,256]{1,0:T(8,128)S(1)}, u32[]{:S(2)}, u32[]{:S(2)}) collective-permute-start(f32[144,256]{1,0:T(8,128)S(1)} %get-tuple-element.207.refs_0_), channel_id=1, source_target_pairs={{0,16},{8,24},{16,0},{24,8},{1,17},{9,25},{17,1},{25,9},{2,18},{10... | collective-permute-start | bytes 442376 | tf_op jit(solution)/shard_map/ppermute | solution.py:573
  85.5 8.5 %collective-permute-start.35 = (f32[16,16,256]{2,1,0:T(8,128)S(1)}, f32[16,16,256]{2,1,0:T(8,128)S(1)}, u32[]{:S(2)}, u32[]{:S(2)}) collective-permute-start(f32[16,16,256]{2,1,0:T(8,128)S(1)} %get-tuple-element.214.near_ref.refs_7_), channel_id=1, source_target_pairs={{0,1},{1,0},{2,3},{3,2},{4,5},{5,4},{6,7},{7,6},{8,9},{9,8},{10,11... | collective-permute-start | bytes 786440 | tf_op jit(solution)/shard_map/ppermute | solution.py:554
  85.6 4.7 %collective-permute-start.32 = (f32[16,256]{1,0:T(8,128)S(1)}, f32[16,256]{1,0:T(8,128)S(1)}, u32[]{:S(2)}, u32[]{:S(2)}) collective-permute-start(f32[16,256]{1,0:T(8,128)S(1)} %get-tuple-element.213._.refs_0_), channel_id=1, source_target_pairs={{0,24},{8,16},{16,8},{24,0},{1,25},{9,17},{17,9},{25,1},{2,26},{10... | collective-permute-start | bytes 49160 | tf_op jit(solution)/shard_map/ppermute | solution.py:573
  87.4 3.7 %collective-permute-start.33 = (f32[16,256]{1,0:T(8,128)S(1)}, f32[16,256]{1,0:T(8,128)S(1)}, u32[]{:S(2)}, u32[]{:S(2)}) collective-permute-start(f32[16,256]{1,0:T(8,128)S(1)} %get-tuple-element.213._.refs_0_), channel_id=1, source_target_pairs={{0,8},{8,0},{16,24},{24,16},{1,9},{9,1},{17,25},{25,17},{2,10},{10... | collective-permute-start | bytes 49160 | tf_op jit(solution)/shard_map/ppermute | solution.py:573
  88.0 3.7 %collective-permute-start.34 = (f32[16,256]{1,0:T(8,128)S(1)}, f32[16,256]{1,0:T(8,128)S(1)}, u32[]{:S(2)}, u32[]{:S(2)}) collective-permute-start(f32[16,256]{1,0:T(8,128)S(1)} %get-tuple-element.213._.refs_0_), channel_id=1, source_target_pairs={{0,16},{8,24},{16,0},{24,8},{1,17},{9,25},{17,1},{25,9},{2,18},{10... | collective-permute-start | bytes 49160 | tf_op jit(solution)/shard_map/ppermute | solution.py:573
  91.9 7.7 %collective-permute-start.39 = (f32[16,16,256]{2,1,0:T(8,128)S(1)}, f32[16,16,256]{2,1,0:T(8,128)S(1)}, u32[]{:S(2)}, u32[]{:S(2)}) collective-permute-start(f32[16,16,256]{2,1,0:T(8,128)S(1)} %get-tuple-element.217.far_ref.refs_8_), channel_id=1, source_target_pairs={{1,2},{2,1},{3,4},{4,3},{5,6},{6,5},{9,10},{10,9},{11,12},{12,11},... | collective-permute-start | bytes 786440 | tf_op jit(solution)/shard_map/ppermute | solution.py:554
  94.8 6.5 %collective-permute-start.36 = (f32[64,256]{1,0:T(8,128)S(1)}, f32[64,256]{1,0:T(8,128)S(1)}, u32[]{:S(2)}, u32[]{:S(2)}) collective-permute-start(f32[64,256]{1,0:T(8,128)S(1)} %get-tuple-element.224.refs_0_), channel_id=1, source_target_pairs={{0,24},{8,16},{16,8},{24,0},{1,25},{9,17},{17,9},{25,1},{2,26},{10... | collective-permute-start | bytes 196616 | tf_op jit(solution)/shard_map/ppermute | solution.py:573
  96.8 4.5 %collective-permute-start.37 = (f32[64,256]{1,0:T(8,128)S(1)}, f32[64,256]{1,0:T(8,128)S(1)}, u32[]{:S(2)}, u32[]{:S(2)}) collective-permute-start(f32[64,256]{1,0:T(8,128)S(1)} %get-tuple-element.224.refs_0_), channel_id=1, source_target_pairs={{0,8},{8,0},{16,24},{24,16},{1,9},{9,1},{17,25},{25,17},{2,10},{10... | collective-permute-start | bytes 196616 | tf_op jit(solution)/shard_map/ppermute | solution.py:573
  97.3 4.3 %collective-permute-start.38 = (f32[64,256]{1,0:T(8,128)S(1)}, f32[64,256]{1,0:T(8,128)S(1)}, u32[]{:S(2)}, u32[]{:S(2)}) collective-permute-start(f32[64,256]{1,0:T(8,128)S(1)} %get-tuple-element.224.refs_0_), channel_id=1, source_target_pairs={{0,16},{8,24},{16,0},{24,8},{1,17},{9,25},{17,1},{25,9},{2,18},{10... | collective-permute-start | bytes 196616 | tf_op jit(solution)/shard_map/ppermute | solution.py:573
  102.1 8.5 %collective-permute-start.44 = (f32[16,16,256]{2,1,0:T(8,128)S(1)}, f32[16,16,256]{2,1,0:T(8,128)S(1)}, u32[]{:S(2)}, u32[]{:S(2)}) collective-permute-start(f32[16,16,256]{2,1,0:T(8,128)S(1)} %get-tuple-element.231.near_ref), channel_id=1, source_target_pairs={{0,1},{1,0},{2,3},{3,2},{4,5},{5,4},{6,7},{7,6},{8,9},{9,8},{10,11... | collective-permute-start | bytes 786440 | tf_op jit(solution)/shard_map/ppermute | solution.py:554
  102.2 4.7 %collective-permute-start.40 = (f32[16,256]{1,0:T(8,128)S(1)}, f32[16,256]{1,0:T(8,128)S(1)}, u32[]{:S(2)}, u32[]{:S(2)}) collective-permute-start(f32[16,256]{1,0:T(8,128)S(1)} %get-tuple-element.230._.refs_0_), channel_id=1, source_target_pairs={{0,24},{8,16},{16,8},{24,0},{1,25},{9,17},{17,9},{25,1},{2,26},{10... | collective-permute-start | bytes 49160 | tf_op jit(solution)/shard_map/ppermute | solution.py:573
  104.7 3.7 %collective-permute-start.42 = (f32[16,256]{1,0:T(8,128)S(1)}, f32[16,256]{1,0:T(8,128)S(1)}, u32[]{:S(2)}, u32[]{:S(2)}) collective-permute-start(f32[16,256]{1,0:T(8,128)S(1)} %get-tuple-element.230._.refs_0_), channel_id=1, source_target_pairs={{0,16},{8,24},{16,0},{24,8},{1,17},{9,25},{17,1},{25,9},{2,18},{10... | collective-permute-start | bytes 49160 | tf_op jit(solution)/shard_map/ppermute | solution.py:573
  108.7 6.3 %collective-permute-start.43 = (f32[16,8,256]{2,1,0:T(8,128)S(1)}, f32[16,8,256]{2,1,0:T(8,128)S(1)}, u32[]{:S(2)}, u32[]{:S(2)}) collective-permute-start(f32[16,8,256]{2,1,0:T(8,128)S(1)} %get-tuple-element.235), channel_id=1, source_target_pairs={{1,2},{2,1},{3,4},{4,3},{5,6},{6,5},{9,10},{10,9},{11,12},{12,11},... | collective-permute-start | bytes 393224 | tf_op jit(solution)/shard_map/ppermute | solution.py:554
  111.3 6.4 %collective-permute-start.48 = (f32[64,256]{1,0:T(8,128)S(1)}, f32[64,256]{1,0:T(8,128)S(1)}, u32[]{:S(2)}, u32[]{:S(2)}) collective-permute-start(f32[64,256]{1,0:T(8,128)S(1)} %get-tuple-element.245.refs_0_), channel_id=1, source_target_pairs={{0,24},{8,16},{16,8},{24,0},{1,25},{9,17},{17,9},{25,1},{2,26},{10... | collective-permute-start | bytes 196616 | tf_op jit(solution)/shard_map/ppermute | solution.py:573
  113.4 6.2 %collective-permute-start.49 = (f32[64,256]{1,0:T(8,128)S(1)}, f32[64,256]{1,0:T(8,128)S(1)}, u32[]{:S(2)}, u32[]{:S(2)}) collective-permute-start(f32[64,256]{1,0:T(8,128)S(1)} %get-tuple-element.245.refs_0_), channel_id=1, source_target_pairs={{0,8},{8,0},{16,24},{24,16},{1,9},{9,1},{17,25},{25,17},{2,10},{10... | collective-permute-start | bytes 196616 | tf_op jit(solution)/shard_map/ppermute | solution.py:573
  113.9 5.7 %collective-permute-start.50 = (f32[64,256]{1,0:T(8,128)S(1)}, f32[64,256]{1,0:T(8,128)S(1)}, u32[]{:S(2)}, u32[]{:S(2)}) collective-permute-start(f32[64,256]{1,0:T(8,128)S(1)} %get-tuple-element.245.refs_0_), channel_id=1, source_target_pairs={{0,16},{8,24},{16,0},{24,8},{1,17},{9,25},{17,1},{25,9},{2,18},{10... | collective-permute-start | bytes 196616 | tf_op jit(solution)/shard_map/ppermute | solution.py:573
  115.2 5.4 %collective-permute-start.45 = (f32[16,256]{1,0:T(8,128)S(1)}, f32[16,256]{1,0:T(8,128)S(1)}, u32[]{:S(2)}, u32[]{:S(2)}) collective-permute-start(f32[16,256]{1,0:T(8,128)S(1)} %get-tuple-element.243._.refs_0_), channel_id=1, source_target_pairs={{0,24},{8,16},{16,8},{24,0},{1,25},{9,17},{17,9},{25,1},{2,26},{10... | collective-permute-start | bytes 49160 | tf_op jit(solution)/shard_map/ppermute | solution.py:573
  117.7 3.7 %collective-permute-start.47 = (f32[16,256]{1,0:T(8,128)S(1)}, f32[16,256]{1,0:T(8,128)S(1)}, u32[]{:S(2)}, u32[]{:S(2)}) collective-permute-start(f32[16,256]{1,0:T(8,128)S(1)} %get-tuple-element.243._.refs_0_), channel_id=1, source_target_pairs={{0,16},{8,24},{16,0},{24,8},{1,17},{9,25},{17,1},{25,9},{2,18},{10... | collective-permute-start | bytes 49160 | tf_op jit(solution)/shard_map/ppermute | solution.py:573
  (10 other events, 52.5 us)

commit v5 on v4

--- a/solution.py
+++ b/solution.py
@@ -159,7 +159,7 @@
 
 def first_data_kernel(
     odd_ref, halo_ref, far_halo_ref, start_ref, dirty_ref, adj_ref, back_head_ref, back_rest_ref,
-    dual_u_ref, dual_t_ref, dual1_ref, data_ref,
+    dual_u_ref, dual_t_ref, dual1_ref, data_ref, part_ref,
 ):
     chans, height, _ = data_ref.shape
     half, touched, free = height // 2, dual_t_ref.shape[1], dual_u_ref.shape[1]
@@ -177,11 +177,15 @@
         dual1_ref[c, :half] = jnp.where(odd, dual[:half], dual[half:])
         dual1_ref[c, half:] = jnp.where(odd, dual[half:], dual[:half])
         dirty = jnp.concatenate([before[edge:], dirty_ref[c], after[edge:]], axis=0)
-        part = jnp.dot(adj_ref[c], stacked(dirty), preferred_element_type=F32)
-        data_ref[c] = times_columns(part, back_head_ref[c], back_rest_ref[c])
+        part_ref[c] = jnp.dot(adj_ref[c], stacked(dirty), preferred_element_type=F32)
         return carry
 
+    def columns(c, carry):
+        data_ref[c] = times_columns(part_ref[c], back_head_ref[c], back_rest_ref[c])
+        return carry
+
     lax.fori_loop(0, chans, body, 0, unroll=True)
+    lax.fori_loop(0, chans, columns, 0, unroll=True)
 
 
 def squares_kernel(*refs):
@@ -364,7 +368,7 @@
         far_mats_ref[c] = far[half:]
         return carry
 
-    lax.fori_loop(0, chans, body, 0, unroll=8)
+    lax.fori_loop(0, chans, body, 0, unroll=True)
 
 
 def first_columns_kernel(odd_ref, own_ref, head_ref, rest_ref, near_ref, far_ref, band_ref, sum_ref):
@@ -394,16 +398,21 @@
     lax.fori_loop(0, part_ref.shape[0], body, 0, unroll=True)
 
 
-def gradient_kernel(part_ref, halo_ref, far_mats_ref, head_ref, rest_ref, data_ref, _, grad_ref):
+def gradient_kernel(part_ref, halo_ref, far_mats_ref, head_ref, rest_ref, data_ref, _, grad_ref, whole_ref):
     chans, height = part_ref.shape[:2]
     half = height // 2
 
+    def add_far(c, carry):
+        far = jnp.dot(far_mats_ref[c], stacked(halo_ref[c]), preferred_element_type=F32)
+        whole_ref[c, :half] = part_ref[c, :half]
+        whole_ref[c, half:] = part_ref[c, half:] + far
+        return carry
+
     def body(c, carry):
-        far = jnp.dot(far_mats_ref[c], stacked(halo_ref[c]), preferred_element_type=F32)
-        part = jnp.concatenate([part_ref[c, :half], part_ref[c, half:] + far], axis=0)
-        grad_ref[c] = times_columns(part, head_ref[c], rest_ref[c]) - data_ref[c]
+        grad_ref[c] = times_columns(whole_ref[c], head_ref[c], rest_ref[c]) - data_ref[c]
         return carry
 
+    lax.fori_loop(0, chans, add_far, 0, unroll=True)
     lax.fori_loop(0, chans, body, 0, unroll=True)
 
 
@@ -640,7 +649,7 @@
     grad = call(first_gradient_kernel, (part, around_head, around_rest), (own,))[0]
     dual_u, dual_t, dual1, data = call(
         first_data_kernel, (odd, near, later, dual_start, dirty_image, adjoint, back_head, back_rest),
-        (wavy, late_rows, own, own), 1,
+        (wavy, late_rows, own, own), 1, scratch=(pltpu.VMEM(*own),),
     )
     est_near, est_far = call(
         first_update_kernel,
@@ -706,7 +715,10 @@
                 name="final_late",
             )(odd, *late, radius, moved_t, dual_final)
             break
-        grad = call(gradient_kernel, (part, far, far_mats, around_head, around_rest, data, sums), (own,))[0]
+        grad = call(
+            gradient_kernel, (part, far, far_mats, around_head, around_rest, data, sums), (own,),
+            scratch=(pltpu.VMEM(*own),),
+        )[0]
         dual_u, dual1, est_near, half_far = call(
             functools.partial(early_kernel, len(early)),
             (*early, radius, moved_u, moved1, est_near, est_far, grad, wav_free, wav_head_t, wav_rest_t),

time: 124 us -> 123 us (level)
  Pallas kernels: 28.4 us -> 24.9 us
  waiting for transfers between devices: 30.8 us -> 33.3 us
    pallas_call x36, Pallas kernels: 24.5 us -> 20.9 us  [call(): pl.pallas_call(kernel, out_shape=[jax.ShapeDtypeStruct(*shape) for shape...]
    ppermute x36, waiting for transfers between devices: 23.8 us -> 26.4 us  [gathered(): lax.ppermute(total, 'chan', [(i, i ^ k * low) for i in range(n)])]
  transfers between devices with their start and end apart: 51 -> 51, of which waited for: 31 -> 34; matrix products, arithmetic and copies ran while one was open for 0% -> 0% of each run, Pallas kernels for 17% -> 15%
where the time goes in v5:
time: 123 us; the launch traced here: 121 us
  starting transfers between devices  61.2 us (50%)
  waiting for transfers between devices  33.3 us (27%)
  Pallas kernels  24.9 us (20%)
  between operations  1.31 us (1%)
    ppermute x36, starting transfers between devices, gathered(): lax.ppermute(total, 'chan', [(i, i ^ k * low) for i in range(n)])  42.6 us
    ppermute x36, waiting for transfers between devices, gathered(): lax.ppermute(total, 'chan', [(i, i ^ k * low) for i in range(n)])  26.4 us
    pallas_call x36, Pallas kernels, call(): pl.pallas_call(kernel, out_shape=[jax.ShapeDtypeStruct(*shape) for shape...  20.9 us
    ppermute x15, starting transfers between devices, trade(): return lax.ppermute(values, 'facet', pairs)  18.6 us
    ppermute x15, waiting for transfers between devices, trade(): return lax.ppermute(values, 'facet', pairs)  6.94 us
  transfers between devices with their start and end apart: 51, of which 34 were waited for; matrix products, arithmetic and copies ran while one was open for 0% of the time, Pallas kernels for 15%

profile of v5, /device:TPU:16, one launch (start us, length us, event | category | flops | bytes accessed | tf_op | source)
XLA Modules:
  0.0 121.3 jit_solution(6993164045092359067)
XLA Ops:
  0.7 1.4 %pack.1 = (f32[16,16,256]{2,1,0:T(8,128)S(1)}, f32[16,16,256]{2,1,0:T(8,128)S(1)}, f32[16,32,256]{2,1,0:T(8,128)S(1)}) custom-call(f32[16,32,256]{2,1,0:T(8,128)} %own_ref.1, f32[16,2,32,256]{3,2,1,0:T(8,128)} %start_ref.1, f32[16,32,256]{2,1,0:T(8,128)} %dirty_ref.3), custom_call_target="tpu_custom_call" | custom-call | tf_op jit(solution)/shard_map/pack/pallas_call | solution.py:615
  2.2 2.4 %collective-permute-start.2 = (f32[16,16,256]{2,1,0:T(8,128)S(1)}, f32[16,16,256]{2,1,0:T(8,128)S(1)}, u32[]{:S(2)}, u32[]{:S(2)}) collective-permute-start(f32[16,16,256]{2,1,0:T(8,128)S(1)} %get-tuple-element.137), channel_id=1, source_target_pairs={{1,2},{2,1},{3,4},{4,3},{5,6},{6,5},{9,10},{10,9},{11,12},{12,11},... | collective-permute-start | bytes 786440 | tf_op jit(solution)/shard_map/ppermute | solution.py:563
  4.7 3.1 %collective-permute-start.1 = (f32[16,16,256]{2,1,0:T(8,128)S(1)}, f32[16,16,256]{2,1,0:T(8,128)S(1)}, u32[]{:S(2)}, u32[]{:S(2)}) collective-permute-start(f32[16,16,256]{2,1,0:T(8,128)S(1)} %get-tuple-element.126), channel_id=1, source_target_pairs={{1,2},{2,1},{3,4},{4,3},{5,6},{6,5},{9,10},{10,9},{11,12},{12,11},... | collective-permute-start | bytes 786440 | tf_op jit(solution)/shard_map/ppermute | solution.py:563
  7.8 3.6 %shard_map.86 = (bf16[16,80,144]{2,1,0:T(8,128)(2,1)S(1)}, bf16[16,48]{1,0:T(8,128)(2,1)S(1)}, bf16[16,16,48]{2,1,0:T(8,128)(2,1)S(1)}, bf16[16,32,144]{2,1,0:T(...) custom-call(s32[16]{0:T(128)S(1)} %copy-done.6, ...), custom_call_target="tpu_custom_call" | custom-call | tf_op jit(solution)/shard_map/pallas_call | solution.py:52
  13.9 1.0 shard_map.87
  16.1 2.0 %collective-permute-start.7 = (f32[16,16,256]{2,1,0:T(8,128)S(1)}, f32[16,16,256]{2,1,0:T(8,128)S(1)}, u32[]{:S(2)}, u32[]{:S(2)}) collective-permute-start(f32[16,16,256]{2,1,0:T(8,128)S(1)} %get-tuple-element.151.far_ref.refs_8_), channel_id=1, source_target_pairs={{1,2},{2,1},{3,4},{4,3},{5,6},{6,5},{9,10},{10,9},{11,12},{12,11},... | collective-permute-start | bytes 786440 | tf_op jit(solution)/shard_map/ppermute | solution.py:563
  18.8 2.5 %collective-permute-start.4 = (f32[144,256]{1,0:T(8,128)S(1)}, f32[144,256]{1,0:T(8,128)S(1)}, u32[]{:S(2)}, u32[]{:S(2)}) collective-permute-start(f32[144,256]{1,0:T(8,128)S(1)} %get-tuple-element.156.refs_0_), channel_id=1, source_target_pairs={{0,24},{8,16},{16,8},{24,0},{1,25},{9,17},{17,9},{25,1},{2,26},{10... | collective-permute-start | bytes 442376 | tf_op jit(solution)/shard_map/ppermute | solution.py:582
  22.4 1.4 %collective-permute-done.7.far_ref.halo_ref = f32[16,16,256]{2,1,0:T(8,128)S(1)} collective-permute-done((f32[16,16,256]{2,1,0:T(8,128)S(1)}, f32[16,16,256]{2,1,0:T(8,128)S(1)}, u32[]{:S(2)}, u32[]{:S(2)}) %collective-permute-start.7) | collective-permute-done | bytes 262176 | tf_op jit(solution)/shard_map/ppermute | solution.py:563
  24.8 1.6 %collective-permute-done.4.refs_1_ = f32[144,256]{1,0:T(8,128)S(1)} collective-permute-done((f32[144,256]{1,0:T(8,128)S(1)}, f32[144,256]{1,0:T(8,128)S(1)}, u32[]{:S(2)}, u32[]{:S(2)}) %collective-permute-start.4) | collective-permute-done | bytes 147488 | tf_op jit(solution)/shard_map/ppermute | solution.py:582
  26.4 3.2 %collective-permute-done.5.refs_2_ = f32[144,256]{1,0:T(8,128)S(1)} collective-permute-done((f32[144,256]{1,0:T(8,128)S(1)}, f32[144,256]{1,0:T(8,128)S(1)}, u32[]{:S(2)}, u32[]{:S(2)}) %collective-permute-start.5) | collective-permute-done | bytes 147488 | tf_op jit(solution)/shard_map/ppermute | solution.py:582
  30.5 2.4 %collective-permute-start.8 = (f32[16,256]{1,0:T(8,128)S(1)}, f32[16,256]{1,0:T(8,128)S(1)}, u32[]{:S(2)}, u32[]{:S(2)}) collective-permute-start(f32[16,256]{1,0:T(8,128)S(1)} %get-tuple-element.162._.refs_0_), channel_id=1, source_target_pairs={{0,24},{8,16},{16,8},{24,0},{1,25},{9,17},{17,9},{25,1},{2,26},{10... | collective-permute-start | bytes 49160 | tf_op jit(solution)/shard_map/ppermute | solution.py:582
  34.0 1.1 collective-permute-done.8.refs_1_
  35.1 1.5 %collective-permute-done.9.refs_2_ = f32[16,256]{1,0:T(8,128)S(1)} collective-permute-done((f32[16,256]{1,0:T(8,128)S(1)}, f32[16,256]{1,0:T(8,128)S(1)}, u32[]{:S(2)}, u32[]{:S(2)}) %collective-permute-start.9) | collective-permute-done | bytes 16416 | tf_op jit(solution)/shard_map/ppermute | solution.py:582
  37.4 1.9 %collective-permute-start.15 = (f32[16,16,256]{2,1,0:T(8,128)S(1)}, f32[16,16,256]{2,1,0:T(8,128)S(1)}, u32[]{:S(2)}, u32[]{:S(2)}) collective-permute-start(f32[16,16,256]{2,1,0:T(8,128)S(1)} %get-tuple-element.166.far_ref.refs_8_), channel_id=1, source_target_pairs={{1,2},{2,1},{3,4},{4,3},{5,6},{6,5},{9,10},{10,9},{11,12},{12,11},... | collective-permute-start | bytes 786440 | tf_op jit(solution)/shard_map/ppermute | solution.py:563
  40.0 1.5 %collective-permute-start.12 = (f32[64,256]{1,0:T(8,128)S(1)}, f32[64,256]{1,0:T(8,128)S(1)}, u32[]{:S(2)}, u32[]{:S(2)}) collective-permute-start(f32[64,256]{1,0:T(8,128)S(1)} %get-tuple-element.173.refs_0_), channel_id=1, source_target_pairs={{0,24},{8,16},{16,8},{24,0},{1,25},{9,17},{17,9},{25,1},{2,26},{10... | collective-permute-start | bytes 196616 | tf_op jit(solution)/shard_map/ppermute | solution.py:582
  42.1 1.5 %collective-permute-start.14 = (f32[64,256]{1,0:T(8,128)S(1)}, f32[64,256]{1,0:T(8,128)S(1)}, u32[]{:S(2)}, u32[]{:S(2)}) collective-permute-start(f32[64,256]{1,0:T(8,128)S(1)} %get-tuple-element.173.refs_0_), channel_id=1, source_target_pairs={{0,16},{8,24},{16,0},{24,8},{1,17},{9,25},{17,1},{25,9},{2,18},{10... | collective-permute-start | bytes 196616 | tf_op jit(solution)/shard_map/ppermute | solution.py:582
  43.6 1.5 %collective-permute-done.15.far_ref.halo_ref = f32[16,16,256]{2,1,0:T(8,128)S(1)} collective-permute-done((f32[16,16,256]{2,1,0:T(8,128)S(1)}, f32[16,16,256]{2,1,0:T(8,128)S(1)}, u32[]{:S(2)}, u32[]{:S(2)}) %collective-permute-start.15) | collective-permute-done | bytes 262176 | tf_op jit(solution)/shard_map/ppermute | solution.py:563
  47.1 2.4 %collective-permute-start.16 = (f32[16,256]{1,0:T(8,128)S(1)}, f32[16,256]{1,0:T(8,128)S(1)}, u32[]{:S(2)}, u32[]{:S(2)}) collective-permute-start(f32[16,256]{1,0:T(8,128)S(1)} %get-tuple-element.179._.refs_0_), channel_id=1, source_target_pairs={{0,24},{8,16},{16,8},{24,0},{1,25},{9,17},{17,9},{25,1},{2,26},{10... | collective-permute-start | bytes 49160 | tf_op jit(solution)/shard_map/ppermute | solution.py:582
  50.7 1.1 collective-permute-done.16.refs_1_
  51.8 1.4 %collective-permute-done.17.refs_2_ = f32[16,256]{1,0:T(8,128)S(1)} collective-permute-done((f32[16,256]{1,0:T(8,128)S(1)}, f32[16,256]{1,0:T(8,128)S(1)}, u32[]{:S(2)}, u32[]{:S(2)}) %collective-permute-start.17) | collective-permute-done | bytes 16416 | tf_op jit(solution)/shard_map/ppermute | solution.py:582
  54.0 2.1 %collective-permute-start.23 = (f32[16,16,256]{2,1,0:T(8,128)S(1)}, f32[16,16,256]{2,1,0:T(8,128)S(1)}, u32[]{:S(2)}, u32[]{:S(2)}) collective-permute-start(f32[16,16,256]{2,1,0:T(8,128)S(1)} %get-tuple-element.183.far_ref.refs_8_), channel_id=1, source_target_pairs={{1,2},{2,1},{3,4},{4,3},{5,6},{6,5},{9,10},{10,9},{11,12},{12,11},... | collective-permute-start | bytes 786440 | tf_op jit(solution)/shard_map/ppermute | solution.py:563
  56.8 1.5 %collective-permute-start.20 = (f32[64,256]{1,0:T(8,128)S(1)}, f32[64,256]{1,0:T(8,128)S(1)}, u32[]{:S(2)}, u32[]{:S(2)}) collective-permute-start(f32[64,256]{1,0:T(8,128)S(1)} %get-tuple-element.190.refs_0_), channel_id=1, source_target_pairs={{0,24},{8,16},{16,8},{24,0},{1,25},{9,17},{17,9},{25,1},{2,26},{10... | collective-permute-start | bytes 196616 | tf_op jit(solution)/shard_map/ppermute | solution.py:582
  59.0 1.4 %collective-permute-start.22 = (f32[64,256]{1,0:T(8,128)S(1)}, f32[64,256]{1,0:T(8,128)S(1)}, u32[]{:S(2)}, u32[]{:S(2)}) collective-permute-start(f32[64,256]{1,0:T(8,128)S(1)} %get-tuple-element.190.refs_0_), channel_id=1, source_target_pairs={{0,16},{8,24},{16,0},{24,8},{1,17},{9,25},{17,1},{25,9},{2,18},{10... | collective-permute-start | bytes 196616 | tf_op jit(solution)/shard_map/ppermute | solution.py:582
  60.4 1.3 %collective-permute-done.23.far_ref.halo_ref = f32[16,16,256]{2,1,0:T(8,128)S(1)} collective-permute-done((f32[16,16,256]{2,1,0:T(8,128)S(1)}, f32[16,16,256]{2,1,0:T(8,128)S(1)}, u32[]{:S(2)}, u32[]{:S(2)}) %collective-permute-start.23) | collective-permute-done | bytes 262176 | tf_op jit(solution)/shard_map/ppermute | solution.py:563
  64.3 2.0 %collective-permute-start.24 = (f32[16,256]{1,0:T(8,128)S(1)}, f32[16,256]{1,0:T(8,128)S(1)}, u32[]{:S(2)}, u32[]{:S(2)}) collective-permute-start(f32[16,256]{1,0:T(8,128)S(1)} %get-tuple-element.196._.refs_0_), channel_id=1, source_target_pairs={{0,24},{8,16},{16,8},{24,0},{1,25},{9,17},{17,9},{25,1},{2,26},{10... | collective-permute-start | bytes 49160 | tf_op jit(solution)/shard_map/ppermute | solution.py:582
  66.8 1.0 collective-permute-start.26
  67.8 1.1 collective-permute-done.24.refs_1_
  69.0 1.0 collective-permute-done.25.refs_2_
  70.8 1.9 %collective-permute-start.31 = (f32[16,16,256]{2,1,0:T(8,128)S(1)}, f32[16,16,256]{2,1,0:T(8,128)S(1)}, u32[]{:S(2)}, u32[]{:S(2)}) collective-permute-start(f32[16,16,256]{2,1,0:T(8,128)S(1)} %get-tuple-element.200.far_ref.refs_8_), channel_id=1, source_target_pairs={{1,2},{2,1},{3,4},{4,3},{5,6},{6,5},{9,10},{10,9},{11,12},{12,11},... | collective-permute-start | bytes 786440 | tf_op jit(solution)/shard_map/ppermute | solution.py:563
  73.5 2.0 %collective-permute-start.28 = (f32[144,256]{1,0:T(8,128)S(1)}, f32[144,256]{1,0:T(8,128)S(1)}, u32[]{:S(2)}, u32[]{:S(2)}) collective-permute-start(f32[144,256]{1,0:T(8,128)S(1)} %get-tuple-element.207.refs_0_), channel_id=1, source_target_pairs={{0,24},{8,16},{16,8},{24,0},{1,25},{9,17},{17,9},{25,1},{2,26},{10... | collective-permute-start | bytes 442376 | tf_op jit(solution)/shard_map/ppermute | solution.py:582
  77.1 1.4 %collective-permute-done.31.far_ref.halo_ref = f32[16,16,256]{2,1,0:T(8,128)S(1)} collective-permute-done((f32[16,16,256]{2,1,0:T(8,128)S(1)}, f32[16,16,256]{2,1,0:T(8,128)S(1)}, u32[]{:S(2)}, u32[]{:S(2)}) %collective-permute-start.31) | collective-permute-done | bytes 262176 | tf_op jit(solution)/shard_map/ppermute | solution.py:563
  79.5 1.7 %collective-permute-done.28.refs_1_ = f32[144,256]{1,0:T(8,128)S(1)} collective-permute-done((f32[144,256]{1,0:T(8,128)S(1)}, f32[144,256]{1,0:T(8,128)S(1)}, u32[]{:S(2)}, u32[]{:S(2)}) %collective-permute-start.28) | collective-permute-done | bytes 147488 | tf_op jit(solution)/shard_map/ppermute | solution.py:582
  81.3 2.0 %collective-permute-done.29.refs_2_ = f32[144,256]{1,0:T(8,128)S(1)} collective-permute-done((f32[144,256]{1,0:T(8,128)S(1)}, f32[144,256]{1,0:T(8,128)S(1)}, u32[]{:S(2)}, u32[]{:S(2)}) %collective-permute-start.29) | collective-permute-done | bytes 147488 | tf_op jit(solution)/shard_map/ppermute | solution.py:582
  84.6 1.8 %collective-permute-start.32 = (f32[16,256]{1,0:T(8,128)S(1)}, f32[16,256]{1,0:T(8,128)S(1)}, u32[]{:S(2)}, u32[]{:S(2)}) collective-permute-start(f32[16,256]{1,0:T(8,128)S(1)} %get-tuple-element.213._.refs_0_), channel_id=1, source_target_pairs={{0,24},{8,16},{16,8},{24,0},{1,25},{9,17},{17,9},{25,1},{2,26},{10... | collective-permute-start | bytes 49160 | tf_op jit(solution)/shard_map/ppermute | solution.py:582
  86.9 1.2 collective-permute-start.34
  88.1 1.1 collective-permute-done.32.refs_1_
  90.9 2.1 %collective-permute-start.39 = (f32[16,16,256]{2,1,0:T(8,128)S(1)}, f32[16,16,256]{2,1,0:T(8,128)S(1)}, u32[]{:S(2)}, u32[]{:S(2)}) collective-permute-start(f32[16,16,256]{2,1,0:T(8,128)S(1)} %get-tuple-element.217.far_ref.refs_8_), channel_id=1, source_target_pairs={{1,2},{2,1},{3,4},{4,3},{5,6},{6,5},{9,10},{10,9},{11,12},{12,11},... | collective-permute-start | bytes 786440 | tf_op jit(solution)/shard_map/ppermute | solution.py:563
  93.7 2.0 %collective-permute-start.36 = (f32[64,256]{1,0:T(8,128)S(1)}, f32[64,256]{1,0:T(8,128)S(1)}, u32[]{:S(2)}, u32[]{:S(2)}) collective-permute-start(f32[64,256]{1,0:T(8,128)S(1)} %get-tuple-element.224.refs_0_), channel_id=1, source_target_pairs={{0,24},{8,16},{16,8},{24,0},{1,25},{9,17},{17,9},{25,1},{2,26},{10... | collective-permute-start | bytes 196616 | tf_op jit(solution)/shard_map/ppermute | solution.py:582
  96.3 1.0 collective-permute-start.38
  97.3 1.3 %collective-permute-done.39.far_ref.halo_ref = f32[16,16,256]{2,1,0:T(8,128)S(1)} collective-permute-done((f32[16,16,256]{2,1,0:T(8,128)S(1)}, f32[16,16,256]{2,1,0:T(8,128)S(1)}, u32[]{:S(2)}, u32[]{:S(2)}) %collective-permute-start.39) | collective-permute-done | bytes 262176 | tf_op jit(solution)/shard_map/ppermute | solution.py:563
  101.2 2.0 %collective-permute-start.40 = (f32[16,256]{1,0:T(8,128)S(1)}, f32[16,256]{1,0:T(8,128)S(1)}, u32[]{:S(2)}, u32[]{:S(2)}) collective-permute-start(f32[16,256]{1,0:T(8,128)S(1)} %get-tuple-element.230._.refs_0_), channel_id=1, source_target_pairs={{0,24},{8,16},{16,8},{24,0},{1,25},{9,17},{17,9},{25,1},{2,26},{10... | collective-permute-start | bytes 49160 | tf_op jit(solution)/shard_map/ppermute | solution.py:582
  104.7 1.1 collective-permute-done.40.refs_1_
  105.9 1.0 collective-permute-done.41.refs_2_
  107.7 1.9 %collective-permute-start.43 = (f32[16,8,256]{2,1,0:T(8,128)S(1)}, f32[16,8,256]{2,1,0:T(8,128)S(1)}, u32[]{:S(2)}, u32[]{:S(2)}) collective-permute-start(f32[16,8,256]{2,1,0:T(8,128)S(1)} %get-tuple-element.235), channel_id=1, source_target_pairs={{1,2},{2,1},{3,4},{4,3},{5,6},{6,5},{9,10},{10,9},{11,12},{12,11},... | collective-permute-start | bytes 393224 | tf_op jit(solution)/shard_map/ppermute | solution.py:563
  110.3 2.1 %collective-permute-start.48 = (f32[64,256]{1,0:T(8,128)S(1)}, f32[64,256]{1,0:T(8,128)S(1)}, u32[]{:S(2)}, u32[]{:S(2)}) collective-permute-start(f32[64,256]{1,0:T(8,128)S(1)} %get-tuple-element.245.refs_0_), channel_id=1, source_target_pairs={{0,24},{8,16},{16,8},{24,0},{1,25},{9,17},{17,9},{25,1},{2,26},{10... | collective-permute-start | bytes 196616 | tf_op jit(solution)/shard_map/ppermute | solution.py:582
  112.8 1.0 collective-permute-start.50
  114.1 2.0 %collective-permute-start.45 = (f32[16,256]{1,0:T(8,128)S(1)}, f32[16,256]{1,0:T(8,128)S(1)}, u32[]{:S(2)}, u32[]{:S(2)}) collective-permute-start(f32[16,256]{1,0:T(8,128)S(1)} %get-tuple-element.243._.refs_0_), channel_id=1, source_target_pairs={{0,24},{8,16},{16,8},{24,0},{1,25},{9,17},{17,9},{25,1},{2,26},{10... | collective-permute-start | bytes 49160 | tf_op jit(solution)/shard_map/ppermute | solution.py:582
  116.7 1.0 collective-permute-start.47
  (108 shorter events, 37.9 us)
Async XLA Ops:
  2.1 9.8 %collective-permute-start = (f32[16,32,256]{2,1,0:T(8,128)S(1)}, f32[16,32,256]{2,1,0:T(8,128)S(1)}, u32[]{:S(2)}, u32[]{:S(2)}) collective-permute-start(f32[16,32,256]{2,1,0:T(8,128)S(1)} %get-tuple-element.125), channel_id=1, source_target_pairs={{0,1},{1,0},{2,3},{3,2},{4,5},{5,4},{6,7},{7,6},{8,9},{9,8},{10,11... | collective-permute-start | bytes 1572872 | tf_op jit(solution)/shard_map/ppermute | solution.py:563
  2.2 9.7 %collective-permute-start.2 = (f32[16,16,256]{2,1,0:T(8,128)S(1)}, f32[16,16,256]{2,1,0:T(8,128)S(1)}, u32[]{:S(2)}, u32[]{:S(2)}) collective-permute-start(f32[16,16,256]{2,1,0:T(8,128)S(1)} %get-tuple-element.137), channel_id=1, source_target_pairs={{1,2},{2,1},{3,4},{4,3},{5,6},{6,5},{9,10},{10,9},{11,12},{12,11},... | collective-permute-start | bytes 786440 | tf_op jit(solution)/shard_map/ppermute | solution.py:563
  4.7 8.6 %collective-permute-start.1 = (f32[16,16,256]{2,1,0:T(8,128)S(1)}, f32[16,16,256]{2,1,0:T(8,128)S(1)}, u32[]{:S(2)}, u32[]{:S(2)}) collective-permute-start(f32[16,16,256]{2,1,0:T(8,128)S(1)} %get-tuple-element.126), channel_id=1, source_target_pairs={{1,2},{2,1},{3,4},{4,3},{5,6},{6,5},{9,10},{10,9},{11,12},{12,11},... | collective-permute-start | bytes 786440 | tf_op jit(solution)/shard_map/ppermute | solution.py:563
  16.1 7.7 %collective-permute-start.7 = (f32[16,16,256]{2,1,0:T(8,128)S(1)}, f32[16,16,256]{2,1,0:T(8,128)S(1)}, u32[]{:S(2)}, u32[]{:S(2)}) collective-permute-start(f32[16,16,256]{2,1,0:T(8,128)S(1)} %get-tuple-element.151.far_ref.refs_8_), channel_id=1, source_target_pairs={{1,2},{2,1},{3,4},{4,3},{5,6},{6,5},{9,10},{10,9},{11,12},{12,11},... | collective-permute-start | bytes 786440 | tf_op jit(solution)/shard_map/ppermute | solution.py:563
  18.8 7.6 %collective-permute-start.4 = (f32[144,256]{1,0:T(8,128)S(1)}, f32[144,256]{1,0:T(8,128)S(1)}, u32[]{:S(2)}, u32[]{:S(2)}) collective-permute-start(f32[144,256]{1,0:T(8,128)S(1)} %get-tuple-element.156.refs_0_), channel_id=1, source_target_pairs={{0,24},{8,16},{16,8},{24,0},{1,25},{9,17},{17,9},{25,1},{2,26},{10... | collective-permute-start | bytes 442376 | tf_op jit(solution)/shard_map/ppermute | solution.py:582
  21.3 8.3 %collective-permute-start.5 = (f32[144,256]{1,0:T(8,128)S(1)}, f32[144,256]{1,0:T(8,128)S(1)}, u32[]{:S(2)}, u32[]{:S(2)}) collective-permute-start(f32[144,256]{1,0:T(8,128)S(1)} %get-tuple-element.156.refs_0_), channel_id=1, source_target_pairs={{0,8},{8,0},{16,24},{24,16},{1,9},{9,1},{17,25},{25,17},{2,10},{10... | collective-permute-start | bytes 442376 | tf_op jit(solution)/shard_map/ppermute | solution.py:582
  21.9 7.8 %collective-permute-start.6 = (f32[144,256]{1,0:T(8,128)S(1)}, f32[144,256]{1,0:T(8,128)S(1)}, u32[]{:S(2)}, u32[]{:S(2)}) collective-permute-start(f32[144,256]{1,0:T(8,128)S(1)} %get-tuple-element.156.refs_0_), channel_id=1, source_target_pairs={{0,16},{8,24},{16,0},{24,8},{1,17},{9,25},{17,1},{25,9},{2,18},{10... | collective-permute-start | bytes 442376 | tf_op jit(solution)/shard_map/ppermute | solution.py:582
  30.3 9.0 %collective-permute-start.11 = (f32[16,16,256]{2,1,0:T(8,128)S(1)}, f32[16,16,256]{2,1,0:T(8,128)S(1)}, u32[]{:S(2)}, u32[]{:S(2)}) collective-permute-start(f32[16,16,256]{2,1,0:T(8,128)S(1)} %get-tuple-element.163.near_ref.refs_7_), channel_id=1, source_target_pairs={{0,1},{1,0},{2,3},{3,2},{4,5},{5,4},{6,7},{7,6},{8,9},{9,8},{10,11... | collective-permute-start | bytes 786440 | tf_op jit(solution)/shard_map/ppermute | solution.py:563
  30.5 4.6 %collective-permute-start.8 = (f32[16,256]{1,0:T(8,128)S(1)}, f32[16,256]{1,0:T(8,128)S(1)}, u32[]{:S(2)}, u32[]{:S(2)}) collective-permute-start(f32[16,256]{1,0:T(8,128)S(1)} %get-tuple-element.162._.refs_0_), channel_id=1, source_target_pairs={{0,24},{8,16},{16,8},{24,0},{1,25},{9,17},{17,9},{25,1},{2,26},{10... | collective-permute-start | bytes 49160 | tf_op jit(solution)/shard_map/ppermute | solution.py:582
  32.9 3.7 %collective-permute-start.9 = (f32[16,256]{1,0:T(8,128)S(1)}, f32[16,256]{1,0:T(8,128)S(1)}, u32[]{:S(2)}, u32[]{:S(2)}) collective-permute-start(f32[16,256]{1,0:T(8,128)S(1)} %get-tuple-element.162._.refs_0_), channel_id=1, source_target_pairs={{0,8},{8,0},{16,24},{24,16},{1,9},{9,1},{17,25},{25,17},{2,10},{10... | collective-permute-start | bytes 49160 | tf_op jit(solution)/shard_map/ppermute | solution.py:582
  33.4 3.7 %collective-permute-start.10 = (f32[16,256]{1,0:T(8,128)S(1)}, f32[16,256]{1,0:T(8,128)S(1)}, u32[]{:S(2)}, u32[]{:S(2)}) collective-permute-start(f32[16,256]{1,0:T(8,128)S(1)} %get-tuple-element.162._.refs_0_), channel_id=1, source_target_pairs={{0,16},{8,24},{16,0},{24,8},{1,17},{9,25},{17,1},{25,9},{2,18},{10... | collective-permute-start | bytes 49160 | tf_op jit(solution)/shard_map/ppermute | solution.py:582
  37.4 7.7 %collective-permute-start.15 = (f32[16,16,256]{2,1,0:T(8,128)S(1)}, f32[16,16,256]{2,1,0:T(8,128)S(1)}, u32[]{:S(2)}, u32[]{:S(2)}) collective-permute-start(f32[16,16,256]{2,1,0:T(8,128)S(1)} %get-tuple-element.166.far_ref.refs_8_), channel_id=1, source_target_pairs={{1,2},{2,1},{3,4},{4,3},{5,6},{6,5},{9,10},{10,9},{11,12},{12,11},... | collective-permute-start | bytes 786440 | tf_op jit(solution)/shard_map/ppermute | solution.py:563
  40.0 6.1 %collective-permute-start.12 = (f32[64,256]{1,0:T(8,128)S(1)}, f32[64,256]{1,0:T(8,128)S(1)}, u32[]{:S(2)}, u32[]{:S(2)}) collective-permute-start(f32[64,256]{1,0:T(8,128)S(1)} %get-tuple-element.173.refs_0_), channel_id=1, source_target_pairs={{0,24},{8,16},{16,8},{24,0},{1,25},{9,17},{17,9},{25,1},{2,26},{10... | collective-permute-start | bytes 196616 | tf_op jit(solution)/shard_map/ppermute | solution.py:582
  41.6 4.6 %collective-permute-start.13 = (f32[64,256]{1,0:T(8,128)S(1)}, f32[64,256]{1,0:T(8,128)S(1)}, u32[]{:S(2)}, u32[]{:S(2)}) collective-permute-start(f32[64,256]{1,0:T(8,128)S(1)} %get-tuple-element.173.refs_0_), channel_id=1, source_target_pairs={{0,8},{8,0},{16,24},{24,16},{1,9},{9,1},{17,25},{25,17},{2,10},{10... | collective-permute-start | bytes 196616 | tf_op jit(solution)/shard_map/ppermute | solution.py:582
  42.1 4.3 %collective-permute-start.14 = (f32[64,256]{1,0:T(8,128)S(1)}, f32[64,256]{1,0:T(8,128)S(1)}, u32[]{:S(2)}, u32[]{:S(2)}) collective-permute-start(f32[64,256]{1,0:T(8,128)S(1)} %get-tuple-element.173.refs_0_), channel_id=1, source_target_pairs={{0,16},{8,24},{16,0},{24,8},{1,17},{9,25},{17,1},{25,9},{2,18},{10... | collective-permute-start | bytes 196616 | tf_op jit(solution)/shard_map/ppermute | solution.py:582
  47.0 9.1 %collective-permute-start.19 = (f32[16,16,256]{2,1,0:T(8,128)S(1)}, f32[16,16,256]{2,1,0:T(8,128)S(1)}, u32[]{:S(2)}, u32[]{:S(2)}) collective-permute-start(f32[16,16,256]{2,1,0:T(8,128)S(1)} %get-tuple-element.180.near_ref.refs_7_), channel_id=1, source_target_pairs={{0,1},{1,0},{2,3},{3,2},{4,5},{5,4},{6,7},{7,6},{8,9},{9,8},{10,11... | collective-permute-start | bytes 786440 | tf_op jit(solution)/shard_map/ppermute | solution.py:563
  47.1 4.7 %collective-permute-start.16 = (f32[16,256]{1,0:T(8,128)S(1)}, f32[16,256]{1,0:T(8,128)S(1)}, u32[]{:S(2)}, u32[]{:S(2)}) collective-permute-start(f32[16,256]{1,0:T(8,128)S(1)} %get-tuple-element.179._.refs_0_), channel_id=1, source_target_pairs={{0,24},{8,16},{16,8},{24,0},{1,25},{9,17},{17,9},{25,1},{2,26},{10... | collective-permute-start | bytes 49160 | tf_op jit(solution)/shard_map/ppermute | solution.py:582
  49.5 3.7 %collective-permute-start.17 = (f32[16,256]{1,0:T(8,128)S(1)}, f32[16,256]{1,0:T(8,128)S(1)}, u32[]{:S(2)}, u32[]{:S(2)}) collective-permute-start(f32[16,256]{1,0:T(8,128)S(1)} %get-tuple-element.179._.refs_0_), channel_id=1, source_target_pairs={{0,8},{8,0},{16,24},{24,16},{1,9},{9,1},{17,25},{25,17},{2,10},{10... | collective-permute-start | bytes 49160 | tf_op jit(solution)/shard_map/ppermute | solution.py:582
  50.0 3.7 %collective-permute-start.18 = (f32[16,256]{1,0:T(8,128)S(1)}, f32[16,256]{1,0:T(8,128)S(1)}, u32[]{:S(2)}, u32[]{:S(2)}) collective-permute-start(f32[16,256]{1,0:T(8,128)S(1)} %get-tuple-element.179._.refs_0_), channel_id=1, source_target_pairs={{0,16},{8,24},{16,0},{24,8},{1,17},{9,25},{17,1},{25,9},{2,18},{10... | collective-permute-start | bytes 49160 | tf_op jit(solution)/shard_map/ppermute | solution.py:582
  54.0 7.7 %collective-permute-start.23 = (f32[16,16,256]{2,1,0:T(8,128)S(1)}, f32[16,16,256]{2,1,0:T(8,128)S(1)}, u32[]{:S(2)}, u32[]{:S(2)}) collective-permute-start(f32[16,16,256]{2,1,0:T(8,128)S(1)} %get-tuple-element.183.far_ref.refs_8_), channel_id=1, source_target_pairs={{1,2},{2,1},{3,4},{4,3},{5,6},{6,5},{9,10},{10,9},{11,12},{12,11},... | collective-permute-start | bytes 786440 | tf_op jit(solution)/shard_map/ppermute | solution.py:563
  56.8 5.9 %collective-permute-start.20 = (f32[64,256]{1,0:T(8,128)S(1)}, f32[64,256]{1,0:T(8,128)S(1)}, u32[]{:S(2)}, u32[]{:S(2)}) collective-permute-start(f32[64,256]{1,0:T(8,128)S(1)} %get-tuple-element.190.refs_0_), channel_id=1, source_target_pairs={{0,24},{8,16},{16,8},{24,0},{1,25},{9,17},{17,9},{25,1},{2,26},{10... | collective-permute-start | bytes 196616 | tf_op jit(solution)/shard_map/ppermute | solution.py:582
  58.4 4.6 %collective-permute-start.21 = (f32[64,256]{1,0:T(8,128)S(1)}, f32[64,256]{1,0:T(8,128)S(1)}, u32[]{:S(2)}, u32[]{:S(2)}) collective-permute-start(f32[64,256]{1,0:T(8,128)S(1)} %get-tuple-element.190.refs_0_), channel_id=1, source_target_pairs={{0,8},{8,0},{16,24},{24,16},{1,9},{9,1},{17,25},{25,17},{2,10},{10... | collective-permute-start | bytes 196616 | tf_op jit(solution)/shard_map/ppermute | solution.py:582
  59.0 4.7 %collective-permute-start.22 = (f32[64,256]{1,0:T(8,128)S(1)}, f32[64,256]{1,0:T(8,128)S(1)}, u32[]{:S(2)}, u32[]{:S(2)}) collective-permute-start(f32[64,256]{1,0:T(8,128)S(1)} %get-tuple-element.190.refs_0_), channel_id=1, source_target_pairs={{0,16},{8,24},{16,0},{24,8},{1,17},{9,25},{17,1},{25,9},{2,18},{10... | collective-permute-start | bytes 196616 | tf_op jit(solution)/shard_map/ppermute | solution.py:582
  64.2 8.6 %collective-permute-start.27 = (f32[16,16,256]{2,1,0:T(8,128)S(1)}, f32[16,16,256]{2,1,0:T(8,128)S(1)}, u32[]{:S(2)}, u32[]{:S(2)}) collective-permute-start(f32[16,16,256]{2,1,0:T(8,128)S(1)} %get-tuple-element.197.near_ref.refs_7_), channel_id=1, source_target_pairs={{0,1},{1,0},{2,3},{3,2},{4,5},{5,4},{6,7},{7,6},{8,9},{9,8},{10,11... | collective-permute-start | bytes 786440 | tf_op jit(solution)/shard_map/ppermute | solution.py:563
  64.3 4.7 %collective-permute-start.24 = (f32[16,256]{1,0:T(8,128)S(1)}, f32[16,256]{1,0:T(8,128)S(1)}, u32[]{:S(2)}, u32[]{:S(2)}) collective-permute-start(f32[16,256]{1,0:T(8,128)S(1)} %get-tuple-element.196._.refs_0_), channel_id=1, source_target_pairs={{0,24},{8,16},{16,8},{24,0},{1,25},{9,17},{17,9},{25,1},{2,26},{10... | collective-permute-start | bytes 49160 | tf_op jit(solution)/shard_map/ppermute | solution.py:582
  66.3 3.7 %collective-permute-start.25 = (f32[16,256]{1,0:T(8,128)S(1)}, f32[16,256]{1,0:T(8,128)S(1)}, u32[]{:S(2)}, u32[]{:S(2)}) collective-permute-start(f32[16,256]{1,0:T(8,128)S(1)} %get-tuple-element.196._.refs_0_), channel_id=1, source_target_pairs={{0,8},{8,0},{16,24},{24,16},{1,9},{9,1},{17,25},{25,17},{2,10},{10... | collective-permute-start | bytes 49160 | tf_op jit(solution)/shard_map/ppermute | solution.py:582
  66.8 3.7 %collective-permute-start.26 = (f32[16,256]{1,0:T(8,128)S(1)}, f32[16,256]{1,0:T(8,128)S(1)}, u32[]{:S(2)}, u32[]{:S(2)}) collective-permute-start(f32[16,256]{1,0:T(8,128)S(1)} %get-tuple-element.196._.refs_0_), channel_id=1, source_target_pairs={{0,16},{8,24},{16,0},{24,8},{1,17},{9,25},{17,1},{25,9},{2,18},{10... | collective-permute-start | bytes 49160 | tf_op jit(solution)/shard_map/ppermute | solution.py:582
  70.8 7.7 %collective-permute-start.31 = (f32[16,16,256]{2,1,0:T(8,128)S(1)}, f32[16,16,256]{2,1,0:T(8,128)S(1)}, u32[]{:S(2)}, u32[]{:S(2)}) collective-permute-start(f32[16,16,256]{2,1,0:T(8,128)S(1)} %get-tuple-element.200.far_ref.refs_8_), channel_id=1, source_target_pairs={{1,2},{2,1},{3,4},{4,3},{5,6},{6,5},{9,10},{10,9},{11,12},{12,11},... | collective-permute-start | bytes 786440 | tf_op jit(solution)/shard_map/ppermute | solution.py:563
  73.5 7.7 %collective-permute-start.28 = (f32[144,256]{1,0:T(8,128)S(1)}, f32[144,256]{1,0:T(8,128)S(1)}, u32[]{:S(2)}, u32[]{:S(2)}) collective-permute-start(f32[144,256]{1,0:T(8,128)S(1)} %get-tuple-element.207.refs_0_), channel_id=1, source_target_pairs={{0,24},{8,16},{16,8},{24,0},{1,25},{9,17},{17,9},{25,1},{2,26},{10... | collective-permute-start | bytes 442376 | tf_op jit(solution)/shard_map/ppermute | solution.py:582
  75.5 7.7 %collective-permute-start.29 = (f32[144,256]{1,0:T(8,128)S(1)}, f32[144,256]{1,0:T(8,128)S(1)}, u32[]{:S(2)}, u32[]{:S(2)}) collective-permute-start(f32[144,256]{1,0:T(8,128)S(1)} %get-tuple-element.207.refs_0_), channel_id=1, source_target_pairs={{0,8},{8,0},{16,24},{24,16},{1,9},{9,1},{17,25},{25,17},{2,10},{10... | collective-permute-start | bytes 442376 | tf_op jit(solution)/shard_map/ppermute | solution.py:582
  76.1 7.8 %collective-permute-start.30 = (f32[144,256]{1,0:T(8,128)S(1)}, f32[144,256]{1,0:T(8,128)S(1)}, u32[]{:S(2)}, u32[]{:S(2)}) collective-permute-start(f32[144,256]{1,0:T(8,128)S(1)} %get-tuple-element.207.refs_0_), channel_id=1, source_target_pairs={{0,16},{8,24},{16,0},{24,8},{1,17},{9,25},{17,1},{25,9},{2,18},{10... | collective-permute-start | bytes 442376 | tf_op jit(solution)/shard_map/ppermute | solution.py:582
  84.5 8.5 %collective-permute-start.35 = (f32[16,16,256]{2,1,0:T(8,128)S(1)}, f32[16,16,256]{2,1,0:T(8,128)S(1)}, u32[]{:S(2)}, u32[]{:S(2)}) collective-permute-start(f32[16,16,256]{2,1,0:T(8,128)S(1)} %get-tuple-element.214.near_ref.refs_7_), channel_id=1, source_target_pairs={{0,1},{1,0},{2,3},{3,2},{4,5},{5,4},{6,7},{7,6},{8,9},{9,8},{10,11... | collective-permute-start | bytes 786440 | tf_op jit(solution)/shard_map/ppermute | solution.py:563
  84.6 4.7 %collective-permute-start.32 = (f32[16,256]{1,0:T(8,128)S(1)}, f32[16,256]{1,0:T(8,128)S(1)}, u32[]{:S(2)}, u32[]{:S(2)}) collective-permute-start(f32[16,256]{1,0:T(8,128)S(1)} %get-tuple-element.213._.refs_0_), channel_id=1, source_target_pairs={{0,24},{8,16},{16,8},{24,0},{1,25},{9,17},{17,9},{25,1},{2,26},{10... | collective-permute-start | bytes 49160 | tf_op jit(solution)/shard_map/ppermute | solution.py:582
  86.4 3.7 %collective-permute-start.33 = (f32[16,256]{1,0:T(8,128)S(1)}, f32[16,256]{1,0:T(8,128)S(1)}, u32[]{:S(2)}, u32[]{:S(2)}) collective-permute-start(f32[16,256]{1,0:T(8,128)S(1)} %get-tuple-element.213._.refs_0_), channel_id=1, source_target_pairs={{0,8},{8,0},{16,24},{24,16},{1,9},{9,1},{17,25},{25,17},{2,10},{10... | collective-permute-start | bytes 49160 | tf_op jit(solution)/shard_map/ppermute | solution.py:582
  86.9 3.7 %collective-permute-start.34 = (f32[16,256]{1,0:T(8,128)S(1)}, f32[16,256]{1,0:T(8,128)S(1)}, u32[]{:S(2)}, u32[]{:S(2)}) collective-permute-start(f32[16,256]{1,0:T(8,128)S(1)} %get-tuple-element.213._.refs_0_), channel_id=1, source_target_pairs={{0,16},{8,24},{16,0},{24,8},{1,17},{9,25},{17,1},{25,9},{2,18},{10... | collective-permute-start | bytes 49160 | tf_op jit(solution)/shard_map/ppermute | solution.py:582
  90.9 7.7 %collective-permute-start.39 = (f32[16,16,256]{2,1,0:T(8,128)S(1)}, f32[16,16,256]{2,1,0:T(8,128)S(1)}, u32[]{:S(2)}, u32[]{:S(2)}) collective-permute-start(f32[16,16,256]{2,1,0:T(8,128)S(1)} %get-tuple-element.217.far_ref.refs_8_), channel_id=1, source_target_pairs={{1,2},{2,1},{3,4},{4,3},{5,6},{6,5},{9,10},{10,9},{11,12},{12,11},... | collective-permute-start | bytes 786440 | tf_op jit(solution)/shard_map/ppermute | solution.py:563
  93.7 5.9 %collective-permute-start.36 = (f32[64,256]{1,0:T(8,128)S(1)}, f32[64,256]{1,0:T(8,128)S(1)}, u32[]{:S(2)}, u32[]{:S(2)}) collective-permute-start(f32[64,256]{1,0:T(8,128)S(1)} %get-tuple-element.224.refs_0_), channel_id=1, source_target_pairs={{0,24},{8,16},{16,8},{24,0},{1,25},{9,17},{17,9},{25,1},{2,26},{10... | collective-permute-start | bytes 196616 | tf_op jit(solution)/shard_map/ppermute | solution.py:582
  95.7 4.3 %collective-permute-start.37 = (f32[64,256]{1,0:T(8,128)S(1)}, f32[64,256]{1,0:T(8,128)S(1)}, u32[]{:S(2)}, u32[]{:S(2)}) collective-permute-start(f32[64,256]{1,0:T(8,128)S(1)} %get-tuple-element.224.refs_0_), channel_id=1, source_target_pairs={{0,8},{8,0},{16,24},{24,16},{1,9},{9,1},{17,25},{25,17},{2,10},{10... | collective-permute-start | bytes 196616 | tf_op jit(solution)/shard_map/ppermute | solution.py:582
  96.3 4.3 %collective-permute-start.38 = (f32[64,256]{1,0:T(8,128)S(1)}, f32[64,256]{1,0:T(8,128)S(1)}, u32[]{:S(2)}, u32[]{:S(2)}) collective-permute-start(f32[64,256]{1,0:T(8,128)S(1)} %get-tuple-element.224.refs_0_), channel_id=1, source_target_pairs={{0,16},{8,24},{16,0},{24,8},{1,17},{9,25},{17,1},{25,9},{2,18},{10... | collective-permute-start | bytes 196616 | tf_op jit(solution)/shard_map/ppermute | solution.py:582
  101.1 8.5 %collective-permute-start.44 = (f32[16,16,256]{2,1,0:T(8,128)S(1)}, f32[16,16,256]{2,1,0:T(8,128)S(1)}, u32[]{:S(2)}, u32[]{:S(2)}) collective-permute-start(f32[16,16,256]{2,1,0:T(8,128)S(1)} %get-tuple-element.231.near_ref), channel_id=1, source_target_pairs={{0,1},{1,0},{2,3},{3,2},{4,5},{5,4},{6,7},{7,6},{8,9},{9,8},{10,11... | collective-permute-start | bytes 786440 | tf_op jit(solution)/shard_map/ppermute | solution.py:563
  101.2 4.7 %collective-permute-start.40 = (f32[16,256]{1,0:T(8,128)S(1)}, f32[16,256]{1,0:T(8,128)S(1)}, u32[]{:S(2)}, u32[]{:S(2)}) collective-permute-start(f32[16,256]{1,0:T(8,128)S(1)} %get-tuple-element.230._.refs_0_), channel_id=1, source_target_pairs={{0,24},{8,16},{16,8},{24,0},{1,25},{9,17},{17,9},{25,1},{2,26},{10... | collective-permute-start | bytes 49160 | tf_op jit(solution)/shard_map/ppermute | solution.py:582
  103.2 3.7 %collective-permute-start.41 = (f32[16,256]{1,0:T(8,128)S(1)}, f32[16,256]{1,0:T(8,128)S(1)}, u32[]{:S(2)}, u32[]{:S(2)}) collective-permute-start(f32[16,256]{1,0:T(8,128)S(1)} %get-tuple-element.230._.refs_0_), channel_id=1, source_target_pairs={{0,8},{8,0},{16,24},{24,16},{1,9},{9,1},{17,25},{25,17},{2,10},{10... | collective-permute-start | bytes 49160 | tf_op jit(solution)/shard_map/ppermute | solution.py:582
  107.7 6.3 %collective-permute-start.43 = (f32[16,8,256]{2,1,0:T(8,128)S(1)}, f32[16,8,256]{2,1,0:T(8,128)S(1)}, u32[]{:S(2)}, u32[]{:S(2)}) collective-permute-start(f32[16,8,256]{2,1,0:T(8,128)S(1)} %get-tuple-element.235), channel_id=1, source_target_pairs={{1,2},{2,1},{3,4},{4,3},{5,6},{6,5},{9,10},{10,9},{11,12},{12,11},... | collective-permute-start | bytes 393224 | tf_op jit(solution)/shard_map/ppermute | solution.py:563
  110.3 6.4 %collective-permute-start.48 = (f32[64,256]{1,0:T(8,128)S(1)}, f32[64,256]{1,0:T(8,128)S(1)}, u32[]{:S(2)}, u32[]{:S(2)}) collective-permute-start(f32[64,256]{1,0:T(8,128)S(1)} %get-tuple-element.245.refs_0_), channel_id=1, source_target_pairs={{0,24},{8,16},{16,8},{24,0},{1,25},{9,17},{17,9},{25,1},{2,26},{10... | collective-permute-start | bytes 196616 | tf_op jit(solution)/shard_map/ppermute | solution.py:582
  112.4 6.2 %collective-permute-start.49 = (f32[64,256]{1,0:T(8,128)S(1)}, f32[64,256]{1,0:T(8,128)S(1)}, u32[]{:S(2)}, u32[]{:S(2)}) collective-permute-start(f32[64,256]{1,0:T(8,128)S(1)} %get-tuple-element.245.refs_0_), channel_id=1, source_target_pairs={{0,8},{8,0},{16,24},{24,16},{1,9},{9,1},{17,25},{25,17},{2,10},{10... | collective-permute-start | bytes 196616 | tf_op jit(solution)/shard_map/ppermute | solution.py:582
  112.8 5.7 %collective-permute-start.50 = (f32[64,256]{1,0:T(8,128)S(1)}, f32[64,256]{1,0:T(8,128)S(1)}, u32[]{:S(2)}, u32[]{:S(2)}) collective-permute-start(f32[64,256]{1,0:T(8,128)S(1)} %get-tuple-element.245.refs_0_), channel_id=1, source_target_pairs={{0,16},{8,24},{16,0},{24,8},{1,17},{9,25},{17,1},{25,9},{2,18},{10... | collective-permute-start | bytes 196616 | tf_op jit(solution)/shard_map/ppermute | solution.py:582
  114.1 5.4 %collective-permute-start.45 = (f32[16,256]{1,0:T(8,128)S(1)}, f32[16,256]{1,0:T(8,128)S(1)}, u32[]{:S(2)}, u32[]{:S(2)}) collective-permute-start(f32[16,256]{1,0:T(8,128)S(1)} %get-tuple-element.243._.refs_0_), channel_id=1, source_target_pairs={{0,24},{8,16},{16,8},{24,0},{1,25},{9,17},{17,9},{25,1},{2,26},{10... | collective-permute-start | bytes 49160 | tf_op jit(solution)/shard_map/ppermute | solution.py:582
  116.7 3.7 %collective-permute-start.47 = (f32[16,256]{1,0:T(8,128)S(1)}, f32[16,256]{1,0:T(8,128)S(1)}, u32[]{:S(2)}, u32[]{:S(2)}) collective-permute-start(f32[16,256]{1,0:T(8,128)S(1)} %get-tuple-element.243._.refs_0_), channel_id=1, source_target_pairs={{0,16},{8,24},{16,0},{24,8},{1,17},{9,25},{17,1},{25,9},{2,18},{10... | collective-permute-start | bytes 49160 | tf_op jit(solution)/shard_map/ppermute | solution.py:582
  (10 other events, 52.1 us)
